TPU v7x, 32 devices: a whole 2x2x4 slice. The times are simulated.
32 devices in a mesh: ctx: 8 (over y, x, core), tp: 4 (over z).
Axes of the slice: x: 2, y: 2, z: 4, core: 2. Of those that a mesh axis runs over, the one named last changes fastest.
Arguments:
- query_rows: bfloat16 [4096, 4096], P('ctx', 'tp'), may hold values from -6 to 6
- key_rows: bfloat16 [4096, 4096], P('ctx', 'tp'), may hold values from -6 to 6
- value_rows: bfloat16 [4096, 4096], P('ctx', 'tp'), may hold values from -6 to 6
- short_weight: float32 [3, 3, 4096], P(None, None, 'tp'), may hold values from -3 to 3
- skip_gain: float32 [4096], P('tp'), may hold values from 0.5 to 1.5
- filter_taps: bfloat16 [4096, 4096], P('tp', 'ctx'), may hold values from 0 to 0.4
- out_weight: bfloat16 [4096, 4096], P('tp'), may hold values from -0.09375 to 0.09375
Outputs:
- layer_out: bfloat16 [4096, 4096], P('ctx', 'tp')
All inputs are finite; a program needn't handle non-finite values.
Results may differ from a plain program's by a relative error of at most 0.017.
Values may be sent and summed in bfloat16 or wider, within the bound.
No kernel may reach another device: no remote copies, remote signals or barrier semaphores. Data moves between devices by JAX's collectives and lax.ppermute only.
A program may use at most 192 MiB of HBM per device.

v0:
```python
from functools import partial
import math

import jax
import jax.numpy as jnp
from jax import lax
from jax.sharding import PartitionSpec as P

TRIPLE = lax.Precision.HIGH


def passed_along(block, axis, distance):
    devices = range(lax.axis_size(axis))
    route = [(i - distance, i) for i in devices if i - distance in devices]
    return lax.ppermute(block, axis, route)


def angle_table(left, right, offset, period):
    rows = lax.broadcasted_iota(jnp.int32, (left, right), 0)
    cols = lax.broadcasted_iota(jnp.int32, (left, right), 1) + offset
    turns = rows * cols % period
    return turns.astype(jnp.float32) * (2.0 * math.pi / period)


def inner_spectrum(rows, table_high, table_low):
    upper = jnp.dot(rows, table_high, preferred_element_type=jnp.float32)
    lower = jnp.dot(rows, table_low, preferred_element_type=jnp.float32)
    return upper + lower


def block_mix(real_component, imaginary_component, cosine_lookup, sine_lookup, sign):
    multiplier = partial(jnp.einsum, precision=TRIPLE, preferred_element_type=jnp.float32)
    cosine_real = multiplier("id,rdy->riy", cosine_lookup, real_component)
    cosine_imaginary = multiplier("id,rdy->riy", cosine_lookup, imaginary_component)
    sine_real = multiplier("id,rdy->riy", sine_lookup, real_component)
    sine_imaginary = multiplier("id,rdy->riy", sine_lookup, imaginary_component)
    return (cosine_real + sign * sine_imaginary, cosine_imaginary - sign * sine_real)


def per_device(query_rows, key_rows, value_rows, short_weight, skip_gain, filter_taps, out_weight):
    span = query_rows.shape[0]
    chans = query_rows.shape[1]
    blocks = lax.axis_size("ctx")
    group = chans // blocks
    period = 2 * span
    padded = 2 * blocks
    forward = angle_table(span, period, 0, period)
    forward = jnp.concatenate([jnp.cos(forward), -jnp.sin(forward)], axis=1)
    table_high = forward.astype(jnp.bfloat16)
    table_low = (forward - table_high.astype(jnp.float32)).astype(jnp.bfloat16)
    parity = 1.0 - 2.0 * (jnp.arange(period) % 2).astype(jnp.float32)
    parity = jnp.concatenate([parity, parity])
    stacked = jnp.stack([query_rows, key_rows, value_rows])
    rims = passed_along(stacked[:, -2:, :], "ctx", 1)
    extended = jnp.concatenate([rims, stacked], axis=1).astype(jnp.float32)
    mixed = (
        short_weight[0][:, None, :] * extended[:, 2:]
        + short_weight[1][:, None, :] * extended[:, 1:-1]
        + short_weight[2][:, None, :] * extended[:, :span]
    )
    gated_in = (mixed[1] * mixed[2]).astype(jnp.bfloat16)
    gated_t = gated_in.T
    inputs_local, taps_local = (
        lax.all_to_all(gated_t, "ctx", split_axis=0, concat_axis=1, tiled=True),
        lax.all_to_all(filter_taps, "ctx", split_axis=0, concat_axis=1, tiled=True),
    )
    spectra = inner_spectrum(
        taps_local.reshape(group * blocks, span), table_high, table_low
    ).reshape(group, blocks, 2 * period)
    earlier = jnp.concatenate(
        [jnp.zeros((group, 1, 2 * period), jnp.float32), spectra[:, :-1]], axis=1
    )
    kernel_spec = earlier + parity * spectra
    input_spec = inner_spectrum(
        inputs_local.reshape(group * blocks, span), table_high, table_low
    ).reshape(group, blocks, 2 * period)
    block_angle = angle_table(padded, blocks, 0, padded)
    cos_fwd = jnp.cos(block_angle)
    sin_fwd = jnp.sin(block_angle)
    input_re, input_im = block_mix(
        input_spec[..., :period], input_spec[..., period:], cos_fwd, sin_fwd, 1.0
    )
    kernel_re, kernel_im = block_mix(
        kernel_spec[..., :period], kernel_spec[..., period:], cos_fwd, sin_fwd, 1.0
    )
    product_re = input_re * kernel_re - input_im * kernel_im
    product_im = input_re * kernel_im + input_im * kernel_re
    back_angle = angle_table(blocks, padded, 0, padded)
    out_re, out_im = block_mix(
        product_re, product_im, jnp.cos(back_angle), jnp.sin(back_angle), -1.0
    )
    inverse = angle_table(period, span, span, period)
    inverse = jnp.concatenate([jnp.cos(inverse), -jnp.sin(inverse)], axis=0) * (
        1.0 / (period * padded)
    )
    joined = jnp.concatenate([out_re, out_im], axis=2).reshape(group * blocks, 2 * period)
    long_local = jnp.dot(
        joined, inverse, precision=TRIPLE, preferred_element_type=jnp.float32
    ).reshape(group, blocks * span)
    long_t = lax.all_to_all(
        long_local.astype(jnp.bfloat16), "ctx", split_axis=1, concat_axis=0, tiled=True
    ).astype(long_local.dtype)
    conv_t = (long_t + skip_gain[:, None] * gated_t.astype(jnp.float32)).astype(jnp.bfloat16)
    gated_out = (mixed[0].T * conv_t.astype(jnp.float32)).astype(jnp.bfloat16)
    term = lax.dot_general(
        gated_out, out_weight, (((0,), (0,)), ((), ())), preferred_element_type=jnp.float32
    )
    return lax.psum_scatter(term.astype(jnp.bfloat16), "tp", scatter_dimension=1, tiled=True)


def solution(mesh):
    placed = (
        P("ctx", "tp"),
        P("ctx", "tp"),
        P("ctx", "tp"),
        P(None, None, "tp"),
        P("tp"),
        P("tp", "ctx"),
        P("tp", None),
    )
    return jax.shard_map(
        per_device, mesh=mesh, in_specs=placed, out_specs=P("ctx", "tp"), check_vma=False
    )
```

profile of v0, /device:TPU:0, one launch (start us, length us, event | category | flops | bytes accessed | tf_op | source)
XLA Modules:
  0.0 309.1 jit_solution(8349163507218990081)
XLA Ops:
  6.5 1.5 copy.31
  8.0 1.9 copy.32
  9.9 1.9 copy.33
  11.8 0.0 copy-start.7
  11.8 1.2 pad_maximum_fusion.1
  13.1 1.4 copy.34
  14.5 2.4 collective-permute-start
  16.9 5.0 %all-to-all-start.1 = ((bf16[8,128,512]{2,1,0:T(8,128)(2,1)}), bf16[8,128,512]{2,1,0:T(8,128)(2,1)S(1)}, u32[]{:S(2)}, u32[]{:S(2)}) async-start(bf16[8,128,512]{2,1,0:T(8,128)(2,1)} %bitcast.120), calls=%async_computation.1 | async-start | bytes 2097152 | tf_op jit(solution)/shard_map/all_to_all | solution.py:65
  21.9 9.1 %sine_negate_fusion.1 = (f32[512,1024]{1,0:T(8,128)S(1)}, f32[512,1024]{1,0:T(8,128)}) fusion(), kind=kLoop, calls=%fused_computation.72 | loop fusion | flops 7864320 | bytes 4194304 | tf_op jit(solution)/shard_map/neg | solution.py:48
  31.0 9.4 %fusion.67 = (f32[1024,512]{1,0:T(8,128)}, f32[1024,512]{1,0:T(8,128)}) fusion(s32[512]{0:T(512)S(1)} %iota_add_fusion), kind=kLoop, calls=%fused_computation.84 | loop fusion | flops 7864320 | bytes 4196352 | tf_op jit(solution)/shard_map/cos | solution.py:93
  40.4 0.0 collective-permute-done
  40.4 1.2 copy.35
  41.6 4.3 %maximum_convert_fusion = f32[3,514,1024]{1,2,0:T(8,128)S(1)} fusion(bf16[1,512,1024]{1,2,0:T(8,128)(2,1)} %bitcast.118, bf16[1,512,1024]{1,2,0:T(8,128)(2,1)} %bitcast.116, bf16[1,512,1024]{1,2,0:T(8,128)(2,1)} %bitcast.114, bf16[3,2,1024]{1,2,0:T(8,128)(2,1)} %copy.35), kind=kLoop, calls=%fused_computation.47 | loop fusion | flops 12632064 | bytes 9474048 | tf_op jit(solution)/shard_map/convert_element_type | solution.py:55
  45.9 5.6 %fusion.12 = f32[3,512,1024]{1,2,0:T(8,128)S(1)} fusion(f32[3,514,1024]{1,2,0:T(8,128)S(1)} %maximum_convert_fusion, f32[3,1024]{1,0:T(4,128)S(1)} %get-tuple-element.8, f32[3,1024]{1,0:T(4,128)S(1)} %get-tuple-element.9, f32[3,1024]{1,0:T(4,128)S(1)} %get-tuple-element.7), kind=kLoop, calls=%fused_computation.18 | loop fusion | flops 7864320 | bytes 25202688 | tf_op jit(solution)/shard_map/add | solution.py:57
  51.5 2.6 copy-done.4
  54.2 1.3 fusion.45
  55.5 0.0 all-to-all-done.1
  55.5 4.2 %all-to-all-start = ((bf16[8,128,512]{2,1,0:T(8,128)(2,1)}), bf16[8,128,512]{2,1,0:T(8,128)(2,1)}, u32[]{:S(2)}, u32[]{:S(2)}) async-start(bf16[8,128,512]{2,1,0:T(8,128)(2,1)} %bitcast.119), calls=%async_computation | async-start | bytes 2097152 | tf_op jit(solution)/shard_map/all_to_all | solution.py:64
  59.7 0.6 reduce-scatter.2.cloned.1.call-start
  60.3 4.2 %fusion.61 = f32[2048,1024]{0,1:T(8,128)S(1)} fusion(bf16[128,8,512]{2,0,1:T(8,128)(2,1)S(1)} %bitcast.111, f32[512,1024]{1,0:T(8,128)S(1)} %get-tuple-element.12, f32[512,1024]{1,0:T(8,128)} %get-tuple-element.13), kind=kOutput, calls=%fused_computation.78 | convolution fusion | flops 2151677952 | bytes 13631488 | tf_op jit(solution)/shard_map/dot_general | solution.py:26
  64.5 5.9 %add_bitcast_fusion = f32[128,8,2048]{2,1,0:T(8,128)} fusion(f32[2048,1024]{0,1:T(8,128)S(1)} %fusion.61, bf16[128,8,512]{2,0,1:T(8,128)(2,1)S(1)} %bitcast.112, f32[512,1024]{1,0:T(8,128)S(1)} %get-tuple-element.12, f32[512,1024]{1,0:T(8,128)S(1)} %copy-done.2), kind=kOutput, calls=%fused_computation.15 | convolution fusion | flops 2154823680 | bytes 22020096 | tf_op jit(solution)/shard_map/dot_general | solution.py:27
  70.4 12.0 %multiply_add_fusion.1 = f32[128,8,2048]{2,1,0:T(8,128)} fusion(f32[128,8,2048]{2,1,0:T(8,128)} %add_bitcast_fusion, f32[128,7,2048]{2,1,0:T(8,128)} %bitcast.108, f32[2048]{0:T(1024)S(1)} %pad_maximum_fusion.3), kind=kLoop, calls=%fused_computation.14 | loop fusion | flops 4194304 | bytes 24125440 | tf_op jit(solution)/shard_map/add | solution.py:73
  82.4 11.2 %fusion.20 = f32[128,1024,16]{1,2,0:T(8,128)} fusion(f32[128,8,2048]{2,1,0:T(8,128)} %multiply_add_fusion.1), kind=kOutput, calls=%fused_computation.33 | convolution fusion | flops 100665088 | bytes 12582912 | tf_op jit(solution)/shard_map/id,rdy->riy/dot_general | solution.py:36
  93.6 6.8 %fusion.22 = f32[128,1024,16]{1,2,0:T(8,128)} fusion(f32[128,8,2048]{2,1,0:T(8,128)S(1)} %copy-done), kind=kOutput, calls=%fused_computation.35 | convolution fusion | flops 100665088 | bytes 12582912 | tf_op jit(solution)/shard_map/id,rdy->riy/dot_general | solution.py:35
  100.4 6.6 %fusion.24 = f32[128,1024,16]{1,2,0:T(8,128)} fusion(f32[128,8,2048]{2,1,0:T(8,128)S(1)} %copy-done), kind=kOutput, calls=%fused_computation.37 | convolution fusion | flops 100665088 | bytes 12582912 | tf_op jit(solution)/shard_map/id,rdy->riy/dot_general | solution.py:33
  107.1 0.0 all-to-all-done
  107.1 4.5 %fusion.65 = f32[1024,2048]{1,0:T(8,128)S(1)} fusion(bf16[128,8,512]{2,0,1:T(8,128)(2,1)} %bitcast.11, f32[512,1024]{1,0:T(8,128)S(1)} %get-tuple-element.12, f32[512,1024]{1,0:T(8,128)} %get-tuple-element.13), kind=kOutput, calls=%fused_computation.82 | convolution fusion | flops 2151677952 | bytes 13631488 | tf_op jit(solution)/shard_map/dot_general | solution.py:26
  111.6 3.9 %add_bitcast_fusion.1 = f32[128,8,2048]{2,1,0:T(8,128)S(1)} fusion(f32[1024,2048]{1,0:T(8,128)S(1)} %fusion.65, bf16[128,8,512]{2,0,1:T(8,128)(2,1)} %bitcast.11, f32[512,1024]{1,0:T(8,128)S(1)} %get-tuple-element.12, f32[512,1024]{1,0:T(8,128)S(1)} %copy-done.3), kind=kOutput, calls=%fused_computation.16 | convolution fusion | flops 2154823680 | bytes 22020096 | tf_op jit(solution)/shard_map/dot_general | solution.py:27
  115.5 6.7 %fusion.26 = f32[128,1024,16]{1,2,0:T(8,128)} fusion(f32[128,8,2048]{2,1,0:T(8,128)S(1)} %add_bitcast_fusion.1), kind=kOutput, calls=%fused_computation.39 | convolution fusion | flops 100665088 | bytes 12582912 | tf_op jit(solution)/shard_map/id,rdy->riy/dot_general | solution.py:34
  122.2 6.6 %fusion.28 = f32[128,1024,16]{1,2,0:T(8,128)} fusion(f32[128,8,2048]{2,1,0:T(8,128)S(1)} %add_bitcast_fusion.1), kind=kOutput, calls=%fused_computation.41 | convolution fusion | flops 100665088 | bytes 12582912 | tf_op jit(solution)/shard_map/id,rdy->riy/dot_general | solution.py:36
  128.8 6.9 %fusion.30 = f32[128,1024,16]{1,2,0:T(8,128)} fusion(f32[128,8,2048]{2,1,0:T(8,128)S(1)} %add_bitcast_fusion.1), kind=kOutput, calls=%fused_computation.43 | convolution fusion | flops 100665088 | bytes 12582912 | tf_op jit(solution)/shard_map/id,rdy->riy/dot_general | solution.py:35
  135.7 6.6 %fusion.32 = f32[128,1024,16]{1,2,0:T(8,128)} fusion(f32[128,8,2048]{2,1,0:T(8,128)S(1)} %add_bitcast_fusion.1), kind=kOutput, calls=%fused_computation.45 | convolution fusion | flops 100665088 | bytes 12582912 | tf_op jit(solution)/shard_map/id,rdy->riy/dot_general | solution.py:33
  142.4 30.1 %multiply_subtract_fusion = (f32[128,1024,16]{1,2,0:T(8,128)}, f32[128,1024,16]{1,2,0:T(8,128)}) fusion(f32[128,1024,16]{1,2,0:T(8,128)} %fusion.22, f32[128,1024,16]{1,2,0:T(8,128)} %fusion.26, f32[128,1024,16]{1,2,0:T(8,128)} %fusion.30, f32[128,1024,16]{1,2,0:T(8,128)} %fusion.24, f32[128,1024,16]{1,2,0:T(8,128)} %fusion.20, ...), kind=kOutput, calls=%fused_computation.13 | convolution fusion | flops 121636608 | bytes 79691776 | tf_op jit(solution)/shard_map/id,rdy->riy/dot_general | solution.py:34
  172.5 0.0 slice-start
  172.5 6.0 %fusion.6 = f32[128,1024,8]{1,2,0:T(8,128)S(1)} fusion(f32[128,1024,16]{1,2,0:T(8,128)} %get-tuple-element.6), kind=kOutput, calls=%fused_computation.6 | convolution fusion | flops 100665088 | bytes 12582912 | tf_op jit(solution)/shard_map/id,rdy->riy/dot_general | solution.py:36
  178.5 0.0 slice-start.1
  178.5 3.4 %fusion.4 = f32[128,1024,8]{1,2,0:T(8,128)S(1)} fusion(f32[128,1024,16]{1,2,0:T(8,128)S(1)} %copy-done.1), kind=kOutput, calls=%fused_computation.4 | convolution fusion | flops 100665088 | bytes 12582912 | tf_op jit(solution)/shard_map/id,rdy->riy/dot_general | solution.py:34
  181.9 3.6 %add_bitcast_fusion.2 = f32[128,8,1024]{2,1,0:T(8,128)S(1)} fusion(f32[128,1024,8]{1,2,0:T(8,128)S(1)} %fusion.6, f32[128,1024,16]{1,2,0:T(8,128)S(1)} %bitcast.107), kind=kOutput, calls=%fused_computation.29 | convolution fusion | flops 102762240 | bytes 16777216 | tf_op jit(solution)/shard_map/id,rdy->riy/dot_general | solution.py:33
  185.5 3.7 %subtract_bitcast_fusion = f32[128,8,1024]{2,1,0:T(8,128)S(1)} fusion(f32[128,1024,8]{1,2,0:T(8,128)S(1)} %fusion.4, f32[128,1024,16]{1,2,0:T(8,128)S(1)} %bitcast.107), kind=kOutput, calls=%fused_computation.28 | convolution fusion | flops 102762240 | bytes 16777216 | tf_op jit(solution)/shard_map/id,rdy->riy/dot_general | solution.py:35
  189.2 0.0 slice-start.3
  189.2 6.9 %fusion.56 = bf16[128,8,512]{2,1,0:T(8,128)(2,1)S(1)} fusion(f32[1024,512]{1,0:T(8,128)S(1)} %copy-done.9, f32[1024,512]{1,0:T(8,128)S(1)} %copy-done.8, f32[128,8,1024]{2,1,0:T(8,128)S(1)} %subtract_bitcast_fusion, f32[128,8,1024]{2,1,0:T(8,128)S(1)} %add_bitcast_fusion.2), kind=kOutput, calls=%fused_computation.77 | convolution fusion | flops 6447169536 | bytes 13631488 | tf_op jit(solution)/shard_map/dot_general | solution.py:97
  196.1 0.0 copy-start.11
  196.2 0.3 copy.38
  196.5 19.3 %all_to_all.42 = bf16[128,8,512]{2,0,1:T(8,128)(2,1)S(1)} all-to-all(bf16[128,8,512]{2,0,1:T(8,128)(2,1)S(1)} %copy.38), channel_id=1, replica_groups=mesh['ctx'=8,'tp'=4] {'ctx'}, dimensions={1} | all-to-all | bytes 2097152 | tf_op jit(solution)/shard_map/all_to_all | solution.py:100
  215.8 0.5 fusion.47
  216.3 9.5 %convolution_convert_fusion = bf16[512,4096]{1,0:T(8,128)(2,1)} fusion(bf16[1024,512]{1,0:T(8,128)(2,1)S(1)} %fusion.47, bf16[1024,4096]{1,0:T(8,128)(2,1)} %param.13), kind=kOutput, calls=%fused_computation.22 | convolution fusion | flops 4297064448 | bytes 13631488 | tf_op jit(solution)/shard_map/dot_general | solution.py:105
  225.8 0.0 reduce-scatter.2.cloned.1.call-update
  225.8 76.3 %reduce-scatter.2.cloned.1.call-done = bf16[512,1024]{1,0:T(8,128)(2,1)} async-done(((bf16[512,4096]{1,0:T(8,128)(2,1)}), bf16[512,1024]{1,0:T(8,128)(2,1)}) %reduce-scatter.2.cloned.1.call-update) | async-done | bytes 1048592 | tf_op jit(solution)/shard_map/reduce_scatter | solution.py:108
  (32 shorter events, 0.1 us)
Async XLA Ops:
  8.0 6.5 %copy-start.5 = (bf16[512,1024]{0,1:T(8,128)(2,1)}, bf16[512,1024]{0,1:T(8,128)(2,1)S(1)}, u32[]{:S(2)}) copy-start(bf16[512,1024]{0,1:T(8,128)(2,1)S(1)} %copy.31) | copy-start | bytes 3145732
  9.9 6.9 %copy-start.6 = (bf16[512,1024]{0,1:T(8,128)(2,1)}, bf16[512,1024]{0,1:T(8,128)(2,1)S(1)}, u32[]{:S(2)}) copy-start(bf16[512,1024]{0,1:T(8,128)(2,1)S(1)} %copy.32) | copy-start | bytes 3145732
  11.8 5.0 %copy-start.7 = (bf16[512,1024]{0,1:T(8,128)(2,1)}, bf16[512,1024]{0,1:T(8,128)(2,1)S(1)}, u32[]{:S(2)}) copy-start(bf16[512,1024]{0,1:T(8,128)(2,1)S(1)} %copy.33) | copy-start | bytes 3145732
  13.1 17.9 %copy-start.10 = (f32[3,3,1024]{2,1,0:T(4,128)S(1)}, f32[3,3,1024]{2,1,0:T(4,128)}, u32[]{:S(2)}) copy-start(f32[3,3,1024]{2,1,0:T(4,128)} %param.10) | copy-start | bytes 110596
  14.5 25.9 %collective-permute-start = (bf16[3,2,1024]{2,1,0:T(2,128)(2,1)S(1)}, bf16[3,2,1024]{2,1,0:T(2,128)(2,1)S(1)}, u32[]{:S(2)}, u32[]{:S(2)}) collective-permute-start(bf16[3,2,1024]{2,1,0:T(2,128)(2,1)S(1)} %copy.34), channel_id=1, source_target_pairs={{0,4},{4,8},{8,12},{12,16},{16,20},{20,24},{24,28},{1,5},{5,9},{9,... | collective-permute-start | bytes 36872 | tf_op jit(solution)/shard_map/ppermute | solution.py:15
  16.9 38.6 %all-to-all-start.1 = ((bf16[8,128,512]{2,1,0:T(8,128)(2,1)}), bf16[8,128,512]{2,1,0:T(8,128)(2,1)S(1)}, u32[]{:S(2)}, u32[]{:S(2)}) async-start(bf16[8,128,512]{2,1,0:T(8,128)(2,1)} %bitcast.120), calls=%async_computation.1 | async-start | bytes 2097152 | tf_op jit(solution)/shard_map/all_to_all | solution.py:65
  51.5 2.7 copy-start.4
  55.5 51.6 %all-to-all-start = ((bf16[8,128,512]{2,1,0:T(8,128)(2,1)}), bf16[8,128,512]{2,1,0:T(8,128)(2,1)}, u32[]{:S(2)}, u32[]{:S(2)}) async-start(bf16[8,128,512]{2,1,0:T(8,128)(2,1)} %bitcast.119), calls=%async_computation | async-start | bytes 2097152 | tf_op jit(solution)/shard_map/all_to_all | solution.py:64
  59.7 242.4 %reduce-scatter.2.cloned.1.call-start = ((), (), s32[]{:S(2)}) async-start(), calls=%async_computation.4 | async-start | bytes 5242880 | tf_op jit(solution)/shard_map/reduce_scatter | solution.py:108
  60.3 4.2 %copy-start.2 = (f32[512,1024]{1,0:T(8,128)S(1)}, f32[512,1024]{1,0:T(8,128)}, u32[]{:S(2)}) copy-start(f32[512,1024]{1,0:T(8,128)} %get-tuple-element.13) | copy-start | bytes 6291460
  82.4 11.2 %copy-start = (f32[128,8,2048]{2,1,0:T(8,128)S(1)}, f32[128,8,2048]{2,1,0:T(8,128)}, u32[]{:S(2)}) copy-start(f32[128,8,2048]{2,1,0:T(8,128)} %multiply_add_fusion.1) | copy-start | bytes 25165828
  107.1 4.5 %copy-start.3 = (f32[512,1024]{1,0:T(8,128)S(1)}, f32[512,1024]{1,0:T(8,128)}, u32[]{:S(2)}) copy-start(f32[512,1024]{1,0:T(8,128)} %get-tuple-element.13) | copy-start | bytes 6291460
  172.5 6.0 %copy-start.1 = (f32[128,1024,16]{1,2,0:T(8,128)S(1)}, f32[128,1024,16]{1,2,0:T(8,128)}, u32[]{:S(2)}) copy-start(f32[128,1024,16]{1,2,0:T(8,128)} %get-tuple-element.6) | copy-start | bytes 25165828
  172.5 9.4 %slice-start = ((s8[8388608]{0:T(1024)(128)(4,1)}), s8[4194304]{0:T(1024)(128)(4,1)S(1)}, s32[]{:S(2)}) async-start(s8[8388608]{0:T(1024)(128)(4,1)} %bitcast.106), calls=%async_computation.5 | async-start | bytes 8388608
  178.5 3.4 %slice-start.1 = ((s8[8388608]{0:T(1024)(128)(4,1)}), s8[4194304]{0:T(1024)(128)(4,1)S(1)}, s32[]{:S(2)}) async-start(s8[8388608]{0:T(1024)(128)(4,1)} %bitcast.106), calls=%async_computation.6 | async-start | bytes 8388608
  185.5 3.7 %copy-start.8 = (f32[1024,512]{1,0:T(8,128)S(1)}, f32[1024,512]{1,0:T(8,128)}, u32[]{:S(2)}) copy-start(f32[1024,512]{1,0:T(8,128)} %get-tuple-element.10) | copy-start | bytes 6291460
  185.5 3.7 %copy-start.9 = (f32[1024,512]{1,0:T(8,128)S(1)}, f32[1024,512]{1,0:T(8,128)}, u32[]{:S(2)}) copy-start(f32[1024,512]{1,0:T(8,128)} %get-tuple-element.11) | copy-start | bytes 6291460
  189.2 26.6 %slice-start.2 = ((s8[6291456]{0:T(1024)(128)(4,1)}), s8[4194304]{0:T(1024)(128)(4,1)S(1)}, s32[]{:S(2)}) async-start(s8[6291456]{0:T(1024)(128)(4,1)} %bitcast.109), calls=%async_computation.7 | async-start | bytes 8388608
  189.2 26.6 %slice-start.3 = ((s8[6291456]{0:T(1024)(128)(4,1)}), s8[2097152]{0:T(1024)(128)(4,1)S(1)}, s32[]{:S(2)}) async-start(s8[6291456]{0:T(1024)(128)(4,1)} %bitcast.109), calls=%async_computation.8 | async-start | bytes 4194304
  196.1 19.7 %copy-start.11 = (f32[1024]{0:T(1024)S(1)}, f32[1024]{0:T(1024)}, u32[]{:S(2)}) copy-start(f32[1024]{0:T(1024)} %param.11) | copy-start | bytes 12292
Sparse Core Ops, SparseCore 0:
  226.0 76.1 reduce-scatter.1
where the time goes:
time: 315 us; the launch traced here: 309 us
  matrix products  133 us (42%)
  waiting for transfers between devices  76.3 us (24%)
  other arithmetic  43.3 us (14%)
  blocking collectives  19.3 us (6%)
  between operations  13.9 us (4%)
  starting transfers between devices  12.2 us (4%)
  local copies, waits for them, and re-layouts  11 us (3%)
    reduce_scatter x1, waiting for transfers between devices, per_device(): lax.psum_scatter(term.astype(jnp.bfloat16), 'tp', scatter_dimension=1, ti...  76.3 us
    dot_general x3, matrix products, block_mix(): multiplier('id,rdy->riy', cosine_lookup, imaginary_component)  40.1 us
    dot_general x3, matrix products, block_mix(): sine_imaginary = multiplier('id,rdy->riy', sine_lookup, imaginary_component)  23.9 us
    all_to_all x1, blocking collectives, per_device(): lax.all_to_all(long_local.astype(jnp.bfloat16), 'ctx', split_axis=1, conc...  19.3 us
    dot_general x3, matrix products, block_mix(): sine_real = multiplier('id,rdy->riy', sine_lookup, real_component)  17.5 us
    dot_general x3, matrix products, block_mix(): cosine_real = multiplier('id,rdy->riy', cosine_lookup, real_component)  16.8 us
    add x1, other arithmetic, per_device(): kernel_spec = earlier + parity * spectra  12 us
    dot_general x2, matrix products, inner_spectrum(): lower = jnp.dot(rows, table_low, preferred_element_type=jnp.float32)  9.73 us
  transfers between devices with their start and end apart: 4, of which 1 were waited for; matrix products, arithmetic and copies ran while one was open for 25% of the time, Pallas kernels for 0%

commit v1 on v0

--- a/solution.py
+++ b/solution.py
@@ -3,7 +3,10 @@
 
 import jax
 import jax.numpy as jnp
+import numpy as np
 from jax import lax
+from jax.experimental import pallas as pl
+from jax.experimental.pallas import tpu as pltpu
 from jax.sharding import PartitionSpec as P
 
 TRIPLE = lax.Precision.HIGH
@@ -37,7 +40,7 @@
     return (cosine_real + sign * sine_imaginary, cosine_imaginary - sign * sine_real)
 
 
-def per_device(query_rows, key_rows, value_rows, short_weight, skip_gain, filter_taps, out_weight):
+def general_per_device(query_rows, key_rows, value_rows, short_weight, skip_gain, filter_taps, out_weight):
     span = query_rows.shape[0]
     chans = query_rows.shape[1]
     blocks = lax.axis_size("ctx")
@@ -108,6 +111,403 @@
     return lax.psum_scatter(term.astype(jnp.bfloat16), "tp", scatter_dimension=1, tiled=True)
 
 
+SUB = 128
+F32 = jnp.float32
+BF16 = jnp.bfloat16
+
+
+def split_table(matrix):
+    high = matrix.astype(jnp.bfloat16)
+    low = (matrix - high.astype(np.float32)).astype(jnp.bfloat16)
+    return np.concatenate([high, high, low], axis=1)
+
+
+def dft_tables(period):
+    index = np.arange(SUB)
+    turns = np.outer(index, index) % SUB * (2.0 * np.pi / SUB)
+    cos, sin = np.cos(turns), np.sin(turns)
+    forward = np.block([[cos, sin], [-sin, cos]]).astype(np.float32)
+    inverse = (np.block([[cos, -sin], [sin, cos]]) / period).astype(np.float32)
+    return split_table(forward), split_table(inverse)
+
+
+def twiddle_table(radix):
+    half = radix // 2
+    turns = np.outer(np.arange(SUB), np.arange(half + 1)) * (2.0 * np.pi / (radix * SUB))
+    return np.concatenate([np.cos(turns), -np.sin(turns)], axis=1).astype(np.float32)
+
+
+def times(value, factor):
+    return None if value is None else value * factor
+
+
+def plus(left, right):
+    if left is None:
+        return right
+    return left if right is None else left + right
+
+
+def minus(left, right):
+    if right is None:
+        return left
+    return -right if left is None else left - right
+
+
+def rotate(value, turn):
+    real, imag = value
+    cos, sin = math.cos(2 * math.pi * turn), math.sin(2 * math.pi * turn)
+    if abs(cos - sin) < 1e-12 and imag is not None:
+        return (real + imag) * cos, (imag - real) * cos
+    return plus(times(real, cos), times(imag, sin)), minus(times(imag, cos), times(real, sin))
+
+
+def real_forward(values):
+    points = 2 * len(values)
+    if points == 2:
+        return [(values[0], None), (values[0], None)]
+    even, odd = real_forward(values[0::2]), real_forward(values[1::2])
+    bins = [None] * (points // 2 + 1)
+    bins[0] = (even[0][0] + odd[0][0], None)
+    bins[points // 2] = (even[0][0] - odd[0][0], None)
+    quarter = points // 4
+    for k in range(1, quarter):
+        turned = rotate(odd[k], k / points)
+        bins[k] = (even[k][0] + turned[0], even[k][1] + turned[1])
+        bins[points // 2 - k] = (even[k][0] - turned[0], turned[1] - even[k][1])
+    bins[quarter] = (even[quarter][0], -odd[quarter][0])
+    return bins
+
+
+def real_inverse(bins):
+    half = len(bins) - 1
+    points = 2 * half
+    if points == 2:
+        return [bins[0][0] + bins[1][0]]
+    even, odd = [], []
+    for k in range(half // 2 + 1):
+        ahead, back = bins[k], bins[half - k]
+        if k == 0:
+            even.append((ahead[0] + back[0], None))
+            odd.append((ahead[0] - back[0], None))
+        elif k == half // 2:
+            even.append((ahead[0] * 2.0, None))
+            odd.append((ahead[1] * -2.0, None))
+        else:
+            even.append((ahead[0] + back[0], ahead[1] - back[1]))
+            difference = (ahead[0] - back[0], ahead[1] + back[1])
+            odd.append(rotate(difference, -k / points))
+    even, odd = real_inverse(even), real_inverse(odd)
+    return [value for pair in zip(even, odd) for value in pair]
+
+
+def split_dot(table, data):
+    high = data.astype(BF16)
+    low = (data - high.astype(F32)).astype(BF16)
+    return jnp.dot(
+        table[...], jnp.concatenate([high, low, high], axis=0), preferred_element_type=F32
+    )
+
+
+def first_stage(series, spectra, twiddle):
+    half = series.shape[0] // SUB
+    lanes = series.shape[1]
+
+    def slab(step, carry):
+        row = pl.multiple_of(step * 8, 8)
+        values = [series[pl.ds(SUB * n + row, 8), :] for n in range(half)]
+        factors = twiddle[pl.ds(row, 8), :]
+        for k, (real, imag) in enumerate(real_forward(values)):
+            if k == 0:
+                spectra[0, pl.ds(row, 8), :] = real
+                spectra[0, pl.ds(SUB + row, 8), :] = jnp.zeros_like(real)
+                continue
+            cos = jnp.broadcast_to(factors[:, k : k + 1], (8, lanes))
+            sin = jnp.broadcast_to(factors[:, half + 1 + k : half + 2 + k], (8, lanes))
+            if imag is None:
+                spectra[k, pl.ds(row, 8), :] = real * cos
+                spectra[k, pl.ds(SUB + row, 8), :] = real * sin
+            else:
+                spectra[k, pl.ds(row, 8), :] = real * cos - imag * sin
+                spectra[k, pl.ds(SUB + row, 8), :] = real * sin + imag * cos
+        return carry
+
+    lax.fori_loop(0, SUB // 8, slab, 0)
+    for k in range(half + 1, spectra.shape[0]):
+        spectra[k] = jnp.zeros(spectra.shape[1:], F32)
+
+
+def last_stage(spectra, series):
+    half = series.shape[0] // SUB
+
+    def slab(step, carry):
+        row = pl.multiple_of(step * 8, 8)
+        bins = []
+        for k in range(half + 1):
+            real = spectra[k, pl.ds(row, 8), :]
+            imag = None if k in (0, half) else spectra[k, pl.ds(SUB + row, 8), :]
+            bins.append((real, imag))
+        for n, value in enumerate(real_inverse(bins)):
+            series[pl.ds(SUB * n + row, 8), :] = value
+        return carry
+
+    lax.fori_loop(0, SUB // 8, slab, 0)
+
+
+def taps_kernel(blocks, me_ref, *refs):
+    pieces, (twiddle, forward, spectra_out, series, spectra) = refs[:blocks], refs[blocks:]
+    span = pieces[0].shape[1]
+    for m in range(blocks):
+        start = pl.multiple_of((me_ref[0] ^ m) * span, span)
+        series[pl.ds(start, span), :] = pieces[m][...].astype(F32).T
+    first_stage(series, spectra, twiddle)
+
+    def pair(p, carry):
+        data = jnp.concatenate([spectra[2 * p], spectra[2 * p + 1]], axis=1)
+        spectra_out[p] = split_dot(forward, data)
+        return carry
+
+    lax.fori_loop(0, spectra_out.shape[0], pair, 0)
+
+
+def conv_kernel(blocks, me_ref, *refs):
+    pieces = refs[:blocks]
+    taps_spectra, twiddle, forward, inverse, skip = refs[blocks : blocks + 5]
+    outs = refs[blocks + 5 : 2 * blocks + 5]
+    series, spectra, result = refs[2 * blocks + 5 :]
+    span, lanes = pieces[0].shape
+    half = series.shape[0] // SUB
+    for m in range(blocks):
+        start = pl.multiple_of((me_ref[0] ^ m) * span, span)
+        series[pl.ds(start, span), :] = pieces[m][...].astype(F32)
+    first_stage(series, spectra, twiddle)
+
+    def pair(p, carry):
+        data = jnp.concatenate([spectra[2 * p], spectra[2 * p + 1]], axis=1)
+        signal = split_dot(forward, data)
+        signal_re, signal_im = signal[:SUB], signal[SUB:]
+        taps_re, taps_im = taps_spectra[p, :SUB, :], taps_spectra[p, SUB:, :]
+        product = jnp.concatenate(
+            [
+                signal_re * taps_re - signal_im * taps_im,
+                signal_re * taps_im + signal_im * taps_re,
+            ],
+            axis=0,
+        )
+        back = split_dot(inverse, product)
+        spectra[2 * p] = back[:, :lanes]
+        spectra[2 * p + 1] = back[:, lanes:]
+        return carry
+
+    lax.fori_loop(0, taps_spectra.shape[0], pair, 0)
+    for k in range(1, half + 1):
+        real, imag = spectra[k, :SUB, :], spectra[k, SUB:, :]
+        cos = jnp.broadcast_to(twiddle[:, k : k + 1], (SUB, lanes))
+        sin = jnp.broadcast_to(twiddle[:, half + 1 + k : half + 2 + k], (SUB, lanes))
+        spectra[k, :SUB, :] = real * cos + imag * sin
+        if k < half:
+            spectra[k, SUB:, :] = imag * cos - real * sin
+    last_stage(spectra, result)
+    for m in range(blocks):
+        start = pl.multiple_of((me_ref[0] ^ m) * span, span)
+        window = pl.ds(start, span)
+        outs[m][...] = (result[window, :] + skip[...] * series[window, :]).astype(BF16)
+
+
+VMEM = pl.BlockSpec(memory_space=pltpu.VMEM)
+SMEM = pl.BlockSpec(memory_space=pltpu.SMEM)
+GRANT = pltpu.CompilerParams(vmem_limit_bytes=40 * 2**20)
+
+
+def taps_spectra_of(me, pieces, twiddle, forward):
+    blocks = len(pieces)
+    lanes, span = pieces[0].shape
+    half = blocks * span // SUB
+    pairs = (half + 2) // 2
+    return pl.pallas_call(
+        partial(taps_kernel, blocks),
+        out_shape=jax.ShapeDtypeStruct((pairs, 2 * SUB, 2 * lanes), F32),
+        in_specs=[SMEM] + [VMEM] * (blocks + 2),
+        out_specs=VMEM,
+        scratch_shapes=[
+            pltpu.VMEM((blocks * span, lanes), F32),
+            pltpu.VMEM((2 * pairs, 2 * SUB, lanes), F32),
+        ],
+        compiler_params=GRANT,
+        name="taps_spectra",
+    )(me, *pieces, twiddle, forward)
+
+
+def long_conv(me, pieces, taps_spectra, twiddle, forward, inverse, skip):
+    blocks = len(pieces)
+    span, lanes = pieces[0].shape
+    pairs = taps_spectra.shape[0]
+    return pl.pallas_call(
+        partial(conv_kernel, blocks),
+        out_shape=[jax.ShapeDtypeStruct((span, lanes), BF16)] * blocks,
+        in_specs=[SMEM] + [VMEM] * (blocks + 5),
+        out_specs=[VMEM] * blocks,
+        scratch_shapes=[
+            pltpu.VMEM((blocks * span, lanes), F32),
+            pltpu.VMEM((2 * pairs, 2 * SUB, lanes), F32),
+            pltpu.VMEM((blocks * span, lanes), F32),
+        ],
+        compiler_params=GRANT,
+        name="long_conv",
+    )(me, *pieces, taps_spectra, twiddle, forward, inverse, skip)
+
+
+def shifted_mix(stream, edge, weight):
+    first = jnp.concatenate([edge[1:2], stream[:-1]], axis=0)
+    second = jnp.concatenate([edge, stream[:-2]], axis=0)
+    return weight[0:1] * stream + weight[1:2] * first + weight[2:3] * second
+
+
+def gate_in_kernel(me_ref, key, value, edges, weight, *outs):
+    mixed = [
+        shifted_mix(ref[...].astype(F32), edges[2 * s : 2 * s + 2].astype(F32), weight[:, s, :])
+        for s, ref in ((1, key), (2, value))
+    ]
+    gated = (mixed[0] * mixed[1]).astype(BF16)
+    for m, out in enumerate(outs):
+
+        @pl.when(pl.program_id(0) == m)
+        def _(out=out):
+            out[...] = gated
+
+
+def gate_in(me, key_rows, value_rows, edges, short_weight, blocks):
+    span, chans = key_rows.shape
+    lanes = chans // blocks
+    column = lambda m, me: (0, me[0] ^ m)
+    return pl.pallas_call(
+        gate_in_kernel,
+        grid_spec=pltpu.PrefetchScalarGridSpec(
+            num_scalar_prefetch=1,
+            grid=(blocks,),
+            in_specs=[
+                pl.BlockSpec((span, lanes), column),
+                pl.BlockSpec((span, lanes), column),
+                pl.BlockSpec((6, lanes), column),
+                pl.BlockSpec((3, 3, lanes), lambda m, me: (0, 0, me[0] ^ m)),
+            ],
+            out_specs=[pl.BlockSpec((span, lanes), lambda m, me: (0, 0))] * blocks,
+        ),
+        out_shape=[jax.ShapeDtypeStruct((span, lanes), BF16)] * blocks,
+        name="gate_in",
+    )(me, key_rows, value_rows, edges, short_weight)
+
+
+def split_taps_kernel(me_ref, taps, *outs):
+    for m, out in enumerate(outs):
+
+        @pl.when(pl.program_id(0) == m)
+        def _(out=out):
+            out[...] = taps[...]
+
+
+def split_taps(me, filter_taps, blocks):
+    chans, span = filter_taps.shape
+    lanes = chans // blocks
+    return pl.pallas_call(
+        split_taps_kernel,
+        grid_spec=pltpu.PrefetchScalarGridSpec(
+            num_scalar_prefetch=1,
+            grid=(blocks,),
+            in_specs=[pl.BlockSpec((lanes, span), lambda m, me: (me[0] ^ m, 0))],
+            out_specs=[pl.BlockSpec((lanes, span), lambda m, me: (0, 0))] * blocks,
+        ),
+        out_shape=[jax.ShapeDtypeStruct((lanes, span), BF16)] * blocks,
+        name="split_taps",
+    )(me, filter_taps)
+
+
+def mix_query_kernel(query, edges, weight, out):
+    out[...] = shifted_mix(query[...].astype(F32), edges[0:2].astype(F32), weight[:, 0, :])
+
+
+def mix_query(query_rows, edges, short_weight):
+    span, chans = query_rows.shape
+    lanes = chans // 4
+    return pl.pallas_call(
+        mix_query_kernel,
+        grid=(4,),
+        in_specs=[
+            pl.BlockSpec((span, lanes), lambda g: (0, g)),
+            pl.BlockSpec((6, lanes), lambda g: (0, g)),
+            pl.BlockSpec((3, 3, lanes), lambda g: (0, 0, g)),
+        ],
+        out_specs=pl.BlockSpec((span, lanes), lambda g: (0, g)),
+        out_shape=jax.ShapeDtypeStruct((span, chans), F32),
+        name="mix_query",
+    )(query_rows, edges, short_weight)
+
+
+def exchange(pieces, axis):
+    devices = range(lax.axis_size(axis))
+    return [pieces[0]] + [
+        lax.ppermute(piece, axis, [(i, i ^ m) for i in devices])
+        for m, piece in enumerate(pieces)
+        if m
+    ]
+
+
+def project(gated_out, out_weight):
+    term = jnp.dot(gated_out, out_weight, preferred_element_type=F32)
+    return lax.psum_scatter(term.astype(BF16), "tp", scatter_dimension=1, tiled=True)
+
+
+def gate_out_kernel(blocks, me_ref, *refs):
+    convs, (mixed, out) = refs[:blocks], refs[blocks:]
+    lanes = convs[0].shape[1]
+    for m in range(blocks):
+        window = pl.ds(pl.multiple_of((me_ref[0] ^ m) * lanes, lanes), lanes)
+        out[:, window] = (mixed[:, window] * convs[m][...].astype(F32)).astype(BF16)
+
+
+def gate_out(me, convs, mixed):
+    span, chans = mixed.shape
+    return pl.pallas_call(
+        partial(gate_out_kernel, len(convs)),
+        out_shape=jax.ShapeDtypeStruct((span, chans), BF16),
+        in_specs=[SMEM] + [VMEM] * (len(convs) + 1),
+        out_specs=VMEM,
+        compiler_params=GRANT,
+        name="gate_out",
+    )(me, *convs, mixed)
+
+
+def fast_per_device(
+    query_rows, key_rows, value_rows, short_weight, skip_gain, filter_taps, out_weight
+):
+    span, chans = query_rows.shape
+    blocks = lax.axis_size("ctx")
+    lanes = chans // blocks
+    length = span * blocks
+    radix = 2 * length // SUB
+    place = lax.axis_index("ctx")
+    me = place.astype(jnp.int32).reshape(1)
+    forward, inverse = (jnp.asarray(t) for t in dft_tables(2 * length))
+    twiddle = jnp.asarray(twiddle_table(radix))
+    edges = jnp.concatenate([x[-2:] for x in (query_rows, key_rows, value_rows)])
+    edges = passed_along(edges, "ctx", 1)
+    taps = exchange(split_taps(me, filter_taps, blocks), "ctx")
+    gated = exchange(gate_in(me, key_rows, value_rows, edges, short_weight, blocks), "ctx")
+    mixed = mix_query(query_rows, edges, short_weight)
+    skip = lax.dynamic_slice(skip_gain, (place * lanes,), (lanes,)).reshape(1, lanes)
+    spectra = taps_spectra_of(me, taps, twiddle, forward)
+    convs = long_conv(me, gated, spectra, twiddle, forward, inverse, skip)
+    convs = exchange(convs, "ctx")
+    gated_out = gate_out(me, convs, mixed)
+    return project(gated_out, out_weight)
+
+
+def per_device(*arrays):
+    span, chans = arrays[0].shape
+    blocks = lax.axis_size("ctx")
+    suits = blocks == 8 and lax.axis_size("tp") == 4 and span == 512 and chans == 8 * SUB
+    return (fast_per_device if suits else general_per_device)(*arrays)
+
+
 def solution(mesh):
     placed = (
         P("ctx", "tp"),

time: 315 us -> 186 us (0.59); the launches traced: 309 us -> 185 us
  matrix products: 133 us -> 9.47 us
  other arithmetic: 43.3 us -> 0.02 us
  Pallas kernels: 0 us -> 42.2 us
  blocking collectives: 19.3 us -> 0 us
  waiting for transfers between devices: 76.3 us -> 89.5 us
  starting transfers between devices: 12.2 us -> 23.1 us
  local copies, waits for them, and re-layouts: 11 us -> 7.49 us
    dot_general x18 -> x1, matrix products: 133 us -> 9.47 us  [project(): term = jnp.dot(gated_out, out_weight, preferred_element_type=F32)]
    pallas_call x0 -> x6, Pallas kernels: none -> 42.2 us  [the longest x1 18.3 us: long_conv(): pl.pallas_call(partial(conv_kernel, blocks), out_shape=[jax.ShapeDtypeStr...]
    ppermute x0 -> x21, starting transfers between devices: none -> 21.3 us  [exchange(): lax.ppermute(piece, axis, [(i, i ^ m) for i in devices])]
    all_to_all x1 -> x0, blocking collectives: 19.3 us -> none  [per_device(): lax.all_to_all(long_local.astype(jnp.bfloat16), 'ctx', split_axis=1, conc...]
    add x3 -> x0, other arithmetic: 17.6 us -> none  [the longest x1 12 us: per_device(): kernel_spec = earlier + parity * spectra]
    ppermute x0 -> x21, waiting for transfers between devices: none -> 10.5 us  [exchange(): lax.ppermute(piece, axis, [(i, i ^ m) for i in devices])]
    cos x1 -> x0, other arithmetic: 9.37 us -> none  [per_device(): jnp.cos(inverse)]
    all_to_all x2 -> x0, starting transfers between devices: 9.26 us -> none  [the longest x1 5.02 us: per_device(): lax.all_to_all(filter_taps, 'ctx', split_axis=0, concat_axis=1, tiled=True)]
  transfers between devices with their start and end apart: 4 -> 23, of which waited for: 1 -> 6; matrix products, arithmetic and copies ran while one was open for 25% -> 1% of each run, Pallas kernels for 0% -> 10%
where the time goes in v1:
time: 186 us; the launch traced here: 185 us
  waiting for transfers between devices  89.5 us (48%)
  Pallas kernels  42.2 us (23%)
  starting transfers between devices  23.1 us (12%)
  between operations  13.5 us (7%)
  matrix products  9.47 us (5%)
  local copies, waits for them, and re-layouts  7.49 us (4%)
    reduce_scatter x1, waiting for transfers between devices, project(): lax.psum_scatter(term.astype(BF16), 'tp', scatter_dimension=1, tiled=True)  78.1 us
    ppermute x21, starting transfers between devices, exchange(): lax.ppermute(piece, axis, [(i, i ^ m) for i in devices])  21.3 us
    pallas_call x1, Pallas kernels, long_conv(): pl.pallas_call(partial(conv_kernel, blocks), out_shape=[jax.ShapeDtypeStr...  18.3 us
    ppermute x21, waiting for transfers between devices, exchange(): lax.ppermute(piece, axis, [(i, i ^ m) for i in devices])  10.5 us
    dot_general x1, matrix products, project(): term = jnp.dot(gated_out, out_weight, preferred_element_type=F32)  9.47 us
    pallas_call x1, Pallas kernels, taps_spectra_of(): pl.pallas_call(partial(taps_kernel, blocks), out_shape=jax.ShapeDtypeStru...  8.02 us
    pallas_call x1, Pallas kernels, gate_in(): pl.pallas_call(gate_in_kernel, grid_spec=pltpu.PrefetchScalarGridSpec(num...  6.58 us
    unnamed x16, local copies, waits for them, and re-layouts  5.24 us
  transfers between devices with their start and end apart: 23, of which 6 were waited for; matrix products, arithmetic and copies ran while one was open for 1% of the time, Pallas kernels for 10%

profile of v1, /device:TPU:0, one launch (start us, length us, event | category | flops | bytes accessed | tf_op | source)
XLA Modules:
  0.0 185.2 jit_solution(9140177680983148160)
XLA Ops:
  6.5 4.9 %split_taps.1 = (bf16[128,512]{1,0:T(8,128)(2,1)}, bf16[128,512]{1,0:T(8,128)(2,1)}, bf16[128,512]{1,0:T(8,128)(2,1)}, bf16[128,512]{1,0:T(8,128)(2,1)}, bf16[12...) custom-call(s32[1]{0:T(128)} %bitcast.me_ref, ...), custom_call_target="tpu_custom_call" | custom-call | tf_op jit(solution)/shard_map/split_taps/pallas_call | solution.py:411
  11.4 2.4 %collective-permute-start.10 = (bf16[128,512]{1,0:T(8,128)(2,1)}, bf16[128,512]{1,0:T(8,128)(2,1)S(1)}, u32[]{:S(2)}, u32[]{:S(2)}) collective-permute-start(bf16[128,512]{1,0:T(8,128)(2,1)} %get-tuple-element.40), channel_id=1, source_target_pairs={{0,12},{4,8},{8,4},{12,0},{16,28},{20,24},{24,20},{28,16},{1,13},{... | collective-permute-start | bytes 393224 | tf_op jit(solution)/shard_map/ppermute | solution.py:448
  13.8 1.5 collective-permute-start.11
  15.3 0.5 collective-permute-start.12
  15.9 1.5 collective-permute-start.13
  17.3 0.7 slice.10
  18.1 0.7 slice.11
  18.8 0.7 slice.9
  19.5 1.8 collective-permute-start
  21.3 0.8 collective-permute-done.edges
  22.2 1.5 collective-permute-start.14
  23.7 6.6 %gate_in.1 = (bf16[512,128]{1,0:T(8,128)(2,1)}, bf16[512,128]{1,0:T(8,128)(2,1)}, bf16[512,128]{1,0:T(8,128)(2,1)}, bf16[512,128]{1,0:T(8,128)(2,1)}, bf16[512,1...) custom-call(s32[1]{0:T(128)} %bitcast.me_ref, ...), custom_call_target="tpu_custom_call" | custom-call | tf_op jit(solution)/shard_map/gate_in/pallas_call | solution.py:382
  30.3 0.0 collective-permute-done.10.refs_3_
  30.3 2.5 %collective-permute-start.8 = (bf16[128,512]{1,0:T(8,128)(2,1)}, bf16[128,512]{1,0:T(8,128)(2,1)S(1)}, u32[]{:S(2)}, u32[]{:S(2)}) collective-permute-start(bf16[128,512]{1,0:T(8,128)(2,1)} %get-tuple-element.38), channel_id=1, source_target_pairs={{0,4},{4,0},{8,12},{12,8},{16,20},{20,16},{24,28},{28,24},{1,5},{5... | collective-permute-start | bytes 393224 | tf_op jit(solution)/shard_map/ppermute | solution.py:448
  32.8 0.0 collective-permute-done.11.refs_4_
  32.8 1.3 collective-permute-start.9
  34.2 0.0 collective-permute-done.12.refs_5_
  34.2 0.0 collective-permute-start.1
  34.2 0.0 collective-permute-done.13.refs_6_
  34.2 0.8 collective-permute-start.2
  34.9 1.1 collective-permute-start.3
  36.0 0.6 collective-permute-start.4
  36.6 2.8 %collective-permute-done.9.refs_2_ = bf16[128,512]{1,0:T(8,128)(2,1)S(1)} collective-permute-done((bf16[128,512]{1,0:T(8,128)(2,1)}, bf16[128,512]{1,0:T(8,128)(2,1)S(1)}, u32[]{:S(2)}, u32[]{:S(2)}) %collective-permute-start.9) | collective-permute-done | bytes 131104 | tf_op jit(solution)/shard_map/ppermute | solution.py:448
  39.4 0.9 collective-permute-start.6
  40.3 1.9 %collective-permute-done.2.refs_2_ = bf16[512,128]{1,0:T(8,128)(2,1)S(1)} collective-permute-done((bf16[512,128]{1,0:T(8,128)(2,1)}, bf16[512,128]{1,0:T(8,128)(2,1)S(1)}, u32[]{:S(2)}, u32[]{:S(2)}) %collective-permute-start.2) | collective-permute-done | bytes 131104 | tf_op jit(solution)/shard_map/ppermute | solution.py:448
  42.2 1.1 collective-permute-start.7
  43.3 0.1 dynamic-slice_bitcast_fusion.refs_12_
  43.4 1.0 copy-done.2
  44.4 0.8 copy-done.4
  45.2 0.9 copy-done.5
  46.1 8.0 %taps_spectra.1.refs_8_ = f32[17,256,256]{2,1,0:T(8,128)S(1)} custom-call(s32[1]{0:T(128)} %bitcast.me_ref, bf16[128,512]{1,0:T(8,128)(2,1)S(1)} %copy-done.5, bf16[128,512]{1,0:T(8,128)(2,1)S(1)} %collective-permute-done.8.refs_1_, bf16[128,512]{1,0:T(8,128)(2,1)S(1)} %collective-permute-done.9.refs_2_, ...), custom_call_target="tpu_custom_call" | custom-call | tf_op jit(solution)/shard_map/taps_spectra/pallas_call | solution.py:326
  54.2 0.0 copy-start.6
  54.2 0.9 copy-done.6
  55.1 18.3 %long_conv.1 = (bf16[512,128]{1,0:T(8,128)(2,1)S(1)}, bf16[512,128]{1,0:T(8,128)(2,1)S(1)}, bf16[512,128]{1,0:T(8,128)(2,1)S(1)}, bf16[512,128]{1,0:T(8,128)(2,1...) custom-call(s32[1]{0:T(128)} %bitcast.me_ref, ...), custom_call_target="tpu_custom_call" | custom-call | tf_op jit(solution)/shard_map/long_conv/pallas_call | solution.py:344
  73.4 0.1 collective-permute-start.15
  73.5 2.0 %collective-permute-start.16 = (bf16[512,128]{1,0:T(8,128)(2,1)S(1)}, bf16[512,128]{1,0:T(8,128)(2,1)S(1)}, u32[]{:S(2)}, u32[]{:S(2)}) collective-permute-start(bf16[512,128]{1,0:T(8,128)(2,1)S(1)} %get-tuple-element.47), channel_id=1, source_target_pairs={{0,8},{4,12},{8,0},{12,4},{16,24},{20,28},{24,16},{28,20},{1,9},{5... | collective-permute-start | bytes 393224 | tf_op jit(solution)/shard_map/ppermute | solution.py:448
  75.5 1.2 collective-permute-start.18
  76.8 0.3 collective-permute-start.19
  77.1 1.9 %collective-permute-start.20 = (bf16[512,128]{1,0:T(8,128)(2,1)S(1)}, bf16[512,128]{1,0:T(8,128)(2,1)S(1)}, u32[]{:S(2)}, u32[]{:S(2)}) collective-permute-start(bf16[512,128]{1,0:T(8,128)(2,1)S(1)} %get-tuple-element.51), channel_id=1, source_target_pairs={{0,24},{4,28},{8,16},{12,20},{16,8},{20,12},{24,0},{28,4},{1,25},{... | collective-permute-start | bytes 393224 | tf_op jit(solution)/shard_map/ppermute | solution.py:448
  79.0 0.9 collective-permute-done.16.refs_2_
  79.9 0.1 collective-permute-start.21
  79.9 4.0 %mix_query.1.refs_8_ = f32[512,1024]{1,0:T(8,128)} custom-call(bf16[512,1024]{1,0:T(8,128)(2,1)} %query.1, bf16[6,1024]{1,0:T(8,128)(2,1)} %copy-done.7, f32[3,3,1024]{2,1,0:T(4,128)} %weight.3), custom_call_target="tpu_custom_call" | custom-call | tf_op jit(solution)/shard_map/mix_query/pallas_call | solution.py:431
  83.9 4.9 %collective-permute-done.19.refs_5_ = bf16[512,128]{1,0:T(8,128)(2,1)S(1)} collective-permute-done((bf16[512,128]{1,0:T(8,128)(2,1)S(1)}, bf16[512,128]{1,0:T(8,128)(2,1)S(1)}, u32[]{:S(2)}, u32[]{:S(2)}) %collective-permute-start.19) | collective-permute-done | bytes 131104 | tf_op jit(solution)/shard_map/ppermute | solution.py:448
  88.8 1.6 copy-done.1
  90.4 0.3 gate_out.1
  90.8 9.5 %convolution_convert_fusion = bf16[512,4096]{1,0:T(8,128)(2,1)} fusion(bf16[512,1024]{1,0:T(8,128)(2,1)S(1)} %gate_out.1, bf16[1024,4096]{1,0:T(8,128)(2,1)} %param.16), kind=kOutput, calls=%fused_computation | convolution fusion | flops 4297064448 | bytes 13631488 | tf_op jit(solution)/shard_map/dot_general | solution.py:455
  100.2 0.0 reduce-scatter.2.cloned.1.call-update
  100.3 78.1 %reduce-scatter.2.cloned.1.call-done = bf16[512,1024]{1,0:T(8,128)(2,1)} async-done(((bf16[512,4096]{1,0:T(8,128)(2,1)}), bf16[512,1024]{1,0:T(8,128)(2,1)}) %reduce-scatter.2.cloned.1.call-update) | async-done | bytes 1048592 | tf_op jit(solution)/shard_map/reduce_scatter | solution.py:456
  (27 shorter events, 0.1 us)
Async XLA Ops:
  6.5 36.7 %copy-start = (f32[1024]{0:T(1024)S(1)}, f32[1024]{0:T(1024)}, u32[]{:S(2)}) copy-start(f32[1024]{0:T(1024)} %param.14) | copy-start | bytes 12292
  6.5 47.6 %copy-start.3 = (bf16[256,768]{1,0:T(8,128)(2,1)S(1)}, bf16[256,768]{1,0:T(8,128)(2,1)}, u32[]{:S(2)}) copy-start(bf16[256,768]{1,0:T(8,128)(2,1)} %constant.19.clone.refs_11_) | copy-start | bytes 1179652
  6.5 171.9 %reduce-scatter.2.cloned.1.call-start = ((), (), s32[]{:S(2)}) async-start(), calls=%async_computation.1 | async-start | bytes 5242880 | tf_op jit(solution)/shard_map/reduce_scatter | solution.py:456
  11.4 18.8 %collective-permute-start.10 = (bf16[128,512]{1,0:T(8,128)(2,1)}, bf16[128,512]{1,0:T(8,128)(2,1)S(1)}, u32[]{:S(2)}, u32[]{:S(2)}) collective-permute-start(bf16[128,512]{1,0:T(8,128)(2,1)} %get-tuple-element.40), channel_id=1, source_target_pairs={{0,12},{4,8},{8,4},{12,0},{16,28},{20,24},{24,20},{28,16},{1,13},{... | collective-permute-start | bytes 393224 | tf_op jit(solution)/shard_map/ppermute | solution.py:448
  13.8 19.0 %collective-permute-start.11 = (bf16[128,512]{1,0:T(8,128)(2,1)}, bf16[128,512]{1,0:T(8,128)(2,1)S(1)}, u32[]{:S(2)}, u32[]{:S(2)}) collective-permute-start(bf16[128,512]{1,0:T(8,128)(2,1)} %get-tuple-element.41), channel_id=1, source_target_pairs={{0,16},{4,20},{8,24},{12,28},{16,0},{20,4},{24,8},{28,12},{1,17},{... | collective-permute-start | bytes 393224 | tf_op jit(solution)/shard_map/ppermute | solution.py:448
  15.3 18.8 %collective-permute-start.12 = (bf16[128,512]{1,0:T(8,128)(2,1)}, bf16[128,512]{1,0:T(8,128)(2,1)S(1)}, u32[]{:S(2)}, u32[]{:S(2)}) collective-permute-start(bf16[128,512]{1,0:T(8,128)(2,1)} %get-tuple-element.42), channel_id=1, source_target_pairs={{0,20},{4,16},{8,28},{12,24},{16,4},{20,0},{24,12},{28,8},{1,21},{... | collective-permute-start | bytes 393224 | tf_op jit(solution)/shard_map/ppermute | solution.py:448
  15.9 18.3 %collective-permute-start.13 = (bf16[128,512]{1,0:T(8,128)(2,1)}, bf16[128,512]{1,0:T(8,128)(2,1)S(1)}, u32[]{:S(2)}, u32[]{:S(2)}) collective-permute-start(bf16[128,512]{1,0:T(8,128)(2,1)} %get-tuple-element.43), channel_id=1, source_target_pairs={{0,24},{4,28},{8,16},{12,20},{16,8},{20,12},{24,0},{28,4},{1,25},{... | collective-permute-start | bytes 393224 | tf_op jit(solution)/shard_map/ppermute | solution.py:448
  19.5 2.6 %collective-permute-start = (bf16[6,1024]{1,0:T(8,128)(2,1)S(1)}, bf16[6,1024]{1,0:T(8,128)(2,1)S(1)}, u32[]{:S(2)}, u32[]{:S(2)}) collective-permute-start(bf16[6,1024]{1,0:T(8,128)(2,1)S(1)} %pad_maximum_fusion), channel_id=1, source_target_pairs={{0,4},{4,8},{8,12},{12,16},{16,20},{20,24},{24,28},{1,5},{5,9},{9,... | collective-permute-start | bytes 36872 | tf_op jit(solution)/shard_map/ppermute | solution.py:18
  22.2 1.5 copy-start.7
  22.2 12.8 %collective-permute-start.14 = (bf16[128,512]{1,0:T(8,128)(2,1)}, bf16[128,512]{1,0:T(8,128)(2,1)S(1)}, u32[]{:S(2)}, u32[]{:S(2)}) collective-permute-start(bf16[128,512]{1,0:T(8,128)(2,1)} %get-tuple-element.44), channel_id=1, source_target_pairs={{0,28},{4,24},{8,20},{12,16},{16,12},{20,8},{24,4},{28,0},{1,29},{... | collective-permute-start | bytes 393224 | tf_op jit(solution)/shard_map/ppermute | solution.py:448
  30.3 5.8 %collective-permute-start.8 = (bf16[128,512]{1,0:T(8,128)(2,1)}, bf16[128,512]{1,0:T(8,128)(2,1)S(1)}, u32[]{:S(2)}, u32[]{:S(2)}) collective-permute-start(bf16[128,512]{1,0:T(8,128)(2,1)} %get-tuple-element.38), channel_id=1, source_target_pairs={{0,4},{4,0},{8,12},{12,8},{16,20},{20,16},{24,28},{28,24},{1,5},{5... | collective-permute-start | bytes 393224 | tf_op jit(solution)/shard_map/ppermute | solution.py:448
  32.8 6.6 %collective-permute-start.9 = (bf16[128,512]{1,0:T(8,128)(2,1)}, bf16[128,512]{1,0:T(8,128)(2,1)S(1)}, u32[]{:S(2)}, u32[]{:S(2)}) collective-permute-start(bf16[128,512]{1,0:T(8,128)(2,1)} %get-tuple-element.39), channel_id=1, source_target_pairs={{0,8},{4,12},{8,0},{12,4},{16,24},{20,28},{24,16},{28,20},{1,9},{5... | collective-permute-start | bytes 393224 | tf_op jit(solution)/shard_map/ppermute | solution.py:448
  34.2 5.2 %collective-permute-start.1 = (bf16[512,128]{1,0:T(8,128)(2,1)}, bf16[512,128]{1,0:T(8,128)(2,1)S(1)}, u32[]{:S(2)}, u32[]{:S(2)}) collective-permute-start(bf16[512,128]{1,0:T(8,128)(2,1)} %get-tuple-element.30), channel_id=1, source_target_pairs={{0,4},{4,0},{8,12},{12,8},{16,20},{20,16},{24,28},{28,24},{1,5},{5... | collective-permute-start | bytes 393224 | tf_op jit(solution)/shard_map/ppermute | solution.py:448
  34.2 8.0 %collective-permute-start.2 = (bf16[512,128]{1,0:T(8,128)(2,1)}, bf16[512,128]{1,0:T(8,128)(2,1)S(1)}, u32[]{:S(2)}, u32[]{:S(2)}) collective-permute-start(bf16[512,128]{1,0:T(8,128)(2,1)} %get-tuple-element.31), channel_id=1, source_target_pairs={{0,8},{4,12},{8,0},{12,4},{16,24},{20,28},{24,16},{28,20},{1,9},{5... | collective-permute-start | bytes 393224 | tf_op jit(solution)/shard_map/ppermute | solution.py:448
  34.9 19.2 %collective-permute-start.3 = (bf16[512,128]{1,0:T(8,128)(2,1)}, bf16[512,128]{1,0:T(8,128)(2,1)S(1)}, u32[]{:S(2)}, u32[]{:S(2)}) collective-permute-start(bf16[512,128]{1,0:T(8,128)(2,1)} %get-tuple-element.32), channel_id=1, source_target_pairs={{0,12},{4,8},{8,4},{12,0},{16,28},{20,24},{24,20},{28,16},{1,13},{... | collective-permute-start | bytes 393224 | tf_op jit(solution)/shard_map/ppermute | solution.py:448
  36.0 18.1 %collective-permute-start.4 = (bf16[512,128]{1,0:T(8,128)(2,1)}, bf16[512,128]{1,0:T(8,128)(2,1)S(1)}, u32[]{:S(2)}, u32[]{:S(2)}) collective-permute-start(bf16[512,128]{1,0:T(8,128)(2,1)} %get-tuple-element.33), channel_id=1, source_target_pairs={{0,16},{4,20},{8,24},{12,28},{16,0},{20,4},{24,8},{28,12},{1,17},{... | collective-permute-start | bytes 393224 | tf_op jit(solution)/shard_map/ppermute | solution.py:448
  39.4 14.8 %collective-permute-start.5 = (bf16[512,128]{1,0:T(8,128)(2,1)}, bf16[512,128]{1,0:T(8,128)(2,1)S(1)}, u32[]{:S(2)}, u32[]{:S(2)}) collective-permute-start(bf16[512,128]{1,0:T(8,128)(2,1)} %get-tuple-element.34), channel_id=1, source_target_pairs={{0,20},{4,16},{8,28},{12,24},{16,4},{20,0},{24,12},{28,8},{1,21},{... | collective-permute-start | bytes 393224 | tf_op jit(solution)/shard_map/ppermute | solution.py:448
  39.4 14.8 %collective-permute-start.6 = (bf16[512,128]{1,0:T(8,128)(2,1)}, bf16[512,128]{1,0:T(8,128)(2,1)S(1)}, u32[]{:S(2)}, u32[]{:S(2)}) collective-permute-start(bf16[512,128]{1,0:T(8,128)(2,1)} %get-tuple-element.35), channel_id=1, source_target_pairs={{0,24},{4,28},{8,16},{12,20},{16,8},{20,12},{24,0},{28,4},{1,25},{... | collective-permute-start | bytes 393224 | tf_op jit(solution)/shard_map/ppermute | solution.py:448
  42.2 12.0 %collective-permute-start.7 = (bf16[512,128]{1,0:T(8,128)(2,1)}, bf16[512,128]{1,0:T(8,128)(2,1)S(1)}, u32[]{:S(2)}, u32[]{:S(2)}) collective-permute-start(bf16[512,128]{1,0:T(8,128)(2,1)} %get-tuple-element.36), channel_id=1, source_target_pairs={{0,28},{4,24},{8,20},{12,16},{16,12},{20,8},{24,4},{28,0},{1,29},{... | collective-permute-start | bytes 393224 | tf_op jit(solution)/shard_map/ppermute | solution.py:448
  43.4 1.0 copy-start.2
  44.4 0.8 copy-start.4
  45.2 0.9 copy-start.5
  54.2 0.9 copy-start.6
  73.4 3.7 %collective-permute-start.15 = (bf16[512,128]{1,0:T(8,128)(2,1)S(1)}, bf16[512,128]{1,0:T(8,128)(2,1)S(1)}, u32[]{:S(2)}, u32[]{:S(2)}) collective-permute-start(bf16[512,128]{1,0:T(8,128)(2,1)S(1)} %get-tuple-element.46), channel_id=1, source_target_pairs={{0,4},{4,0},{8,12},{12,8},{16,20},{20,16},{24,28},{28,24},{1,5},{5... | collective-permute-start | bytes 393224 | tf_op jit(solution)/shard_map/ppermute | solution.py:448
  73.5 6.4 %collective-permute-start.16 = (bf16[512,128]{1,0:T(8,128)(2,1)S(1)}, bf16[512,128]{1,0:T(8,128)(2,1)S(1)}, u32[]{:S(2)}, u32[]{:S(2)}) collective-permute-start(bf16[512,128]{1,0:T(8,128)(2,1)S(1)} %get-tuple-element.47), channel_id=1, source_target_pairs={{0,8},{4,12},{8,0},{12,4},{16,24},{20,28},{24,16},{28,20},{1,9},{5... | collective-permute-start | bytes 393224 | tf_op jit(solution)/shard_map/ppermute | solution.py:448
  75.5 8.4 %collective-permute-start.17 = (bf16[512,128]{1,0:T(8,128)(2,1)S(1)}, bf16[512,128]{1,0:T(8,128)(2,1)S(1)}, u32[]{:S(2)}, u32[]{:S(2)}) collective-permute-start(bf16[512,128]{1,0:T(8,128)(2,1)S(1)} %get-tuple-element.48), channel_id=1, source_target_pairs={{0,12},{4,8},{8,4},{12,0},{16,28},{20,24},{24,20},{28,16},{1,13},{... | collective-permute-start | bytes 393224 | tf_op jit(solution)/shard_map/ppermute | solution.py:448
  75.5 8.4 %collective-permute-start.18 = (bf16[512,128]{1,0:T(8,128)(2,1)S(1)}, bf16[512,128]{1,0:T(8,128)(2,1)S(1)}, u32[]{:S(2)}, u32[]{:S(2)}) collective-permute-start(bf16[512,128]{1,0:T(8,128)(2,1)S(1)} %get-tuple-element.49), channel_id=1, source_target_pairs={{0,16},{4,20},{8,24},{12,28},{16,0},{20,4},{24,8},{28,12},{1,17},{... | collective-permute-start | bytes 393224 | tf_op jit(solution)/shard_map/ppermute | solution.py:448
  76.8 12.1 %collective-permute-start.19 = (bf16[512,128]{1,0:T(8,128)(2,1)S(1)}, bf16[512,128]{1,0:T(8,128)(2,1)S(1)}, u32[]{:S(2)}, u32[]{:S(2)}) collective-permute-start(bf16[512,128]{1,0:T(8,128)(2,1)S(1)} %get-tuple-element.50), channel_id=1, source_target_pairs={{0,20},{4,16},{8,28},{12,24},{16,4},{20,0},{24,12},{28,8},{1,21},{... | collective-permute-start | bytes 393224 | tf_op jit(solution)/shard_map/ppermute | solution.py:448
  77.1 11.7 %collective-permute-start.20 = (bf16[512,128]{1,0:T(8,128)(2,1)S(1)}, bf16[512,128]{1,0:T(8,128)(2,1)S(1)}, u32[]{:S(2)}, u32[]{:S(2)}) collective-permute-start(bf16[512,128]{1,0:T(8,128)(2,1)S(1)} %get-tuple-element.51), channel_id=1, source_target_pairs={{0,24},{4,28},{8,16},{12,20},{16,8},{20,12},{24,0},{28,4},{1,25},{... | collective-permute-start | bytes 393224 | tf_op jit(solution)/shard_map/ppermute | solution.py:448
  79.9 8.9 %collective-permute-start.21 = (bf16[512,128]{1,0:T(8,128)(2,1)S(1)}, bf16[512,128]{1,0:T(8,128)(2,1)S(1)}, u32[]{:S(2)}, u32[]{:S(2)}) collective-permute-start(bf16[512,128]{1,0:T(8,128)(2,1)S(1)} %get-tuple-element.52), channel_id=1, source_target_pairs={{0,28},{4,24},{8,20},{12,16},{16,12},{20,8},{24,4},{28,0},{1,29},{... | collective-permute-start | bytes 393224 | tf_op jit(solution)/shard_map/ppermute | solution.py:448
  88.8 1.6 copy-start.1
Sparse Core Ops, SparseCore 0:
  100.4 77.9 reduce-scatter.1

commit v2 on v1

--- a/solution.py
+++ b/solution.py
@@ -451,54 +451,221 @@
     ]
 
 
-def project(gated_out, out_weight):
-    term = jnp.dot(gated_out, out_weight, preferred_element_type=F32)
-    return lax.psum_scatter(term.astype(BF16), "tp", scatter_dimension=1, tiled=True)
-
-
-def gate_out_kernel(blocks, me_ref, *refs):
-    convs, (mixed, out) = refs[:blocks], refs[blocks:]
+def gate_out_kernel(blocks, place, *refs):
+    convs, (mixed, far_weight, head, tail, right, left) = refs[:blocks], refs[blocks:]
     lanes = convs[0].shape[1]
+    rows = head.shape[0]
+    stage, last = place[1], place[2]
     for m in range(blocks):
-        window = pl.ds(pl.multiple_of((me_ref[0] ^ m) * lanes, lanes), lanes)
-        out[:, window] = (mixed[:, window] * convs[m][...].astype(F32)).astype(BF16)
-
-
-def gate_out(me, convs, mixed):
+        window = pl.ds(pl.multiple_of((place[0] ^ m) * lanes, lanes), lanes)
+        gated = (mixed[:, window] * convs[m][...].astype(F32)).astype(BF16)
+        head[:, window] = gated[:rows]
+        tail[:, window] = gated[rows:]
+    for index, out in ((0, right), (last, left)):
+
+        @pl.when(stage == index)
+        def _(out=out):
+            term = jnp.dot(tail[...], far_weight[...], preferred_element_type=F32)
+            out[...] = term.astype(BF16)
+
+        @pl.when(stage != index)
+        def _(out=out):
+            out[...] = head[...]
+
+
+def gate_out(place, convs, mixed, out_weight):
     span, chans = mixed.shape
+    whole = lambda shape: pl.BlockSpec(shape, lambda g, place: (0,) * len(shape))
     return pl.pallas_call(
         partial(gate_out_kernel, len(convs)),
-        out_shape=jax.ShapeDtypeStruct((span, chans), BF16),
-        in_specs=[SMEM] + [VMEM] * (len(convs) + 1),
-        out_specs=VMEM,
+        grid_spec=pltpu.PrefetchScalarGridSpec(
+            num_scalar_prefetch=1,
+            grid=(1,),
+            in_specs=[whole(x.shape) for x in (*convs, mixed)]
+            + [pl.BlockSpec((chans, chans), lambda g, place: (0, place[3]))],
+            out_specs=[whole((span // 2, chans))] * 4,
+        ),
+        out_shape=[jax.ShapeDtypeStruct((span // 2, chans), BF16)] * 4,
         compiler_params=GRANT,
         name="gate_out",
-    )(me, *convs, mixed)
+    )(place, *convs, mixed, out_weight)
+
+
+def weight_rows(out_weight, stages):
+    stage, place = lax.axis_index("tp"), lax.axis_index("ctx")
+    chans = out_weight.shape[0]
+    rows = chans // lax.axis_size("ctx")
+    found = []
+    for d in range(1, stages):
+        column = (stage + d) % stages * chans
+        part = lax.dynamic_slice(out_weight, (place * rows, column), (rows, chans))
+        found.append(lax.ppermute(part, "tp", [(i, (i + d) % stages) for i in range(stages)]))
+    return jnp.stack(found)
+
+
+def gather_weight(part):
+    devices = range(lax.axis_size("ctx"))
+    near = [(i, i ^ (4 if i & 1 else 2)) for i in devices]
+    other = [(i, i ^ (2 if i & 1 else 4)) for i in devices]
+    two = jnp.stack([part, lax.ppermute(part, "ctx", near)])
+    four = jnp.concatenate([two, lax.ppermute(two, "ctx", other)])
+    return four, lax.ppermute(four, "ctx", [(i, i ^ 1) for i in devices])
+
+
+def add_parts(order, data, weights, chosen):
+    total = None
+    for half, weight in enumerate(weights):
+        count, _, lanes, columns = weight.shape
+        picked = jnp.concatenate(
+            [
+                data[:, pl.ds(pl.multiple_of(order[4 * half + q] * lanes, lanes), lanes)]
+                for q in range(count)
+            ],
+            axis=1,
+        )
+        block = weight[:, chosen].reshape(count * lanes, columns)
+        term = jnp.dot(picked, block, preferred_element_type=F32)
+        total = term if total is None else total + term
+    return total
+
+
+def early_kernel(order, own, first, second, own_weight, near_weight, far_weight, out):
+    weights = (near_weight, far_weight)
+    out[...] = jnp.dot(own[...], own_weight[...], preferred_element_type=F32)
+    out[...] += add_parts(order, first, weights, order[8])
+    out[...] += add_parts(order, second, weights, order[9])
+
+
+def early_sum(order, own, first, second, out_weight, near_weight, far_weight):
+    rows, chans = own.shape
+    whole = lambda shape: pl.BlockSpec(shape, lambda g, order: (0,) * len(shape))
+    return pl.pallas_call(
+        early_kernel,
+        grid_spec=pltpu.PrefetchScalarGridSpec(
+            num_scalar_prefetch=1,
+            grid=(1,),
+            in_specs=[whole(own.shape)] * 3
+            + [pl.BlockSpec((chans, chans), lambda g, order: (0, order[11]))]
+            + [whole(near_weight.shape)] * 2,
+            out_specs=whole((rows, chans)),
+        ),
+        out_shape=jax.ShapeDtypeStruct((rows, chans), F32),
+        compiler_params=GRANT,
+        name="early_sum",
+    )(order, own, first, second, out_weight, near_weight, far_weight)
+
+
+def final_kernel(order, *refs):
+    thirds, (early, own, right2, right3, left2, left3) = refs[:4], refs[4:10]
+    near_weight, far_weight, out, picked = refs[10:]
+    rows = early.shape[0]
+    stage, last = order[11], order[12]
+    for k, third in enumerate(thirds):
+
+        @pl.when(stage == k)
+        def _(third=third):
+            picked[...] = third[...]
+
+    total = early[...] + add_parts(order, picked, (near_weight, far_weight), order[10])
+    out[:rows] = total.astype(BF16)
+    right = jnp.where(stage == last, right2[...].astype(F32), right3[...].astype(F32))
+    left = jnp.where(stage == 0, left2[...].astype(F32), left3[...].astype(F32))
+    out[rows:] = (own[...].astype(F32) + right + left).astype(BF16)
+
+
+def final_sum(order, thirds, early, own, arrived, near_weight, far_weight):
+    rows, chans = own.shape
+    return pl.pallas_call(
+        final_kernel,
+        out_shape=jax.ShapeDtypeStruct((2 * rows, chans), BF16),
+        in_specs=[SMEM] + [VMEM] * 12,
+        out_specs=VMEM,
+        scratch_shapes=[pltpu.VMEM((rows, chans), BF16)],
+        compiler_params=GRANT,
+        name="final_sum",
+    )(order, *thirds, early, own, *arrived, near_weight, far_weight)
+
+
+def weight_order():
+    place, stage = lax.axis_index("ctx"), lax.axis_index("tp")
+    a = jnp.where(place % 2 == 0, 2, 4)
+    masks = [0 * a, a, 6 - a, 0 * a + 6]
+    swapped = [0 * a + 1, (6 - a) ^ 1, a ^ 1, 0 * a + 7]
+    parts = [place ^ mask for mask in masks + swapped]
+    distances = [jnp.array(row)[stage] - 1 for row in ((3, 3, 1, 1), (2, 1, 3, 2), (1, 2, 2, 3))]
+    last = lax.axis_size("tp") - 1
+    return jnp.stack(parts + distances + [stage, last + 0 * stage]).astype(jnp.int32)
+
+
+def project(place, convs, mixed, out_weight, weight_part):
+    stages = lax.axis_size("tp")
+    stage = lax.axis_index("tp")
+    order = weight_order()
+    head, tail, right0, left0 = gate_out(place, convs, mixed, out_weight)
+    chans = head.shape[1]
+    ahead = [(i, i + 1) for i in range(stages - 1)]
+    astern = [(i + 1, i) for i in range(stages - 1)]
+    to_right = lambda x: lax.ppermute(x, "tp", ahead)
+    to_left = lambda x: lax.ppermute(x, "tp", astern)
+    got_right0, got_left0 = to_right(right0), to_left(left0)
+    terms = jnp.dot(tail, out_weight, preferred_element_type=F32).astype(BF16)
+
+    def term(index):
+        return lax.dynamic_slice(terms, (0, index * chans), (terms.shape[0], chans)).astype(F32)
+
+    def add(index, arrived):
+        return (term(index) + arrived.astype(F32)).astype(BF16)
+
+    right1 = jnp.where(
+        stage == 0, head, jnp.where(stage == 1, add(3, got_right0), got_right0)
+    )
+    left1 = jnp.where(stage == 3, head, jnp.where(stage == 2, add(0, got_left0), got_left0))
+    got_right1, got_left1 = to_right(right1), to_left(left1)
+    right2 = jnp.where(
+        stage == 1, got_right1, add(jnp.where(stage == 0, 2, 3), got_right1)
+    )
+    left2 = jnp.where(stage == 2, got_left1, add(jnp.where(stage == 3, 1, 0), got_left1))
+    got_right2, got_left2 = to_right(right2), to_left(left2)
+    right3 = jnp.where(stage == 2, got_right2, add(jnp.minimum(stage + 1, 3), got_right2))
+    left3 = jnp.where(stage == 1, got_left2, add(jnp.maximum(stage - 1, 0), got_left2))
+    got_right3, got_left3 = to_right(right3), to_left(left3)
+
+    near_weight, far_weight = gather_weight(weight_part)
+    first = jnp.where(stage < 2, got_left0, got_right0)
+    second = jnp.where(stage % 2 == 0, got_left1, got_right1)
+    early = early_sum(order, head, first, second, out_weight, near_weight, far_weight)
+    own = term(stage).astype(BF16)
+    thirds = (got_left3, got_left2, got_right2, got_right3)
+    arrived = (got_right2, got_right3, got_left2, got_left3)
+    return final_sum(order, thirds, early, own, arrived, near_weight, far_weight)
 
 
 def fast_per_device(
     query_rows, key_rows, value_rows, short_weight, skip_gain, filter_taps, out_weight
 ):
     span, chans = query_rows.shape
-    blocks = lax.axis_size("ctx")
+    blocks, stages = lax.axis_size("ctx"), lax.axis_size("tp")
     lanes = chans // blocks
     length = span * blocks
     radix = 2 * length // SUB
-    place = lax.axis_index("ctx")
+    place, stage = lax.axis_index("ctx"), lax.axis_index("tp")
     me = place.astype(jnp.int32).reshape(1)
+    far = jnp.where(stage == 0, stages - 1, 0)
+    spot = jnp.stack([place, stage, stages - 1 + 0 * stage, far]).astype(jnp.int32)
     forward, inverse = (jnp.asarray(t) for t in dft_tables(2 * length))
     twiddle = jnp.asarray(twiddle_table(radix))
     edges = jnp.concatenate([x[-2:] for x in (query_rows, key_rows, value_rows)])
     edges = passed_along(edges, "ctx", 1)
     taps = exchange(split_taps(me, filter_taps, blocks), "ctx")
     gated = exchange(gate_in(me, key_rows, value_rows, edges, short_weight, blocks), "ctx")
+    weight_part = weight_rows(out_weight, stages)
     mixed = mix_query(query_rows, edges, short_weight)
     skip = lax.dynamic_slice(skip_gain, (place * lanes,), (lanes,)).reshape(1, lanes)
     spectra = taps_spectra_of(me, taps, twiddle, forward)
     convs = long_conv(me, gated, spectra, twiddle, forward, inverse, skip)
     convs = exchange(convs, "ctx")
-    gated_out = gate_out(me, convs, mixed)
-    return project(gated_out, out_weight)
+    weight_part, *convs = lax.optimization_barrier((weight_part, *convs))
+    return project(spot, convs, mixed, out_weight, weight_part)
 
 
 def per_device(*arrays):

time: 186 us -> 190 us (1.022)
  waiting for transfers between devices: 89.5 us -> 53.3 us
  starting transfers between devices: 23.1 us -> 50.6 us
  Pallas kernels: 42.2 us -> 53.8 us
  between operations: 13.5 us -> 2.41 us
  other arithmetic: 0.02 us -> 10.6 us
  matrix products: 9.47 us -> 2.39 us
  local copies, waits for them, and re-layouts: 7.49 us -> 14.3 us
    reduce_scatter x1 -> x0, waiting for transfers between devices: 78.1 us -> none  [project(): lax.psum_scatter(term.astype(BF16), 'tp', scatter_dimension=1, tiled=True)]
    ppermute x0 -> x14, waiting for transfers between devices: none -> 41.9 us  [the longest x4 15.5 us: project(): to_right = lambda x: lax.ppermute(x, 'tp', ahead)]
    ppermute x0 -> x14, starting transfers between devices: none -> 28.6 us  [the longest x4 14.8 us: project(): to_right = lambda x: lax.ppermute(x, 'tp', ahead)]
    pallas_call x1 -> x3, Pallas kernels: 0.34 us -> 12.1 us  [the longest x1 5.44 us: final_sum(): pl.pallas_call(final_kernel, out_shape=jax.ShapeDtypeStruct((2 * rows, ch...]
    dot_general x1, matrix products: 9.47 us -> 2.39 us  [project(): terms = jnp.dot(tail, out_weight, preferred_element_type=F32).astype(BF16)]
    select_n x0 -> x2, other arithmetic: none -> 5.16 us  [the longest x1 3.48 us: project(): jnp.where(stage == 1, got_right1, add(jnp.where(stage == 0, 2, 3), got_ri...]
    unnamed x16 -> x44, local copies, waits for them, and re-layouts: 5.24 us -> 8.89 us
    dynamic_slice x0 -> x1, other arithmetic: none -> 3.41 us  [term(): lax.dynamic_slice(terms, (0, index * chans), (terms.shape[0], chans))]
  transfers between devices with their start and end apart: 23 -> 36, of which waited for: 6 -> 12; matrix products, arithmetic and copies ran while one was open for 1% -> 10% of each run, Pallas kernels for 10% -> 23%
where the time goes in v2:
time: 190 us; the launch traced here: 187 us
  Pallas kernels  53.8 us (28%)
  waiting for transfers between devices  53.3 us (28%)
  starting transfers between devices  50.6 us (27%)
  local copies, waits for them, and re-layouts  14.3 us (8%)
  other arithmetic  10.6 us (6%)
  between operations  2.41 us (1%)
  matrix products  2.39 us (1%)
    ppermute x21, starting transfers between devices, exchange(): lax.ppermute(piece, axis, [(i, i ^ m) for i in devices])  19.9 us
    pallas_call x1, Pallas kernels, long_conv(): pl.pallas_call(partial(conv_kernel, blocks), out_shape=[jax.ShapeDtypeStr...  18.3 us
    ppermute x4, waiting for transfers between devices, project(): to_right = lambda x: lax.ppermute(x, 'tp', ahead)  15.5 us
    ppermute x4, starting transfers between devices, project(): to_right = lambda x: lax.ppermute(x, 'tp', ahead)  14.8 us
    ppermute x1, waiting for transfers between devices, gather_weight(): two = jnp.stack([part, lax.ppermute(part, 'ctx', near)])  11.5 us
    ppermute x21, waiting for transfers between devices, exchange(): lax.ppermute(piece, axis, [(i, i ^ m) for i in devices])  11.3 us
    ppermute x4, waiting for transfers between devices, project(): to_left = lambda x: lax.ppermute(x, 'tp', astern)  11.2 us
    unnamed x44, local copies, waits for them, and re-layouts  8.89 us
  transfers between devices with their start and end apart: 36, of which 12 were waited for; matrix products, arithmetic and copies ran while one was open for 10% of the time, Pallas kernels for 23%

profile of v2, /device:TPU:0, one launch (start us, length us, event | category | flops | bytes accessed | tf_op | source)
XLA Modules:
  0.0 187.4 jit_solution(9718931885491815829)
XLA Ops:
  0.0 4.9 %split_taps.1 = (bf16[128,512]{1,0:T(8,128)(2,1)}, bf16[128,512]{1,0:T(8,128)(2,1)}, bf16[128,512]{1,0:T(8,128)(2,1)}, bf16[128,512]{1,0:T(8,128)(2,1)}, bf16[12...) custom-call(s32[1]{0:T(128)} %bitcast.me_ref, ...), custom_call_target="tpu_custom_call" | custom-call | tf_op jit(solution)/shard_map/split_taps/pallas_call | solution.py:411
  5.4 2.6 %collective-permute-start.12 = (bf16[128,512]{1,0:T(8,128)(2,1)}, bf16[128,512]{1,0:T(8,128)(2,1)S(1)}, u32[]{:S(2)}, u32[]{:S(2)}) collective-permute-start(bf16[128,512]{1,0:T(8,128)(2,1)} %get-tuple-element.52), channel_id=1, source_target_pairs={{0,8},{4,12},{8,0},{12,4},{16,24},{20,28},{24,16},{28,20},{1,9},{5... | collective-permute-start | bytes 393224 | tf_op jit(solution)/shard_map/ppermute | solution.py:448
  10.1 2.1 %collective-permute-start.3 = (bf16[6,1024]{1,0:T(8,128)(2,1)S(1)}, bf16[6,1024]{1,0:T(8,128)(2,1)S(1)}, u32[]{:S(2)}, u32[]{:S(2)}) collective-permute-start(bf16[6,1024]{1,0:T(8,128)(2,1)S(1)} %pad_maximum_fusion.3), channel_id=1, source_target_pairs={{0,4},{4,8},{8,12},{12,16},{16,20},{20,24},{24,28},{1,5},{5,9},{9,... | collective-permute-start | bytes 36872 | tf_op jit(solution)/shard_map/ppermute | solution.py:18
  12.2 2.6 %collective-permute-start.13 = (bf16[128,512]{1,0:T(8,128)(2,1)}, bf16[128,512]{1,0:T(8,128)(2,1)S(1)}, u32[]{:S(2)}, u32[]{:S(2)}) collective-permute-start(bf16[128,512]{1,0:T(8,128)(2,1)} %get-tuple-element.53), channel_id=1, source_target_pairs={{0,12},{4,8},{8,4},{12,0},{16,28},{20,24},{24,20},{28,16},{1,13},{... | collective-permute-start | bytes 393224 | tf_op jit(solution)/shard_map/ppermute | solution.py:448
  14.9 2.2 %collective-permute-start.16 = (bf16[128,512]{1,0:T(8,128)(2,1)}, bf16[128,512]{1,0:T(8,128)(2,1)S(1)}, u32[]{:S(2)}, u32[]{:S(2)}) collective-permute-start(bf16[128,512]{1,0:T(8,128)(2,1)} %get-tuple-element.56), channel_id=1, source_target_pairs={{0,24},{4,28},{8,16},{12,20},{16,8},{20,12},{24,0},{28,4},{1,25},{... | collective-permute-start | bytes 393224 | tf_op jit(solution)/shard_map/ppermute | solution.py:448
  17.0 3.1 %collective-permute-start.17 = (bf16[128,512]{1,0:T(8,128)(2,1)}, bf16[128,512]{1,0:T(8,128)(2,1)S(1)}, u32[]{:S(2)}, u32[]{:S(2)}) collective-permute-start(bf16[128,512]{1,0:T(8,128)(2,1)} %get-tuple-element.57), channel_id=1, source_target_pairs={{0,28},{4,24},{8,20},{12,16},{16,12},{20,8},{24,4},{28,0},{1,29},{... | collective-permute-start | bytes 393224 | tf_op jit(solution)/shard_map/ppermute | solution.py:448
  20.1 6.6 %gate_in.1 = (bf16[512,128]{1,0:T(8,128)(2,1)}, bf16[512,128]{1,0:T(8,128)(2,1)}, bf16[512,128]{1,0:T(8,128)(2,1)}, bf16[512,128]{1,0:T(8,128)(2,1)}, bf16[512,1...) custom-call(s32[1]{0:T(128)} %bitcast.me_ref, ...), custom_call_target="tpu_custom_call" | custom-call | tf_op jit(solution)/shard_map/gate_in/pallas_call | solution.py:382
  26.9 1.8 collective-permute-start.6
  30.4 1.2 fusion.8
  31.6 2.0 %collective-permute-start = (bf16[128,1024]{1,0:T(8,128)(2,1)S(1)}, bf16[128,1024]{1,0:T(8,128)(2,1)S(1)}, u32[]{:S(2)}, u32[]{:S(2)}) collective-permute-start(bf16[128,1024]{1,0:T(8,128)(2,1)S(1)} %get-tuple-element.79), channel_id=1, source_target_pairs={{0,1},{1,2},{2,3},{3,0},{4,5},{5,6},{6,7},{7,4},{8,9},{9,10},{10,1... | collective-permute-start | bytes 786440 | tf_op jit(solution)/shard_map/ppermute | solution.py:502
  33.6 3.3 %collective-permute-start.2 = (bf16[128,1024]{1,0:T(8,128)(2,1)S(1)}, bf16[128,1024]{1,0:T(8,128)(2,1)S(1)}, u32[]{:S(2)}, u32[]{:S(2)}) collective-permute-start(bf16[128,1024]{1,0:T(8,128)(2,1)S(1)} %get-tuple-element.80), channel_id=1, source_target_pairs={{0,3},{1,0},{2,1},{3,2},{4,7},{5,4},{6,5},{7,6},{8,11},{9,8},{10,9... | collective-permute-start | bytes 786440 | tf_op jit(solution)/shard_map/ppermute | solution.py:502
  38.1 2.5 %collective-permute-start.1 = (bf16[128,1024]{1,0:T(8,128)(2,1)S(1)}, bf16[128,1024]{1,0:T(8,128)(2,1)S(1)}, u32[]{:S(2)}, u32[]{:S(2)}) collective-permute-start(bf16[128,1024]{1,0:T(8,128)(2,1)S(1)} %get-tuple-element.81), channel_id=1, source_target_pairs={{0,2},{1,3},{2,0},{3,1},{4,6},{5,7},{6,4},{7,5},{8,10},{9,11},{10,... | collective-permute-start | bytes 786440 | tf_op jit(solution)/shard_map/ppermute | solution.py:502
  40.7 8.0 %taps_spectra.1.refs_8_ = f32[17,256,256]{2,1,0:T(8,128)S(1)} custom-call(s32[1]{0:T(128)} %bitcast.me_ref, bf16[128,512]{1,0:T(8,128)(2,1)S(1)} %copy-done.11, bf16[128,512]{1,0:T(8,128)(2,1)S(1)} %collective-permute-done.11.refs_1_, bf16[128,512]{1,0:T(8,128)(2,1)S(1)} %collective-permute-done.12.refs_2_, ...), custom_call_target="tpu_custom_call" | custom-call | tf_op jit(solution)/shard_map/taps_spectra/pallas_call | solution.py:326
  48.8 18.3 %long_conv.1 = (bf16[512,128]{1,0:T(8,128)(2,1)S(1)}, bf16[512,128]{1,0:T(8,128)(2,1)S(1)}, bf16[512,128]{1,0:T(8,128)(2,1)S(1)}, bf16[512,128]{1,0:T(8,128)(2,1...) custom-call(s32[1]{0:T(128)} %bitcast.me_ref, ...), custom_call_target="tpu_custom_call" | custom-call | tf_op jit(solution)/shard_map/long_conv/pallas_call | solution.py:344
  67.6 1.4 collective-permute-start.20
  69.4 1.4 collective-permute-start.22
  71.3 2.3 %collective-permute-done.19.refs_2_ = bf16[512,128]{1,0:T(8,128)(2,1)S(1)} collective-permute-done((bf16[512,128]{1,0:T(8,128)(2,1)S(1)}, bf16[512,128]{1,0:T(8,128)(2,1)S(1)}, u32[]{:S(2)}, u32[]{:S(2)}) %collective-permute-start.19) | collective-permute-done | bytes 131104 | tf_op jit(solution)/shard_map/ppermute | solution.py:448
  73.7 1.8 collective-permute-done.20.refs_3_
  75.5 7.1 %collective-permute-done.22.refs_5_ = bf16[512,128]{1,0:T(8,128)(2,1)S(1)} collective-permute-done((bf16[512,128]{1,0:T(8,128)(2,1)S(1)}, bf16[512,128]{1,0:T(8,128)(2,1)S(1)}, u32[]{:S(2)}, u32[]{:S(2)}) %collective-permute-start.22) | collective-permute-done | bytes 131104 | tf_op jit(solution)/shard_map/ppermute | solution.py:448
  83.1 11.5 %collective-permute-done.33 = bf16[3,128,1024]{2,1,0:T(8,128)(2,1)S(1)} collective-permute-done((bf16[3,128,1024]{2,1,0:T(8,128)(2,1)S(1)}, bf16[3,128,1024]{2,1,0:T(8,128)(2,1)S(1)}, u32[]{:S(2)}, u32[]{:S(2)}) %collective-permute-start.33) | collective-permute-done | bytes 786464 | tf_op jit(solution)/shard_map/ppermute | solution.py:510
  95.7 3.9 %mix_query.1.refs_8_ = f32[512,1024]{1,0:T(8,128)} custom-call(bf16[512,1024]{1,0:T(8,128)(2,1)} %query.1, bf16[6,1024]{1,0:T(8,128)(2,1)} %copy-done.18, f32[3,3,1024]{2,1,0:T(4,128)} %weight.3), custom_call_target="tpu_custom_call" | custom-call | tf_op jit(solution)/shard_map/mix_query/pallas_call | solution.py:431
  99.7 3.4 %copy-done.1 = bf16[1024,4096]{1,0:T(8,128)(2,1)S(1)} copy-done((bf16[1024,4096]{1,0:T(8,128)(2,1)S(1)}, bf16[1024,4096]{1,0:T(8,128)(2,1)}, u32[]{:S(2)}) %copy-start.1) | copy-done | bytes 8388632
  103.0 1.6 copy-done.2
  104.6 1.8 gate_out.1
  106.4 1.3 collective-permute-start.25
  107.7 4.6 %collective-permute-start.29 = (bf16[256,1024]{1,0:T(8,128)(2,1)S(1)}, bf16[256,1024]{1,0:T(8,128)(2,1)S(1)}, u32[]{:S(2)}, u32[]{:S(2)}) collective-permute-start(bf16[256,1024]{1,0:T(8,128)(2,1)S(1)} %get-tuple-element.77), channel_id=1, source_target_pairs={{0,1},{1,2},{2,3},{4,5},{5,6},{6,7},{8,9},{9,10},{10,11},{12,13},{... | collective-permute-start | bytes 1572872 | tf_op jit(solution)/shard_map/ppermute | solution.py:608
  112.3 3.7 %collective-permute-done.34 = bf16[2,3,128,1024]{3,2,1,0:T(8,128)(2,1)} collective-permute-done((bf16[2,3,128,1024]{3,2,1,0:T(8,128)(2,1)S(1)}, bf16[2,3,128,1024]{3,2,1,0:T(8,128)(2,1)}, u32[]{:S(2)}, u32[]{:S(2)}) %collective-permute-start.34) | collective-permute-done | bytes 1572896 | tf_op jit(solution)/shard_map/ppermute | solution.py:511
  116.1 1.7 pad_maximum_fusion.near_weight.refs_10_
  117.9 2.4 %convolution_convert_fusion = bf16[256,4096]{1,0:T(8,128)(2,1)S(1)} fusion(bf16[256,1024]{1,0:T(8,128)(2,1)S(1)} %get-tuple-element.75, bf16[1024,4096]{1,0:T(8,128)(2,1)S(1)} %copy-done.1), kind=kOutput, calls=%fused_computation | convolution fusion | flops 2148532224 | bytes 11010048 | tf_op jit(solution)/shard_map/dot_general | solution.py:611
  120.3 1.4 collective-permute-done.25
  121.7 1.2 collective-permute-done.29
  122.8 1.7 fusion.6
  124.5 5.2 %collective-permute-start.30 = (bf16[256,1024]{1,0:T(8,128)(2,1)}, bf16[256,1024]{1,0:T(8,128)(2,1)}, u32[]{:S(2)}, u32[]{:S(2)}) collective-permute-start(bf16[256,1024]{1,0:T(8,128)(2,1)} %get-tuple-element.82), channel_id=1, source_target_pairs={{0,1},{1,2},{2,3},{4,5},{5,6},{6,7},{8,9},{9,10},{10,11},{12,13},{... | collective-permute-start | bytes 1572872 | tf_op jit(solution)/shard_map/ppermute | solution.py:608
  129.7 1.5 collective-permute-start.26
  131.2 7.6 %collective-permute-done.30 = bf16[256,1024]{1,0:T(8,128)(2,1)} collective-permute-done((bf16[256,1024]{1,0:T(8,128)(2,1)}, bf16[256,1024]{1,0:T(8,128)(2,1)}, u32[]{:S(2)}, u32[]{:S(2)}) %collective-permute-start.30) | collective-permute-done | bytes 524320 | tf_op jit(solution)/shard_map/ppermute | solution.py:608
  138.9 4.9 %collective-permute-done.26 = bf16[256,1024]{1,0:T(8,128)(2,1)} collective-permute-done((bf16[256,1024]{1,0:T(8,128)(2,1)}, bf16[256,1024]{1,0:T(8,128)(2,1)}, u32[]{:S(2)}, u32[]{:S(2)}) %collective-permute-start.26) | collective-permute-done | bytes 524320 | tf_op jit(solution)/shard_map/ppermute | solution.py:609
  143.8 3.5 %fusion.4 = (bf16[256,1024]{1,0:T(8,128)(2,1)}, bf16[256,1024]{1,0:T(8,128)(2,1)}, bf16[256,1024]{1,0:T(8,128)(2,1)}) fusion(bf16[256,1024]{1,0:T(8,128)(2,1)} %collective-permute-done.30, bf16[256,4096]{1,0:T(8,128)(2,1)} %copy-done.15, s32[]{:T(128)S(6)} %select_n.150, pred[]{:T(512)S(6)} %eq.32, bf16[256,1024]{1,0:T(8,128)(2,1)} %collective-permute-done.26, ...), kind=kLoop, calls=%fused_computation.13 | loop fusion | flops 2883584 | bytes 3670027 | tf_op jit(solution)/shard_map/jit(_where)/select_n | solution.py:624
  147.2 2.8 %collective-permute-start.31 = (bf16[256,1024]{1,0:T(8,128)(2,1)}, bf16[256,1024]{1,0:T(8,128)(2,1)}, u32[]{:S(2)}, u32[]{:S(2)}) collective-permute-start(bf16[256,1024]{1,0:T(8,128)(2,1)} %get-tuple-element.87), channel_id=1, source_target_pairs={{0,1},{1,2},{2,3},{4,5},{5,6},{6,7},{8,9},{9,10},{10,11},{12,13},{... | collective-permute-start | bytes 1572872 | tf_op jit(solution)/shard_map/ppermute | solution.py:608
  150.0 1.3 collective-permute-start.27
  151.3 6.7 %collective-permute-done.31.refs_2_.refs_6_ = bf16[256,1024]{1,0:T(8,128)(2,1)} collective-permute-done((bf16[256,1024]{1,0:T(8,128)(2,1)}, bf16[256,1024]{1,0:T(8,128)(2,1)}, u32[]{:S(2)}, u32[]{:S(2)}) %collective-permute-start.31) | collective-permute-done | bytes 524320 | tf_op jit(solution)/shard_map/ppermute | solution.py:608
  158.0 4.9 %collective-permute-done.27.refs_1_.refs_8_ = bf16[256,1024]{1,0:T(8,128)(2,1)} collective-permute-done((bf16[256,1024]{1,0:T(8,128)(2,1)}, bf16[256,1024]{1,0:T(8,128)(2,1)}, u32[]{:S(2)}, u32[]{:S(2)}) %collective-permute-start.27) | collective-permute-done | bytes 524320 | tf_op jit(solution)/shard_map/ppermute | solution.py:609
  162.9 3.4 %constant_dynamic-slice_fusion = (bf16[256,1024]{1,0:T(8,128)(2,1)}, bf16[256,1024]{1,0:T(8,128)(2,1)}, bf16[256,1024]{1,0:T(8,128)(2,1)}) fusion(bf16[256,4096]{1,0:T(8,128)(2,1)} %copy-done.15, s32[]{:T(128)S(6)} %select_n.159, bf16[256,1024]{1,0:T(8,128)(2,1)} %collective-permute-done.31.refs_2_.refs_6_, s32[]{:T(128)S(6)} %select_n.152, pred[]{:T(512)S(6)} %eq.33, ...), kind=kLoop, calls=%fused_computation.21 | loop fusion | flops 2621440 | bytes 4194318 | tf_op jit(solution)/shard_map/dynamic_slice | solution.py:614
  166.3 2.3 %collective-permute-start.32 = (bf16[256,1024]{1,0:T(8,128)(2,1)}, bf16[256,1024]{1,0:T(8,128)(2,1)}, u32[]{:S(2)}, u32[]{:S(2)}) collective-permute-start(bf16[256,1024]{1,0:T(8,128)(2,1)} %get-tuple-element.85), channel_id=1, source_target_pairs={{0,1},{1,2},{2,3},{4,5},{5,6},{6,7},{8,9},{9,10},{10,11},{12,13},{... | collective-permute-start | bytes 1572872 | tf_op jit(solution)/shard_map/ppermute | solution.py:608
  168.5 1.3 collective-permute-start.28
  174.9 1.0 copy-done.5
  176.0 1.0 copy-done.6
  177.0 4.9 %early_sum.1.refs_4_ = f32[256,1024]{1,0:T(8,128)S(1)} custom-call(s32[13]{0:T(128)S(1)} %stack.71.order, bf16[256,1024]{1,0:T(8,128)(2,1)S(1)} %copy-done.5, bf16[256,1024]{1,0:T(8,128)(2,1)S(1)} %copy-done.6, bf16[256,1024]{1,0:T(8,128)(2,1)S(1)} %copy-done.3, bf16[1024,4096]{1,0:T(8,128)(2,1)} %own_weight.1, ...), custom_call_target="tpu_custom_call" | custom-call | tf_op jit(solution)/shard_map/early_sum/pallas_call | solution.py:542
  182.0 5.4 %final_sum.1 = bf16[512,1024]{1,0:T(8,128)(2,1)} custom-call(s32[13]{0:T(128)S(1)} %stack.71.order, bf16[256,1024]{1,0:T(8,128)(2,1)} %collective-permute-done.28.refs_0_.refs_9_, bf16[256,1024]{1,0:T(8,128)(2,1)} %collective-permute-done.27.refs_1_.refs_8_, bf16[256,1024]{1,0:T(8,128)(2,1)} %collective-permute-done.31.refs_2_.refs_6_, ...), custom_call_target="tpu_custom_call" | custom-call | tf_op jit(solution)/shard_map/final_sum/pallas_call | solution.py:578
  (94 shorter events, 12.2 us)
Async XLA Ops:
  0.0 40.6 %copy-start = (f32[1024]{0:T(1024)S(1)}, f32[1024]{0:T(1024)}, u32[]{:S(2)}) copy-start(f32[1024]{0:T(1024)} %param.17) | copy-start | bytes 12292
  0.0 40.7 %copy-start.10 = (f32[128,66]{1,0:T(8,128)S(1)}, f32[128,66]{1,0:T(8,128)}, u32[]{:S(2)}) copy-start(f32[128,66]{1,0:T(8,128)} %constant.82.clone.refs_8_.refs_9_) | copy-start | bytes 101380
  0.0 40.7 %copy-start.8 = (bf16[256,768]{1,0:T(8,128)(2,1)S(1)}, bf16[256,768]{1,0:T(8,128)(2,1)}, u32[]{:S(2)}) copy-start(bf16[256,768]{1,0:T(8,128)(2,1)} %constant.80.clone.refs_9_.refs_10_) | copy-start | bytes 1179652
  4.9 35.8 %copy-start.11 = (bf16[128,512]{1,0:T(8,128)(2,1)S(1)}, bf16[128,512]{1,0:T(8,128)(2,1)}, u32[]{:S(2)}) copy-start(bf16[128,512]{1,0:T(8,128)(2,1)} %get-tuple-element.50.refs_0_) | copy-start | bytes 393220
  4.9 10.0 %collective-permute-start.11 = (bf16[128,512]{1,0:T(8,128)(2,1)}, bf16[128,512]{1,0:T(8,128)(2,1)S(1)}, u32[]{:S(2)}, u32[]{:S(2)}) collective-permute-start(bf16[128,512]{1,0:T(8,128)(2,1)} %get-tuple-element.51), channel_id=1, source_target_pairs={{0,4},{4,0},{8,12},{12,8},{16,20},{20,16},{24,28},{28,24},{1,5},{5... | collective-permute-start | bytes 393224 | tf_op jit(solution)/shard_map/ppermute | solution.py:448
  5.4 11.7 %collective-permute-start.12 = (bf16[128,512]{1,0:T(8,128)(2,1)}, bf16[128,512]{1,0:T(8,128)(2,1)S(1)}, u32[]{:S(2)}, u32[]{:S(2)}) collective-permute-start(bf16[128,512]{1,0:T(8,128)(2,1)} %get-tuple-element.52), channel_id=1, source_target_pairs={{0,8},{4,12},{8,0},{12,4},{16,24},{20,28},{24,16},{28,20},{1,9},{5... | collective-permute-start | bytes 393224 | tf_op jit(solution)/shard_map/ppermute | solution.py:448
  10.1 4.7 %collective-permute-start.3 = (bf16[6,1024]{1,0:T(8,128)(2,1)S(1)}, bf16[6,1024]{1,0:T(8,128)(2,1)S(1)}, u32[]{:S(2)}, u32[]{:S(2)}) collective-permute-start(bf16[6,1024]{1,0:T(8,128)(2,1)S(1)} %pad_maximum_fusion.3), channel_id=1, source_target_pairs={{0,4},{4,8},{8,12},{12,16},{16,20},{20,24},{24,28},{1,5},{5,9},{9,... | collective-permute-start | bytes 36872 | tf_op jit(solution)/shard_map/ppermute | solution.py:18
  12.2 14.5 %collective-permute-start.13 = (bf16[128,512]{1,0:T(8,128)(2,1)}, bf16[128,512]{1,0:T(8,128)(2,1)S(1)}, u32[]{:S(2)}, u32[]{:S(2)}) collective-permute-start(bf16[128,512]{1,0:T(8,128)(2,1)} %get-tuple-element.53), channel_id=1, source_target_pairs={{0,12},{4,8},{8,4},{12,0},{16,28},{20,24},{24,20},{28,16},{1,13},{... | collective-permute-start | bytes 393224 | tf_op jit(solution)/shard_map/ppermute | solution.py:448
  14.8 12.0 %collective-permute-start.14 = (bf16[128,512]{1,0:T(8,128)(2,1)}, bf16[128,512]{1,0:T(8,128)(2,1)S(1)}, u32[]{:S(2)}, u32[]{:S(2)}) collective-permute-start(bf16[128,512]{1,0:T(8,128)(2,1)} %get-tuple-element.54), channel_id=1, source_target_pairs={{0,16},{4,20},{8,24},{12,28},{16,0},{20,4},{24,8},{28,12},{1,17},{... | collective-permute-start | bytes 393224 | tf_op jit(solution)/shard_map/ppermute | solution.py:448
  14.8 12.1 %collective-permute-start.15 = (bf16[128,512]{1,0:T(8,128)(2,1)}, bf16[128,512]{1,0:T(8,128)(2,1)S(1)}, u32[]{:S(2)}, u32[]{:S(2)}) collective-permute-start(bf16[128,512]{1,0:T(8,128)(2,1)} %get-tuple-element.55), channel_id=1, source_target_pairs={{0,20},{4,16},{8,28},{12,24},{16,4},{20,0},{24,12},{28,8},{1,21},{... | collective-permute-start | bytes 393224 | tf_op jit(solution)/shard_map/ppermute | solution.py:448
  14.9 13.8 %collective-permute-start.16 = (bf16[128,512]{1,0:T(8,128)(2,1)}, bf16[128,512]{1,0:T(8,128)(2,1)S(1)}, u32[]{:S(2)}, u32[]{:S(2)}) collective-permute-start(bf16[128,512]{1,0:T(8,128)(2,1)} %get-tuple-element.56), channel_id=1, source_target_pairs={{0,24},{4,28},{8,16},{12,20},{16,8},{20,12},{24,0},{28,4},{1,25},{... | collective-permute-start | bytes 393224 | tf_op jit(solution)/shard_map/ppermute | solution.py:448
  17.0 12.3 %collective-permute-start.17 = (bf16[128,512]{1,0:T(8,128)(2,1)}, bf16[128,512]{1,0:T(8,128)(2,1)S(1)}, u32[]{:S(2)}, u32[]{:S(2)}) collective-permute-start(bf16[128,512]{1,0:T(8,128)(2,1)} %get-tuple-element.57), channel_id=1, source_target_pairs={{0,28},{4,24},{8,20},{12,16},{16,12},{20,8},{24,4},{28,0},{1,29},{... | collective-permute-start | bytes 393224 | tf_op jit(solution)/shard_map/ppermute | solution.py:448
  26.7 4.9 %collective-permute-start.4 = (bf16[512,128]{1,0:T(8,128)(2,1)}, bf16[512,128]{1,0:T(8,128)(2,1)S(1)}, u32[]{:S(2)}, u32[]{:S(2)}) collective-permute-start(bf16[512,128]{1,0:T(8,128)(2,1)} %get-tuple-element.43), channel_id=1, source_target_pairs={{0,4},{4,0},{8,12},{12,8},{16,20},{20,16},{24,28},{28,24},{1,5},{5... | collective-permute-start | bytes 393224 | tf_op jit(solution)/shard_map/ppermute | solution.py:448
  26.8 6.8 %collective-permute-start.5 = (bf16[512,128]{1,0:T(8,128)(2,1)}, bf16[512,128]{1,0:T(8,128)(2,1)S(1)}, u32[]{:S(2)}, u32[]{:S(2)}) collective-permute-start(bf16[512,128]{1,0:T(8,128)(2,1)} %get-tuple-element.44), channel_id=1, source_target_pairs={{0,8},{4,12},{8,0},{12,4},{16,24},{20,28},{24,16},{28,20},{1,9},{5... | collective-permute-start | bytes 393224 | tf_op jit(solution)/shard_map/ppermute | solution.py:448
  26.9 10.0 %collective-permute-start.6 = (bf16[512,128]{1,0:T(8,128)(2,1)}, bf16[512,128]{1,0:T(8,128)(2,1)S(1)}, u32[]{:S(2)}, u32[]{:S(2)}) collective-permute-start(bf16[512,128]{1,0:T(8,128)(2,1)} %get-tuple-element.45), channel_id=1, source_target_pairs={{0,12},{4,8},{8,4},{12,0},{16,28},{20,24},{24,20},{28,16},{1,13},{... | collective-permute-start | bytes 393224 | tf_op jit(solution)/shard_map/ppermute | solution.py:448
  28.6 9.0 %collective-permute-start.7 = (bf16[512,128]{1,0:T(8,128)(2,1)}, bf16[512,128]{1,0:T(8,128)(2,1)S(1)}, u32[]{:S(2)}, u32[]{:S(2)}) collective-permute-start(bf16[512,128]{1,0:T(8,128)(2,1)} %get-tuple-element.46), channel_id=1, source_target_pairs={{0,16},{4,20},{8,24},{12,28},{16,0},{20,4},{24,8},{28,12},{1,17},{... | collective-permute-start | bytes 393224 | tf_op jit(solution)/shard_map/ppermute | solution.py:448
  29.4 8.7 %collective-permute-start.8 = (bf16[512,128]{1,0:T(8,128)(2,1)}, bf16[512,128]{1,0:T(8,128)(2,1)S(1)}, u32[]{:S(2)}, u32[]{:S(2)}) collective-permute-start(bf16[512,128]{1,0:T(8,128)(2,1)} %get-tuple-element.47), channel_id=1, source_target_pairs={{0,20},{4,16},{8,28},{12,24},{16,4},{20,0},{24,12},{28,8},{1,21},{... | collective-permute-start | bytes 393224 | tf_op jit(solution)/shard_map/ppermute | solution.py:448
  31.5 17.2 %copy-start.9 = (bf16[256,768]{1,0:T(8,128)(2,1)S(1)}, bf16[256,768]{1,0:T(8,128)(2,1)}, u32[]{:S(2)}) copy-start(bf16[256,768]{1,0:T(8,128)(2,1)} %constant.81.clone.refs_11_) | copy-start | bytes 1179652
  31.6 17.2 %copy-start.12 = (bf16[512,128]{1,0:T(8,128)(2,1)S(1)}, bf16[512,128]{1,0:T(8,128)(2,1)}, u32[]{:S(2)}) copy-start(bf16[512,128]{1,0:T(8,128)(2,1)} %get-tuple-element.42.refs_0_) | copy-start | bytes 393220
  31.6 36.0 %collective-permute-start = (bf16[128,1024]{1,0:T(8,128)(2,1)S(1)}, bf16[128,1024]{1,0:T(8,128)(2,1)S(1)}, u32[]{:S(2)}, u32[]{:S(2)}) collective-permute-start(bf16[128,1024]{1,0:T(8,128)(2,1)S(1)} %get-tuple-element.79), channel_id=1, source_target_pairs={{0,1},{1,2},{2,3},{3,0},{4,5},{5,6},{6,7},{7,4},{8,9},{9,10},{10,1... | collective-permute-start | bytes 786440 | tf_op jit(solution)/shard_map/ppermute | solution.py:502
  33.6 35.5 %collective-permute-start.2 = (bf16[128,1024]{1,0:T(8,128)(2,1)S(1)}, bf16[128,1024]{1,0:T(8,128)(2,1)S(1)}, u32[]{:S(2)}, u32[]{:S(2)}) collective-permute-start(bf16[128,1024]{1,0:T(8,128)(2,1)S(1)} %get-tuple-element.80), channel_id=1, source_target_pairs={{0,3},{1,0},{2,1},{3,2},{4,7},{5,4},{6,5},{7,6},{8,11},{9,8},{10,9... | collective-permute-start | bytes 786440 | tf_op jit(solution)/shard_map/ppermute | solution.py:502
  36.9 11.8 %collective-permute-start.9 = (bf16[512,128]{1,0:T(8,128)(2,1)}, bf16[512,128]{1,0:T(8,128)(2,1)S(1)}, u32[]{:S(2)}, u32[]{:S(2)}) collective-permute-start(bf16[512,128]{1,0:T(8,128)(2,1)} %get-tuple-element.48), channel_id=1, source_target_pairs={{0,24},{4,28},{8,16},{12,20},{16,8},{20,12},{24,0},{28,4},{1,25},{... | collective-permute-start | bytes 393224 | tf_op jit(solution)/shard_map/ppermute | solution.py:448
  37.7 11.1 %collective-permute-start.10 = (bf16[512,128]{1,0:T(8,128)(2,1)}, bf16[512,128]{1,0:T(8,128)(2,1)S(1)}, u32[]{:S(2)}, u32[]{:S(2)}) collective-permute-start(bf16[512,128]{1,0:T(8,128)(2,1)} %get-tuple-element.49), channel_id=1, source_target_pairs={{0,28},{4,24},{8,20},{12,16},{16,12},{20,8},{24,4},{28,0},{1,29},{... | collective-permute-start | bytes 393224 | tf_op jit(solution)/shard_map/ppermute | solution.py:448
  38.1 31.3 %collective-permute-start.1 = (bf16[128,1024]{1,0:T(8,128)(2,1)S(1)}, bf16[128,1024]{1,0:T(8,128)(2,1)S(1)}, u32[]{:S(2)}, u32[]{:S(2)}) collective-permute-start(bf16[128,1024]{1,0:T(8,128)(2,1)S(1)} %get-tuple-element.81), channel_id=1, source_target_pairs={{0,2},{1,3},{2,0},{3,1},{4,6},{5,7},{6,4},{7,5},{8,10},{9,11},{10,... | collective-permute-start | bytes 786440 | tf_op jit(solution)/shard_map/ppermute | solution.py:502
  67.1 3.7 %collective-permute-start.18 = (bf16[512,128]{1,0:T(8,128)(2,1)S(1)}, bf16[512,128]{1,0:T(8,128)(2,1)S(1)}, u32[]{:S(2)}, u32[]{:S(2)}) collective-permute-start(bf16[512,128]{1,0:T(8,128)(2,1)S(1)} %get-tuple-element.59), channel_id=1, source_target_pairs={{0,4},{4,0},{8,12},{12,8},{16,20},{20,16},{24,28},{28,24},{1,5},{5... | collective-permute-start | bytes 393224 | tf_op jit(solution)/shard_map/ppermute | solution.py:448
  67.2 6.4 %collective-permute-start.19 = (bf16[512,128]{1,0:T(8,128)(2,1)S(1)}, bf16[512,128]{1,0:T(8,128)(2,1)S(1)}, u32[]{:S(2)}, u32[]{:S(2)}) collective-permute-start(bf16[512,128]{1,0:T(8,128)(2,1)S(1)} %get-tuple-element.60), channel_id=1, source_target_pairs={{0,8},{4,12},{8,0},{12,4},{16,24},{20,28},{24,16},{28,20},{1,9},{5... | collective-permute-start | bytes 393224 | tf_op jit(solution)/shard_map/ppermute | solution.py:448
  67.6 7.8 %collective-permute-start.20 = (bf16[512,128]{1,0:T(8,128)(2,1)S(1)}, bf16[512,128]{1,0:T(8,128)(2,1)S(1)}, u32[]{:S(2)}, u32[]{:S(2)}) collective-permute-start(bf16[512,128]{1,0:T(8,128)(2,1)S(1)} %get-tuple-element.61), channel_id=1, source_target_pairs={{0,12},{4,8},{8,4},{12,0},{16,28},{20,24},{24,20},{28,16},{1,13},{... | collective-permute-start | bytes 393224 | tf_op jit(solution)/shard_map/ppermute | solution.py:448
  69.1 6.5 %collective-permute-start.21 = (bf16[512,128]{1,0:T(8,128)(2,1)S(1)}, bf16[512,128]{1,0:T(8,128)(2,1)S(1)}, u32[]{:S(2)}, u32[]{:S(2)}) collective-permute-start(bf16[512,128]{1,0:T(8,128)(2,1)S(1)} %get-tuple-element.62), channel_id=1, source_target_pairs={{0,16},{4,20},{8,24},{12,28},{16,0},{20,4},{24,8},{28,12},{1,17},{... | collective-permute-start | bytes 393224 | tf_op jit(solution)/shard_map/ppermute | solution.py:448
  69.4 13.3 %collective-permute-start.22 = (bf16[512,128]{1,0:T(8,128)(2,1)S(1)}, bf16[512,128]{1,0:T(8,128)(2,1)S(1)}, u32[]{:S(2)}, u32[]{:S(2)}) collective-permute-start(bf16[512,128]{1,0:T(8,128)(2,1)S(1)} %get-tuple-element.63), channel_id=1, source_target_pairs={{0,20},{4,16},{8,28},{12,24},{16,4},{20,0},{24,12},{28,8},{1,21},{... | collective-permute-start | bytes 393224 | tf_op jit(solution)/shard_map/ppermute | solution.py:448
  70.8 11.9 %collective-permute-start.23 = (bf16[512,128]{1,0:T(8,128)(2,1)S(1)}, bf16[512,128]{1,0:T(8,128)(2,1)S(1)}, u32[]{:S(2)}, u32[]{:S(2)}) collective-permute-start(bf16[512,128]{1,0:T(8,128)(2,1)S(1)} %get-tuple-element.64), channel_id=1, source_target_pairs={{0,24},{4,28},{8,16},{12,20},{16,8},{20,12},{24,0},{28,4},{1,25},{... | collective-permute-start | bytes 393224 | tf_op jit(solution)/shard_map/ppermute | solution.py:448
  73.5 9.1 %collective-permute-start.24 = (bf16[512,128]{1,0:T(8,128)(2,1)S(1)}, bf16[512,128]{1,0:T(8,128)(2,1)S(1)}, u32[]{:S(2)}, u32[]{:S(2)}) collective-permute-start(bf16[512,128]{1,0:T(8,128)(2,1)S(1)} %get-tuple-element.65), channel_id=1, source_target_pairs={{0,28},{4,24},{8,20},{12,16},{16,12},{20,8},{24,4},{28,0},{1,29},{... | collective-permute-start | bytes 393224 | tf_op jit(solution)/shard_map/ppermute | solution.py:448
  73.6 21.0 %copy-start.13 = (bf16[3,128,1024]{2,1,0:T(8,128)(2,1)}, bf16[3,128,1024]{2,1,0:T(8,128)(2,1)S(1)}, u32[]{:S(2)}) copy-start(bf16[3,128,1024]{2,1,0:T(8,128)(2,1)S(1)} %pad_maximum_fusion.2) | copy-start | bytes 2359300
  82.7 12.0 %collective-permute-start.33 = (bf16[3,128,1024]{2,1,0:T(8,128)(2,1)S(1)}, bf16[3,128,1024]{2,1,0:T(8,128)(2,1)S(1)}, u32[]{:S(2)}, u32[]{:S(2)}) collective-permute-start(bf16[3,128,1024]{2,1,0:T(8,128)(2,1)S(1)} %pad_maximum_fusion.2), channel_id=1, source_target_pairs={{0,8},{4,20},{8,0},{12,28},{16,24},{20,4},{24,16},{28,12},{1,9},{5... | collective-permute-start | bytes 2359304 | tf_op jit(solution)/shard_map/ppermute | solution.py:510
  95.5 20.5 %collective-permute-start.34 = (bf16[2,3,128,1024]{3,2,1,0:T(8,128)(2,1)S(1)}, bf16[2,3,128,1024]{3,2,1,0:T(8,128)(2,1)}, u32[]{:S(2)}, u32[]{:S(2)}) collective-permute-start(bf16[2,3,128,1024]{3,2,1,0:T(8,128)(2,1)S(1)} %pad_maximum_fusion.1), channel_id=1, source_target_pairs={{0,16},{4,12},{8,24},{12,4},{16,0},{20,28},{24,8},{28,20},{1,17},{... | collective-permute-start | bytes 4718600 | tf_op jit(solution)/shard_map/ppermute | solution.py:511
  104.6 11.4 %copy-start.17 = (bf16[3,128,1024]{2,1,0:T(8,128)(2,1)S(1)}, bf16[3,128,1024]{2,1,0:T(8,128)(2,1)}, u32[]{:S(2)}) copy-start(bf16[3,128,1024]{2,1,0:T(8,128)(2,1)} %copy-done.16) | copy-start | bytes 2359300
  106.4 16.4 %copy-start.4 = (bf16[256,1024]{1,0:T(8,128)(2,1)}, bf16[256,1024]{1,0:T(8,128)(2,1)S(1)}, u32[]{:S(2)}) copy-start(bf16[256,1024]{1,0:T(8,128)(2,1)S(1)} %get-tuple-element.74.own) | copy-start | bytes 1572868
  106.4 15.2 %collective-permute-start.25 = (bf16[256,1024]{1,0:T(8,128)(2,1)S(1)}, bf16[256,1024]{1,0:T(8,128)(2,1)S(1)}, u32[]{:S(2)}, u32[]{:S(2)}) collective-permute-start(bf16[256,1024]{1,0:T(8,128)(2,1)S(1)} %get-tuple-element.76), channel_id=1, source_target_pairs={{1,0},{2,1},{3,2},{5,4},{6,5},{7,6},{9,8},{10,9},{11,10},{13,12},{... | collective-permute-start | bytes 1572872 | tf_op jit(solution)/shard_map/ppermute | solution.py:609
  107.7 15.1 %collective-permute-start.29 = (bf16[256,1024]{1,0:T(8,128)(2,1)S(1)}, bf16[256,1024]{1,0:T(8,128)(2,1)S(1)}, u32[]{:S(2)}, u32[]{:S(2)}) collective-permute-start(bf16[256,1024]{1,0:T(8,128)(2,1)S(1)} %get-tuple-element.77), channel_id=1, source_target_pairs={{0,1},{1,2},{2,3},{4,5},{5,6},{6,7},{8,9},{9,10},{10,11},{12,13},{... | collective-permute-start | bytes 1572872 | tf_op jit(solution)/shard_map/ppermute | solution.py:608
  117.8 56.1 %collective-permute-start.35 = (bf16[4,3,128,1024]{3,2,1,0:T(8,128)(2,1)S(1)}, bf16[4,3,128,1024]{3,2,1,0:T(8,128)(2,1)}, u32[]{:S(2)}, u32[]{:S(2)}) collective-permute-start(bf16[4,3,128,1024]{3,2,1,0:T(8,128)(2,1)S(1)} %pad_maximum_fusion.near_weight.refs_10_), channel_id=1, source_target_pairs={{0,4},{4,0},{8,12},{12,8},{16,20},{20,16},{24,28},{28,24},{1,5},{5... | collective-permute-start | bytes 9437192 | tf_op jit(solution)/shard_map/ppermute | solution.py:512
  124.5 14.3 %collective-permute-start.30 = (bf16[256,1024]{1,0:T(8,128)(2,1)}, bf16[256,1024]{1,0:T(8,128)(2,1)}, u32[]{:S(2)}, u32[]{:S(2)}) collective-permute-start(bf16[256,1024]{1,0:T(8,128)(2,1)} %get-tuple-element.82), channel_id=1, source_target_pairs={{0,1},{1,2},{2,3},{4,5},{5,6},{6,7},{8,9},{9,10},{10,11},{12,13},{... | collective-permute-start | bytes 1572872 | tf_op jit(solution)/shard_map/ppermute | solution.py:608
  129.7 14.1 %collective-permute-start.26 = (bf16[256,1024]{1,0:T(8,128)(2,1)}, bf16[256,1024]{1,0:T(8,128)(2,1)}, u32[]{:S(2)}, u32[]{:S(2)}) collective-permute-start(bf16[256,1024]{1,0:T(8,128)(2,1)} %get-tuple-element.83), channel_id=1, source_target_pairs={{1,0},{2,1},{3,2},{5,4},{6,5},{7,6},{9,8},{10,9},{11,10},{13,12},{... | collective-permute-start | bytes 1572872 | tf_op jit(solution)/shard_map/ppermute | solution.py:609
  131.2 38.7 %copy-start.21 = (s32[4]{0:T(128)S(1)}, s32[4]{0:T(128)}, u32[]{:S(2)}) copy-start(s32[4]{0:T(128)} %constant.85.clone) | copy-start | bytes 52
  131.2 39.3 %copy-start.20 = (s32[4]{0:T(128)S(1)}, s32[4]{0:T(128)}, u32[]{:S(2)}) copy-start(s32[4]{0:T(128)} %constant.84.clone) | copy-start | bytes 52
  131.2 41.2 %copy-start.19 = (s32[4]{0:T(128)S(1)}, s32[4]{0:T(128)}, u32[]{:S(2)}) copy-start(s32[4]{0:T(128)} %constant.83.clone) | copy-start | bytes 52
  147.2 10.8 %collective-permute-start.31 = (bf16[256,1024]{1,0:T(8,128)(2,1)}, bf16[256,1024]{1,0:T(8,128)(2,1)}, u32[]{:S(2)}, u32[]{:S(2)}) collective-permute-start(bf16[256,1024]{1,0:T(8,128)(2,1)} %get-tuple-element.87), channel_id=1, source_target_pairs={{0,1},{1,2},{2,3},{4,5},{5,6},{6,7},{8,9},{9,10},{10,11},{12,13},{... | collective-permute-start | bytes 1572872 | tf_op jit(solution)/shard_map/ppermute | solution.py:608
  150.0 12.9 %collective-permute-start.27 = (bf16[256,1024]{1,0:T(8,128)(2,1)}, bf16[256,1024]{1,0:T(8,128)(2,1)}, u32[]{:S(2)}, u32[]{:S(2)}) collective-permute-start(bf16[256,1024]{1,0:T(8,128)(2,1)} %get-tuple-element.88), channel_id=1, source_target_pairs={{1,0},{2,1},{3,2},{5,4},{6,5},{7,6},{9,8},{10,9},{11,10},{13,12},{... | collective-permute-start | bytes 1572872 | tf_op jit(solution)/shard_map/ppermute | solution.py:609
  166.3 15.7 %collective-permute-start.32 = (bf16[256,1024]{1,0:T(8,128)(2,1)}, bf16[256,1024]{1,0:T(8,128)(2,1)}, u32[]{:S(2)}, u32[]{:S(2)}) collective-permute-start(bf16[256,1024]{1,0:T(8,128)(2,1)} %get-tuple-element.85), channel_id=1, source_target_pairs={{0,1},{1,2},{2,3},{4,5},{5,6},{6,7},{8,9},{9,10},{10,11},{12,13},{... | collective-permute-start | bytes 1572872 | tf_op jit(solution)/shard_map/ppermute | solution.py:608
  168.5 13.4 %collective-permute-start.28 = (bf16[256,1024]{1,0:T(8,128)(2,1)}, bf16[256,1024]{1,0:T(8,128)(2,1)}, u32[]{:S(2)}, u32[]{:S(2)}) collective-permute-start(bf16[256,1024]{1,0:T(8,128)(2,1)} %get-tuple-element.86), channel_id=1, source_target_pairs={{1,0},{2,1},{3,2},{5,4},{6,5},{7,6},{9,8},{10,9},{11,10},{13,12},{... | collective-permute-start | bytes 1572872 | tf_op jit(solution)/shard_map/ppermute | solution.py:609
  (10 other events, 35.0 us)

commit v3 on v1

--- a/solution.py
+++ b/solution.py
@@ -253,12 +253,14 @@
     lax.fori_loop(0, SUB // 8, slab, 0)
 
 
-def taps_kernel(blocks, me_ref, *refs):
-    pieces, (twiddle, forward, spectra_out, series, spectra) = refs[:blocks], refs[blocks:]
-    span = pieces[0].shape[1]
-    for m in range(blocks):
-        start = pl.multiple_of((me_ref[0] ^ m) * span, span)
-        series[pl.ds(start, span), :] = pieces[m][...].astype(F32).T
+def taps_kernel(chips, me_ref, *refs):
+    pairs, (swapped, twiddle, forward, spectra_out, series, spectra) = refs[:chips], refs[chips:]
+    _, lanes, span = swapped.shape
+    mine = pl.ds(pl.multiple_of(me_ref[0] % 2 * lanes, lanes), lanes)
+    for q in range(chips):
+        for m, piece in ((2 * q, pairs[q][mine, :]), (2 * q + 1, swapped[q])):
+            start = pl.multiple_of((me_ref[0] ^ m) * span, span)
+            series[pl.ds(start, span), :] = piece.astype(F32).T
     first_stage(series, spectra, twiddle)
 
     def pair(p, carry):
@@ -269,13 +271,13 @@
     lax.fori_loop(0, spectra_out.shape[0], pair, 0)
 
 
-def conv_kernel(blocks, me_ref, *refs):
-    pieces = refs[:blocks]
-    taps_spectra, twiddle, forward, inverse, skip = refs[blocks : blocks + 5]
-    outs = refs[blocks + 5 : 2 * blocks + 5]
-    series, spectra, result = refs[2 * blocks + 5 :]
-    span, lanes = pieces[0].shape
+def conv_kernel(blocks, me_ref, stay, swapped, *refs):
+    others = refs[: blocks // 2 - 1]
+    taps_spectra, twiddle, forward, inverse, skip = refs[blocks // 2 - 1 : blocks // 2 + 4]
+    out, series, spectra = refs[blocks // 2 + 4 :]
+    span, lanes = stay.shape
     half = series.shape[0] // SUB
+    pieces = [stay, swapped.at[0]] + [ref.at[core] for ref in others for core in range(2)]
     for m in range(blocks):
         start = pl.multiple_of((me_ref[0] ^ m) * span, span)
         series[pl.ds(start, span), :] = pieces[m][...].astype(F32)
@@ -306,119 +308,234 @@
         spectra[k, :SUB, :] = real * cos + imag * sin
         if k < half:
             spectra[k, SUB:, :] = imag * cos - real * sin
-    last_stage(spectra, result)
+    last_stage(spectra, out)
     for m in range(blocks):
+        window = pl.ds(m * span, span)
+        out[window, :] += skip[...] * series[window, :]
+
+
+def spread_kernel(me_ref, conv, *outs):
+    span = outs[0].shape[0]
+    for m, out in enumerate(outs):
         start = pl.multiple_of((me_ref[0] ^ m) * span, span)
-        window = pl.ds(start, span)
-        outs[m][...] = (result[window, :] + skip[...] * series[window, :]).astype(BF16)
+        out[...] = conv[pl.ds(start, span), :].astype(BF16)
 
 
 VMEM = pl.BlockSpec(memory_space=pltpu.VMEM)
 SMEM = pl.BlockSpec(memory_space=pltpu.SMEM)
-GRANT = pltpu.CompilerParams(vmem_limit_bytes=40 * 2**20)
-
-
-def taps_spectra_of(me, pieces, twiddle, forward):
-    blocks = len(pieces)
-    lanes, span = pieces[0].shape
-    half = blocks * span // SUB
-    pairs = (half + 2) // 2
-    return pl.pallas_call(
-        partial(taps_kernel, blocks),
-        out_shape=jax.ShapeDtypeStruct((pairs, 2 * SUB, 2 * lanes), F32),
-        in_specs=[SMEM] + [VMEM] * (blocks + 2),
+HBM = pl.BlockSpec(memory_space=pltpu.HBM)
+
+
+def grant(mebibytes):
+    return pltpu.CompilerParams(vmem_limit_bytes=mebibytes * 2**20)
+
+
+def cost(microseconds):
+    return pl.CostEstimate(flops=microseconds * 10**9, bytes_accessed=0, transcendentals=0)
+
+
+GRANT = grant(16)
+
+
+def taps_spectra_of(me, pairs, swapped, twiddle, forward):
+    chips, lanes, span = swapped.shape
+    length = 2 * chips * span
+    count = (length // SUB + 2) // 2
+    return pl.pallas_call(
+        partial(taps_kernel, chips),
+        out_shape=jax.ShapeDtypeStruct((count, 2 * SUB, 2 * lanes), F32),
+        in_specs=[SMEM] + [VMEM] * (chips + 3),
+        out_specs=VMEM,
+        scratch_shapes=[
+            pltpu.VMEM((length, lanes), F32),
+            pltpu.VMEM((2 * count, 2 * SUB, lanes), F32),
+        ],
+        compiler_params=GRANT,
+        cost_estimate=cost(8),
+        name="taps_spectra",
+    )(me, *pairs, swapped, twiddle, forward)
+
+
+def long_conv(me, stay, swapped, others, taps_spectra, twiddle, forward, inverse, skip):
+    span, lanes = stay.shape
+    blocks = 2 * len(others) + 2
+    pairs = taps_spectra.shape[0]
+    return pl.pallas_call(
+        partial(conv_kernel, blocks),
+        out_shape=jax.ShapeDtypeStruct((blocks * span, lanes), F32),
+        in_specs=[SMEM] + [VMEM] * (len(others) + 7),
         out_specs=VMEM,
         scratch_shapes=[
             pltpu.VMEM((blocks * span, lanes), F32),
             pltpu.VMEM((2 * pairs, 2 * SUB, lanes), F32),
         ],
+        compiler_params=grant(20),
+        cost_estimate=cost(20),
+        name="long_conv",
+    )(me, stay, swapped, *others, taps_spectra, twiddle, forward, inverse, skip)
+
+
+def spread(me, conv, blocks):
+    rows, lanes = conv.shape
+    return pl.pallas_call(
+        spread_kernel,
+        out_shape=[jax.ShapeDtypeStruct((rows // blocks, lanes), BF16)] * blocks,
+        in_specs=[SMEM, VMEM],
+        out_specs=[VMEM] * blocks,
         compiler_params=GRANT,
-        name="taps_spectra",
-    )(me, *pieces, twiddle, forward)
-
-
-def long_conv(me, pieces, taps_spectra, twiddle, forward, inverse, skip):
-    blocks = len(pieces)
-    span, lanes = pieces[0].shape
-    pairs = taps_spectra.shape[0]
-    return pl.pallas_call(
-        partial(conv_kernel, blocks),
-        out_shape=[jax.ShapeDtypeStruct((span, lanes), BF16)] * blocks,
-        in_specs=[SMEM] + [VMEM] * (blocks + 5),
-        out_specs=[VMEM] * blocks,
-        scratch_shapes=[
-            pltpu.VMEM((blocks * span, lanes), F32),
-            pltpu.VMEM((2 * pairs, 2 * SUB, lanes), F32),
-            pltpu.VMEM((blocks * span, lanes), F32),
-        ],
-        compiler_params=GRANT,
-        name="long_conv",
-    )(me, *pieces, taps_spectra, twiddle, forward, inverse, skip)
+        name="spread",
+    )(me, conv)
 
 
 def shifted_mix(stream, edge, weight):
-    first = jnp.concatenate([edge[1:2], stream[:-1]], axis=0)
-    second = jnp.concatenate([edge, stream[:-2]], axis=0)
+    row = lax.broadcasted_iota(jnp.int32, stream.shape, 0)
+    first = jnp.where(row == 0, edge[1:2], pltpu.roll(stream, 1, 0))
+    second = pltpu.roll(stream, 2, 0)
+    second = jnp.where(row == 0, edge[0:1], jnp.where(row == 1, edge[1:2], second))
     return weight[0:1] * stream + weight[1:2] * first + weight[2:3] * second
 
 
-def gate_in_kernel(me_ref, key, value, edges, weight, *outs):
-    mixed = [
-        shifted_mix(ref[...].astype(F32), edges[2 * s : 2 * s + 2].astype(F32), weight[:, s, :])
-        for s, ref in ((1, key), (2, value))
+def rims_kernel(query, key, value, out, held, sems):
+    span = query.shape[0]
+    copies = [
+        pltpu.make_async_copy(ref.at[pl.ds(span - 16, 16), :], held.at[s], sems.at[s])
+        for s, ref in enumerate((query, key, value))
     ]
-    gated = (mixed[0] * mixed[1]).astype(BF16)
-    for m, out in enumerate(outs):
-
-        @pl.when(pl.program_id(0) == m)
-        def _(out=out):
-            out[...] = gated
+    for copy in copies:
+        copy.start()
+    for s, copy in enumerate(copies):
+        copy.wait()
+        out[2 * s : 2 * s + 2, :] = held[s, 14:16, :]
+
+
+def rims(*streams):
+    chans = streams[0].shape[1]
+    return pl.pallas_call(
+        rims_kernel,
+        in_specs=[HBM] * 3,
+        out_specs=VMEM,
+        out_shape=jax.ShapeDtypeStruct((6, chans), BF16),
+        scratch_shapes=[pltpu.VMEM((3, 16, chans), BF16), pltpu.SemaphoreType.DMA((3,))],
+        compiler_params=grant(56),
+        name="rims",
+    )(*streams)
+
+
+def gate_in_kernel(me_ref, key, value, edges, weight, stay, same, swap, held, sems):
+    lanes = stay.shape[1]
+    chips = swap.shape[0]
+    mine = me_ref[0] % 2
+    copies = []
+    for q in range(chips):
+        start = pl.multiple_of(((me_ref[0] // 2) ^ q) * 2 * lanes, 2 * lanes)
+        for s, ref in enumerate((key, value)):
+            source = ref.at[:, pl.ds(start, 2 * lanes)]
+            copies.append(pltpu.make_async_copy(source, held.at[q, s], sems.at[q, s]))
+            copies[-1].start()
+    for q in range(chips):
+        start = ((me_ref[0] // 2) ^ q) * 2 * lanes
+        for copy in copies[2 * q : 2 * q + 2]:
+            copy.wait()
+        for side in range(2):
+            inner = pl.ds(pl.multiple_of((mine ^ side) * lanes, lanes), lanes)
+            outer = pl.ds(pl.multiple_of(start + (mine ^ side) * lanes, lanes), lanes)
+            mixed = [
+                shifted_mix(
+                    held[q, s, :, inner].astype(F32),
+                    edges[2 * s + 2 : 2 * s + 4, outer].astype(F32),
+                    weight[:, s + 1, outer],
+                )
+                for s in range(2)
+            ]
+            gated = (mixed[0] * mixed[1]).astype(BF16)
+            if side:
+                swap[q] = gated
+            elif q:
+                same[q - 1] = gated
+            else:
+                stay[...] = gated
 
 
 def gate_in(me, key_rows, value_rows, edges, short_weight, blocks):
     span, chans = key_rows.shape
     lanes = chans // blocks
-    column = lambda m, me: (0, me[0] ^ m)
+    chips = blocks // 2
+    shapes = [(span, lanes), (chips - 1, span, lanes), (chips, span, lanes)]
     return pl.pallas_call(
         gate_in_kernel,
-        grid_spec=pltpu.PrefetchScalarGridSpec(
-            num_scalar_prefetch=1,
-            grid=(blocks,),
-            in_specs=[
-                pl.BlockSpec((span, lanes), column),
-                pl.BlockSpec((span, lanes), column),
-                pl.BlockSpec((6, lanes), column),
-                pl.BlockSpec((3, 3, lanes), lambda m, me: (0, 0, me[0] ^ m)),
-            ],
-            out_specs=[pl.BlockSpec((span, lanes), lambda m, me: (0, 0))] * blocks,
-        ),
-        out_shape=[jax.ShapeDtypeStruct((span, lanes), BF16)] * blocks,
+        in_specs=[SMEM, HBM, HBM, VMEM, VMEM],
+        out_specs=[VMEM] * 3,
+        out_shape=[jax.ShapeDtypeStruct(shape, BF16) for shape in shapes],
+        scratch_shapes=[
+            pltpu.VMEM((chips, 2, span, 2 * lanes), BF16),
+            pltpu.SemaphoreType.DMA((chips, 2)),
+        ],
+        compiler_params=grant(56),
         name="gate_in",
     )(me, key_rows, value_rows, edges, short_weight)
 
 
-def split_taps_kernel(me_ref, taps, *outs):
-    for m, out in enumerate(outs):
-
-        @pl.when(pl.program_id(0) == m)
-        def _(out=out):
-            out[...] = taps[...]
-
-
-def split_taps(me, filter_taps, blocks):
+def split_taps_kernel(me_ref, taps, *refs):
+    outs, sems = refs[:-1], refs[-1]
+    rows = outs[0].shape[0]
+    copies = []
+    for q, out in enumerate(outs):
+        window = pl.ds(pl.multiple_of(((me_ref[0] // 2) ^ q) * rows, rows), rows)
+        copies.append(pltpu.make_async_copy(taps.at[window, :], out, sems.at[q]))
+        copies[-1].start()
+    for copy in copies:
+        copy.wait()
+
+
+def split_taps(me, filter_taps, chips):
     chans, span = filter_taps.shape
-    lanes = chans // blocks
     return pl.pallas_call(
         split_taps_kernel,
-        grid_spec=pltpu.PrefetchScalarGridSpec(
-            num_scalar_prefetch=1,
-            grid=(blocks,),
-            in_specs=[pl.BlockSpec((lanes, span), lambda m, me: (me[0] ^ m, 0))],
-            out_specs=[pl.BlockSpec((lanes, span), lambda m, me: (0, 0))] * blocks,
-        ),
-        out_shape=[jax.ShapeDtypeStruct((lanes, span), BF16)] * blocks,
+        in_specs=[SMEM, HBM],
+        out_specs=[VMEM] * chips,
+        out_shape=[jax.ShapeDtypeStruct((chans // chips, span), BF16)] * chips,
+        scratch_shapes=[pltpu.SemaphoreType.DMA((chips,))],
+        compiler_params=GRANT,
         name="split_taps",
     )(me, filter_taps)
+
+
+def other_core_kernel(me_ref, *refs):
+    pairs, out = refs[:-1], refs[-1]
+    rows = out.shape[1]
+    for q, pair in enumerate(pairs):
+        window = pl.ds(pl.multiple_of((1 - me_ref[0] % 2) * rows, rows), rows)
+        out[q] = pair[window, :]
+
+
+def other_core(me, pairs):
+    rows, span = pairs[0].shape
+    return pl.pallas_call(
+        other_core_kernel,
+        in_specs=[SMEM] + [VMEM] * len(pairs),
+        out_specs=VMEM,
+        out_shape=jax.ShapeDtypeStruct((len(pairs), rows // 2, span), BF16),
+        compiler_params=GRANT,
+        name="other_core",
+    )(me, *pairs)
+
+
+def pair_kernel(same, swapped, *outs):
+    for q, out in enumerate(outs):
+        out[0] = same[q]
+        out[1] = swapped[q + 1]
+
+
+def pair_up(same, swapped):
+    count, span, lanes = same.shape
+    return pl.pallas_call(
+        pair_kernel,
+        out_shape=[jax.ShapeDtypeStruct((2, span, lanes), BF16)] * count,
+        in_specs=[VMEM] * 2,
+        out_specs=[VMEM] * count,
+        compiler_params=GRANT,
+        name="pair_up",
+    )(same, swapped)
 
 
 def mix_query_kernel(query, edges, weight, out):
@@ -438,6 +555,7 @@
         ],
         out_specs=pl.BlockSpec((span, lanes), lambda g: (0, g)),
         out_shape=jax.ShapeDtypeStruct((span, chans), F32),
+        compiler_params=GRANT,
         name="mix_query",
     )(query_rows, edges, short_weight)
 
@@ -451,54 +569,437 @@
     ]
 
 
-def project(gated_out, out_weight):
-    term = jnp.dot(gated_out, out_weight, preferred_element_type=F32)
-    return lax.psum_scatter(term.astype(BF16), "tp", scatter_dimension=1, tiled=True)
-
-
-def gate_out_kernel(blocks, me_ref, *refs):
-    convs, (mixed, out) = refs[:blocks], refs[blocks:]
+def after(values, others):
+    return lax.optimization_barrier((values, others))[0]
+
+
+HEAD, PASS, ADD = 0, 1, 2
+SENT = np.array(
+    [
+        (HEAD, ADD, ADD, 2, 1),
+        (ADD, PASS, ADD, 3, 2),
+        (PASS, ADD, PASS, 3, 3),
+        (PASS, PASS, PASS, 3, 3),
+    ],
+    np.int32,
+)
+
+
+def gate_out_kernel(blocks, spot, *refs):
+    convs, (mixed, far_weight, gated, sent) = refs[:blocks], refs[blocks:]
     lanes = convs[0].shape[1]
+    rows = gated.shape[1]
     for m in range(blocks):
-        window = pl.ds(pl.multiple_of((me_ref[0] ^ m) * lanes, lanes), lanes)
-        out[:, window] = (mixed[:, window] * convs[m][...].astype(F32)).astype(BF16)
-
-
-def gate_out(me, convs, mixed):
+        window = pl.ds(pl.multiple_of((spot[0] ^ m) * lanes, lanes), lanes)
+        piece = (mixed[:, window] * convs[m][...].astype(F32)).astype(BF16)
+        gated[0, :, window] = piece[:rows]
+        gated[1, :, window] = piece[rows:]
+    first_sent(spot, gated, far_weight, sent)
+
+
+def first_sent(spot, gated, far_weight, sent):
+    @pl.when(spot[1] == 0)
+    def _():
+        term = jnp.dot(gated[1], far_weight[...], preferred_element_type=F32)
+        sent[...] = term.astype(BF16)
+
+    @pl.when(spot[1] != 0)
+    def _():
+        sent[...] = gated[0]
+
+
+def gate_out(spot, convs, mixed, far_weight):
     span, chans = mixed.shape
     return pl.pallas_call(
         partial(gate_out_kernel, len(convs)),
-        out_shape=jax.ShapeDtypeStruct((span, chans), BF16),
-        in_specs=[SMEM] + [VMEM] * (len(convs) + 1),
-        out_specs=VMEM,
+        in_specs=[SMEM] + [VMEM] * (len(convs) + 2),
+        out_specs=[VMEM] * 2,
+        out_shape=[
+            jax.ShapeDtypeStruct((2, span // 2, chans), BF16),
+            jax.ShapeDtypeStruct((span // 2, chans), BF16),
+        ],
         compiler_params=GRANT,
         name="gate_out",
-    )(me, *convs, mixed)
+    )(spot, *convs, mixed, far_weight)
+
+
+def partner_sent(spot, gated, far_weight):
+    return pl.pallas_call(
+        first_sent,
+        in_specs=[SMEM, VMEM, VMEM],
+        out_specs=VMEM,
+        out_shape=jax.ShapeDtypeStruct(gated.shape[1:], BF16),
+        compiler_params=GRANT,
+        cost_estimate=cost(1),
+        name="partner_sent",
+    )(spot, gated, far_weight)
+
+
+def step_kernel(step, plan, head, term, got, out):
+    mode = plan[step - 1]
+
+    @pl.when(mode == HEAD)
+    def _():
+        out[...] = head[...]
+
+    @pl.when(mode == PASS)
+    def _():
+        out[...] = got[...]
+
+    @pl.when(mode == ADD)
+    def _():
+        out[...] = (term[...].astype(F32) + got[...].astype(F32)).astype(BF16)
+
+
+def next_step(plan, step, chain, gated, terms, got):
+    rows, chans = got.shape
+    whole = pl.BlockSpec((rows, chans), lambda g, plan: (0, 0))
+    return pl.pallas_call(
+        partial(step_kernel, step),
+        grid_spec=pltpu.PrefetchScalarGridSpec(
+            num_scalar_prefetch=1,
+            grid=(1,),
+            in_specs=[
+                pl.BlockSpec((None, rows, chans), lambda g, plan: (0, 0, 0)),
+                pl.BlockSpec(
+                    (None, None, rows, chans), lambda g, plan: (chain, step // 3, 0, 0)
+                ),
+                whole,
+            ],
+            out_specs=whole,
+        ),
+        out_shape=jax.ShapeDtypeStruct((rows, chans), BF16),
+        compiler_params=GRANT,
+        cost_estimate=cost(1),
+        name="next_step",
+    )(plan, gated, terms, got)
+
+
+def terms_kernel(plan, mine, partners, weight, out, held, sems):
+    count, chans = held.shape[:2]
+    copies = []
+    for k in range(count):
+        columns = pl.ds(pl.multiple_of(plan[3 + k] * chans, chans), chans)
+        copies.append(pltpu.make_async_copy(weight.at[:, columns], held.at[k], sems.at[k]))
+        copies[-1].start()
+    for k, copy in enumerate(copies):
+        copy.wait()
+        for chain, gated in enumerate((mine, partners)):
+            term = jnp.dot(gated[1], held[k], preferred_element_type=F32)
+            out[chain, k] = term.astype(BF16)
+
+
+def sent_terms(plan, mine, partners, out_weight):
+    _, rows, chans = mine.shape
+    return pl.pallas_call(
+        terms_kernel,
+        in_specs=[SMEM, VMEM, VMEM, HBM],
+        out_specs=VMEM,
+        out_shape=jax.ShapeDtypeStruct((2, 2, rows, chans), BF16),
+        scratch_shapes=[pltpu.VMEM((2, chans, chans), BF16), pltpu.SemaphoreType.DMA((2,))],
+        compiler_params=GRANT,
+        cost_estimate=cost(4),
+        name="sent_terms",
+    )(plan, mine, partners, out_weight)
+
+
+def spread_weight(out_weight, ready):
+    stages, blocks = lax.axis_size("tp"), lax.axis_size("ctx")
+    stage, place = lax.axis_index("tp"), lax.axis_index("ctx")
+    chans = out_weight.shape[0]
+    hops = jnp.where(place % 2 == 0, 1, stages - 1)
+    found = []
+    for rows, row, hop, static in (
+        (2 * chans // blocks, place // 2, hops, (1, stages - 1)),
+        (chans // blocks, place, 2 + 0 * place, (2, 2)),
+    ):
+        start = after((row * rows, (stage + hop) % stages * chans), ready)
+        part = lax.dynamic_slice(out_weight, start, (rows, chans))
+        route = [
+            (c * stages + k, c * stages + (k + static[c % 2]) % stages)
+            for c in range(blocks)
+            for k in range(stages)
+        ]
+        found.append(lax.ppermute(part, ("ctx", "tp"), route))
+    return found
+
+
+def gather_weight(part):
+    devices = range(lax.axis_size("ctx"))
+    near = [(i, i ^ (4 if i & 1 else 2)) for i in devices]
+    other = [(i, i ^ (2 if i & 1 else 4)) for i in devices]
+    two = [part, lax.ppermute(part, "ctx", near)]
+    return jnp.stack(two), jnp.stack([lax.ppermute(x, "ctx", other) for x in two])
+
+
+def pairs_of(refs):
+    return list(zip(refs[::2], refs[1::2]))
+
+
+def spots(first, pair):
+    return (first, pair[0]), (first + 2, pair[1])
+
+
+def add_parts(order, data, *weights):
+    total = None
+    for first, weight in weights:
+        count, lanes, columns = weight.shape
+        picked = []
+        for q in range(count):
+            index = order[first + q]
+            index = index // 2 if lanes == 2 * SUB else index
+            picked.append(data[:, pl.ds(pl.multiple_of(index * lanes, lanes), lanes)])
+        block = weight[...].reshape(count * lanes, columns)
+        picked = jnp.concatenate(picked, axis=1)
+        term = jnp.dot(picked, block, preferred_element_type=F32)
+        total = term if total is None else total + term
+    return total
+
+
+def early_kernel(order, mine, got0, got1, partner0, partner1, weight, *refs):
+    (near, near2, far2), (out, own, first, own_weight, sem) = pairs_of(refs[:6]), refs[6:]
+    turn_count = order[8]
+    rows, chans = got0.shape
+    columns = pl.ds(pl.multiple_of(order[9] * chans, chans), chans)
+    copy = pltpu.make_async_copy(weight.at[:, columns], own_weight, sem)
+    copy.start()
+
+    @pl.when(turn_count >= 2)
+    def _():
+        first[:rows, :] = got0[...]
+        first[rows:, :] = partner0[...]
+
+    @pl.when(turn_count < 2)
+    def _():
+        first[:rows, :] = got1[...]
+        first[rows:, :] = partner1[...]
+
+    @pl.when(turn_count >= 1)
+    def _():
+        out[...] = add_parts(order, first, *spots(0, near))
+
+    @pl.when(turn_count < 1)
+    def _():
+        out[...] = jnp.zeros_like(out)
+
+    @pl.when(turn_count == 3)
+    def _():
+        first[:rows, :] = got1[...]
+        first[rows:, :] = partner1[...]
+        out[...] += add_parts(order, first, *spots(0, near2), *spots(4, far2))
+
+    copy.wait()
+    out[:rows, :] += jnp.dot(mine[0], own_weight[...], preferred_element_type=F32)
+    own[...] = jnp.dot(mine[1], own_weight[...], preferred_element_type=F32)
+
+
+def early_sum(order, mine, arrivals, out_weight, weights):
+    _, rows, chans = mine.shape
+    whole = lambda shape: pl.BlockSpec(shape, lambda g, order: (0,) * len(shape))
+    return pl.pallas_call(
+        early_kernel,
+        grid_spec=pltpu.PrefetchScalarGridSpec(
+            num_scalar_prefetch=1,
+            grid=(1,),
+            in_specs=[whole(mine.shape)]
+            + [whole((rows, chans))] * 4
+            + [HBM]
+            + [whole(x.shape) for x in weights],
+            out_specs=[whole((2 * rows, chans)), whole((rows, chans))],
+            scratch_shapes=[
+                pltpu.VMEM((2 * rows, chans), BF16),
+                pltpu.VMEM((chans, chans), BF16),
+                pltpu.SemaphoreType.DMA,
+            ],
+        ),
+        out_shape=[
+            jax.ShapeDtypeStruct((2 * rows, chans), F32),
+            jax.ShapeDtypeStruct((rows, chans), F32),
+        ],
+        compiler_params=grant(24),
+        cost_estimate=cost(5),
+        name="early_sum",
+    )(order, mine, *arrivals, out_weight, *weights)
+
+
+def late_sum(order, early, got2, got3, weights, total):
+    behind = order[8]
+
+    @pl.when(behind < 2)
+    def _():
+        total[...] = early[...]
+
+    @pl.when(behind == 2)
+    def _():
+        total[...] = early[...] + add_parts(order, got2, *spots(0, weights[0]), *spots(4, weights[1]))
+
+    @pl.when(behind == 3)
+    def _():
+        total[...] = early[...] + add_parts(order, got3, *spots(4, weights[2]))
+
+    summed = jnp.where(behind == 3, got2[...].astype(F32), got3[...].astype(F32))
+    return jnp.where(behind == 0, 0.0, summed)
+
+
+def partner_kernel(order, early, got2, got3, *refs):
+    weights, (out, total) = pairs_of(refs[:6]), refs[6:]
+    out[1] = late_sum(order, early, got2, got3, weights, total).astype(BF16)
+    out[0] = total[...].astype(BF16)
+
+
+def partner_sum(order, early, arrivals, weights):
+    rows, chans = arrivals[0].shape
+    whole = lambda shape: pl.BlockSpec(shape, lambda g, order: (0,) * len(shape))
+    return pl.pallas_call(
+        partner_kernel,
+        grid_spec=pltpu.PrefetchScalarGridSpec(
+            num_scalar_prefetch=1,
+            grid=(1,),
+            in_specs=[pl.BlockSpec((rows, chans), lambda g, order: (1, 0))]
+            + [whole((rows, chans))] * 2
+            + [whole(x.shape) for x in weights],
+            out_specs=whole((2, rows, chans)),
+            scratch_shapes=[pltpu.VMEM((rows, chans), F32)],
+        ),
+        out_shape=jax.ShapeDtypeStruct((2, rows, chans), BF16),
+        compiler_params=grant(24),
+        cost_estimate=cost(2),
+        name="partner_sum",
+    )(order, early, *arrivals, *weights)
+
+
+def mine_kernel(order, early, own, got2, got3, *refs):
+    weights, (out, total) = pairs_of(refs[:6]), refs[6:]
+    rows = early.shape[0]
+    out[rows:, :] = late_sum(order, early, got2, got3, weights, total) + own[...]
+    out[:rows, :] = total[...]
+
+
+def mine_sum(order, early, own, arrivals, weights):
+    rows, chans = arrivals[0].shape
+    whole = lambda shape: pl.BlockSpec(shape, lambda g, order: (0,) * len(shape))
+    return pl.pallas_call(
+        mine_kernel,
+        grid_spec=pltpu.PrefetchScalarGridSpec(
+            num_scalar_prefetch=1,
+            grid=(1,),
+            in_specs=[pl.BlockSpec((rows, chans), lambda g, order: (0, 0))]
+            + [whole((rows, chans))] * 3
+            + [whole(x.shape) for x in weights],
+            out_specs=whole((2 * rows, chans)),
+            scratch_shapes=[pltpu.VMEM((rows, chans), F32)],
+        ),
+        out_shape=jax.ShapeDtypeStruct((2 * rows, chans), F32),
+        compiler_params=grant(24),
+        cost_estimate=cost(3),
+        name="mine_sum",
+    )(order, early, own, *arrivals, *weights)
+
+
+def join_kernel(mine, partners, out):
+    rows = partners.shape[1]
+    for half in range(2):
+        part = slice(half * rows, (half + 1) * rows)
+        out[part, :] = (mine[part, :] + partners[half].astype(F32)).astype(BF16)
+
+
+def join_sums(mine, partners):
+    return pl.pallas_call(
+        join_kernel,
+        in_specs=[VMEM] * 2,
+        out_specs=VMEM,
+        out_shape=jax.ShapeDtypeStruct(mine.shape, BF16),
+        compiler_params=GRANT,
+        name="join_sums",
+    )(mine, partners)
+
+
+def weight_order():
+    place, stage = lax.axis_index("ctx"), lax.axis_index("tp")
+    up = place % 2 == 0
+    last = lax.axis_size("tp") - 1
+    a = jnp.where(up, 2, 4)
+    masks = [0 * a, a, 6 - a, 0 * a + 6]
+    swapped = [0 * a + 1, (6 - a) ^ 1, a ^ 1, 0 * a + 7]
+    parts = [place ^ mask for mask in masks + swapped]
+    return jnp.stack(parts + [jnp.where(up, stage, last - stage), stage]).astype(jnp.int32)
+
+
+def project(spot, plan, order, convs, mixed, out_weight, weight_parts):
+    stages, blocks = lax.axis_size("tp"), lax.axis_size("ctx")
+    chans = out_weight.shape[0]
+    far_weight = lax.dynamic_slice(out_weight, (0, spot[2] * chans), (chans, chans))
+    mine, sent = gate_out(spot, convs, mixed, far_weight)
+    route = []
+    for c in range(blocks):
+        for k in range(stages):
+            to = k + (1 if c % 2 == 0 else -1)
+            if 0 <= to < stages:
+                route.append((c * stages + k, c * stages + to))
+    onward = lambda x: lax.ppermute(x, ("ctx", "tp"), route)
+    core_swap = lambda x: lax.ppermute(x, "ctx", [(i, i ^ 1) for i in range(blocks)])
+    partners = core_swap(mine)
+    partner_first = partner_sent(spot, partners, far_weight)
+    got = [[onward(sent), onward(partner_first)]]
+    terms = sent_terms(plan, mine, partners, out_weight)
+    steps = []
+    for step in range(1, stages):
+        row = []
+        for chain, gated in enumerate((mine, partners)):
+            row.append(next_step(plan, step, chain, gated, terms, got[-1][chain]))
+        steps.append(row)
+        got.append([onward(x) for x in row])
+
+    near, near2 = (gather_weight(part) for part in after(weight_parts, partner_first))
+    far2, far = ([core_swap(x) for x in pair] for pair in (near2, near))
+    arrivals = [got[0][0], got[1][0], got[0][1], got[1][1]]
+    early, own = early_sum(order, mine, arrivals, out_weight, (*near, *near2, *far2))
+    late = (*near2, *far2, *far)
+    theirs = partner_sum(after(order, got[3][0]), early, [got[2][1], got[3][1]], late)
+    ours = mine_sum(order, early, own, [got[2][0], got[3][0]], late)
+    return join_sums(ours, core_swap(theirs))
 
 
 def fast_per_device(
     query_rows, key_rows, value_rows, short_weight, skip_gain, filter_taps, out_weight
 ):
     span, chans = query_rows.shape
-    blocks = lax.axis_size("ctx")
+    blocks, stages = lax.axis_size("ctx"), lax.axis_size("tp")
     lanes = chans // blocks
     length = span * blocks
     radix = 2 * length // SUB
-    place = lax.axis_index("ctx")
+    place, stage = lax.axis_index("ctx"), lax.axis_index("tp")
     me = place.astype(jnp.int32).reshape(1)
+    up = place % 2 == 0
+    behind = jnp.where(up, stage, stages - 1 - stage)
+    far = jnp.where(up, stages - 1, 0)
+    spot = jnp.stack([place, behind, far]).astype(jnp.int32)
+    plan = lax.dynamic_index_in_dim(jnp.asarray(SENT), behind, keepdims=False)
+    plan = jnp.where(up | (jnp.arange(5) < 3), plan, stages - 1 - plan)
+    me, spot, plan, order = lax.optimization_barrier((me, spot, plan, weight_order()))
+    skip = lax.dynamic_slice(skip_gain, (place * lanes,), (lanes,)).reshape(1, lanes)
     forward, inverse = (jnp.asarray(t) for t in dft_tables(2 * length))
     twiddle = jnp.asarray(twiddle_table(radix))
-    edges = jnp.concatenate([x[-2:] for x in (query_rows, key_rows, value_rows)])
-    edges = passed_along(edges, "ctx", 1)
-    taps = exchange(split_taps(me, filter_taps, blocks), "ctx")
-    gated = exchange(gate_in(me, key_rows, value_rows, edges, short_weight, blocks), "ctx")
+    devices = range(blocks)
+    core_swap = lambda x: lax.ppermute(x, "ctx", [(i, i ^ 1) for i in devices])
+    to_chips = lambda xs: [
+        lax.ppermute(x, "ctx", [(i, i ^ (2 * q + 2)) for i in devices])
+        for q, x in enumerate(xs)
+    ]
+    edges = passed_along(rims(query_rows, key_rows, value_rows), "ctx", 1)
+    pairs = split_taps(after(me, edges), filter_taps, blocks // 2)
+    pairs = [pairs[0]] + to_chips(pairs[1:])
+    stay, same, swap = gate_in(me, key_rows, value_rows, edges, short_weight, blocks)
+    swapped = core_swap(swap)
+    packed = pair_up(same, swapped)
+    others = to_chips(packed)
+    taps_swapped = core_swap(other_core(me, pairs))
     mixed = mix_query(query_rows, edges, short_weight)
-    skip = lax.dynamic_slice(skip_gain, (place * lanes,), (lanes,)).reshape(1, lanes)
-    spectra = taps_spectra_of(me, taps, twiddle, forward)
-    convs = long_conv(me, gated, spectra, twiddle, forward, inverse, skip)
-    convs = exchange(convs, "ctx")
-    gated_out = gate_out(me, convs, mixed)
-    return project(gated_out, out_weight)
+    spectra = taps_spectra_of(me, pairs, taps_swapped, twiddle, forward)
+    weight_parts = spread_weight(out_weight, taps_swapped)
+    conv = long_conv(me, stay, swapped, others, spectra, twiddle, forward, inverse, skip)
+    convs = exchange(spread(after(me, weight_parts), conv, blocks), "ctx")
+    return project(spot, plan, order, convs, mixed, out_weight, weight_parts)
 
 
 def per_device(*arrays):

time: 186 us -> 151 us (0.81)
  waiting for transfers between devices: 89.5 us -> 31.4 us
  starting transfers between devices: 23.1 us -> 56.6 us
  between operations: 13.5 us -> 1.31 us
  matrix products: 9.47 us -> 0 us
  Pallas kernels: 42.2 us -> 50.8 us
  other arithmetic: 0.02 us -> 2.02 us
    reduce_scatter x1 -> x0, waiting for transfers between devices: 78.1 us -> none  [project(): lax.psum_scatter(term.astype(BF16), 'tp', scatter_dimension=1, tiled=True)]
    ppermute x0 -> x30, starting transfers between devices: none -> 47.8 us  [the longest x8 26.3 us: project(): onward = lambda x: lax.ppermute(x, ('ctx', 'tp'), route)]
    ppermute x0 -> x30, waiting for transfers between devices: none -> 25.1 us  [the longest x8 10.1 us: project(): onward = lambda x: lax.ppermute(x, ('ctx', 'tp'), route)]
    ppermute x21 -> x7, starting transfers between devices: 21.3 us -> 6.45 us  [exchange(): lax.ppermute(piece, axis, [(i, i ^ m) for i in devices])]
    pallas_call x5 -> x21, Pallas kernels: 38.2 us -> 49.8 us  [the longest x1 19.1 us: long_conv(): pl.pallas_call(partial(conv_kernel, blocks), out_shape=jax.ShapeDtypeStru...]
    dot_general x1 -> x0, matrix products: 9.47 us -> none  [project(): term = jnp.dot(gated_out, out_weight, preferred_element_type=F32)]
    dynamic_slice x0 -> x3, local copies, waits for them, and re-layouts: none -> 5.09 us  [the longest x2 3.18 us: spread_weight(): part = lax.dynamic_slice(out_weight, start, (rows, chans))]
    ppermute x21 -> x7, waiting for transfers between devices: 10.5 us -> 6.11 us  [exchange(): lax.ppermute(piece, axis, [(i, i ^ m) for i in devices])]
  transfers between devices with their start and end apart: 23 -> 38, of which waited for: 6 -> 13; matrix products, arithmetic and copies ran while one was open for 1% -> 5% of each run, Pallas kernels for 10% -> 30%
where the time goes in v3:
time: 151 us; the launch traced here: 150 us
  starting transfers between devices  56.6 us (37%)
  Pallas kernels  50.8 us (34%)
  waiting for transfers between devices  31.4 us (21%)
  local copies, waits for them, and re-layouts  7.96 us (5%)
  other arithmetic  2.02 us (1%)
    ppermute x8, starting transfers between devices, project(): onward = lambda x: lax.ppermute(x, ('ctx', 'tp'), route)  26.3 us
    pallas_call x1, Pallas kernels, long_conv(): pl.pallas_call(partial(conv_kernel, blocks), out_shape=jax.ShapeDtypeStru...  19.1 us
    ppermute x6, starting transfers between devices, fast_per_device(): lax.ppermute(x, 'ctx', [(i, i ^ 2 * q + 2) for i in devices])  10.8 us
    ppermute x8, waiting for transfers between devices, project(): onward = lambda x: lax.ppermute(x, ('ctx', 'tp'), route)  10.1 us
    pallas_call x1, Pallas kernels, taps_spectra_of(): pl.pallas_call(partial(taps_kernel, chips), out_shape=jax.ShapeDtypeStruc...  7.93 us
    ppermute x7, starting transfers between devices, exchange(): lax.ppermute(piece, axis, [(i, i ^ m) for i in devices])  6.45 us
    ppermute x6, waiting for transfers between devices, fast_per_device(): lax.ppermute(x, 'ctx', [(i, i ^ 2 * q + 2) for i in devices])  6.17 us
    ppermute x7, waiting for transfers between devices, exchange(): lax.ppermute(piece, axis, [(i, i ^ m) for i in devices])  6.11 us
  transfers between devices with their start and end apart: 38, of which 13 were waited for; matrix products, arithmetic and copies ran while one was open for 5% of the time, Pallas kernels for 30%

profile of v3, /device:TPU:0, one launch (start us, length us, event | category | flops | bytes accessed | tf_op | source)
XLA Modules:
  0.0 150.2 jit_solution(3519156854365030357)
XLA Ops:
  0.0 1.5 %rims.1 = bf16[6,1024]{1,0:T(8,128)(2,1)} custom-call(bf16[512,1024]{1,0:T(8,128)(2,1)} %query.3, bf16[512,1024]{1,0:T(8,128)(2,1)} %key.3, bf16[512,1024]{1,0:T(8,128)(2,1)} %value.3), custom_call_target="tpu_custom_call" | custom-call | tf_op jit(solution)/shard_map/rims/pallas_call | solution.py:413
  1.5 2.4 %collective-permute-start = (bf16[6,1024]{1,0:T(8,128)(2,1)}, bf16[6,1024]{1,0:T(8,128)(2,1)S(1)}, u32[]{:S(2)}, u32[]{:S(2)}) collective-permute-start(bf16[6,1024]{1,0:T(8,128)(2,1)} %rims.1), channel_id=1, source_target_pairs={{0,4},{4,8},{8,12},{12,16},{16,20},{20,24},{24,28},{1,5},{5,9},{9,... | collective-permute-start | bytes 36872 | tf_op jit(solution)/shard_map/ppermute | solution.py:18
  5.1 4.9 %collective-permute-start.1 = (bf16[256,512]{1,0:T(8,128)(2,1)S(1)}, bf16[256,512]{1,0:T(8,128)(2,1)S(1)}, u32[]{:S(2)}, u32[]{:S(2)}) collective-permute-start(bf16[256,512]{1,0:T(8,128)(2,1)S(1)} %get-tuple-element.45), channel_id=1, source_target_pairs={{0,8},{4,12},{8,0},{12,4},{16,24},{20,28},{24,16},{28,20},{1,9},{5... | collective-permute-start | bytes 786440 | tf_op jit(solution)/shard_map/ppermute | solution.py:986
  10.0 1.5 %collective-permute-start.2 = (bf16[256,512]{1,0:T(8,128)(2,1)S(1)}, bf16[256,512]{1,0:T(8,128)(2,1)S(1)}, u32[]{:S(2)}, u32[]{:S(2)}) collective-permute-start(bf16[256,512]{1,0:T(8,128)(2,1)S(1)} %get-tuple-element.46), channel_id=1, source_target_pairs={{0,16},{4,20},{8,24},{12,28},{16,0},{20,4},{24,8},{28,12},{1,17},{... | collective-permute-start | bytes 786440 | tf_op jit(solution)/shard_map/ppermute | solution.py:986
  11.5 0.9 collective-permute-start.3
  12.4 4.2 %gate_in.1 = (bf16[512,128]{1,0:T(8,128)(2,1)}, bf16[3,512,128]{2,1,0:T(8,128)(2,1)}, bf16[4,512,128]{2,1,0:T(8,128)(2,1)}) custom-call(s32[1]{0:T(128)} %bitcast.me_ref, bf16[512,1024]{1,0:T(8,128)(2,1)} %key.3, bf16[512,1024]{1,0:T(8,128)(2,1)} %value.3, bf16[6,1024]{1,0:T(8,128)(2,1)} %copy-done.5, f32[3,3,1024]{2,1,0:T(4,128)} %weight.5), custom_call_target="tpu_custom_call" | custom-call | tf_op jit(solution)/shard_map/gate_in/pallas_call | solution.py:464
  17.1 5.7 %collective-permute-done.2.refs_2_ = bf16[256,512]{1,0:T(8,128)(2,1)S(1)} collective-permute-done((bf16[256,512]{1,0:T(8,128)(2,1)S(1)}, bf16[256,512]{1,0:T(8,128)(2,1)S(1)}, u32[]{:S(2)}, u32[]{:S(2)}) %collective-permute-start.2) | collective-permute-done | bytes 262176 | tf_op jit(solution)/shard_map/ppermute | solution.py:986
  23.1 1.0 copy-done.3
  24.1 0.8 pair_up.1
  24.9 1.5 %collective-permute-start.10 = (bf16[2,512,128]{2,1,0:T(8,128)(2,1)}, bf16[2,512,128]{2,1,0:T(8,128)(2,1)S(1)}, u32[]{:S(2)}, u32[]{:S(2)}) collective-permute-start(bf16[2,512,128]{2,1,0:T(8,128)(2,1)} %get-tuple-element.58), channel_id=1, source_target_pairs={{0,24},{4,28},{8,16},{12,20},{16,8},{20,12},{24,0},{28,4},{1,25},{... | collective-permute-start | bytes 786440 | tf_op jit(solution)/shard_map/ppermute | solution.py:986
  27.0 1.4 collective-permute-start.9
  28.4 1.8 %dynamic_slice.18 = bf16[128,1024]{1,0:T(8,128)(2,1)} dynamic-slice(bf16[1024,4096]{1,0:T(8,128)(2,1)} %weight.7, s32[]{:T(128)S(6)} %select_n.75, s32[]{:T(128)S(6)} %select_n.76), dynamic_slice_sizes={128,1024} | dynamic-slice | bytes 524292 | tf_op jit(solution)/shard_map/dynamic_slice | solution.py:717
  30.2 2.6 %collective-permute-start.6 = (bf16[128,1024]{1,0:T(8,128)(2,1)}, bf16[128,1024]{1,0:T(8,128)(2,1)}, u32[]{:S(2)}, u32[]{:S(2)}) collective-permute-start(bf16[128,1024]{1,0:T(8,128)(2,1)} %dynamic_slice.18), channel_id=1, source_target_pairs={{0,2},{1,3},{2,0},{3,1},{4,6},{5,7},{6,4},{7,5},{8,10},{9,11},{10,... | collective-permute-start | bytes 786440 | tf_op jit(solution)/shard_map/ppermute | solution.py:723
  32.8 1.4 dynamic_slice.17
  34.2 1.6 %collective-permute-start.5 = (bf16[256,1024]{1,0:T(8,128)(2,1)S(1)}, bf16[256,1024]{1,0:T(8,128)(2,1)S(1)}, u32[]{:S(2)}, u32[]{:S(2)}) collective-permute-start(bf16[256,1024]{1,0:T(8,128)(2,1)S(1)} %dynamic_slice.17), channel_id=1, source_target_pairs={{0,1},{1,2},{2,3},{3,0},{4,7},{5,4},{6,5},{7,6},{8,9},{9,10},{10,1... | collective-permute-start | bytes 1572872 | tf_op jit(solution)/shard_map/ppermute | solution.py:723
  35.8 1.0 copy-done.8
  36.8 7.9 %taps_spectra.1.refs_3_ = f32[17,256,256]{2,1,0:T(8,128)S(1)} custom-call(s32[1]{0:T(128)} %bitcast.me_ref, bf16[256,512]{1,0:T(8,128)(2,1)S(1)} %get-tuple-element.44.refs_0_, bf16[256,512]{1,0:T(8,128)(2,1)S(1)} %collective-permute-done.1.refs_1_, bf16[256,512]{1,0:T(8,128)(2,1)S(1)} %collective-permute-done.2.refs_2_, ...), custom_call_target="tpu_custom_call" | custom-call | flops 8000000000 | tf_op jit(solution)/shard_map/taps_spectra/pallas_call | solution.py:344
  44.8 19.1 %long_conv.1.conv = f32[4096,128]{1,0:T(8,128)S(1)} custom-call(s32[1]{0:T(128)} %bitcast.me_ref, bf16[512,128]{1,0:T(8,128)(2,1)S(1)} %copy-done.7, bf16[4,512,128]{2,1,0:T(8,128)(2,1)S(1)} %collective-permute-done.7.swapped, bf16[2,512,128]{2,1,0:T(8,128)(2,1)S(1)} %collective-permute-done.8.refs_0_, bf16[2,512,128]{2,1,0:T(8,128)(2,1)} %collective-permute-done.9.refs_1_, ...), custom_call_target="tpu_custom_call" | custom-call | flops 20000000000 | tf_op jit(solution)/shard_map/long_conv/pallas_call | solution.py:363
  66.2 1.3 collective-permute-start.13
  68.1 1.0 collective-permute-start.15
  69.2 1.5 %collective-permute-start.16 = (bf16[512,128]{1,0:T(8,128)(2,1)S(1)}, bf16[512,128]{1,0:T(8,128)(2,1)S(1)}, u32[]{:S(2)}, u32[]{:S(2)}) collective-permute-start(bf16[512,128]{1,0:T(8,128)(2,1)S(1)} %get-tuple-element.65), channel_id=1, source_target_pairs={{0,24},{4,28},{8,16},{12,20},{16,8},{20,12},{24,0},{28,4},{1,25},{... | collective-permute-start | bytes 393224 | tf_op jit(solution)/shard_map/ppermute | solution.py:566
  70.7 1.2 collective-permute-start.17
  72.0 1.9 %constant_dynamic-slice_fusion.refs_9_.far_weight = bf16[1024,1024]{1,0:T(8,128)(2,1)S(1)} fusion(bf16[1024,4096]{1,0:T(8,128)(2,1)} %weight.7, s32[]{:T(128)S(6)} %select_n.78), kind=kLoop, calls=%fused_computation.7 | loop fusion | bytes 4194308 | tf_op jit(solution)/shard_map/dynamic_slice | solution.py:931
  73.9 1.1 mix_query.1.refs_8_
  75.0 4.4 %collective-permute-done.14.refs_4_ = bf16[512,128]{1,0:T(8,128)(2,1)S(1)} collective-permute-done((bf16[512,128]{1,0:T(8,128)(2,1)S(1)}, bf16[512,128]{1,0:T(8,128)(2,1)S(1)}, u32[]{:S(2)}, u32[]{:S(2)}) %collective-permute-start.14) | collective-permute-done | bytes 131104 | tf_op jit(solution)/shard_map/ppermute | solution.py:566
  79.4 1.7 %collective-permute-done.15.refs_5_ = bf16[512,128]{1,0:T(8,128)(2,1)S(1)} collective-permute-done((bf16[512,128]{1,0:T(8,128)(2,1)S(1)}, bf16[512,128]{1,0:T(8,128)(2,1)S(1)}, u32[]{:S(2)}, u32[]{:S(2)}) %collective-permute-start.15) | collective-permute-done | bytes 131104 | tf_op jit(solution)/shard_map/ppermute | solution.py:566
  81.1 1.6 %gate_out.1 = (bf16[2,256,1024]{2,1,0:T(8,128)(2,1)S(1)}, bf16[256,1024]{1,0:T(8,128)(2,1)S(1)}) custom-call(s32[3]{0:T(128)S(1)} %pad_add_fusion.spot, bf16[512,128]{1,0:T(8,128)(2,1)S(1)} %get-tuple-element.59.refs_0_, bf16[512,128]{1,0:T(8,128)(2,1)S(1)} %collective-permute-done.11.refs_1_, bf16[512,128]{1,0:T(8,128)(2,1)S(1)} %collective-permute-done.12.refs_2_, ...), custom_call_target="tpu_custom_call" | custom-call | tf_op jit(solution)/shard_map/gate_out/pallas_call | solution.py:613
  82.8 1.8 %collective-permute-start.18 = (bf16[256,1024]{1,0:T(8,128)(2,1)S(1)}, bf16[256,1024]{1,0:T(8,128)(2,1)S(1)}, u32[]{:S(2)}, u32[]{:S(2)}) collective-permute-start(bf16[256,1024]{1,0:T(8,128)(2,1)S(1)} %get-tuple-element.68), channel_id=1, source_target_pairs={{0,1},{1,2},{2,3},{5,4},{6,5},{7,6},{8,9},{9,10},{10,11},{13,12},{... | collective-permute-start | bytes 1572872 | tf_op jit(solution)/shard_map/ppermute | solution.py:939
  84.6 0.9 collective-permute-done.19.partners.gated.head
  85.5 1.3 partner_sent.1
  86.7 1.3 collective-permute-start.21
  88.7 3.9 %sent_terms.1.term = bf16[2,2,256,1024]{3,2,1,0:T(8,128)(2,1)S(1)} custom-call(s32[5]{0:T(128)S(1)} %or_select_fusion.plan, bf16[2,256,1024]{2,1,0:T(8,128)(2,1)S(1)} %get-tuple-element.67.mine.head, bf16[2,256,1024]{2,1,0:T(8,128)(2,1)S(1)} %collective-permute-done.19.partners.gated.head, bf16[1024,4096]{1,0:T(8,128)(2,1)S(1)} %bitcast.25), custom_call_target="tpu_custom_call" | custom-call | flops 4000000000 | tf_op jit(solution)/shard_map/sent_terms/pallas_call | solution.py:694
  93.2 4.9 %collective-permute-start.20 = (bf16[256,1024]{1,0:T(8,128)(2,1)S(1)}, bf16[256,1024]{1,0:T(8,128)(2,1)S(1)}, u32[]{:S(2)}, u32[]{:S(2)}) collective-permute-start(bf16[256,1024]{1,0:T(8,128)(2,1)S(1)} %next_step.6), channel_id=1, source_target_pairs={{0,1},{1,2},{2,3},{5,4},{6,5},{7,6},{8,9},{9,10},{10,11},{13,12},{... | collective-permute-start | bytes 1572872 | tf_op jit(solution)/shard_map/ppermute | solution.py:939
  98.7 3.4 %collective-permute-start.22 = (bf16[256,1024]{1,0:T(8,128)(2,1)S(1)}, bf16[256,1024]{1,0:T(8,128)(2,1)S(1)}, u32[]{:S(2)}, u32[]{:S(2)}) collective-permute-start(bf16[256,1024]{1,0:T(8,128)(2,1)S(1)} %next_step.7), channel_id=1, source_target_pairs={{0,1},{1,2},{2,3},{5,4},{6,5},{7,6},{8,9},{9,10},{10,11},{13,12},{... | collective-permute-start | bytes 1572872 | tf_op jit(solution)/shard_map/ppermute | solution.py:939
  102.8 1.5 %collective-permute-start.24 = (bf16[256,1024]{1,0:T(8,128)(2,1)S(1)}, bf16[256,1024]{1,0:T(8,128)(2,1)S(1)}, u32[]{:S(2)}, u32[]{:S(2)}) collective-permute-start(bf16[256,1024]{1,0:T(8,128)(2,1)S(1)} %copy-done.12), channel_id=1, source_target_pairs={{0,16},{4,12},{8,24},{12,4},{16,0},{20,28},{24,8},{28,20},{1,17},{... | collective-permute-start | bytes 1572872 | tf_op jit(solution)/shard_map/ppermute | solution.py:732
  104.8 1.5 %collective-permute-start.27 = (bf16[128,1024]{1,0:T(8,128)(2,1)}, bf16[128,1024]{1,0:T(8,128)(2,1)S(1)}, u32[]{:S(2)}, u32[]{:S(2)}) collective-permute-start(bf16[128,1024]{1,0:T(8,128)(2,1)} %collective-permute-done.6), channel_id=1, source_target_pairs={{0,16},{4,12},{8,24},{12,4},{16,0},{20,28},{24,8},{28,20},{1,17},{... | collective-permute-start | bytes 786440 | tf_op jit(solution)/shard_map/ppermute | solution.py:732
  107.0 4.7 %collective-permute-done.26 = bf16[128,1024]{1,0:T(8,128)(2,1)S(1)} collective-permute-done((bf16[128,1024]{1,0:T(8,128)(2,1)}, bf16[128,1024]{1,0:T(8,128)(2,1)S(1)}, u32[]{:S(2)}, u32[]{:S(2)}) %collective-permute-start.26) | collective-permute-done | bytes 262176 | tf_op jit(solution)/shard_map/ppermute | solution.py:731
  111.7 3.2 %collective-permute-start.31 = (bf16[256,1024]{1,0:T(8,128)(2,1)S(1)}, bf16[256,1024]{1,0:T(8,128)(2,1)S(1)}, u32[]{:S(2)}, u32[]{:S(2)}) collective-permute-start(bf16[256,1024]{1,0:T(8,128)(2,1)S(1)} %next_step.8), channel_id=1, source_target_pairs={{0,1},{1,2},{2,3},{5,4},{6,5},{7,6},{8,9},{9,10},{10,11},{13,12},{... | collective-permute-start | bytes 1572872 | tf_op jit(solution)/shard_map/ppermute | solution.py:939
  114.8 1.0 pad_maximum_fusion.2.refs_2_.refs_0_
  117.8 4.3 %collective-permute-start.35 = (bf16[256,1024]{1,0:T(8,128)(2,1)S(1)}, bf16[256,1024]{1,0:T(8,128)(2,1)S(1)}, u32[]{:S(2)}, u32[]{:S(2)}) collective-permute-start(bf16[256,1024]{1,0:T(8,128)(2,1)S(1)} %next_step.10), channel_id=1, source_target_pairs={{0,1},{1,2},{2,3},{5,4},{6,5},{7,6},{8,9},{9,10},{10,11},{13,12},{... | collective-permute-start | bytes 1572872 | tf_op jit(solution)/shard_map/ppermute | solution.py:939
  122.3 1.1 collective-permute-done.28
  124.8 4.0 %collective-permute-done.35.got.got2 = bf16[256,1024]{1,0:T(8,128)(2,1)S(1)} collective-permute-done((bf16[256,1024]{1,0:T(8,128)(2,1)S(1)}, bf16[256,1024]{1,0:T(8,128)(2,1)S(1)}, u32[]{:S(2)}, u32[]{:S(2)}) %collective-permute-start.35) | collective-permute-done | bytes 524320 | tf_op jit(solution)/shard_map/ppermute | solution.py:939
  128.8 4.4 %collective-permute-start.32 = (bf16[256,1024]{1,0:T(8,128)(2,1)S(1)}, bf16[256,1024]{1,0:T(8,128)(2,1)S(1)}, u32[]{:S(2)}, u32[]{:S(2)}) collective-permute-start(bf16[256,1024]{1,0:T(8,128)(2,1)S(1)} %next_step.9), channel_id=1, source_target_pairs={{0,1},{1,2},{2,3},{5,4},{6,5},{7,6},{8,9},{9,10},{10,11},{13,12},{... | collective-permute-start | bytes 1572872 | tf_op jit(solution)/shard_map/ppermute | solution.py:939
  133.9 3.1 %collective-permute-start.36 = (bf16[256,1024]{1,0:T(8,128)(2,1)S(1)}, bf16[256,1024]{1,0:T(8,128)(2,1)S(1)}, u32[]{:S(2)}, u32[]{:S(2)}) collective-permute-start(bf16[256,1024]{1,0:T(8,128)(2,1)S(1)} %next_step.11), channel_id=1, source_target_pairs={{0,1},{1,2},{2,3},{5,4},{6,5},{7,6},{8,9},{9,10},{10,11},{13,12},{... | collective-permute-start | bytes 1572872 | tf_op jit(solution)/shard_map/ppermute | solution.py:939
  137.0 2.4 %early_sum.1 = (f32[512,1024]{1,0:T(8,128)S(1)}, f32[256,1024]{1,0:T(8,128)S(1)}) custom-call(s32[10]{0:T(128)S(1)} %stack.86.order, bf16[2,256,1024]{2,1,0:T(8,128)(2,1)S(1)} %get-tuple-element.67.mine.head, bf16[256,1024]{1,0:T(8,128)(2,1)S(1)} %collective-permute-done.18.got.got0, bf16[256,1024]{1,0:T(8,128)(2,1)S(1)} %collective-permute-done.20.got1.got, ...), custom_call_target="tpu_custom_call" | custom-call | flops 5000000000 | tf_op jit(solution)/shard_map/early_sum/pallas_call | solution.py:799
  139.8 5.6 %collective-permute-done.36.got3 = bf16[256,1024]{1,0:T(8,128)(2,1)S(1)} collective-permute-done((bf16[256,1024]{1,0:T(8,128)(2,1)S(1)}, bf16[256,1024]{1,0:T(8,128)(2,1)S(1)}, u32[]{:S(2)}, u32[]{:S(2)}) %collective-permute-start.36) | collective-permute-done | bytes 524320 | tf_op jit(solution)/shard_map/ppermute | solution.py:939
  147.2 1.8 %collective-permute-done.37.partners = bf16[2,256,1024]{2,1,0:T(8,128)(2,1)S(1)} collective-permute-done((bf16[2,256,1024]{2,1,0:T(8,128)(2,1)S(1)}, bf16[2,256,1024]{2,1,0:T(8,128)(2,1)S(1)}, u32[]{:S(2)}, u32[]{:S(2)}) %collective-permute-start.37) | collective-permute-done | bytes 1048608 | tf_op jit(solution)/shard_map/ppermute | solution.py:940
  149.0 1.1 join_sums.1
  (93 shorter events, 14.6 us)
Async XLA Ops:
  0.0 23.0 %copy-start = (f32[1024]{0:T(1024)S(1)}, f32[1024]{0:T(1024)}, u32[]{:S(2)}) copy-start(f32[1024]{0:T(1024)} %param.15) | copy-start | bytes 12292
  0.0 4.9 %copy-start.2 = (bf16[1024,512]{1,0:T(8,128)(2,1)S(1)}, bf16[1024,512]{1,0:T(8,128)(2,1)}, u32[]{:S(2)}) copy-start(bf16[1024,512]{1,0:T(8,128)(2,1)} %taps.1) | copy-start | bytes 3145732
  1.5 3.4 %collective-permute-start = (bf16[6,1024]{1,0:T(8,128)(2,1)}, bf16[6,1024]{1,0:T(8,128)(2,1)S(1)}, u32[]{:S(2)}, u32[]{:S(2)}) collective-permute-start(bf16[6,1024]{1,0:T(8,128)(2,1)} %rims.1), channel_id=1, source_target_pairs={{0,4},{4,8},{8,12},{12,16},{16,20},{20,24},{24,28},{1,5},{5,9},{9,... | collective-permute-start | bytes 36872 | tf_op jit(solution)/shard_map/ppermute | solution.py:18
  4.9 7.4 %copy-start.5 = (bf16[6,1024]{1,0:T(8,128)(2,1)}, bf16[6,1024]{1,0:T(8,128)(2,1)S(1)}, u32[]{:S(2)}) copy-start(bf16[6,1024]{1,0:T(8,128)(2,1)S(1)} %collective-permute-done.edges) | copy-start | bytes 36868
  5.1 12.0 %collective-permute-start.1 = (bf16[256,512]{1,0:T(8,128)(2,1)S(1)}, bf16[256,512]{1,0:T(8,128)(2,1)S(1)}, u32[]{:S(2)}, u32[]{:S(2)}) collective-permute-start(bf16[256,512]{1,0:T(8,128)(2,1)S(1)} %get-tuple-element.45), channel_id=1, source_target_pairs={{0,8},{4,12},{8,0},{12,4},{16,24},{20,28},{24,16},{28,20},{1,9},{5... | collective-permute-start | bytes 786440 | tf_op jit(solution)/shard_map/ppermute | solution.py:986
  10.0 12.9 %collective-permute-start.2 = (bf16[256,512]{1,0:T(8,128)(2,1)S(1)}, bf16[256,512]{1,0:T(8,128)(2,1)S(1)}, u32[]{:S(2)}, u32[]{:S(2)}) collective-permute-start(bf16[256,512]{1,0:T(8,128)(2,1)S(1)} %get-tuple-element.46), channel_id=1, source_target_pairs={{0,16},{4,20},{8,24},{12,28},{16,0},{20,4},{24,8},{28,12},{1,17},{... | collective-permute-start | bytes 786440 | tf_op jit(solution)/shard_map/ppermute | solution.py:986
  11.5 11.3 %collective-permute-start.3 = (bf16[256,512]{1,0:T(8,128)(2,1)S(1)}, bf16[256,512]{1,0:T(8,128)(2,1)S(1)}, u32[]{:S(2)}, u32[]{:S(2)}) collective-permute-start(bf16[256,512]{1,0:T(8,128)(2,1)S(1)} %get-tuple-element.47), channel_id=1, source_target_pairs={{0,24},{4,28},{8,16},{12,20},{16,8},{20,12},{24,0},{28,4},{1,25},{... | collective-permute-start | bytes 786440 | tf_op jit(solution)/shard_map/ppermute | solution.py:986
  16.6 19.3 %copy-start.10 = (f32[128,66]{1,0:T(8,128)S(1)}, f32[128,66]{1,0:T(8,128)}, u32[]{:S(2)}) copy-start(f32[128,66]{1,0:T(8,128)} %constant.84.clone.refs_5_.refs_4_) | copy-start | bytes 101380
  16.6 6.5 %collective-permute-start.7 = (bf16[4,512,128]{2,1,0:T(8,128)(2,1)}, bf16[4,512,128]{2,1,0:T(8,128)(2,1)S(1)}, u32[]{:S(2)}, u32[]{:S(2)}) collective-permute-start(bf16[4,512,128]{2,1,0:T(8,128)(2,1)} %get-tuple-element.54), channel_id=1, source_target_pairs={{0,4},{4,0},{8,12},{12,8},{16,20},{20,16},{24,28},{28,24},{1,5},{5... | collective-permute-start | bytes 1572872 | tf_op jit(solution)/shard_map/ppermute | solution.py:984
  22.9 5.6 %collective-permute-start.4 = (bf16[4,128,512]{2,1,0:T(8,128)(2,1)S(1)}, bf16[4,128,512]{2,1,0:T(8,128)(2,1)S(1)}, u32[]{:S(2)}, u32[]{:S(2)}) collective-permute-start(bf16[4,128,512]{2,1,0:T(8,128)(2,1)S(1)} %other_core.1), channel_id=1, source_target_pairs={{0,4},{4,0},{8,12},{12,8},{16,20},{20,16},{24,28},{28,24},{1,5},{5... | collective-permute-start | bytes 1572872 | tf_op jit(solution)/shard_map/ppermute | solution.py:984
  24.9 19.8 %collective-permute-start.10 = (bf16[2,512,128]{2,1,0:T(8,128)(2,1)}, bf16[2,512,128]{2,1,0:T(8,128)(2,1)S(1)}, u32[]{:S(2)}, u32[]{:S(2)}) collective-permute-start(bf16[2,512,128]{2,1,0:T(8,128)(2,1)} %get-tuple-element.58), channel_id=1, source_target_pairs={{0,24},{4,28},{8,16},{12,20},{16,8},{20,12},{24,0},{28,4},{1,25},{... | collective-permute-start | bytes 786440 | tf_op jit(solution)/shard_map/ppermute | solution.py:986
  26.4 18.3 %collective-permute-start.8 = (bf16[2,512,128]{2,1,0:T(8,128)(2,1)}, bf16[2,512,128]{2,1,0:T(8,128)(2,1)S(1)}, u32[]{:S(2)}, u32[]{:S(2)}) collective-permute-start(bf16[2,512,128]{2,1,0:T(8,128)(2,1)} %get-tuple-element.56), channel_id=1, source_target_pairs={{0,8},{4,12},{8,0},{12,4},{16,24},{20,28},{24,16},{28,20},{1,9},{5... | collective-permute-start | bytes 786440 | tf_op jit(solution)/shard_map/ppermute | solution.py:986
  27.0 17.8 %collective-permute-start.9 = (bf16[2,512,128]{2,1,0:T(8,128)(2,1)S(1)}, bf16[2,512,128]{2,1,0:T(8,128)(2,1)}, u32[]{:S(2)}, u32[]{:S(2)}) collective-permute-start(bf16[2,512,128]{2,1,0:T(8,128)(2,1)S(1)} %get-tuple-element.57), channel_id=1, source_target_pairs={{0,16},{4,20},{8,24},{12,28},{16,0},{20,4},{24,8},{28,12},{1,17},{... | collective-permute-start | bytes 786440 | tf_op jit(solution)/shard_map/ppermute | solution.py:986
  30.2 33.7 %collective-permute-start.6 = (bf16[128,1024]{1,0:T(8,128)(2,1)}, bf16[128,1024]{1,0:T(8,128)(2,1)}, u32[]{:S(2)}, u32[]{:S(2)}) collective-permute-start(bf16[128,1024]{1,0:T(8,128)(2,1)} %dynamic_slice.18), channel_id=1, source_target_pairs={{0,2},{1,3},{2,0},{3,1},{4,6},{5,7},{6,4},{7,5},{8,10},{9,11},{10,... | collective-permute-start | bytes 786440 | tf_op jit(solution)/shard_map/ppermute | solution.py:723
  34.2 10.6 %copy-start.7 = (bf16[512,128]{1,0:T(8,128)(2,1)S(1)}, bf16[512,128]{1,0:T(8,128)(2,1)}, u32[]{:S(2)}) copy-start(bf16[512,128]{1,0:T(8,128)(2,1)} %get-tuple-element.53.stay) | copy-start | bytes 393220
  34.2 29.8 %collective-permute-start.5 = (bf16[256,1024]{1,0:T(8,128)(2,1)S(1)}, bf16[256,1024]{1,0:T(8,128)(2,1)S(1)}, u32[]{:S(2)}, u32[]{:S(2)}) collective-permute-start(bf16[256,1024]{1,0:T(8,128)(2,1)S(1)} %dynamic_slice.17), channel_id=1, source_target_pairs={{0,1},{1,2},{2,3},{3,0},{4,7},{5,4},{6,5},{7,6},{8,9},{9,10},{10,1... | collective-permute-start | bytes 1572872 | tf_op jit(solution)/shard_map/ppermute | solution.py:723
  36.8 8.0 %copy-start.9 = (bf16[256,768]{1,0:T(8,128)(2,1)S(1)}, bf16[256,768]{1,0:T(8,128)(2,1)}, u32[]{:S(2)}) copy-start(bf16[256,768]{1,0:T(8,128)(2,1)} %constant.83.clone.refs_6_) | copy-start | bytes 1179652
  64.1 5.1 %collective-permute-start.11 = (bf16[512,128]{1,0:T(8,128)(2,1)S(1)}, bf16[512,128]{1,0:T(8,128)(2,1)S(1)}, u32[]{:S(2)}, u32[]{:S(2)}) collective-permute-start(bf16[512,128]{1,0:T(8,128)(2,1)S(1)} %get-tuple-element.60), channel_id=1, source_target_pairs={{0,4},{4,0},{8,12},{12,8},{16,20},{20,16},{24,28},{28,24},{1,5},{5... | collective-permute-start | bytes 393224 | tf_op jit(solution)/shard_map/ppermute | solution.py:566
  64.2 6.5 %collective-permute-start.12 = (bf16[512,128]{1,0:T(8,128)(2,1)S(1)}, bf16[512,128]{1,0:T(8,128)(2,1)S(1)}, u32[]{:S(2)}, u32[]{:S(2)}) collective-permute-start(bf16[512,128]{1,0:T(8,128)(2,1)S(1)} %get-tuple-element.61), channel_id=1, source_target_pairs={{0,8},{4,12},{8,0},{12,4},{16,24},{20,28},{24,16},{28,20},{1,9},{5... | collective-permute-start | bytes 393224 | tf_op jit(solution)/shard_map/ppermute | solution.py:566
  66.2 8.8 %collective-permute-start.13 = (bf16[512,128]{1,0:T(8,128)(2,1)S(1)}, bf16[512,128]{1,0:T(8,128)(2,1)S(1)}, u32[]{:S(2)}, u32[]{:S(2)}) collective-permute-start(bf16[512,128]{1,0:T(8,128)(2,1)S(1)} %get-tuple-element.62), channel_id=1, source_target_pairs={{0,12},{4,8},{8,4},{12,0},{16,28},{20,24},{24,20},{28,16},{1,13},{... | collective-permute-start | bytes 393224 | tf_op jit(solution)/shard_map/ppermute | solution.py:566
  67.5 11.9 %collective-permute-start.14 = (bf16[512,128]{1,0:T(8,128)(2,1)S(1)}, bf16[512,128]{1,0:T(8,128)(2,1)S(1)}, u32[]{:S(2)}, u32[]{:S(2)}) collective-permute-start(bf16[512,128]{1,0:T(8,128)(2,1)S(1)} %get-tuple-element.63), channel_id=1, source_target_pairs={{0,16},{4,20},{8,24},{12,28},{16,0},{20,4},{24,8},{28,12},{1,17},{... | collective-permute-start | bytes 393224 | tf_op jit(solution)/shard_map/ppermute | solution.py:566
  68.1 13.0 %collective-permute-start.15 = (bf16[512,128]{1,0:T(8,128)(2,1)S(1)}, bf16[512,128]{1,0:T(8,128)(2,1)S(1)}, u32[]{:S(2)}, u32[]{:S(2)}) collective-permute-start(bf16[512,128]{1,0:T(8,128)(2,1)S(1)} %get-tuple-element.64), channel_id=1, source_target_pairs={{0,20},{4,16},{8,28},{12,24},{16,4},{20,0},{24,12},{28,8},{1,21},{... | collective-permute-start | bytes 393224 | tf_op jit(solution)/shard_map/ppermute | solution.py:566
  69.2 11.9 %collective-permute-start.16 = (bf16[512,128]{1,0:T(8,128)(2,1)S(1)}, bf16[512,128]{1,0:T(8,128)(2,1)S(1)}, u32[]{:S(2)}, u32[]{:S(2)}) collective-permute-start(bf16[512,128]{1,0:T(8,128)(2,1)S(1)} %get-tuple-element.65), channel_id=1, source_target_pairs={{0,24},{4,28},{8,16},{12,20},{16,8},{20,12},{24,0},{28,4},{1,25},{... | collective-permute-start | bytes 393224 | tf_op jit(solution)/shard_map/ppermute | solution.py:566
  70.7 3.2 %copy-start.6 = (bf16[6,1024]{1,0:T(8,128)(2,1)S(1)}, bf16[6,1024]{1,0:T(8,128)(2,1)}, u32[]{:S(2)}) copy-start(bf16[6,1024]{1,0:T(8,128)(2,1)} %copy-done.5) | copy-start | bytes 36868
  70.7 10.4 %collective-permute-start.17 = (bf16[512,128]{1,0:T(8,128)(2,1)S(1)}, bf16[512,128]{1,0:T(8,128)(2,1)S(1)}, u32[]{:S(2)}, u32[]{:S(2)}) collective-permute-start(bf16[512,128]{1,0:T(8,128)(2,1)S(1)} %get-tuple-element.66), channel_id=1, source_target_pairs={{0,28},{4,24},{8,20},{12,16},{16,12},{20,8},{24,4},{28,0},{1,29},{... | collective-permute-start | bytes 393224 | tf_op jit(solution)/shard_map/ppermute | solution.py:566
  72.0 16.7 %slice-start = ((s8[8388608]{0:T(1024)(128)(4,1)}), s8[4194304]{0:T(1024)(128)(4,1)S(1)}, s32[]{:S(2)}) async-start(s8[8388608]{0:T(1024)(128)(4,1)} %bitcast.24), calls=%async_computation | async-start | bytes 8388608
  81.1 7.6 %slice-start.1 = ((s8[8388608]{0:T(1024)(128)(4,1)}), s8[4194304]{0:T(1024)(128)(4,1)S(1)}, s32[]{:S(2)}) async-start(s8[8388608]{0:T(1024)(128)(4,1)} %bitcast.24), calls=%async_computation.1 | async-start | bytes 8388608
  82.7 5.4 %copy-start.12 = (bf16[256,1024]{1,0:T(8,128)(2,1)S(1)}, bf16[256,1024]{1,0:T(8,128)(2,1)}, u32[]{:S(2)}) copy-start(bf16[256,1024]{1,0:T(8,128)(2,1)} %copy-done.11) | copy-start | bytes 1572868
  82.7 2.7 %collective-permute-start.19 = (bf16[2,256,1024]{2,1,0:T(8,128)(2,1)S(1)}, bf16[2,256,1024]{2,1,0:T(8,128)(2,1)S(1)}, u32[]{:S(2)}, u32[]{:S(2)}) collective-permute-start(bf16[2,256,1024]{2,1,0:T(8,128)(2,1)S(1)} %get-tuple-element.67.mine.head), channel_id=1, source_target_pairs={{0,4},{4,0},{8,12},{12,8},{16,20},{20,16},{24,28},{28,24},{1,5},{5... | collective-permute-start | bytes 3145736 | tf_op jit(solution)/shard_map/ppermute | solution.py:940
  82.8 9.8 %collective-permute-start.18 = (bf16[256,1024]{1,0:T(8,128)(2,1)S(1)}, bf16[256,1024]{1,0:T(8,128)(2,1)S(1)}, u32[]{:S(2)}, u32[]{:S(2)}) collective-permute-start(bf16[256,1024]{1,0:T(8,128)(2,1)S(1)} %get-tuple-element.68), channel_id=1, source_target_pairs={{0,1},{1,2},{2,3},{5,4},{6,5},{7,6},{8,9},{9,10},{10,11},{13,12},{... | collective-permute-start | bytes 1572872 | tf_op jit(solution)/shard_map/ppermute | solution.py:939
  86.7 11.4 %collective-permute-start.21 = (bf16[256,1024]{1,0:T(8,128)(2,1)S(1)}, bf16[256,1024]{1,0:T(8,128)(2,1)S(1)}, u32[]{:S(2)}, u32[]{:S(2)}) collective-permute-start(bf16[256,1024]{1,0:T(8,128)(2,1)S(1)} %partner_sent.1), channel_id=1, source_target_pairs={{0,1},{1,2},{2,3},{5,4},{6,5},{7,6},{8,9},{9,10},{10,11},{13,12},{... | collective-permute-start | bytes 1572872 | tf_op jit(solution)/shard_map/ppermute | solution.py:939
  88.1 16.2 %collective-permute-start.23 = (bf16[256,1024]{1,0:T(8,128)(2,1)S(1)}, bf16[256,1024]{1,0:T(8,128)(2,1)S(1)}, u32[]{:S(2)}, u32[]{:S(2)}) collective-permute-start(bf16[256,1024]{1,0:T(8,128)(2,1)S(1)} %copy-done.12), channel_id=1, source_target_pairs={{0,8},{4,20},{8,0},{12,28},{16,24},{20,4},{24,16},{28,12},{1,9},{5... | collective-permute-start | bytes 1572872 | tf_op jit(solution)/shard_map/ppermute | solution.py:731
  93.2 11.6 %collective-permute-start.20 = (bf16[256,1024]{1,0:T(8,128)(2,1)S(1)}, bf16[256,1024]{1,0:T(8,128)(2,1)S(1)}, u32[]{:S(2)}, u32[]{:S(2)}) collective-permute-start(bf16[256,1024]{1,0:T(8,128)(2,1)S(1)} %next_step.6), channel_id=1, source_target_pairs={{0,1},{1,2},{2,3},{5,4},{6,5},{7,6},{8,9},{9,10},{10,11},{13,12},{... | collective-permute-start | bytes 1572872 | tf_op jit(solution)/shard_map/ppermute | solution.py:939
  98.7 17.1 %collective-permute-start.22 = (bf16[256,1024]{1,0:T(8,128)(2,1)S(1)}, bf16[256,1024]{1,0:T(8,128)(2,1)S(1)}, u32[]{:S(2)}, u32[]{:S(2)}) collective-permute-start(bf16[256,1024]{1,0:T(8,128)(2,1)S(1)} %next_step.7), channel_id=1, source_target_pairs={{0,1},{1,2},{2,3},{5,4},{6,5},{7,6},{8,9},{9,10},{10,11},{13,12},{... | collective-permute-start | bytes 1572872 | tf_op jit(solution)/shard_map/ppermute | solution.py:939
  102.1 9.5 %collective-permute-start.26 = (bf16[128,1024]{1,0:T(8,128)(2,1)}, bf16[128,1024]{1,0:T(8,128)(2,1)S(1)}, u32[]{:S(2)}, u32[]{:S(2)}) collective-permute-start(bf16[128,1024]{1,0:T(8,128)(2,1)} %collective-permute-done.6), channel_id=1, source_target_pairs={{0,8},{4,20},{8,0},{12,28},{16,24},{20,4},{24,16},{28,12},{1,9},{5... | collective-permute-start | bytes 786440 | tf_op jit(solution)/shard_map/ppermute | solution.py:731
  102.8 14.6 %collective-permute-start.24 = (bf16[256,1024]{1,0:T(8,128)(2,1)S(1)}, bf16[256,1024]{1,0:T(8,128)(2,1)S(1)}, u32[]{:S(2)}, u32[]{:S(2)}) collective-permute-start(bf16[256,1024]{1,0:T(8,128)(2,1)S(1)} %copy-done.12), channel_id=1, source_target_pairs={{0,16},{4,12},{8,24},{12,4},{16,0},{20,28},{24,8},{28,20},{1,17},{... | collective-permute-start | bytes 1572872 | tf_op jit(solution)/shard_map/ppermute | solution.py:732
  104.3 13.5 %collective-permute-start.25 = (bf16[256,1024]{1,0:T(8,128)(2,1)S(1)}, bf16[256,1024]{1,0:T(8,128)(2,1)S(1)}, u32[]{:S(2)}, u32[]{:S(2)}) collective-permute-start(bf16[256,1024]{1,0:T(8,128)(2,1)S(1)} %collective-permute-done.23), channel_id=1, source_target_pairs={{0,16},{4,12},{8,24},{12,4},{16,0},{20,28},{24,8},{28,20},{1,17},{... | collective-permute-start | bytes 1572872 | tf_op jit(solution)/shard_map/ppermute | solution.py:732
  104.8 17.4 %collective-permute-start.27 = (bf16[128,1024]{1,0:T(8,128)(2,1)}, bf16[128,1024]{1,0:T(8,128)(2,1)S(1)}, u32[]{:S(2)}, u32[]{:S(2)}) collective-permute-start(bf16[128,1024]{1,0:T(8,128)(2,1)} %collective-permute-done.6), channel_id=1, source_target_pairs={{0,16},{4,12},{8,24},{12,4},{16,0},{20,28},{24,8},{28,20},{1,17},{... | collective-permute-start | bytes 786440 | tf_op jit(solution)/shard_map/ppermute | solution.py:732
  111.7 12.0 %collective-permute-start.31 = (bf16[256,1024]{1,0:T(8,128)(2,1)S(1)}, bf16[256,1024]{1,0:T(8,128)(2,1)S(1)}, u32[]{:S(2)}, u32[]{:S(2)}) collective-permute-start(bf16[256,1024]{1,0:T(8,128)(2,1)S(1)} %next_step.8), channel_id=1, source_target_pairs={{0,1},{1,2},{2,3},{5,4},{6,5},{7,6},{8,9},{9,10},{10,11},{13,12},{... | collective-permute-start | bytes 1572872 | tf_op jit(solution)/shard_map/ppermute | solution.py:939
  115.8 7.6 %collective-permute-start.28 = (bf16[128,1024]{1,0:T(8,128)(2,1)S(1)}, bf16[128,1024]{1,0:T(8,128)(2,1)S(1)}, u32[]{:S(2)}, u32[]{:S(2)}) collective-permute-start(bf16[128,1024]{1,0:T(8,128)(2,1)S(1)} %collective-permute-done.26), channel_id=1, source_target_pairs={{0,16},{4,12},{8,24},{12,4},{16,0},{20,28},{24,8},{28,20},{1,17},{... | collective-permute-start | bytes 786440 | tf_op jit(solution)/shard_map/ppermute | solution.py:732
  117.4 16.5 %collective-permute-start.29 = (bf16[2,128,1024]{2,1,0:T(8,128)(2,1)S(1)}, bf16[2,128,1024]{2,1,0:T(8,128)(2,1)S(1)}, u32[]{:S(2)}, u32[]{:S(2)}) collective-permute-start(bf16[2,128,1024]{2,1,0:T(8,128)(2,1)S(1)} %pad_maximum_fusion.2.refs_2_.refs_0_), channel_id=1, source_target_pairs={{0,4},{4,0},{8,12},{12,8},{16,20},{20,16},{24,28},{28,24},{1,5},{5... | collective-permute-start | bytes 1572872 | tf_op jit(solution)/shard_map/ppermute | solution.py:940
  117.8 10.9 %collective-permute-start.35 = (bf16[256,1024]{1,0:T(8,128)(2,1)S(1)}, bf16[256,1024]{1,0:T(8,128)(2,1)S(1)}, u32[]{:S(2)}, u32[]{:S(2)}) collective-permute-start(bf16[256,1024]{1,0:T(8,128)(2,1)S(1)} %next_step.10), channel_id=1, source_target_pairs={{0,1},{1,2},{2,3},{5,4},{6,5},{7,6},{8,9},{9,10},{10,11},{13,12},{... | collective-permute-start | bytes 1572872 | tf_op jit(solution)/shard_map/ppermute | solution.py:939
  122.2 17.6 %collective-permute-start.33 = (bf16[2,256,1024]{2,1,0:T(8,128)(2,1)S(1)}, bf16[2,256,1024]{2,1,0:T(8,128)(2,1)S(1)}, u32[]{:S(2)}, u32[]{:S(2)}) collective-permute-start(bf16[2,256,1024]{2,1,0:T(8,128)(2,1)S(1)} %pad_maximum_fusion.refs_0_), channel_id=1, source_target_pairs={{0,4},{4,0},{8,12},{12,8},{16,20},{20,16},{24,28},{28,24},{1,5},{5... | collective-permute-start | bytes 3145736 | tf_op jit(solution)/shard_map/ppermute | solution.py:940
  123.5 22.0 %collective-permute-start.34 = (bf16[2,256,1024]{2,1,0:T(8,128)(2,1)S(1)}, bf16[2,256,1024]{2,1,0:T(8,128)(2,1)S(1)}, u32[]{:S(2)}, u32[]{:S(2)}) collective-permute-start(bf16[2,256,1024]{2,1,0:T(8,128)(2,1)S(1)} %pad_maximum_fusion.1.refs_1_), channel_id=1, source_target_pairs={{0,4},{4,0},{8,12},{12,8},{16,20},{20,16},{24,28},{28,24},{1,5},{5... | collective-permute-start | bytes 3145736 | tf_op jit(solution)/shard_map/ppermute | solution.py:940
  123.6 13.3 %collective-permute-start.30 = (bf16[2,128,1024]{2,1,0:T(8,128)(2,1)S(1)}, bf16[2,128,1024]{2,1,0:T(8,128)(2,1)S(1)}, u32[]{:S(2)}, u32[]{:S(2)}) collective-permute-start(bf16[2,128,1024]{2,1,0:T(8,128)(2,1)S(1)} %pad_maximum_fusion.3.refs_3_.refs_1_), channel_id=1, source_target_pairs={{0,4},{4,0},{8,12},{12,8},{16,20},{20,16},{24,28},{28,24},{1,5},{5... | collective-permute-start | bytes 1572872 | tf_op jit(solution)/shard_map/ppermute | solution.py:940
  128.8 11.1 %collective-permute-start.32 = (bf16[256,1024]{1,0:T(8,128)(2,1)S(1)}, bf16[256,1024]{1,0:T(8,128)(2,1)S(1)}, u32[]{:S(2)}, u32[]{:S(2)}) collective-permute-start(bf16[256,1024]{1,0:T(8,128)(2,1)S(1)} %next_step.9), channel_id=1, source_target_pairs={{0,1},{1,2},{2,3},{5,4},{6,5},{7,6},{8,9},{9,10},{10,11},{13,12},{... | collective-permute-start | bytes 1572872 | tf_op jit(solution)/shard_map/ppermute | solution.py:939
  133.9 11.6 %collective-permute-start.36 = (bf16[256,1024]{1,0:T(8,128)(2,1)S(1)}, bf16[256,1024]{1,0:T(8,128)(2,1)S(1)}, u32[]{:S(2)}, u32[]{:S(2)}) collective-permute-start(bf16[256,1024]{1,0:T(8,128)(2,1)S(1)} %next_step.11), channel_id=1, source_target_pairs={{0,1},{1,2},{2,3},{5,4},{6,5},{7,6},{8,9},{9,10},{10,11},{13,12},{... | collective-permute-start | bytes 1572872 | tf_op jit(solution)/shard_map/ppermute | solution.py:939
  146.3 2.7 %collective-permute-start.37 = (bf16[2,256,1024]{2,1,0:T(8,128)(2,1)S(1)}, bf16[2,256,1024]{2,1,0:T(8,128)(2,1)S(1)}, u32[]{:S(2)}, u32[]{:S(2)}) collective-permute-start(bf16[2,256,1024]{2,1,0:T(8,128)(2,1)S(1)} %partner_sum.1), channel_id=1, source_target_pairs={{0,4},{4,0},{8,12},{12,8},{16,20},{20,16},{24,28},{28,24},{1,5},{5... | collective-permute-start | bytes 3145736 | tf_op jit(solution)/shard_map/ppermute | solution.py:940
  (5 other events, 9.2 us)

commit v4 on v3

--- a/solution.py
+++ b/solution.py
@@ -208,6 +208,13 @@
     )
 
 
+def over_pairs(count, pair):
+    whole = count // 4 * 4
+    lax.fori_loop(0, whole, pair, 0, unroll=4)
+    for p in range(whole, count):
+        pair(p, 0)
+
+
 def first_stage(series, spectra, twiddle):
     half = series.shape[0] // SUB
     lanes = series.shape[1]
@@ -236,16 +243,24 @@
         spectra[k] = jnp.zeros(spectra.shape[1:], F32)
 
 
-def last_stage(spectra, series):
+def last_stage(spectra, series, twiddle):
     half = series.shape[0] // SUB
+    lanes = series.shape[1]
 
     def slab(step, carry):
         row = pl.multiple_of(step * 8, 8)
+        factors = twiddle[pl.ds(row, 8), :]
         bins = []
         for k in range(half + 1):
             real = spectra[k, pl.ds(row, 8), :]
-            imag = None if k in (0, half) else spectra[k, pl.ds(SUB + row, 8), :]
-            bins.append((real, imag))
+            if k == 0:
+                bins.append((real, None))
+                continue
+            imag = spectra[k, pl.ds(SUB + row, 8), :]
+            cos = jnp.broadcast_to(factors[:, k : k + 1], (8, lanes))
+            sin = jnp.broadcast_to(factors[:, half + 1 + k : half + 2 + k], (8, lanes))
+            turned = real * cos + imag * sin
+            bins.append((turned, None if k == half else imag * cos - real * sin))
         for n, value in enumerate(real_inverse(bins)):
             series[pl.ds(SUB * n + row, 8), :] = value
         return carry
@@ -268,7 +283,7 @@
         spectra_out[p] = split_dot(forward, data)
         return carry
 
-    lax.fori_loop(0, spectra_out.shape[0], pair, 0)
+    over_pairs(spectra_out.shape[0], pair)
 
 
 def conv_kernel(blocks, me_ref, stay, swapped, *refs):
@@ -276,7 +291,6 @@
     taps_spectra, twiddle, forward, inverse, skip = refs[blocks // 2 - 1 : blocks // 2 + 4]
     out, series, spectra = refs[blocks // 2 + 4 :]
     span, lanes = stay.shape
-    half = series.shape[0] // SUB
     pieces = [stay, swapped.at[0]] + [ref.at[core] for ref in others for core in range(2)]
     for m in range(blocks):
         start = pl.multiple_of((me_ref[0] ^ m) * span, span)
@@ -300,15 +314,8 @@
         spectra[2 * p + 1] = back[:, lanes:]
         return carry
 
-    lax.fori_loop(0, taps_spectra.shape[0], pair, 0)
-    for k in range(1, half + 1):
-        real, imag = spectra[k, :SUB, :], spectra[k, SUB:, :]
-        cos = jnp.broadcast_to(twiddle[:, k : k + 1], (SUB, lanes))
-        sin = jnp.broadcast_to(twiddle[:, half + 1 + k : half + 2 + k], (SUB, lanes))
-        spectra[k, :SUB, :] = real * cos + imag * sin
-        if k < half:
-            spectra[k, SUB:, :] = imag * cos - real * sin
-    last_stage(spectra, out)
+    over_pairs(taps_spectra.shape[0], pair)
+    last_stage(spectra, out, twiddle)
     for m in range(blocks):
         window = pl.ds(m * span, span)
         out[window, :] += skip[...] * series[window, :]
@@ -708,13 +715,10 @@
     stage, place = lax.axis_index("tp"), lax.axis_index("ctx")
     chans = out_weight.shape[0]
     hops = jnp.where(place % 2 == 0, 1, stages - 1)
+    corners = jnp.stack([place // 2, (stage + hops) % stages, place, (stage + 2) % stages])
+    parts = weight_corners(after(corners.astype(jnp.int32), ready), out_weight, blocks)
     found = []
-    for rows, row, hop, static in (
-        (2 * chans // blocks, place // 2, hops, (1, stages - 1)),
-        (chans // blocks, place, 2 + 0 * place, (2, 2)),
-    ):
-        start = after((row * rows, (stage + hop) % stages * chans), ready)
-        part = lax.dynamic_slice(out_weight, start, (rows, chans))
+    for part, static in zip(parts, ((1, stages - 1), (2, 2))):
         route = [
             (c * stages + k, c * stages + (k + static[c % 2]) % stages)
             for c in range(blocks)
@@ -722,6 +726,34 @@
         ]
         found.append(lax.ppermute(part, ("ctx", "tp"), route))
     return found
+
+
+def corners_kernel(corners, weight, *refs):
+    outs, sems = refs[:-1], refs[-1]
+    copies = []
+    for n, out in enumerate(outs):
+        rows, chans = out.shape
+        row = pl.multiple_of(corners[2 * n] * rows, rows)
+        column = pl.multiple_of(corners[2 * n + 1] * chans, chans)
+        source = weight.at[pl.ds(row, rows), pl.ds(column, chans)]
+        copies.append(pltpu.make_async_copy(source, out, sems.at[n]))
+        copies[-1].start()
+    for copy in copies:
+        copy.wait()
+
+
+def weight_corners(corners, out_weight, blocks):
+    chans = out_weight.shape[0]
+    shapes = [(2 * chans // blocks, chans), (chans // blocks, chans)]
+    return pl.pallas_call(
+        corners_kernel,
+        in_specs=[SMEM, HBM],
+        out_specs=[VMEM] * 2,
+        out_shape=[jax.ShapeDtypeStruct(shape, BF16) for shape in shapes],
+        scratch_shapes=[pltpu.SemaphoreType.DMA((2,))],
+        compiler_params=grant(56),
+        name="weight_corners",
+    )(corners, out_weight)
 
 
 def gather_weight(part):

time: 151 us -> 145 us (0.960)
  Pallas kernels: 50.8 us -> 45.1 us
  starting transfers between devices: 56.6 us -> 61.4 us
  local copies, waits for them, and re-layouts: 7.96 us -> 3.7 us
    pallas_call x1, Pallas kernels: 19.1 us -> 13.5 us  [long_conv(): pl.pallas_call(partial(conv_kernel, blocks), out_shape=jax.ShapeDtypeStru...]
    dynamic_slice x2 -> x0, local copies, waits for them, and re-layouts: 3.18 us -> none  [spread_weight(): part = lax.dynamic_slice(out_weight, start, (rows, chans))]
    pallas_call x0 -> x1, Pallas kernels: none -> 2.67 us  [weight_corners(): pl.pallas_call(corners_kernel, in_specs=[SMEM, HBM], out_specs=[VMEM] * 2...]
    ppermute x8, starting transfers between devices: 26.3 us -> 28.8 us  [project(): onward = lambda x: lax.ppermute(x, ('ctx', 'tp'), route)]
    ppermute x8, waiting for transfers between devices: 10.1 us -> 7.69 us  [project(): onward = lambda x: lax.ppermute(x, ('ctx', 'tp'), route)]
    pallas_call x1, Pallas kernels: 7.93 us -> 5.94 us  [taps_spectra_of(): pl.pallas_call(partial(taps_kernel, chips), out_shape=jax.ShapeDtypeStruc...]
    ppermute x4, waiting for transfers between devices: 1.53 us -> 3.38 us  [gather_weight(): lax.ppermute(x, 'ctx', other)]
    ppermute x7, starting transfers between devices: 6.45 us -> 8.04 us  [exchange(): lax.ppermute(piece, axis, [(i, i ^ m) for i in devices])]
  transfers between devices with their start and end apart: 38 -> 38, of which waited for: 13 -> 12; matrix products, arithmetic and copies ran while one was open for 5% -> 3% of each run, Pallas kernels for 30% -> 28%
where the time goes in v4:
time: 145 us; the launch traced here: 143 us
  starting transfers between devices  61.4 us (42%)
  Pallas kernels  45.1 us (31%)
  waiting for transfers between devices  30 us (21%)
  local copies, waits for them, and re-layouts  3.7 us (3%)
  other arithmetic  1.66 us (1%)
    ppermute x8, starting transfers between devices, project(): onward = lambda x: lax.ppermute(x, ('ctx', 'tp'), route)  28.8 us
    pallas_call x1, Pallas kernels, long_conv(): pl.pallas_call(partial(conv_kernel, blocks), out_shape=jax.ShapeDtypeStru...  13.5 us
    ppermute x6, starting transfers between devices, fast_per_device(): lax.ppermute(x, 'ctx', [(i, i ^ 2 * q + 2) for i in devices])  10.8 us
    ppermute x7, starting transfers between devices, exchange(): lax.ppermute(piece, axis, [(i, i ^ m) for i in devices])  8.04 us
    ppermute x8, waiting for transfers between devices, project(): onward = lambda x: lax.ppermute(x, ('ctx', 'tp'), route)  7.69 us
    ppermute x7, waiting for transfers between devices, exchange(): lax.ppermute(piece, axis, [(i, i ^ m) for i in devices])  6.78 us
    ppermute x6, waiting for transfers between devices, fast_per_device(): lax.ppermute(x, 'ctx', [(i, i ^ 2 * q + 2) for i in devices])  6.18 us
    pallas_call x1, Pallas kernels, taps_spectra_of(): pl.pallas_call(partial(taps_kernel, chips), out_shape=jax.ShapeDtypeStruc...  5.94 us
  transfers between devices with their start and end apart: 38, of which 12 were waited for; matrix products, arithmetic and copies ran while one was open for 3% of the time, Pallas kernels for 28%

profile of v4, /device:TPU:0, one launch (start us, length us, event | category | flops | bytes accessed | tf_op | source)
XLA Modules:
  0.0 143.0 jit_solution(18017463534993102660)
XLA Ops:
  0.0 1.5 %rims.1 = bf16[6,1024]{1,0:T(8,128)(2,1)} custom-call(bf16[512,1024]{1,0:T(8,128)(2,1)} %query.3, bf16[512,1024]{1,0:T(8,128)(2,1)} %key.3, bf16[512,1024]{1,0:T(8,128)(2,1)} %value.3), custom_call_target="tpu_custom_call" | custom-call | tf_op jit(solution)/shard_map/rims/pallas_call | solution.py:420
  1.5 2.4 %collective-permute-start = (bf16[6,1024]{1,0:T(8,128)(2,1)}, bf16[6,1024]{1,0:T(8,128)(2,1)S(1)}, u32[]{:S(2)}, u32[]{:S(2)}) collective-permute-start(bf16[6,1024]{1,0:T(8,128)(2,1)} %rims.1), channel_id=1, source_target_pairs={{0,4},{4,8},{8,12},{12,16},{16,20},{20,24},{24,28},{1,5},{5,9},{9,... | collective-permute-start | bytes 36872 | tf_op jit(solution)/shard_map/ppermute | solution.py:18
  5.1 4.9 %collective-permute-start.1 = (bf16[256,512]{1,0:T(8,128)(2,1)S(1)}, bf16[256,512]{1,0:T(8,128)(2,1)S(1)}, u32[]{:S(2)}, u32[]{:S(2)}) collective-permute-start(bf16[256,512]{1,0:T(8,128)(2,1)S(1)} %get-tuple-element.44), channel_id=1, source_target_pairs={{0,8},{4,12},{8,0},{12,4},{16,24},{20,28},{24,16},{28,20},{1,9},{5... | collective-permute-start | bytes 786440 | tf_op jit(solution)/shard_map/ppermute | solution.py:1018
  10.0 1.5 %collective-permute-start.2 = (bf16[256,512]{1,0:T(8,128)(2,1)S(1)}, bf16[256,512]{1,0:T(8,128)(2,1)S(1)}, u32[]{:S(2)}, u32[]{:S(2)}) collective-permute-start(bf16[256,512]{1,0:T(8,128)(2,1)S(1)} %get-tuple-element.45), channel_id=1, source_target_pairs={{0,16},{4,20},{8,24},{12,28},{16,0},{20,4},{24,8},{28,12},{1,17},{... | collective-permute-start | bytes 786440 | tf_op jit(solution)/shard_map/ppermute | solution.py:1018
  11.5 0.9 collective-permute-start.3
  12.4 4.2 %gate_in.1 = (bf16[512,128]{1,0:T(8,128)(2,1)}, bf16[3,512,128]{2,1,0:T(8,128)(2,1)}, bf16[4,512,128]{2,1,0:T(8,128)(2,1)}) custom-call(s32[1]{0:T(128)} %bitcast.me_ref, bf16[512,1024]{1,0:T(8,128)(2,1)} %key.3, bf16[512,1024]{1,0:T(8,128)(2,1)} %value.3, bf16[6,1024]{1,0:T(8,128)(2,1)} %copy-done.5, f32[3,3,1024]{2,1,0:T(4,128)} %weight.7), custom_call_target="tpu_custom_call" | custom-call | tf_op jit(solution)/shard_map/gate_in/pallas_call | solution.py:471
  17.1 5.7 %collective-permute-done.2.refs_2_ = bf16[256,512]{1,0:T(8,128)(2,1)S(1)} collective-permute-done((bf16[256,512]{1,0:T(8,128)(2,1)S(1)}, bf16[256,512]{1,0:T(8,128)(2,1)S(1)}, u32[]{:S(2)}, u32[]{:S(2)}) %collective-permute-start.2) | collective-permute-done | bytes 262176 | tf_op jit(solution)/shard_map/ppermute | solution.py:1018
  23.7 1.0 copy-done.3
  24.7 1.6 %collective-permute-start.10 = (bf16[2,512,128]{2,1,0:T(8,128)(2,1)S(1)}, bf16[2,512,128]{2,1,0:T(8,128)(2,1)S(1)}, u32[]{:S(2)}, u32[]{:S(2)}) collective-permute-start(bf16[2,512,128]{2,1,0:T(8,128)(2,1)S(1)} %get-tuple-element.56), channel_id=1, source_target_pairs={{0,24},{4,28},{8,16},{12,20},{16,8},{20,12},{24,0},{28,4},{1,25},{... | collective-permute-start | bytes 786440 | tf_op jit(solution)/shard_map/ppermute | solution.py:1018
  26.9 1.4 collective-permute-start.9
  28.3 2.7 %weight_corners.1 = (bf16[256,1024]{1,0:T(8,128)(2,1)}, bf16[128,1024]{1,0:T(8,128)(2,1)}) custom-call(s32[4]{0:T(128)} %pad_add_fusion.1.corners, bf16[1024,4096]{1,0:T(8,128)(2,1)} %weight.9), custom_call_target="tpu_custom_call" | custom-call | tf_op jit(solution)/shard_map/weight_corners/pallas_call | solution.py:748
  30.9 1.6 %collective-permute-start.5 = (bf16[256,1024]{1,0:T(8,128)(2,1)}, bf16[256,1024]{1,0:T(8,128)(2,1)S(1)}, u32[]{:S(2)}, u32[]{:S(2)}) collective-permute-start(bf16[256,1024]{1,0:T(8,128)(2,1)} %get-tuple-element.48), channel_id=1, source_target_pairs={{0,1},{1,2},{2,3},{3,0},{4,7},{5,4},{6,5},{7,6},{8,9},{9,10},{10,1... | collective-permute-start | bytes 1572872 | tf_op jit(solution)/shard_map/ppermute | solution.py:727
  32.6 2.6 %collective-permute-start.6 = (bf16[128,1024]{1,0:T(8,128)(2,1)}, bf16[128,1024]{1,0:T(8,128)(2,1)S(1)}, u32[]{:S(2)}, u32[]{:S(2)}) collective-permute-start(bf16[128,1024]{1,0:T(8,128)(2,1)} %get-tuple-element.49), channel_id=1, source_target_pairs={{0,2},{1,3},{2,0},{3,1},{4,6},{5,7},{6,4},{7,5},{8,10},{9,11},{10,... | collective-permute-start | bytes 786440 | tf_op jit(solution)/shard_map/ppermute | solution.py:727
  35.2 5.9 %taps_spectra.1.refs_3_ = f32[17,256,256]{2,1,0:T(8,128)S(1)} custom-call(s32[1]{0:T(128)} %bitcast.me_ref, bf16[256,512]{1,0:T(8,128)(2,1)S(1)} %get-tuple-element.43.refs_0_, bf16[256,512]{1,0:T(8,128)(2,1)S(1)} %collective-permute-done.1.refs_1_, bf16[256,512]{1,0:T(8,128)(2,1)S(1)} %collective-permute-done.2.refs_2_, ...), custom_call_target="tpu_custom_call" | custom-call | flops 8000000000 | tf_op jit(solution)/shard_map/taps_spectra/pallas_call | solution.py:351
  41.2 13.5 %long_conv.1.conv = f32[4096,128]{1,0:T(8,128)S(1)} custom-call(s32[1]{0:T(128)} %bitcast.me_ref, bf16[512,128]{1,0:T(8,128)(2,1)S(1)} %copy-done.7, bf16[4,512,128]{2,1,0:T(8,128)(2,1)S(1)} %collective-permute-done.7.swapped, bf16[2,512,128]{2,1,0:T(8,128)(2,1)S(1)} %collective-permute-done.8.refs_0_, ...), custom_call_target="tpu_custom_call" | custom-call | flops 20000000000 | tf_op jit(solution)/shard_map/long_conv/pallas_call | solution.py:370
  54.8 2.1 %collective-permute-start.11 = (bf16[512,128]{1,0:T(8,128)(2,1)S(1)}, bf16[512,128]{1,0:T(8,128)(2,1)S(1)}, u32[]{:S(2)}, u32[]{:S(2)}) collective-permute-start(bf16[512,128]{1,0:T(8,128)(2,1)S(1)} %get-tuple-element.58), channel_id=1, source_target_pairs={{0,4},{4,0},{8,12},{12,8},{16,20},{20,16},{24,28},{28,24},{1,5},{5... | collective-permute-start | bytes 393224 | tf_op jit(solution)/shard_map/ppermute | solution.py:573
  58.7 1.0 collective-permute-start.13
  60.4 1.3 collective-permute-start.15
  61.7 1.5 %collective-permute-start.16 = (bf16[512,128]{1,0:T(8,128)(2,1)S(1)}, bf16[512,128]{1,0:T(8,128)(2,1)S(1)}, u32[]{:S(2)}, u32[]{:S(2)}) collective-permute-start(bf16[512,128]{1,0:T(8,128)(2,1)S(1)} %get-tuple-element.63), channel_id=1, source_target_pairs={{0,24},{4,28},{8,16},{12,20},{16,8},{20,12},{24,0},{28,4},{1,25},{... | collective-permute-start | bytes 393224 | tf_op jit(solution)/shard_map/ppermute | solution.py:573
  63.2 0.9 collective-permute-start.17
  64.1 1.9 %constant_dynamic-slice_fusion.refs_9_.far_weight = bf16[1024,1024]{1,0:T(8,128)(2,1)S(1)} fusion(bf16[1024,4096]{1,0:T(8,128)(2,1)} %weight.9, s32[]{:T(128)S(6)} %select_n.62), kind=kLoop, calls=%fused_computation.8 | loop fusion | bytes 4194308 | tf_op jit(solution)/shard_map/dynamic_slice | solution.py:963
  66.1 1.1 mix_query.1.refs_8_
  67.1 4.5 %collective-permute-done.14.refs_4_ = bf16[512,128]{1,0:T(8,128)(2,1)S(1)} collective-permute-done((bf16[512,128]{1,0:T(8,128)(2,1)S(1)}, bf16[512,128]{1,0:T(8,128)(2,1)S(1)}, u32[]{:S(2)}, u32[]{:S(2)}) %collective-permute-start.14) | collective-permute-done | bytes 131104 | tf_op jit(solution)/shard_map/ppermute | solution.py:573
  71.6 2.3 %collective-permute-done.15.refs_5_ = bf16[512,128]{1,0:T(8,128)(2,1)S(1)} collective-permute-done((bf16[512,128]{1,0:T(8,128)(2,1)S(1)}, bf16[512,128]{1,0:T(8,128)(2,1)S(1)}, u32[]{:S(2)}, u32[]{:S(2)}) %collective-permute-start.15) | collective-permute-done | bytes 131104 | tf_op jit(solution)/shard_map/ppermute | solution.py:573
  73.9 1.6 %gate_out.1 = (bf16[2,256,1024]{2,1,0:T(8,128)(2,1)S(1)}, bf16[256,1024]{1,0:T(8,128)(2,1)S(1)}) custom-call(s32[3]{0:T(128)S(1)} %pad_add_fusion.spot, bf16[512,128]{1,0:T(8,128)(2,1)S(1)} %get-tuple-element.57.refs_0_, bf16[512,128]{1,0:T(8,128)(2,1)S(1)} %collective-permute-done.11.refs_1_, bf16[512,128]{1,0:T(8,128)(2,1)S(1)} %collective-permute-done.12.refs_2_, ...), custom_call_target="tpu_custom_call" | custom-call | tf_op jit(solution)/shard_map/gate_out/pallas_call | solution.py:620
  75.6 2.5 %collective-permute-start.18 = (bf16[256,1024]{1,0:T(8,128)(2,1)S(1)}, bf16[256,1024]{1,0:T(8,128)(2,1)S(1)}, u32[]{:S(2)}, u32[]{:S(2)}) collective-permute-start(bf16[256,1024]{1,0:T(8,128)(2,1)S(1)} %get-tuple-element.66), channel_id=1, source_target_pairs={{0,1},{1,2},{2,3},{5,4},{6,5},{7,6},{8,9},{9,10},{10,11},{13,12},{... | collective-permute-start | bytes 1572872 | tf_op jit(solution)/shard_map/ppermute | solution.py:971
  78.3 1.3 partner_sent.1
  79.5 1.5 %collective-permute-start.21 = (bf16[256,1024]{1,0:T(8,128)(2,1)S(1)}, bf16[256,1024]{1,0:T(8,128)(2,1)S(1)}, u32[]{:S(2)}, u32[]{:S(2)}) collective-permute-start(bf16[256,1024]{1,0:T(8,128)(2,1)S(1)} %partner_sent.1), channel_id=1, source_target_pairs={{0,1},{1,2},{2,3},{5,4},{6,5},{7,6},{8,9},{9,10},{10,11},{13,12},{... | collective-permute-start | bytes 1572872 | tf_op jit(solution)/shard_map/ppermute | solution.py:971
  81.6 3.9 %sent_terms.1.term = bf16[2,2,256,1024]{3,2,1,0:T(8,128)(2,1)S(1)} custom-call(s32[5]{0:T(128)S(1)} %or_select_fusion.plan, bf16[2,256,1024]{2,1,0:T(8,128)(2,1)S(1)} %get-tuple-element.65.mine.head, bf16[2,256,1024]{2,1,0:T(8,128)(2,1)S(1)} %collective-permute-done.19.partners.gated.head, bf16[1024,4096]{1,0:T(8,128)(2,1)S(1)} %bitcast.28), custom_call_target="tpu_custom_call" | custom-call | flops 4000000000 | tf_op jit(solution)/shard_map/sent_terms/pallas_call | solution.py:701
  86.1 6.1 %collective-permute-start.20 = (bf16[256,1024]{1,0:T(8,128)(2,1)S(1)}, bf16[256,1024]{1,0:T(8,128)(2,1)S(1)}, u32[]{:S(2)}, u32[]{:S(2)}) collective-permute-start(bf16[256,1024]{1,0:T(8,128)(2,1)S(1)} %next_step.6), channel_id=1, source_target_pairs={{0,1},{1,2},{2,3},{5,4},{6,5},{7,6},{8,9},{9,10},{10,11},{13,12},{... | collective-permute-start | bytes 1572872 | tf_op jit(solution)/shard_map/ppermute | solution.py:971
  92.9 2.8 %collective-permute-start.22 = (bf16[256,1024]{1,0:T(8,128)(2,1)S(1)}, bf16[256,1024]{1,0:T(8,128)(2,1)S(1)}, u32[]{:S(2)}, u32[]{:S(2)}) collective-permute-start(bf16[256,1024]{1,0:T(8,128)(2,1)S(1)} %next_step.7), channel_id=1, source_target_pairs={{0,1},{1,2},{2,3},{5,4},{6,5},{7,6},{8,9},{9,10},{10,11},{13,12},{... | collective-permute-start | bytes 1572872 | tf_op jit(solution)/shard_map/ppermute | solution.py:971
  95.7 1.2 collective-permute-start.26
  96.9 0.9 collective-permute-start.24
  97.8 1.1 collective-permute-start.25
  98.9 1.5 %collective-permute-start.27 = (bf16[128,1024]{1,0:T(8,128)(2,1)S(1)}, bf16[128,1024]{1,0:T(8,128)(2,1)S(1)}, u32[]{:S(2)}, u32[]{:S(2)}) collective-permute-start(bf16[128,1024]{1,0:T(8,128)(2,1)S(1)} %collective-permute-done.6), channel_id=1, source_target_pairs={{0,16},{4,12},{8,24},{12,4},{16,0},{20,28},{24,8},{28,20},{1,17},{... | collective-permute-start | bytes 786440 | tf_op jit(solution)/shard_map/ppermute | solution.py:764
  101.2 3.8 %collective-permute-done.26 = bf16[128,1024]{1,0:T(8,128)(2,1)S(1)} collective-permute-done((bf16[128,1024]{1,0:T(8,128)(2,1)S(1)}, bf16[128,1024]{1,0:T(8,128)(2,1)S(1)}, u32[]{:S(2)}, u32[]{:S(2)}) %collective-permute-start.26) | collective-permute-done | bytes 262176 | tf_op jit(solution)/shard_map/ppermute | solution.py:763
  105.0 3.9 %collective-permute-start.31 = (bf16[256,1024]{1,0:T(8,128)(2,1)S(1)}, bf16[256,1024]{1,0:T(8,128)(2,1)S(1)}, u32[]{:S(2)}, u32[]{:S(2)}) collective-permute-start(bf16[256,1024]{1,0:T(8,128)(2,1)S(1)} %next_step.8), channel_id=1, source_target_pairs={{0,1},{1,2},{2,3},{5,4},{6,5},{7,6},{8,9},{9,10},{10,11},{13,12},{... | collective-permute-start | bytes 1572872 | tf_op jit(solution)/shard_map/ppermute | solution.py:971
  110.5 1.2 collective-permute-done.25
  111.7 3.2 %collective-permute-start.35 = (bf16[256,1024]{1,0:T(8,128)(2,1)S(1)}, bf16[256,1024]{1,0:T(8,128)(2,1)S(1)}, u32[]{:S(2)}, u32[]{:S(2)}) collective-permute-start(bf16[256,1024]{1,0:T(8,128)(2,1)S(1)} %next_step.10), channel_id=1, source_target_pairs={{0,1},{1,2},{2,3},{5,4},{6,5},{7,6},{8,9},{9,10},{10,11},{13,12},{... | collective-permute-start | bytes 1572872 | tf_op jit(solution)/shard_map/ppermute | solution.py:971
  115.2 2.2 %collective-permute-done.28 = bf16[128,1024]{1,0:T(8,128)(2,1)S(1)} collective-permute-done((bf16[128,1024]{1,0:T(8,128)(2,1)S(1)}, bf16[128,1024]{1,0:T(8,128)(2,1)S(1)}, u32[]{:S(2)}, u32[]{:S(2)}) %collective-permute-start.28) | collective-permute-done | bytes 262176 | tf_op jit(solution)/shard_map/ppermute | solution.py:764
  118.6 3.0 %collective-permute-done.35.got.got2 = bf16[256,1024]{1,0:T(8,128)(2,1)S(1)} collective-permute-done((bf16[256,1024]{1,0:T(8,128)(2,1)S(1)}, bf16[256,1024]{1,0:T(8,128)(2,1)S(1)}, u32[]{:S(2)}, u32[]{:S(2)}) %collective-permute-start.35) | collective-permute-done | bytes 524320 | tf_op jit(solution)/shard_map/ppermute | solution.py:971
  121.6 4.4 %collective-permute-start.32 = (bf16[256,1024]{1,0:T(8,128)(2,1)S(1)}, bf16[256,1024]{1,0:T(8,128)(2,1)S(1)}, u32[]{:S(2)}, u32[]{:S(2)}) collective-permute-start(bf16[256,1024]{1,0:T(8,128)(2,1)S(1)} %next_step.9), channel_id=1, source_target_pairs={{0,1},{1,2},{2,3},{5,4},{6,5},{7,6},{8,9},{9,10},{10,11},{13,12},{... | collective-permute-start | bytes 1572872 | tf_op jit(solution)/shard_map/ppermute | solution.py:971
  126.7 4.4 %collective-permute-start.36 = (bf16[256,1024]{1,0:T(8,128)(2,1)S(1)}, bf16[256,1024]{1,0:T(8,128)(2,1)S(1)}, u32[]{:S(2)}, u32[]{:S(2)}) collective-permute-start(bf16[256,1024]{1,0:T(8,128)(2,1)S(1)} %next_step.11), channel_id=1, source_target_pairs={{0,1},{1,2},{2,3},{5,4},{6,5},{7,6},{8,9},{9,10},{10,11},{13,12},{... | collective-permute-start | bytes 1572872 | tf_op jit(solution)/shard_map/ppermute | solution.py:971
  131.1 2.4 %early_sum.1 = (f32[512,1024]{1,0:T(8,128)S(1)}, f32[256,1024]{1,0:T(8,128)S(1)}) custom-call(s32[10]{0:T(128)S(1)} %stack.99.order, bf16[2,256,1024]{2,1,0:T(8,128)(2,1)S(1)} %get-tuple-element.65.mine.head, bf16[256,1024]{1,0:T(8,128)(2,1)S(1)} %collective-permute-done.18.got.got0, bf16[256,1024]{1,0:T(8,128)(2,1)S(1)} %collective-permute-done.20.got1.got, ...), custom_call_target="tpu_custom_call" | custom-call | flops 5000000000 | tf_op jit(solution)/shard_map/early_sum/pallas_call | solution.py:831
  133.6 4.7 %collective-permute-done.36.got3 = bf16[256,1024]{1,0:T(8,128)(2,1)S(1)} collective-permute-done((bf16[256,1024]{1,0:T(8,128)(2,1)S(1)}, bf16[256,1024]{1,0:T(8,128)(2,1)S(1)}, u32[]{:S(2)}, u32[]{:S(2)}) %collective-permute-start.36) | collective-permute-done | bytes 524320 | tf_op jit(solution)/shard_map/ppermute | solution.py:971
  139.2 0.8 mine_sum.1.mine
  140.0 1.8 %collective-permute-done.37.partners = bf16[2,256,1024]{2,1,0:T(8,128)(2,1)S(1)} collective-permute-done((bf16[2,256,1024]{2,1,0:T(8,128)(2,1)S(1)}, bf16[2,256,1024]{2,1,0:T(8,128)(2,1)S(1)}, u32[]{:S(2)}, u32[]{:S(2)}) %collective-permute-start.37) | collective-permute-done | bytes 1048608 | tf_op jit(solution)/shard_map/ppermute | solution.py:972
  141.8 1.1 join_sums.1
  (89 shorter events, 12.5 us)
Async XLA Ops:
  0.0 23.0 %copy-start = (f32[1024]{0:T(1024)S(1)}, f32[1024]{0:T(1024)}, u32[]{:S(2)}) copy-start(f32[1024]{0:T(1024)} %param.15) | copy-start | bytes 12292
  0.0 4.9 %copy-start.2 = (bf16[1024,512]{1,0:T(8,128)(2,1)S(1)}, bf16[1024,512]{1,0:T(8,128)(2,1)}, u32[]{:S(2)}) copy-start(bf16[1024,512]{1,0:T(8,128)(2,1)} %taps.1) | copy-start | bytes 3145732
  1.5 3.4 %collective-permute-start = (bf16[6,1024]{1,0:T(8,128)(2,1)}, bf16[6,1024]{1,0:T(8,128)(2,1)S(1)}, u32[]{:S(2)}, u32[]{:S(2)}) collective-permute-start(bf16[6,1024]{1,0:T(8,128)(2,1)} %rims.1), channel_id=1, source_target_pairs={{0,4},{4,8},{8,12},{12,16},{16,20},{20,24},{24,28},{1,5},{5,9},{9,... | collective-permute-start | bytes 36872 | tf_op jit(solution)/shard_map/ppermute | solution.py:18
  4.9 7.4 %copy-start.5 = (bf16[6,1024]{1,0:T(8,128)(2,1)}, bf16[6,1024]{1,0:T(8,128)(2,1)S(1)}, u32[]{:S(2)}) copy-start(bf16[6,1024]{1,0:T(8,128)(2,1)S(1)} %collective-permute-done.edges) | copy-start | bytes 36868
  5.1 12.0 %collective-permute-start.1 = (bf16[256,512]{1,0:T(8,128)(2,1)S(1)}, bf16[256,512]{1,0:T(8,128)(2,1)S(1)}, u32[]{:S(2)}, u32[]{:S(2)}) collective-permute-start(bf16[256,512]{1,0:T(8,128)(2,1)S(1)} %get-tuple-element.44), channel_id=1, source_target_pairs={{0,8},{4,12},{8,0},{12,4},{16,24},{20,28},{24,16},{28,20},{1,9},{5... | collective-permute-start | bytes 786440 | tf_op jit(solution)/shard_map/ppermute | solution.py:1018
  10.0 12.9 %collective-permute-start.2 = (bf16[256,512]{1,0:T(8,128)(2,1)S(1)}, bf16[256,512]{1,0:T(8,128)(2,1)S(1)}, u32[]{:S(2)}, u32[]{:S(2)}) collective-permute-start(bf16[256,512]{1,0:T(8,128)(2,1)S(1)} %get-tuple-element.45), channel_id=1, source_target_pairs={{0,16},{4,20},{8,24},{12,28},{16,0},{20,4},{24,8},{28,12},{1,17},{... | collective-permute-start | bytes 786440 | tf_op jit(solution)/shard_map/ppermute | solution.py:1018
  11.5 11.3 %collective-permute-start.3 = (bf16[256,512]{1,0:T(8,128)(2,1)S(1)}, bf16[256,512]{1,0:T(8,128)(2,1)S(1)}, u32[]{:S(2)}, u32[]{:S(2)}) collective-permute-start(bf16[256,512]{1,0:T(8,128)(2,1)S(1)} %get-tuple-element.46), channel_id=1, source_target_pairs={{0,24},{4,28},{8,16},{12,20},{16,8},{20,12},{24,0},{28,4},{1,25},{... | collective-permute-start | bytes 786440 | tf_op jit(solution)/shard_map/ppermute | solution.py:1018
  16.6 7.1 %collective-permute-start.7 = (bf16[4,512,128]{2,1,0:T(8,128)(2,1)}, bf16[4,512,128]{2,1,0:T(8,128)(2,1)S(1)}, u32[]{:S(2)}, u32[]{:S(2)}) collective-permute-start(bf16[4,512,128]{2,1,0:T(8,128)(2,1)} %get-tuple-element.52), channel_id=1, source_target_pairs={{0,4},{4,0},{8,12},{12,8},{16,20},{20,16},{24,28},{28,24},{1,5},{5... | collective-permute-start | bytes 1572872 | tf_op jit(solution)/shard_map/ppermute | solution.py:1016
  22.9 5.4 %collective-permute-start.4 = (bf16[4,128,512]{2,1,0:T(8,128)(2,1)S(1)}, bf16[4,128,512]{2,1,0:T(8,128)(2,1)S(1)}, u32[]{:S(2)}, u32[]{:S(2)}) collective-permute-start(bf16[4,128,512]{2,1,0:T(8,128)(2,1)S(1)} %other_core.1), channel_id=1, source_target_pairs={{0,4},{4,0},{8,12},{12,8},{16,20},{20,16},{24,28},{28,24},{1,5},{5... | collective-permute-start | bytes 1572872 | tf_op jit(solution)/shard_map/ppermute | solution.py:1016
  24.7 16.4 %collective-permute-start.10 = (bf16[2,512,128]{2,1,0:T(8,128)(2,1)S(1)}, bf16[2,512,128]{2,1,0:T(8,128)(2,1)S(1)}, u32[]{:S(2)}, u32[]{:S(2)}) collective-permute-start(bf16[2,512,128]{2,1,0:T(8,128)(2,1)S(1)} %get-tuple-element.56), channel_id=1, source_target_pairs={{0,24},{4,28},{8,16},{12,20},{16,8},{20,12},{24,0},{28,4},{1,25},{... | collective-permute-start | bytes 786440 | tf_op jit(solution)/shard_map/ppermute | solution.py:1018
  26.3 14.8 %collective-permute-start.8 = (bf16[2,512,128]{2,1,0:T(8,128)(2,1)S(1)}, bf16[2,512,128]{2,1,0:T(8,128)(2,1)S(1)}, u32[]{:S(2)}, u32[]{:S(2)}) collective-permute-start(bf16[2,512,128]{2,1,0:T(8,128)(2,1)S(1)} %get-tuple-element.54), channel_id=1, source_target_pairs={{0,8},{4,12},{8,0},{12,4},{16,24},{20,28},{24,16},{28,20},{1,9},{5... | collective-permute-start | bytes 786440 | tf_op jit(solution)/shard_map/ppermute | solution.py:1018
  26.9 8.3 %copy-start.8 = (bf16[256,768]{1,0:T(8,128)(2,1)S(1)}, bf16[256,768]{1,0:T(8,128)(2,1)}, u32[]{:S(2)}) copy-start(bf16[256,768]{1,0:T(8,128)(2,1)} %constant.80.clone.refs_6_.refs_5_) | copy-start | bytes 1179652
  26.9 8.3 %copy-start.10 = (f32[128,66]{1,0:T(8,128)S(1)}, f32[128,66]{1,0:T(8,128)}, u32[]{:S(2)}) copy-start(f32[128,66]{1,0:T(8,128)} %constant.82.clone.refs_5_.refs_4_) | copy-start | bytes 101380
  26.9 14.3 %collective-permute-start.9 = (bf16[2,512,128]{2,1,0:T(8,128)(2,1)S(1)}, bf16[2,512,128]{2,1,0:T(8,128)(2,1)S(1)}, u32[]{:S(2)}, u32[]{:S(2)}) collective-permute-start(bf16[2,512,128]{2,1,0:T(8,128)(2,1)S(1)} %get-tuple-element.55), channel_id=1, source_target_pairs={{0,16},{4,20},{8,24},{12,28},{16,0},{20,4},{24,8},{28,12},{1,17},{... | collective-permute-start | bytes 786440 | tf_op jit(solution)/shard_map/ppermute | solution.py:1018
  30.9 23.7 %collective-permute-start.5 = (bf16[256,1024]{1,0:T(8,128)(2,1)}, bf16[256,1024]{1,0:T(8,128)(2,1)S(1)}, u32[]{:S(2)}, u32[]{:S(2)}) collective-permute-start(bf16[256,1024]{1,0:T(8,128)(2,1)} %get-tuple-element.48), channel_id=1, source_target_pairs={{0,1},{1,2},{2,3},{3,0},{4,7},{5,4},{6,5},{7,6},{8,9},{9,10},{10,1... | collective-permute-start | bytes 1572872 | tf_op jit(solution)/shard_map/ppermute | solution.py:727
  32.6 8.6 %copy-start.7 = (bf16[512,128]{1,0:T(8,128)(2,1)S(1)}, bf16[512,128]{1,0:T(8,128)(2,1)}, u32[]{:S(2)}) copy-start(bf16[512,128]{1,0:T(8,128)(2,1)} %get-tuple-element.51.stay) | copy-start | bytes 393220
  32.6 8.6 %copy-start.9 = (bf16[256,768]{1,0:T(8,128)(2,1)S(1)}, bf16[256,768]{1,0:T(8,128)(2,1)}, u32[]{:S(2)}) copy-start(bf16[256,768]{1,0:T(8,128)(2,1)} %constant.81.clone.refs_6_) | copy-start | bytes 1179652
  32.6 22.1 %collective-permute-start.6 = (bf16[128,1024]{1,0:T(8,128)(2,1)}, bf16[128,1024]{1,0:T(8,128)(2,1)S(1)}, u32[]{:S(2)}, u32[]{:S(2)}) collective-permute-start(bf16[128,1024]{1,0:T(8,128)(2,1)} %get-tuple-element.49), channel_id=1, source_target_pairs={{0,2},{1,3},{2,0},{3,1},{4,6},{5,7},{6,4},{7,5},{8,10},{9,11},{10,... | collective-permute-start | bytes 786440 | tf_op jit(solution)/shard_map/ppermute | solution.py:727
  54.8 6.9 %collective-permute-start.11 = (bf16[512,128]{1,0:T(8,128)(2,1)S(1)}, bf16[512,128]{1,0:T(8,128)(2,1)S(1)}, u32[]{:S(2)}, u32[]{:S(2)}) collective-permute-start(bf16[512,128]{1,0:T(8,128)(2,1)S(1)} %get-tuple-element.58), channel_id=1, source_target_pairs={{0,4},{4,0},{8,12},{12,8},{16,20},{20,16},{24,28},{28,24},{1,5},{5... | collective-permute-start | bytes 393224 | tf_op jit(solution)/shard_map/ppermute | solution.py:573
  56.9 6.3 %collective-permute-start.12 = (bf16[512,128]{1,0:T(8,128)(2,1)S(1)}, bf16[512,128]{1,0:T(8,128)(2,1)S(1)}, u32[]{:S(2)}, u32[]{:S(2)}) collective-permute-start(bf16[512,128]{1,0:T(8,128)(2,1)S(1)} %get-tuple-element.59), channel_id=1, source_target_pairs={{0,8},{4,12},{8,0},{12,4},{16,24},{20,28},{24,16},{28,20},{1,9},{5... | collective-permute-start | bytes 393224 | tf_op jit(solution)/shard_map/ppermute | solution.py:573
  58.7 8.5 %collective-permute-start.13 = (bf16[512,128]{1,0:T(8,128)(2,1)S(1)}, bf16[512,128]{1,0:T(8,128)(2,1)S(1)}, u32[]{:S(2)}, u32[]{:S(2)}) collective-permute-start(bf16[512,128]{1,0:T(8,128)(2,1)S(1)} %get-tuple-element.60), channel_id=1, source_target_pairs={{0,12},{4,8},{8,4},{12,0},{16,28},{20,24},{24,20},{28,16},{1,13},{... | collective-permute-start | bytes 393224 | tf_op jit(solution)/shard_map/ppermute | solution.py:573
  59.6 12.0 %collective-permute-start.14 = (bf16[512,128]{1,0:T(8,128)(2,1)S(1)}, bf16[512,128]{1,0:T(8,128)(2,1)S(1)}, u32[]{:S(2)}, u32[]{:S(2)}) collective-permute-start(bf16[512,128]{1,0:T(8,128)(2,1)S(1)} %get-tuple-element.61), channel_id=1, source_target_pairs={{0,16},{4,20},{8,24},{12,28},{16,0},{20,4},{24,8},{28,12},{1,17},{... | collective-permute-start | bytes 393224 | tf_op jit(solution)/shard_map/ppermute | solution.py:573
  60.4 13.5 %collective-permute-start.15 = (bf16[512,128]{1,0:T(8,128)(2,1)S(1)}, bf16[512,128]{1,0:T(8,128)(2,1)S(1)}, u32[]{:S(2)}, u32[]{:S(2)}) collective-permute-start(bf16[512,128]{1,0:T(8,128)(2,1)S(1)} %get-tuple-element.62), channel_id=1, source_target_pairs={{0,20},{4,16},{8,28},{12,24},{16,4},{20,0},{24,12},{28,8},{1,21},{... | collective-permute-start | bytes 393224 | tf_op jit(solution)/shard_map/ppermute | solution.py:573
  61.7 12.2 %collective-permute-start.16 = (bf16[512,128]{1,0:T(8,128)(2,1)S(1)}, bf16[512,128]{1,0:T(8,128)(2,1)S(1)}, u32[]{:S(2)}, u32[]{:S(2)}) collective-permute-start(bf16[512,128]{1,0:T(8,128)(2,1)S(1)} %get-tuple-element.63), channel_id=1, source_target_pairs={{0,24},{4,28},{8,16},{12,20},{16,8},{20,12},{24,0},{28,4},{1,25},{... | collective-permute-start | bytes 393224 | tf_op jit(solution)/shard_map/ppermute | solution.py:573
  63.2 2.8 %copy-start.6 = (bf16[6,1024]{1,0:T(8,128)(2,1)S(1)}, bf16[6,1024]{1,0:T(8,128)(2,1)}, u32[]{:S(2)}) copy-start(bf16[6,1024]{1,0:T(8,128)(2,1)} %copy-done.5) | copy-start | bytes 36868
  63.2 10.7 %collective-permute-start.17 = (bf16[512,128]{1,0:T(8,128)(2,1)S(1)}, bf16[512,128]{1,0:T(8,128)(2,1)S(1)}, u32[]{:S(2)}, u32[]{:S(2)}) collective-permute-start(bf16[512,128]{1,0:T(8,128)(2,1)S(1)} %get-tuple-element.64), channel_id=1, source_target_pairs={{0,28},{4,24},{8,20},{12,16},{16,12},{20,8},{24,4},{28,0},{1,29},{... | collective-permute-start | bytes 393224 | tf_op jit(solution)/shard_map/ppermute | solution.py:573
  64.1 17.5 %slice-start = ((s8[8388608]{0:T(1024)(128)(4,1)}), s8[4194304]{0:T(1024)(128)(4,1)S(1)}, s32[]{:S(2)}) async-start(s8[8388608]{0:T(1024)(128)(4,1)} %bitcast.27), calls=%async_computation | async-start | bytes 8388608
  73.9 7.7 %slice-start.1 = ((s8[8388608]{0:T(1024)(128)(4,1)}), s8[4194304]{0:T(1024)(128)(4,1)S(1)}, s32[]{:S(2)}) async-start(s8[8388608]{0:T(1024)(128)(4,1)} %bitcast.27), calls=%async_computation.1 | async-start | bytes 8388608
  75.5 2.7 %collective-permute-start.19 = (bf16[2,256,1024]{2,1,0:T(8,128)(2,1)S(1)}, bf16[2,256,1024]{2,1,0:T(8,128)(2,1)S(1)}, u32[]{:S(2)}, u32[]{:S(2)}) collective-permute-start(bf16[2,256,1024]{2,1,0:T(8,128)(2,1)S(1)} %get-tuple-element.65.mine.head), channel_id=1, source_target_pairs={{0,4},{4,0},{8,12},{12,8},{16,20},{20,16},{24,28},{28,24},{1,5},{5... | collective-permute-start | bytes 3145736 | tf_op jit(solution)/shard_map/ppermute | solution.py:972
  75.6 9.9 %collective-permute-start.18 = (bf16[256,1024]{1,0:T(8,128)(2,1)S(1)}, bf16[256,1024]{1,0:T(8,128)(2,1)S(1)}, u32[]{:S(2)}, u32[]{:S(2)}) collective-permute-start(bf16[256,1024]{1,0:T(8,128)(2,1)S(1)} %get-tuple-element.66), channel_id=1, source_target_pairs={{0,1},{1,2},{2,3},{5,4},{6,5},{7,6},{8,9},{9,10},{10,11},{13,12},{... | collective-permute-start | bytes 1572872 | tf_op jit(solution)/shard_map/ppermute | solution.py:971
  79.5 12.7 %collective-permute-start.21 = (bf16[256,1024]{1,0:T(8,128)(2,1)S(1)}, bf16[256,1024]{1,0:T(8,128)(2,1)S(1)}, u32[]{:S(2)}, u32[]{:S(2)}) collective-permute-start(bf16[256,1024]{1,0:T(8,128)(2,1)S(1)} %partner_sent.1), channel_id=1, source_target_pairs={{0,1},{1,2},{2,3},{5,4},{6,5},{7,6},{8,9},{9,10},{10,11},{13,12},{... | collective-permute-start | bytes 1572872 | tf_op jit(solution)/shard_map/ppermute | solution.py:971
  81.0 16.8 %collective-permute-start.23 = (bf16[256,1024]{1,0:T(8,128)(2,1)S(1)}, bf16[256,1024]{1,0:T(8,128)(2,1)S(1)}, u32[]{:S(2)}, u32[]{:S(2)}) collective-permute-start(bf16[256,1024]{1,0:T(8,128)(2,1)S(1)} %collective-permute-done.5), channel_id=1, source_target_pairs={{0,8},{4,20},{8,0},{12,28},{16,24},{20,4},{24,16},{28,12},{1,9},{5... | collective-permute-start | bytes 1572872 | tf_op jit(solution)/shard_map/ppermute | solution.py:763
  86.1 12.8 %collective-permute-start.20 = (bf16[256,1024]{1,0:T(8,128)(2,1)S(1)}, bf16[256,1024]{1,0:T(8,128)(2,1)S(1)}, u32[]{:S(2)}, u32[]{:S(2)}) collective-permute-start(bf16[256,1024]{1,0:T(8,128)(2,1)S(1)} %next_step.6), channel_id=1, source_target_pairs={{0,1},{1,2},{2,3},{5,4},{6,5},{7,6},{8,9},{9,10},{10,11},{13,12},{... | collective-permute-start | bytes 1572872 | tf_op jit(solution)/shard_map/ppermute | solution.py:971
  92.9 16.0 %collective-permute-start.22 = (bf16[256,1024]{1,0:T(8,128)(2,1)S(1)}, bf16[256,1024]{1,0:T(8,128)(2,1)S(1)}, u32[]{:S(2)}, u32[]{:S(2)}) collective-permute-start(bf16[256,1024]{1,0:T(8,128)(2,1)S(1)} %next_step.7), channel_id=1, source_target_pairs={{0,1},{1,2},{2,3},{5,4},{6,5},{7,6},{8,9},{9,10},{10,11},{13,12},{... | collective-permute-start | bytes 1572872 | tf_op jit(solution)/shard_map/ppermute | solution.py:971
  95.7 9.3 %collective-permute-start.26 = (bf16[128,1024]{1,0:T(8,128)(2,1)S(1)}, bf16[128,1024]{1,0:T(8,128)(2,1)S(1)}, u32[]{:S(2)}, u32[]{:S(2)}) collective-permute-start(bf16[128,1024]{1,0:T(8,128)(2,1)S(1)} %collective-permute-done.6), channel_id=1, source_target_pairs={{0,8},{4,20},{8,0},{12,28},{16,24},{20,4},{24,16},{28,12},{1,9},{5... | collective-permute-start | bytes 786440 | tf_op jit(solution)/shard_map/ppermute | solution.py:763
  96.9 13.5 %collective-permute-start.24 = (bf16[256,1024]{1,0:T(8,128)(2,1)S(1)}, bf16[256,1024]{1,0:T(8,128)(2,1)S(1)}, u32[]{:S(2)}, u32[]{:S(2)}) collective-permute-start(bf16[256,1024]{1,0:T(8,128)(2,1)S(1)} %collective-permute-done.5), channel_id=1, source_target_pairs={{0,16},{4,12},{8,24},{12,4},{16,0},{20,28},{24,8},{28,20},{1,17},{... | collective-permute-start | bytes 1572872 | tf_op jit(solution)/shard_map/ppermute | solution.py:764
  97.8 13.9 %collective-permute-start.25 = (bf16[256,1024]{1,0:T(8,128)(2,1)S(1)}, bf16[256,1024]{1,0:T(8,128)(2,1)S(1)}, u32[]{:S(2)}, u32[]{:S(2)}) collective-permute-start(bf16[256,1024]{1,0:T(8,128)(2,1)S(1)} %collective-permute-done.23), channel_id=1, source_target_pairs={{0,16},{4,12},{8,24},{12,4},{16,0},{20,28},{24,8},{28,20},{1,17},{... | collective-permute-start | bytes 1572872 | tf_op jit(solution)/shard_map/ppermute | solution.py:764
  98.9 16.1 %collective-permute-start.27 = (bf16[128,1024]{1,0:T(8,128)(2,1)S(1)}, bf16[128,1024]{1,0:T(8,128)(2,1)S(1)}, u32[]{:S(2)}, u32[]{:S(2)}) collective-permute-start(bf16[128,1024]{1,0:T(8,128)(2,1)S(1)} %collective-permute-done.6), channel_id=1, source_target_pairs={{0,16},{4,12},{8,24},{12,4},{16,0},{20,28},{24,8},{28,20},{1,17},{... | collective-permute-start | bytes 786440 | tf_op jit(solution)/shard_map/ppermute | solution.py:764
  105.0 12.4 %collective-permute-start.31 = (bf16[256,1024]{1,0:T(8,128)(2,1)S(1)}, bf16[256,1024]{1,0:T(8,128)(2,1)S(1)}, u32[]{:S(2)}, u32[]{:S(2)}) collective-permute-start(bf16[256,1024]{1,0:T(8,128)(2,1)S(1)} %next_step.8), channel_id=1, source_target_pairs={{0,1},{1,2},{2,3},{5,4},{6,5},{7,6},{8,9},{9,10},{10,11},{13,12},{... | collective-permute-start | bytes 1572872 | tf_op jit(solution)/shard_map/ppermute | solution.py:971
  108.9 8.4 %collective-permute-start.28 = (bf16[128,1024]{1,0:T(8,128)(2,1)S(1)}, bf16[128,1024]{1,0:T(8,128)(2,1)S(1)}, u32[]{:S(2)}, u32[]{:S(2)}) collective-permute-start(bf16[128,1024]{1,0:T(8,128)(2,1)S(1)} %collective-permute-done.26), channel_id=1, source_target_pairs={{0,16},{4,12},{8,24},{12,4},{16,0},{20,28},{24,8},{28,20},{1,17},{... | collective-permute-start | bytes 786440 | tf_op jit(solution)/shard_map/ppermute | solution.py:764
  110.4 16.3 %collective-permute-start.29 = (bf16[2,128,1024]{2,1,0:T(8,128)(2,1)S(1)}, bf16[2,128,1024]{2,1,0:T(8,128)(2,1)S(1)}, u32[]{:S(2)}, u32[]{:S(2)}) collective-permute-start(bf16[2,128,1024]{2,1,0:T(8,128)(2,1)S(1)} %pad_maximum_fusion.2.refs_2_.refs_0_), channel_id=1, source_target_pairs={{0,4},{4,0},{8,12},{12,8},{16,20},{20,16},{24,28},{28,24},{1,5},{5... | collective-permute-start | bytes 1572872 | tf_op jit(solution)/shard_map/ppermute | solution.py:972
  111.7 9.9 %collective-permute-start.35 = (bf16[256,1024]{1,0:T(8,128)(2,1)S(1)}, bf16[256,1024]{1,0:T(8,128)(2,1)S(1)}, u32[]{:S(2)}, u32[]{:S(2)}) collective-permute-start(bf16[256,1024]{1,0:T(8,128)(2,1)S(1)} %next_step.10), channel_id=1, source_target_pairs={{0,1},{1,2},{2,3},{5,4},{6,5},{7,6},{8,9},{9,10},{10,11},{13,12},{... | collective-permute-start | bytes 1572872 | tf_op jit(solution)/shard_map/ppermute | solution.py:971
  115.1 18.5 %collective-permute-start.33 = (bf16[2,256,1024]{2,1,0:T(8,128)(2,1)S(1)}, bf16[2,256,1024]{2,1,0:T(8,128)(2,1)S(1)}, u32[]{:S(2)}, u32[]{:S(2)}) collective-permute-start(bf16[2,256,1024]{2,1,0:T(8,128)(2,1)S(1)} %pad_maximum_fusion.refs_0_), channel_id=1, source_target_pairs={{0,4},{4,0},{8,12},{12,8},{16,20},{20,16},{24,28},{28,24},{1,5},{5... | collective-permute-start | bytes 3145736 | tf_op jit(solution)/shard_map/ppermute | solution.py:972
  117.3 21.0 %collective-permute-start.34 = (bf16[2,256,1024]{2,1,0:T(8,128)(2,1)S(1)}, bf16[2,256,1024]{2,1,0:T(8,128)(2,1)S(1)}, u32[]{:S(2)}, u32[]{:S(2)}) collective-permute-start(bf16[2,256,1024]{2,1,0:T(8,128)(2,1)S(1)} %pad_maximum_fusion.1.refs_1_), channel_id=1, source_target_pairs={{0,4},{4,0},{8,12},{12,8},{16,20},{20,16},{24,28},{28,24},{1,5},{5... | collective-permute-start | bytes 3145736 | tf_op jit(solution)/shard_map/ppermute | solution.py:972
  117.4 13.7 %collective-permute-start.30 = (bf16[2,128,1024]{2,1,0:T(8,128)(2,1)S(1)}, bf16[2,128,1024]{2,1,0:T(8,128)(2,1)S(1)}, u32[]{:S(2)}, u32[]{:S(2)}) collective-permute-start(bf16[2,128,1024]{2,1,0:T(8,128)(2,1)S(1)} %pad_maximum_fusion.3.refs_3_.refs_1_), channel_id=1, source_target_pairs={{0,4},{4,0},{8,12},{12,8},{16,20},{20,16},{24,28},{28,24},{1,5},{5... | collective-permute-start | bytes 1572872 | tf_op jit(solution)/shard_map/ppermute | solution.py:972
  121.6 11.9 %collective-permute-start.32 = (bf16[256,1024]{1,0:T(8,128)(2,1)S(1)}, bf16[256,1024]{1,0:T(8,128)(2,1)S(1)}, u32[]{:S(2)}, u32[]{:S(2)}) collective-permute-start(bf16[256,1024]{1,0:T(8,128)(2,1)S(1)} %next_step.9), channel_id=1, source_target_pairs={{0,1},{1,2},{2,3},{5,4},{6,5},{7,6},{8,9},{9,10},{10,11},{13,12},{... | collective-permute-start | bytes 1572872 | tf_op jit(solution)/shard_map/ppermute | solution.py:971
  126.7 11.6 %collective-permute-start.36 = (bf16[256,1024]{1,0:T(8,128)(2,1)S(1)}, bf16[256,1024]{1,0:T(8,128)(2,1)S(1)}, u32[]{:S(2)}, u32[]{:S(2)}) collective-permute-start(bf16[256,1024]{1,0:T(8,128)(2,1)S(1)} %next_step.11), channel_id=1, source_target_pairs={{0,1},{1,2},{2,3},{5,4},{6,5},{7,6},{8,9},{9,10},{10,11},{13,12},{... | collective-permute-start | bytes 1572872 | tf_op jit(solution)/shard_map/ppermute | solution.py:971
  139.1 2.7 %collective-permute-start.37 = (bf16[2,256,1024]{2,1,0:T(8,128)(2,1)S(1)}, bf16[2,256,1024]{2,1,0:T(8,128)(2,1)S(1)}, u32[]{:S(2)}, u32[]{:S(2)}) collective-permute-start(bf16[2,256,1024]{2,1,0:T(8,128)(2,1)S(1)} %partner_sum.1), channel_id=1, source_target_pairs={{0,4},{4,0},{8,12},{12,8},{16,20},{20,16},{24,28},{28,24},{1,5},{5... | collective-permute-start | bytes 3145736 | tf_op jit(solution)/shard_map/ppermute | solution.py:972
  (3 other events, 6.6 us)

commit v5 on v4

--- a/solution.py
+++ b/solution.py
@@ -321,11 +321,17 @@
         out[window, :] += skip[...] * series[window, :]
 
 
-def spread_kernel(me_ref, conv, *outs):
-    span = outs[0].shape[0]
-    for m, out in enumerate(outs):
+def spread_kernel(me_ref, conv, stay, same, swap):
+    chips, span, _ = swap.shape
+    for m in range(2 * chips):
         start = pl.multiple_of((me_ref[0] ^ m) * span, span)
-        out[...] = conv[pl.ds(start, span), :].astype(BF16)
+        piece = conv[pl.ds(start, span), :].astype(BF16)
+        if m % 2:
+            swap[m // 2] = piece
+        elif m:
+            same[m // 2 - 1] = piece
+        else:
+            stay[...] = piece
 
 
 VMEM = pl.BlockSpec(memory_space=pltpu.VMEM)
@@ -384,11 +390,13 @@
 
 def spread(me, conv, blocks):
     rows, lanes = conv.shape
+    span, chips = rows // blocks, blocks // 2
+    shapes = [(span, lanes), (chips - 1, span, lanes), (chips, span, lanes)]
     return pl.pallas_call(
         spread_kernel,
-        out_shape=[jax.ShapeDtypeStruct((rows // blocks, lanes), BF16)] * blocks,
+        out_shape=[jax.ShapeDtypeStruct(shape, BF16) for shape in shapes],
         in_specs=[SMEM, VMEM],
-        out_specs=[VMEM] * blocks,
+        out_specs=[VMEM] * 3,
         compiler_params=GRANT,
         name="spread",
     )(me, conv)
@@ -567,15 +575,6 @@
     )(query_rows, edges, short_weight)
 
 
-def exchange(pieces, axis):
-    devices = range(lax.axis_size(axis))
-    return [pieces[0]] + [
-        lax.ppermute(piece, axis, [(i, i ^ m) for i in devices])
-        for m, piece in enumerate(pieces)
-        if m
-    ]
-
-
 def after(values, others):
     return lax.optimization_barrier((values, others))[0]
 
@@ -593,7 +592,9 @@
 
 
 def gate_out_kernel(blocks, spot, *refs):
-    convs, (mixed, far_weight, gated, sent) = refs[:blocks], refs[blocks:]
+    stay, swapped, *others = refs[: blocks // 2 + 1]
+    mixed, far_weight, gated, sent = refs[blocks // 2 + 1 :]
+    convs = [stay, swapped.at[0]] + [ref.at[core] for ref in others for core in range(2)]
     lanes = convs[0].shape[1]
     rows = gated.shape[1]
     for m in range(blocks):
@@ -618,7 +619,7 @@
 def gate_out(spot, convs, mixed, far_weight):
     span, chans = mixed.shape
     return pl.pallas_call(
-        partial(gate_out_kernel, len(convs)),
+        partial(gate_out_kernel, 2 * len(convs) - 2),
         in_specs=[SMEM] + [VMEM] * (len(convs) + 2),
         out_specs=[VMEM] * 2,
         out_shape=[
@@ -710,13 +711,17 @@
     )(plan, mine, partners, out_weight)
 
 
-def spread_weight(out_weight, ready):
+def pick_weight(out_weight):
     stages, blocks = lax.axis_size("tp"), lax.axis_size("ctx")
     stage, place = lax.axis_index("tp"), lax.axis_index("ctx")
     chans = out_weight.shape[0]
     hops = jnp.where(place % 2 == 0, 1, stages - 1)
     corners = jnp.stack([place // 2, (stage + hops) % stages, place, (stage + 2) % stages])
-    parts = weight_corners(after(corners.astype(jnp.int32), ready), out_weight, blocks)
+    return weight_corners(corners.astype(jnp.int32), out_weight, blocks)
+
+
+def turn_weight(parts):
+    stages, blocks = lax.axis_size("tp"), lax.axis_size("ctx")
     found = []
     for part, static in zip(parts, ((1, stages - 1), (2, 2))):
         route = [
@@ -1021,16 +1026,19 @@
     edges = passed_along(rims(query_rows, key_rows, value_rows), "ctx", 1)
     pairs = split_taps(after(me, edges), filter_taps, blocks // 2)
     pairs = [pairs[0]] + to_chips(pairs[1:])
-    stay, same, swap = gate_in(me, key_rows, value_rows, edges, short_weight, blocks)
+    weight_parts = pick_weight(out_weight)
+    stay, same, swap = gate_in(after(me, weight_parts), key_rows, value_rows, edges, short_weight, blocks)
     swapped = core_swap(swap)
     packed = pair_up(same, swapped)
     others = to_chips(packed)
     taps_swapped = core_swap(other_core(me, pairs))
     mixed = mix_query(query_rows, edges, short_weight)
     spectra = taps_spectra_of(me, pairs, taps_swapped, twiddle, forward)
-    weight_parts = spread_weight(out_weight, taps_swapped)
+    weight_parts = turn_weight(after(weight_parts, taps_swapped))
     conv = long_conv(me, stay, swapped, others, spectra, twiddle, forward, inverse, skip)
-    convs = exchange(spread(after(me, weight_parts), conv, blocks), "ctx")
+    stay, same, swap = spread(after(me, weight_parts), conv, blocks)
+    swapped = core_swap(swap)
+    convs = [stay, swapped] + to_chips(pair_up(same, swapped))
     return project(spot, plan, order, convs, mixed, out_weight, weight_parts)
 
 

time: 145 us -> 141 us (0.972)
  starting transfers between devices: 61.4 us -> 57.4 us
    ppermute x9 -> x2, starting transfers between devices: 12.3 us -> 4.17 us  [turn_weight(): found.append(lax.ppermute(part, ('ctx', 'tp'), route))]
    ppermute x9 -> x2, waiting for transfers between devices: 6.79 us -> 0.01 us  [turn_weight(): found.append(lax.ppermute(part, ('ctx', 'tp'), route))]
    ppermute x6 -> x9, waiting for transfers between devices: 6.18 us -> 11 us  [fast_per_device(): lax.ppermute(x, 'ctx', [(i, i ^ 2 * q + 2) for i in devices])]
    ppermute x6 -> x9, starting transfers between devices: 10.8 us -> 14.4 us  [fast_per_device(): lax.ppermute(x, 'ctx', [(i, i ^ 2 * q + 2) for i in devices])]
    ppermute x2 -> x3, waiting for transfers between devices: 0.01 us -> 1.54 us  [fast_per_device(): core_swap = lambda x: lax.ppermute(x, 'ctx', [(i, i ^ 1) for i in devices])]
    ppermute x4, waiting for transfers between devices: 3.38 us -> 1.87 us  [gather_weight(): lax.ppermute(x, 'ctx', other)]
  transfers between devices with their start and end apart: 38 -> 35, of which waited for: 12 -> 14; matrix products, arithmetic and copies ran while one was open for 3% -> 4% of each run, Pallas kernels for 28% -> 28%
where the time goes in v5:
time: 141 us; the launch traced here: 140 us
  starting transfers between devices  57.4 us (41%)
  Pallas kernels  45.2 us (32%)
  waiting for transfers between devices  29.5 us (21%)
  local copies, waits for them, and re-layouts  3.79 us (3%)
  other arithmetic  2.76 us (2%)
    ppermute x8, starting transfers between devices, project(): onward = lambda x: lax.ppermute(x, ('ctx', 'tp'), route)  27.7 us
    ppermute x9, starting transfers between devices, fast_per_device(): lax.ppermute(x, 'ctx', [(i, i ^ 2 * q + 2) for i in devices])  14.4 us
    pallas_call x1, Pallas kernels, long_conv(): pl.pallas_call(partial(conv_kernel, blocks), out_shape=jax.ShapeDtypeStru...  13.6 us
    ppermute x9, waiting for transfers between devices, fast_per_device(): lax.ppermute(x, 'ctx', [(i, i ^ 2 * q + 2) for i in devices])  11 us
    ppermute x8, waiting for transfers between devices, project(): onward = lambda x: lax.ppermute(x, ('ctx', 'tp'), route)  9.03 us
    pallas_call x1, Pallas kernels, taps_spectra_of(): pl.pallas_call(partial(taps_kernel, chips), out_shape=jax.ShapeDtypeStruc...  5.94 us
    ppermute x4, starting transfers between devices, gather_weight(): lax.ppermute(x, 'ctx', other)  4.44 us
    pallas_call x1, Pallas kernels, gate_in(): pl.pallas_call(gate_in_kernel, in_specs=[SMEM, HBM, HBM, VMEM, VMEM], out...  4.26 us
  transfers between devices with their start and end apart: 35, of which 14 were waited for; matrix products, arithmetic and copies ran while one was open for 4% of the time, Pallas kernels for 28%

profile of v5, /device:TPU:0, one launch (start us, length us, event | category | flops | bytes accessed | tf_op | source)
XLA Modules:
  0.0 139.9 jit_solution(10271154867095358825)
XLA Ops:
  0.0 1.5 %rims.1 = bf16[6,1024]{1,0:T(8,128)(2,1)} custom-call(bf16[512,1024]{1,0:T(8,128)(2,1)} %query.3, bf16[512,1024]{1,0:T(8,128)(2,1)} %key.3, bf16[512,1024]{1,0:T(8,128)(2,1)} %value.3), custom_call_target="tpu_custom_call" | custom-call | tf_op jit(solution)/shard_map/rims/pallas_call | solution.py:428
  1.5 2.4 %collective-permute-start = (bf16[6,1024]{1,0:T(8,128)(2,1)}, bf16[6,1024]{1,0:T(8,128)(2,1)S(1)}, u32[]{:S(2)}, u32[]{:S(2)}) collective-permute-start(bf16[6,1024]{1,0:T(8,128)(2,1)} %rims.1), channel_id=1, source_target_pairs={{0,4},{4,8},{8,12},{12,16},{16,20},{20,24},{24,28},{1,5},{5,9},{9,... | collective-permute-start | bytes 36872 | tf_op jit(solution)/shard_map/ppermute | solution.py:18
  5.1 4.9 %collective-permute-start.1 = (bf16[256,512]{1,0:T(8,128)(2,1)S(1)}, bf16[256,512]{1,0:T(8,128)(2,1)S(1)}, u32[]{:S(2)}, u32[]{:S(2)}) collective-permute-start(bf16[256,512]{1,0:T(8,128)(2,1)S(1)} %get-tuple-element.46), channel_id=1, source_target_pairs={{0,8},{4,12},{8,0},{12,4},{16,24},{20,28},{24,16},{28,20},{1,9},{5... | collective-permute-start | bytes 786440 | tf_op jit(solution)/shard_map/ppermute | solution.py:1023
  10.0 1.5 %collective-permute-start.2 = (bf16[256,512]{1,0:T(8,128)(2,1)S(1)}, bf16[256,512]{1,0:T(8,128)(2,1)S(1)}, u32[]{:S(2)}, u32[]{:S(2)}) collective-permute-start(bf16[256,512]{1,0:T(8,128)(2,1)S(1)} %get-tuple-element.47), channel_id=1, source_target_pairs={{0,16},{4,20},{8,24},{12,28},{16,0},{20,4},{24,8},{28,12},{1,17},{... | collective-permute-start | bytes 786440 | tf_op jit(solution)/shard_map/ppermute | solution.py:1023
  11.5 0.9 collective-permute-start.3
  13.0 2.7 %weight_corners.1 = (bf16[256,1024]{1,0:T(8,128)(2,1)}, bf16[128,1024]{1,0:T(8,128)(2,1)}) custom-call(s32[4]{0:T(128)} %pad_add_fusion.1.corners, bf16[1024,4096]{1,0:T(8,128)(2,1)} %weight.9), custom_call_target="tpu_custom_call" | custom-call | tf_op jit(solution)/shard_map/weight_corners/pallas_call | solution.py:753
  15.7 4.3 %gate_in.1 = (bf16[512,128]{1,0:T(8,128)(2,1)}, bf16[3,512,128]{2,1,0:T(8,128)(2,1)}, bf16[4,512,128]{2,1,0:T(8,128)(2,1)}) custom-call(s32[1]{0:T(128)} %bitcast.me_ref, bf16[512,1024]{1,0:T(8,128)(2,1)} %key.3, bf16[512,1024]{1,0:T(8,128)(2,1)} %value.3, bf16[6,1024]{1,0:T(8,128)(2,1)} %copy-done.5, f32[3,3,1024]{2,1,0:T(4,128)} %weight.7), custom_call_target="tpu_custom_call" | custom-call | tf_op jit(solution)/shard_map/gate_in/pallas_call | solution.py:479
  20.1 2.7 %collective-permute-done.2.refs_2_ = bf16[256,512]{1,0:T(8,128)(2,1)S(1)} collective-permute-done((bf16[256,512]{1,0:T(8,128)(2,1)S(1)}, bf16[256,512]{1,0:T(8,128)(2,1)S(1)}, u32[]{:S(2)}, u32[]{:S(2)}) %collective-permute-start.2) | collective-permute-done | bytes 262176 | tf_op jit(solution)/shard_map/ppermute | solution.py:1023
  23.0 1.0 copy-done.3
  24.1 1.6 %collective-permute-start.10 = (bf16[2,512,128]{2,1,0:T(8,128)(2,1)S(1)}, bf16[2,512,128]{2,1,0:T(8,128)(2,1)S(1)}, u32[]{:S(2)}, u32[]{:S(2)}) collective-permute-start(bf16[2,512,128]{2,1,0:T(8,128)(2,1)S(1)} %get-tuple-element.58), channel_id=1, source_target_pairs={{0,24},{4,28},{8,16},{12,20},{16,8},{20,12},{24,0},{28,4},{1,25},{... | collective-permute-start | bytes 786440 | tf_op jit(solution)/shard_map/ppermute | solution.py:1023
  25.7 1.1 collective-permute-start.8
  27.6 1.6 %collective-permute-start.5 = (bf16[256,1024]{1,0:T(8,128)(2,1)}, bf16[256,1024]{1,0:T(8,128)(2,1)}, u32[]{:S(2)}, u32[]{:S(2)}) collective-permute-start(bf16[256,1024]{1,0:T(8,128)(2,1)} %get-tuple-element.49), channel_id=1, source_target_pairs={{0,1},{1,2},{2,3},{3,0},{4,7},{5,4},{6,5},{7,6},{8,9},{9,10},{10,1... | collective-permute-start | bytes 1572872 | tf_op jit(solution)/shard_map/ppermute | solution.py:732
  29.2 2.6 %collective-permute-start.6 = (bf16[128,1024]{1,0:T(8,128)(2,1)}, bf16[128,1024]{1,0:T(8,128)(2,1)S(1)}, u32[]{:S(2)}, u32[]{:S(2)}) collective-permute-start(bf16[128,1024]{1,0:T(8,128)(2,1)} %get-tuple-element.50), channel_id=1, source_target_pairs={{0,2},{1,3},{2,0},{3,1},{4,6},{5,7},{6,4},{7,5},{8,10},{9,11},{10,... | collective-permute-start | bytes 786440 | tf_op jit(solution)/shard_map/ppermute | solution.py:732
  31.8 5.9 %taps_spectra.1.refs_3_ = f32[17,256,256]{2,1,0:T(8,128)S(1)} custom-call(s32[1]{0:T(128)} %bitcast.me_ref, bf16[256,512]{1,0:T(8,128)(2,1)S(1)} %get-tuple-element.45.refs_0_, bf16[256,512]{1,0:T(8,128)(2,1)S(1)} %collective-permute-done.1.refs_1_, bf16[256,512]{1,0:T(8,128)(2,1)S(1)} %collective-permute-done.2.refs_2_, ...), custom_call_target="tpu_custom_call" | custom-call | flops 8000000000 | tf_op jit(solution)/shard_map/taps_spectra/pallas_call | solution.py:357
  37.8 1.0 collective-permute-done.8.refs_0_
  39.4 13.6 %long_conv.1.conv = f32[4096,128]{1,0:T(8,128)S(1)} custom-call(s32[1]{0:T(128)} %bitcast.me_ref, bf16[512,128]{1,0:T(8,128)(2,1)S(1)} %copy-done.7, bf16[4,512,128]{2,1,0:T(8,128)(2,1)S(1)} %collective-permute-done.7.swapped, bf16[2,512,128]{2,1,0:T(8,128)(2,1)S(1)} %collective-permute-done.8.refs_0_, ...), custom_call_target="tpu_custom_call" | custom-call | flops 20000000000 | tf_op jit(solution)/shard_map/long_conv/pallas_call | solution.py:376
  53.6 1.5 %collective-permute-done.11.swapped.refs_1_ = bf16[4,512,128]{2,1,0:T(8,128)(2,1)S(1)} collective-permute-done((bf16[4,512,128]{2,1,0:T(8,128)(2,1)S(1)}, bf16[4,512,128]{2,1,0:T(8,128)(2,1)S(1)}, u32[]{:S(2)}, u32[]{:S(2)}) %collective-permute-start.11) | collective-permute-done | bytes 524320 | tf_op jit(solution)/shard_map/ppermute | solution.py:1021
  55.9 1.5 %collective-permute-start.13 = (bf16[2,512,128]{2,1,0:T(8,128)(2,1)S(1)}, bf16[2,512,128]{2,1,0:T(8,128)(2,1)S(1)}, u32[]{:S(2)}, u32[]{:S(2)}) collective-permute-start(bf16[2,512,128]{2,1,0:T(8,128)(2,1)S(1)} %get-tuple-element.63), channel_id=1, source_target_pairs={{0,16},{4,20},{8,24},{12,28},{16,0},{20,4},{24,8},{28,12},{1,17},{... | collective-permute-start | bytes 786440 | tf_op jit(solution)/shard_map/ppermute | solution.py:1023
  57.4 1.4 %collective-permute-start.14 = (bf16[2,512,128]{2,1,0:T(8,128)(2,1)S(1)}, bf16[2,512,128]{2,1,0:T(8,128)(2,1)S(1)}, u32[]{:S(2)}, u32[]{:S(2)}) collective-permute-start(bf16[2,512,128]{2,1,0:T(8,128)(2,1)S(1)} %get-tuple-element.64), channel_id=1, source_target_pairs={{0,24},{4,28},{8,16},{12,20},{16,8},{20,12},{24,0},{28,4},{1,25},{... | collective-permute-start | bytes 786440 | tf_op jit(solution)/shard_map/ppermute | solution.py:1023
  60.1 1.9 %constant_dynamic-slice_fusion.refs_6_.far_weight = bf16[1024,1024]{1,0:T(8,128)(2,1)S(1)} fusion(bf16[1024,4096]{1,0:T(8,128)(2,1)} %weight.9, s32[]{:T(128)S(6)} %select_n.62), kind=kLoop, calls=%fused_computation.8 | loop fusion | bytes 4194308 | tf_op jit(solution)/shard_map/dynamic_slice | solution.py:968
  62.0 1.1 mix_query.1.refs_5_
  63.1 1.3 collective-permute-done.12.refs_2_
  64.4 4.4 %collective-permute-done.13.refs_3_ = bf16[2,512,128]{2,1,0:T(8,128)(2,1)S(1)} collective-permute-done((bf16[2,512,128]{2,1,0:T(8,128)(2,1)S(1)}, bf16[2,512,128]{2,1,0:T(8,128)(2,1)S(1)}, u32[]{:S(2)}, u32[]{:S(2)}) %collective-permute-start.13) | collective-permute-done | bytes 262176 | tf_op jit(solution)/shard_map/ppermute | solution.py:1023
  68.8 0.9 collective-permute-done.14.refs_4_
  69.7 1.6 %gate_out.1 = (bf16[2,256,1024]{2,1,0:T(8,128)(2,1)S(1)}, bf16[256,1024]{1,0:T(8,128)(2,1)S(1)}) custom-call(s32[3]{0:T(128)S(1)} %pad_add_fusion.spot, bf16[512,128]{1,0:T(8,128)(2,1)S(1)} %get-tuple-element.59.refs_0_, bf16[4,512,128]{2,1,0:T(8,128)(2,1)S(1)} %collective-permute-done.11.swapped.refs_1_, ...), custom_call_target="tpu_custom_call" | custom-call | tf_op jit(solution)/shard_map/gate_out/pallas_call | solution.py:621
  71.4 2.8 %collective-permute-start.15 = (bf16[256,1024]{1,0:T(8,128)(2,1)S(1)}, bf16[256,1024]{1,0:T(8,128)(2,1)S(1)}, u32[]{:S(2)}, u32[]{:S(2)}) collective-permute-start(bf16[256,1024]{1,0:T(8,128)(2,1)S(1)} %get-tuple-element.66), channel_id=1, source_target_pairs={{0,1},{1,2},{2,3},{5,4},{6,5},{7,6},{8,9},{9,10},{10,11},{13,12},{... | collective-permute-start | bytes 1572872 | tf_op jit(solution)/shard_map/ppermute | solution.py:976
  74.2 1.3 partner_sent.1
  75.5 2.8 %collective-permute-start.18 = (bf16[256,1024]{1,0:T(8,128)(2,1)S(1)}, bf16[256,1024]{1,0:T(8,128)(2,1)S(1)}, u32[]{:S(2)}, u32[]{:S(2)}) collective-permute-start(bf16[256,1024]{1,0:T(8,128)(2,1)S(1)} %partner_sent.1), channel_id=1, source_target_pairs={{0,1},{1,2},{2,3},{5,4},{6,5},{7,6},{8,9},{9,10},{10,11},{13,12},{... | collective-permute-start | bytes 1572872 | tf_op jit(solution)/shard_map/ppermute | solution.py:976
  78.3 1.4 %collective-permute-start.20 = (bf16[256,1024]{1,0:T(8,128)(2,1)}, bf16[256,1024]{1,0:T(8,128)(2,1)S(1)}, u32[]{:S(2)}, u32[]{:S(2)}) collective-permute-start(bf16[256,1024]{1,0:T(8,128)(2,1)} %collective-permute-done.5), channel_id=1, source_target_pairs={{0,8},{4,20},{8,0},{12,28},{16,24},{20,4},{24,16},{28,12},{1,9},{5... | collective-permute-start | bytes 1572872 | tf_op jit(solution)/shard_map/ppermute | solution.py:768
  79.8 3.7 %sent_terms.1.term = bf16[2,2,256,1024]{3,2,1,0:T(8,128)(2,1)S(1)} custom-call(s32[5]{0:T(128)S(1)} %or_select_fusion.plan, bf16[2,256,1024]{2,1,0:T(8,128)(2,1)S(1)} %get-tuple-element.65.mine.head, bf16[2,256,1024]{2,1,0:T(8,128)(2,1)S(1)} %collective-permute-done.16.partners.gated.head, bf16[1024,4096]{1,0:T(8,128)(2,1)S(1)} %bitcast.28), custom_call_target="tpu_custom_call" | custom-call | flops 4000000000 | tf_op jit(solution)/shard_map/sent_terms/pallas_call | solution.py:702
  84.1 4.4 %collective-permute-start.17 = (bf16[256,1024]{1,0:T(8,128)(2,1)S(1)}, bf16[256,1024]{1,0:T(8,128)(2,1)S(1)}, u32[]{:S(2)}, u32[]{:S(2)}) collective-permute-start(bf16[256,1024]{1,0:T(8,128)(2,1)S(1)} %next_step.6), channel_id=1, source_target_pairs={{0,1},{1,2},{2,3},{5,4},{6,5},{7,6},{8,9},{9,10},{10,11},{13,12},{... | collective-permute-start | bytes 1572872 | tf_op jit(solution)/shard_map/ppermute | solution.py:976
  89.1 2.5 %collective-permute-start.19 = (bf16[256,1024]{1,0:T(8,128)(2,1)S(1)}, bf16[256,1024]{1,0:T(8,128)(2,1)S(1)}, u32[]{:S(2)}, u32[]{:S(2)}) collective-permute-start(bf16[256,1024]{1,0:T(8,128)(2,1)S(1)} %next_step.7), channel_id=1, source_target_pairs={{0,1},{1,2},{2,3},{5,4},{6,5},{7,6},{8,9},{9,10},{10,11},{13,12},{... | collective-permute-start | bytes 1572872 | tf_op jit(solution)/shard_map/ppermute | solution.py:976
  91.6 1.4 %collective-permute-start.23 = (bf16[128,1024]{1,0:T(8,128)(2,1)S(1)}, bf16[128,1024]{1,0:T(8,128)(2,1)S(1)}, u32[]{:S(2)}, u32[]{:S(2)}) collective-permute-start(bf16[128,1024]{1,0:T(8,128)(2,1)S(1)} %copy-done.12), channel_id=1, source_target_pairs={{0,8},{4,20},{8,0},{12,28},{16,24},{20,4},{24,16},{28,12},{1,9},{5... | collective-permute-start | bytes 786440 | tf_op jit(solution)/shard_map/ppermute | solution.py:768
  93.9 1.2 collective-permute-start.22
  96.8 4.1 %collective-permute-done.23 = bf16[128,1024]{1,0:T(8,128)(2,1)S(1)} collective-permute-done((bf16[128,1024]{1,0:T(8,128)(2,1)S(1)}, bf16[128,1024]{1,0:T(8,128)(2,1)S(1)}, u32[]{:S(2)}, u32[]{:S(2)}) %collective-permute-start.23) | collective-permute-done | bytes 262176 | tf_op jit(solution)/shard_map/ppermute | solution.py:768
  100.9 3.3 %collective-permute-start.28 = (bf16[256,1024]{1,0:T(8,128)(2,1)S(1)}, bf16[256,1024]{1,0:T(8,128)(2,1)S(1)}, u32[]{:S(2)}, u32[]{:S(2)}) collective-permute-start(bf16[256,1024]{1,0:T(8,128)(2,1)S(1)} %next_step.8), channel_id=1, source_target_pairs={{0,1},{1,2},{2,3},{5,4},{6,5},{7,6},{8,9},{9,10},{10,11},{13,12},{... | collective-permute-start | bytes 1572872 | tf_op jit(solution)/shard_map/ppermute | solution.py:976
  104.3 1.6 %collective-permute-start.25 = (bf16[128,1024]{1,0:T(8,128)(2,1)S(1)}, bf16[128,1024]{1,0:T(8,128)(2,1)S(1)}, u32[]{:S(2)}, u32[]{:S(2)}) collective-permute-start(bf16[128,1024]{1,0:T(8,128)(2,1)S(1)} %collective-permute-done.23), channel_id=1, source_target_pairs={{0,16},{4,12},{8,24},{12,4},{16,0},{20,28},{24,8},{28,20},{1,17},{... | collective-permute-start | bytes 786440 | tf_op jit(solution)/shard_map/ppermute | solution.py:769
  105.9 1.1 pad_maximum_fusion.refs_0_
  108.0 3.8 %collective-permute-start.32 = (bf16[256,1024]{1,0:T(8,128)(2,1)S(1)}, bf16[256,1024]{1,0:T(8,128)(2,1)S(1)}, u32[]{:S(2)}, u32[]{:S(2)}) collective-permute-start(bf16[256,1024]{1,0:T(8,128)(2,1)S(1)} %next_step.10), channel_id=1, source_target_pairs={{0,1},{1,2},{2,3},{5,4},{6,5},{7,6},{8,9},{9,10},{10,11},{13,12},{... | collective-permute-start | bytes 1572872 | tf_op jit(solution)/shard_map/ppermute | solution.py:976
  112.1 1.6 %collective-permute-done.25 = bf16[128,1024]{1,0:T(8,128)(2,1)S(1)} collective-permute-done((bf16[128,1024]{1,0:T(8,128)(2,1)S(1)}, bf16[128,1024]{1,0:T(8,128)(2,1)S(1)}, u32[]{:S(2)}, u32[]{:S(2)}) %collective-permute-start.25) | collective-permute-done | bytes 262176 | tf_op jit(solution)/shard_map/ppermute | solution.py:769
  115.0 3.5 %collective-permute-done.32.got.got2 = bf16[256,1024]{1,0:T(8,128)(2,1)S(1)} collective-permute-done((bf16[256,1024]{1,0:T(8,128)(2,1)S(1)}, bf16[256,1024]{1,0:T(8,128)(2,1)S(1)}, u32[]{:S(2)}, u32[]{:S(2)}) %collective-permute-start.32) | collective-permute-done | bytes 524320 | tf_op jit(solution)/shard_map/ppermute | solution.py:976
  118.5 4.4 %collective-permute-start.29 = (bf16[256,1024]{1,0:T(8,128)(2,1)S(1)}, bf16[256,1024]{1,0:T(8,128)(2,1)S(1)}, u32[]{:S(2)}, u32[]{:S(2)}) collective-permute-start(bf16[256,1024]{1,0:T(8,128)(2,1)S(1)} %next_step.9), channel_id=1, source_target_pairs={{0,1},{1,2},{2,3},{5,4},{6,5},{7,6},{8,9},{9,10},{10,11},{13,12},{... | collective-permute-start | bytes 1572872 | tf_op jit(solution)/shard_map/ppermute | solution.py:976
  123.6 3.7 %collective-permute-start.33 = (bf16[256,1024]{1,0:T(8,128)(2,1)S(1)}, bf16[256,1024]{1,0:T(8,128)(2,1)S(1)}, u32[]{:S(2)}, u32[]{:S(2)}) collective-permute-start(bf16[256,1024]{1,0:T(8,128)(2,1)S(1)} %next_step.11), channel_id=1, source_target_pairs={{0,1},{1,2},{2,3},{5,4},{6,5},{7,6},{8,9},{9,10},{10,11},{13,12},{... | collective-permute-start | bytes 1572872 | tf_op jit(solution)/shard_map/ppermute | solution.py:976
  127.4 2.4 %early_sum.1 = (f32[512,1024]{1,0:T(8,128)S(1)}, f32[256,1024]{1,0:T(8,128)S(1)}) custom-call(s32[10]{0:T(128)S(1)} %stack.99.order, bf16[2,256,1024]{2,1,0:T(8,128)(2,1)S(1)} %get-tuple-element.65.mine.head, bf16[256,1024]{1,0:T(8,128)(2,1)S(1)} %collective-permute-done.15.got.got0, bf16[256,1024]{1,0:T(8,128)(2,1)S(1)} %collective-permute-done.17.got1.got, ...), custom_call_target="tpu_custom_call" | custom-call | flops 5000000000 | tf_op jit(solution)/shard_map/early_sum/pallas_call | solution.py:836
  129.7 5.4 %collective-permute-done.33.got3 = bf16[256,1024]{1,0:T(8,128)(2,1)S(1)} collective-permute-done((bf16[256,1024]{1,0:T(8,128)(2,1)S(1)}, bf16[256,1024]{1,0:T(8,128)(2,1)S(1)}, u32[]{:S(2)}, u32[]{:S(2)}) %collective-permute-start.33) | collective-permute-done | bytes 524320 | tf_op jit(solution)/shard_map/ppermute | solution.py:976
  136.1 0.9 mine_sum.1.mine
  137.0 1.8 %collective-permute-done.34.partners = bf16[2,256,1024]{2,1,0:T(8,128)(2,1)S(1)} collective-permute-done((bf16[2,256,1024]{2,1,0:T(8,128)(2,1)S(1)}, bf16[2,256,1024]{2,1,0:T(8,128)(2,1)S(1)}, u32[]{:S(2)}, u32[]{:S(2)}) %collective-permute-start.34) | collective-permute-done | bytes 1048608 | tf_op jit(solution)/shard_map/ppermute | solution.py:977
  138.8 1.1 join_sums.1
  (88 shorter events, 13.6 us)
Async XLA Ops:
  0.0 22.9 %copy-start = (f32[1024]{0:T(1024)S(1)}, f32[1024]{0:T(1024)}, u32[]{:S(2)}) copy-start(f32[1024]{0:T(1024)} %param.15) | copy-start | bytes 12292
  1.5 3.4 %collective-permute-start = (bf16[6,1024]{1,0:T(8,128)(2,1)}, bf16[6,1024]{1,0:T(8,128)(2,1)S(1)}, u32[]{:S(2)}, u32[]{:S(2)}) collective-permute-start(bf16[6,1024]{1,0:T(8,128)(2,1)} %rims.1), channel_id=1, source_target_pairs={{0,4},{4,8},{8,12},{12,16},{16,20},{20,24},{24,28},{1,5},{5,9},{9,... | collective-permute-start | bytes 36872 | tf_op jit(solution)/shard_map/ppermute | solution.py:18
  4.9 10.8 %copy-start.5 = (bf16[6,1024]{1,0:T(8,128)(2,1)}, bf16[6,1024]{1,0:T(8,128)(2,1)S(1)}, u32[]{:S(2)}) copy-start(bf16[6,1024]{1,0:T(8,128)(2,1)S(1)} %collective-permute-done.edges) | copy-start | bytes 36868
  5.1 15.0 %collective-permute-start.1 = (bf16[256,512]{1,0:T(8,128)(2,1)S(1)}, bf16[256,512]{1,0:T(8,128)(2,1)S(1)}, u32[]{:S(2)}, u32[]{:S(2)}) collective-permute-start(bf16[256,512]{1,0:T(8,128)(2,1)S(1)} %get-tuple-element.46), channel_id=1, source_target_pairs={{0,8},{4,12},{8,0},{12,4},{16,24},{20,28},{24,16},{28,20},{1,9},{5... | collective-permute-start | bytes 786440 | tf_op jit(solution)/shard_map/ppermute | solution.py:1023
  10.0 12.9 %collective-permute-start.2 = (bf16[256,512]{1,0:T(8,128)(2,1)S(1)}, bf16[256,512]{1,0:T(8,128)(2,1)S(1)}, u32[]{:S(2)}, u32[]{:S(2)}) collective-permute-start(bf16[256,512]{1,0:T(8,128)(2,1)S(1)} %get-tuple-element.47), channel_id=1, source_target_pairs={{0,16},{4,20},{8,24},{12,28},{16,0},{20,4},{24,8},{28,12},{1,17},{... | collective-permute-start | bytes 786440 | tf_op jit(solution)/shard_map/ppermute | solution.py:1023
  11.5 11.3 %collective-permute-start.3 = (bf16[256,512]{1,0:T(8,128)(2,1)S(1)}, bf16[256,512]{1,0:T(8,128)(2,1)S(1)}, u32[]{:S(2)}, u32[]{:S(2)}) collective-permute-start(bf16[256,512]{1,0:T(8,128)(2,1)S(1)} %get-tuple-element.48), channel_id=1, source_target_pairs={{0,24},{4,28},{8,16},{12,20},{16,8},{20,12},{24,0},{28,4},{1,25},{... | collective-permute-start | bytes 786440 | tf_op jit(solution)/shard_map/ppermute | solution.py:1023
  15.7 16.1 %copy-start.8 = (bf16[256,768]{1,0:T(8,128)(2,1)S(1)}, bf16[256,768]{1,0:T(8,128)(2,1)}, u32[]{:S(2)}) copy-start(bf16[256,768]{1,0:T(8,128)(2,1)} %constant.80.clone.refs_6_.refs_5_) | copy-start | bytes 1179652
  15.7 16.1 %copy-start.10 = (f32[128,66]{1,0:T(8,128)S(1)}, f32[128,66]{1,0:T(8,128)}, u32[]{:S(2)}) copy-start(f32[128,66]{1,0:T(8,128)} %constant.82.clone.refs_5_.refs_4_) | copy-start | bytes 101380
  20.0 3.0 %collective-permute-start.7 = (bf16[4,512,128]{2,1,0:T(8,128)(2,1)}, bf16[4,512,128]{2,1,0:T(8,128)(2,1)S(1)}, u32[]{:S(2)}, u32[]{:S(2)}) collective-permute-start(bf16[4,512,128]{2,1,0:T(8,128)(2,1)} %get-tuple-element.54), channel_id=1, source_target_pairs={{0,4},{4,0},{8,12},{12,8},{16,20},{20,16},{24,28},{28,24},{1,5},{5... | collective-permute-start | bytes 1572872 | tf_op jit(solution)/shard_map/ppermute | solution.py:1021
  22.9 4.8 %collective-permute-start.4 = (bf16[4,128,512]{2,1,0:T(8,128)(2,1)S(1)}, bf16[4,128,512]{2,1,0:T(8,128)(2,1)S(1)}, u32[]{:S(2)}, u32[]{:S(2)}) collective-permute-start(bf16[4,128,512]{2,1,0:T(8,128)(2,1)S(1)} %other_core.1), channel_id=1, source_target_pairs={{0,4},{4,0},{8,12},{12,8},{16,20},{20,16},{24,28},{28,24},{1,5},{5... | collective-permute-start | bytes 1572872 | tf_op jit(solution)/shard_map/ppermute | solution.py:1021
  24.1 13.7 %collective-permute-start.10 = (bf16[2,512,128]{2,1,0:T(8,128)(2,1)S(1)}, bf16[2,512,128]{2,1,0:T(8,128)(2,1)S(1)}, u32[]{:S(2)}, u32[]{:S(2)}) collective-permute-start(bf16[2,512,128]{2,1,0:T(8,128)(2,1)S(1)} %get-tuple-element.58), channel_id=1, source_target_pairs={{0,24},{4,28},{8,16},{12,20},{16,8},{20,12},{24,0},{28,4},{1,25},{... | collective-permute-start | bytes 786440 | tf_op jit(solution)/shard_map/ppermute | solution.py:1023
  25.7 13.1 %collective-permute-start.8 = (bf16[2,512,128]{2,1,0:T(8,128)(2,1)S(1)}, bf16[2,512,128]{2,1,0:T(8,128)(2,1)S(1)}, u32[]{:S(2)}, u32[]{:S(2)}) collective-permute-start(bf16[2,512,128]{2,1,0:T(8,128)(2,1)S(1)} %get-tuple-element.56), channel_id=1, source_target_pairs={{0,8},{4,12},{8,0},{12,4},{16,24},{20,28},{24,16},{28,20},{1,9},{5... | collective-permute-start | bytes 786440 | tf_op jit(solution)/shard_map/ppermute | solution.py:1023
  26.8 12.6 %copy-start.7 = (bf16[512,128]{1,0:T(8,128)(2,1)S(1)}, bf16[512,128]{1,0:T(8,128)(2,1)}, u32[]{:S(2)}) copy-start(bf16[512,128]{1,0:T(8,128)(2,1)} %get-tuple-element.53.stay) | copy-start | bytes 393220
  26.8 12.6 %copy-start.9 = (bf16[256,768]{1,0:T(8,128)(2,1)S(1)}, bf16[256,768]{1,0:T(8,128)(2,1)}, u32[]{:S(2)}) copy-start(bf16[256,768]{1,0:T(8,128)(2,1)} %constant.81.clone.refs_6_) | copy-start | bytes 1179652
  26.8 12.6 %collective-permute-start.9 = (bf16[2,512,128]{2,1,0:T(8,128)(2,1)S(1)}, bf16[2,512,128]{2,1,0:T(8,128)(2,1)S(1)}, u32[]{:S(2)}, u32[]{:S(2)}) collective-permute-start(bf16[2,512,128]{2,1,0:T(8,128)(2,1)S(1)} %get-tuple-element.57), channel_id=1, source_target_pairs={{0,16},{4,20},{8,24},{12,28},{16,0},{20,4},{24,8},{28,12},{1,17},{... | collective-permute-start | bytes 786440 | tf_op jit(solution)/shard_map/ppermute | solution.py:1023
  27.6 25.3 %collective-permute-start.5 = (bf16[256,1024]{1,0:T(8,128)(2,1)}, bf16[256,1024]{1,0:T(8,128)(2,1)}, u32[]{:S(2)}, u32[]{:S(2)}) collective-permute-start(bf16[256,1024]{1,0:T(8,128)(2,1)} %get-tuple-element.49), channel_id=1, source_target_pairs={{0,1},{1,2},{2,3},{3,0},{4,7},{5,4},{6,5},{7,6},{8,9},{9,10},{10,1... | collective-permute-start | bytes 1572872 | tf_op jit(solution)/shard_map/ppermute | solution.py:732
  29.2 23.7 %collective-permute-start.6 = (bf16[128,1024]{1,0:T(8,128)(2,1)}, bf16[128,1024]{1,0:T(8,128)(2,1)S(1)}, u32[]{:S(2)}, u32[]{:S(2)}) collective-permute-start(bf16[128,1024]{1,0:T(8,128)(2,1)} %get-tuple-element.50), channel_id=1, source_target_pairs={{0,2},{1,3},{2,0},{3,1},{4,6},{5,7},{6,4},{7,5},{8,10},{9,11},{10,... | collective-permute-start | bytes 786440 | tf_op jit(solution)/shard_map/ppermute | solution.py:732
  52.9 5.8 %copy-start.11 = (bf16[128,1024]{1,0:T(8,128)(2,1)}, bf16[128,1024]{1,0:T(8,128)(2,1)S(1)}, u32[]{:S(2)}) copy-start(bf16[128,1024]{1,0:T(8,128)(2,1)S(1)} %collective-permute-done.6) | copy-start | bytes 786436
  53.0 9.0 %copy-start.1 = (bf16[512,1024]{1,0:T(8,128)(2,1)S(1)}, bf16[512,1024]{1,0:T(8,128)(2,1)}, u32[]{:S(2)}) copy-start(bf16[512,1024]{1,0:T(8,128)(2,1)} %query.3) | copy-start | bytes 3145732
  53.0 9.0 %copy-start.4 = (f32[3,3,1024]{2,1,0:T(4,128)S(1)}, f32[3,3,1024]{2,1,0:T(4,128)}, u32[]{:S(2)}) copy-start(f32[3,3,1024]{2,1,0:T(4,128)} %weight.7) | copy-start | bytes 110596
  53.0 9.0 %copy-start.6 = (bf16[6,1024]{1,0:T(8,128)(2,1)S(1)}, bf16[6,1024]{1,0:T(8,128)(2,1)}, u32[]{:S(2)}) copy-start(bf16[6,1024]{1,0:T(8,128)(2,1)} %copy-done.5) | copy-start | bytes 36868
  53.1 2.0 %collective-permute-start.11 = (bf16[4,512,128]{2,1,0:T(8,128)(2,1)S(1)}, bf16[4,512,128]{2,1,0:T(8,128)(2,1)S(1)}, u32[]{:S(2)}, u32[]{:S(2)}) collective-permute-start(bf16[4,512,128]{2,1,0:T(8,128)(2,1)S(1)} %get-tuple-element.60), channel_id=1, source_target_pairs={{0,4},{4,0},{8,12},{12,8},{16,20},{20,16},{24,28},{28,24},{1,5},{5... | collective-permute-start | bytes 1572872 | tf_op jit(solution)/shard_map/ppermute | solution.py:1021
  55.2 9.2 %collective-permute-start.12 = (bf16[2,512,128]{2,1,0:T(8,128)(2,1)S(1)}, bf16[2,512,128]{2,1,0:T(8,128)(2,1)S(1)}, u32[]{:S(2)}, u32[]{:S(2)}) collective-permute-start(bf16[2,512,128]{2,1,0:T(8,128)(2,1)S(1)} %get-tuple-element.62), channel_id=1, source_target_pairs={{0,8},{4,12},{8,0},{12,4},{16,24},{20,28},{24,16},{28,20},{1,9},{5... | collective-permute-start | bytes 786440 | tf_op jit(solution)/shard_map/ppermute | solution.py:1023
  55.9 12.9 %collective-permute-start.13 = (bf16[2,512,128]{2,1,0:T(8,128)(2,1)S(1)}, bf16[2,512,128]{2,1,0:T(8,128)(2,1)S(1)}, u32[]{:S(2)}, u32[]{:S(2)}) collective-permute-start(bf16[2,512,128]{2,1,0:T(8,128)(2,1)S(1)} %get-tuple-element.63), channel_id=1, source_target_pairs={{0,16},{4,20},{8,24},{12,28},{16,0},{20,4},{24,8},{28,12},{1,17},{... | collective-permute-start | bytes 786440 | tf_op jit(solution)/shard_map/ppermute | solution.py:1023
  57.4 12.4 %collective-permute-start.14 = (bf16[2,512,128]{2,1,0:T(8,128)(2,1)S(1)}, bf16[2,512,128]{2,1,0:T(8,128)(2,1)S(1)}, u32[]{:S(2)}, u32[]{:S(2)}) collective-permute-start(bf16[2,512,128]{2,1,0:T(8,128)(2,1)S(1)} %get-tuple-element.64), channel_id=1, source_target_pairs={{0,24},{4,28},{8,16},{12,20},{16,8},{20,12},{24,0},{28,4},{1,25},{... | collective-permute-start | bytes 786440 | tf_op jit(solution)/shard_map/ppermute | solution.py:1023
  60.0 19.7 %slice-start = ((s8[8388608]{0:T(1024)(128)(4,1)}), s8[4194304]{0:T(1024)(128)(4,1)S(1)}, s32[]{:S(2)}) async-start(s8[8388608]{0:T(1024)(128)(4,1)} %bitcast.27), calls=%async_computation | async-start | bytes 8388608
  69.7 10.0 %slice-start.1 = ((s8[8388608]{0:T(1024)(128)(4,1)}), s8[4194304]{0:T(1024)(128)(4,1)S(1)}, s32[]{:S(2)}) async-start(s8[8388608]{0:T(1024)(128)(4,1)} %bitcast.27), calls=%async_computation.1 | async-start | bytes 8388608
  71.3 2.9 %collective-permute-start.16 = (bf16[2,256,1024]{2,1,0:T(8,128)(2,1)S(1)}, bf16[2,256,1024]{2,1,0:T(8,128)(2,1)S(1)}, u32[]{:S(2)}, u32[]{:S(2)}) collective-permute-start(bf16[2,256,1024]{2,1,0:T(8,128)(2,1)S(1)} %get-tuple-element.65.mine.head), channel_id=1, source_target_pairs={{0,4},{4,0},{8,12},{12,8},{16,20},{20,16},{24,28},{28,24},{1,5},{5... | collective-permute-start | bytes 3145736 | tf_op jit(solution)/shard_map/ppermute | solution.py:977
  71.4 12.0 %collective-permute-start.15 = (bf16[256,1024]{1,0:T(8,128)(2,1)S(1)}, bf16[256,1024]{1,0:T(8,128)(2,1)S(1)}, u32[]{:S(2)}, u32[]{:S(2)}) collective-permute-start(bf16[256,1024]{1,0:T(8,128)(2,1)S(1)} %get-tuple-element.66), channel_id=1, source_target_pairs={{0,1},{1,2},{2,3},{5,4},{6,5},{7,6},{8,9},{9,10},{10,11},{13,12},{... | collective-permute-start | bytes 1572872 | tf_op jit(solution)/shard_map/ppermute | solution.py:976
  75.5 12.9 %collective-permute-start.18 = (bf16[256,1024]{1,0:T(8,128)(2,1)S(1)}, bf16[256,1024]{1,0:T(8,128)(2,1)S(1)}, u32[]{:S(2)}, u32[]{:S(2)}) collective-permute-start(bf16[256,1024]{1,0:T(8,128)(2,1)S(1)} %partner_sent.1), channel_id=1, source_target_pairs={{0,1},{1,2},{2,3},{5,4},{6,5},{7,6},{8,9},{9,10},{10,11},{13,12},{... | collective-permute-start | bytes 1572872 | tf_op jit(solution)/shard_map/ppermute | solution.py:976
  78.3 15.5 %collective-permute-start.20 = (bf16[256,1024]{1,0:T(8,128)(2,1)}, bf16[256,1024]{1,0:T(8,128)(2,1)S(1)}, u32[]{:S(2)}, u32[]{:S(2)}) collective-permute-start(bf16[256,1024]{1,0:T(8,128)(2,1)} %collective-permute-done.5), channel_id=1, source_target_pairs={{0,8},{4,20},{8,0},{12,28},{16,24},{20,4},{24,16},{28,12},{1,9},{5... | collective-permute-start | bytes 1572872 | tf_op jit(solution)/shard_map/ppermute | solution.py:768
  84.1 7.6 %copy-start.12 = (bf16[128,1024]{1,0:T(8,128)(2,1)S(1)}, bf16[128,1024]{1,0:T(8,128)(2,1)}, u32[]{:S(2)}) copy-start(bf16[128,1024]{1,0:T(8,128)(2,1)} %copy-done.11) | copy-start | bytes 786436
  84.1 11.0 %collective-permute-start.17 = (bf16[256,1024]{1,0:T(8,128)(2,1)S(1)}, bf16[256,1024]{1,0:T(8,128)(2,1)S(1)}, u32[]{:S(2)}, u32[]{:S(2)}) collective-permute-start(bf16[256,1024]{1,0:T(8,128)(2,1)S(1)} %next_step.6), channel_id=1, source_target_pairs={{0,1},{1,2},{2,3},{5,4},{6,5},{7,6},{8,9},{9,10},{10,11},{13,12},{... | collective-permute-start | bytes 1572872 | tf_op jit(solution)/shard_map/ppermute | solution.py:976
  89.1 15.2 %collective-permute-start.19 = (bf16[256,1024]{1,0:T(8,128)(2,1)S(1)}, bf16[256,1024]{1,0:T(8,128)(2,1)S(1)}, u32[]{:S(2)}, u32[]{:S(2)}) collective-permute-start(bf16[256,1024]{1,0:T(8,128)(2,1)S(1)} %next_step.7), channel_id=1, source_target_pairs={{0,1},{1,2},{2,3},{5,4},{6,5},{7,6},{8,9},{9,10},{10,11},{13,12},{... | collective-permute-start | bytes 1572872 | tf_op jit(solution)/shard_map/ppermute | solution.py:976
  91.6 9.3 %collective-permute-start.23 = (bf16[128,1024]{1,0:T(8,128)(2,1)S(1)}, bf16[128,1024]{1,0:T(8,128)(2,1)S(1)}, u32[]{:S(2)}, u32[]{:S(2)}) collective-permute-start(bf16[128,1024]{1,0:T(8,128)(2,1)S(1)} %copy-done.12), channel_id=1, source_target_pairs={{0,8},{4,20},{8,0},{12,28},{16,24},{20,4},{24,16},{28,12},{1,9},{5... | collective-permute-start | bytes 786440 | tf_op jit(solution)/shard_map/ppermute | solution.py:768
  93.0 14.7 %collective-permute-start.21 = (bf16[256,1024]{1,0:T(8,128)(2,1)}, bf16[256,1024]{1,0:T(8,128)(2,1)S(1)}, u32[]{:S(2)}, u32[]{:S(2)}) collective-permute-start(bf16[256,1024]{1,0:T(8,128)(2,1)} %collective-permute-done.5), channel_id=1, source_target_pairs={{0,16},{4,12},{8,24},{12,4},{16,0},{20,28},{24,8},{28,20},{1,17},{... | collective-permute-start | bytes 1572872 | tf_op jit(solution)/shard_map/ppermute | solution.py:769
  93.9 14.2 %collective-permute-start.22 = (bf16[256,1024]{1,0:T(8,128)(2,1)S(1)}, bf16[256,1024]{1,0:T(8,128)(2,1)S(1)}, u32[]{:S(2)}, u32[]{:S(2)}) collective-permute-start(bf16[256,1024]{1,0:T(8,128)(2,1)S(1)} %collective-permute-done.20), channel_id=1, source_target_pairs={{0,16},{4,12},{8,24},{12,4},{16,0},{20,28},{24,8},{28,20},{1,17},{... | collective-permute-start | bytes 1572872 | tf_op jit(solution)/shard_map/ppermute | solution.py:769
  95.1 16.9 %collective-permute-start.24 = (bf16[128,1024]{1,0:T(8,128)(2,1)S(1)}, bf16[128,1024]{1,0:T(8,128)(2,1)S(1)}, u32[]{:S(2)}, u32[]{:S(2)}) collective-permute-start(bf16[128,1024]{1,0:T(8,128)(2,1)S(1)} %copy-done.12), channel_id=1, source_target_pairs={{0,16},{4,12},{8,24},{12,4},{16,0},{20,28},{24,8},{28,20},{1,17},{... | collective-permute-start | bytes 786440 | tf_op jit(solution)/shard_map/ppermute | solution.py:769
  100.9 12.8 %collective-permute-start.28 = (bf16[256,1024]{1,0:T(8,128)(2,1)S(1)}, bf16[256,1024]{1,0:T(8,128)(2,1)S(1)}, u32[]{:S(2)}, u32[]{:S(2)}) collective-permute-start(bf16[256,1024]{1,0:T(8,128)(2,1)S(1)} %next_step.8), channel_id=1, source_target_pairs={{0,1},{1,2},{2,3},{5,4},{6,5},{7,6},{8,9},{9,10},{10,11},{13,12},{... | collective-permute-start | bytes 1572872 | tf_op jit(solution)/shard_map/ppermute | solution.py:976
  104.3 9.4 %collective-permute-start.25 = (bf16[128,1024]{1,0:T(8,128)(2,1)S(1)}, bf16[128,1024]{1,0:T(8,128)(2,1)S(1)}, u32[]{:S(2)}, u32[]{:S(2)}) collective-permute-start(bf16[128,1024]{1,0:T(8,128)(2,1)S(1)} %collective-permute-done.23), channel_id=1, source_target_pairs={{0,16},{4,12},{8,24},{12,4},{16,0},{20,28},{24,8},{28,20},{1,17},{... | collective-permute-start | bytes 786440 | tf_op jit(solution)/shard_map/ppermute | solution.py:769
  107.7 15.9 %collective-permute-start.26 = (bf16[2,128,1024]{2,1,0:T(8,128)(2,1)S(1)}, bf16[2,128,1024]{2,1,0:T(8,128)(2,1)S(1)}, u32[]{:S(2)}, u32[]{:S(2)}) collective-permute-start(bf16[2,128,1024]{2,1,0:T(8,128)(2,1)S(1)} %pad_maximum_fusion.2.refs_2_.refs_0_), channel_id=1, source_target_pairs={{0,4},{4,0},{8,12},{12,8},{16,20},{20,16},{24,28},{28,24},{1,5},{5... | collective-permute-start | bytes 1572872 | tf_op jit(solution)/shard_map/ppermute | solution.py:977
  108.0 10.5 %collective-permute-start.32 = (bf16[256,1024]{1,0:T(8,128)(2,1)S(1)}, bf16[256,1024]{1,0:T(8,128)(2,1)S(1)}, u32[]{:S(2)}, u32[]{:S(2)}) collective-permute-start(bf16[256,1024]{1,0:T(8,128)(2,1)S(1)} %next_step.10), channel_id=1, source_target_pairs={{0,1},{1,2},{2,3},{5,4},{6,5},{7,6},{8,9},{9,10},{10,11},{13,12},{... | collective-permute-start | bytes 1572872 | tf_op jit(solution)/shard_map/ppermute | solution.py:976
  112.0 17.8 %collective-permute-start.30 = (bf16[2,256,1024]{2,1,0:T(8,128)(2,1)S(1)}, bf16[2,256,1024]{2,1,0:T(8,128)(2,1)S(1)}, u32[]{:S(2)}, u32[]{:S(2)}) collective-permute-start(bf16[2,256,1024]{2,1,0:T(8,128)(2,1)S(1)} %pad_maximum_fusion.refs_0_), channel_id=1, source_target_pairs={{0,4},{4,0},{8,12},{12,8},{16,20},{20,16},{24,28},{28,24},{1,5},{5... | collective-permute-start | bytes 3145736 | tf_op jit(solution)/shard_map/ppermute | solution.py:977
  113.7 21.5 %collective-permute-start.31 = (bf16[2,256,1024]{2,1,0:T(8,128)(2,1)S(1)}, bf16[2,256,1024]{2,1,0:T(8,128)(2,1)S(1)}, u32[]{:S(2)}, u32[]{:S(2)}) collective-permute-start(bf16[2,256,1024]{2,1,0:T(8,128)(2,1)S(1)} %pad_maximum_fusion.1.refs_1_), channel_id=1, source_target_pairs={{0,4},{4,0},{8,12},{12,8},{16,20},{20,16},{24,28},{28,24},{1,5},{5... | collective-permute-start | bytes 3145736 | tf_op jit(solution)/shard_map/ppermute | solution.py:977
  113.7 13.6 %collective-permute-start.27 = (bf16[2,128,1024]{2,1,0:T(8,128)(2,1)S(1)}, bf16[2,128,1024]{2,1,0:T(8,128)(2,1)S(1)}, u32[]{:S(2)}, u32[]{:S(2)}) collective-permute-start(bf16[2,128,1024]{2,1,0:T(8,128)(2,1)S(1)} %pad_maximum_fusion.3.refs_3_.refs_1_), channel_id=1, source_target_pairs={{0,4},{4,0},{8,12},{12,8},{16,20},{20,16},{24,28},{28,24},{1,5},{5... | collective-permute-start | bytes 1572872 | tf_op jit(solution)/shard_map/ppermute | solution.py:977
  118.5 11.2 %collective-permute-start.29 = (bf16[256,1024]{1,0:T(8,128)(2,1)S(1)}, bf16[256,1024]{1,0:T(8,128)(2,1)S(1)}, u32[]{:S(2)}, u32[]{:S(2)}) collective-permute-start(bf16[256,1024]{1,0:T(8,128)(2,1)S(1)} %next_step.9), channel_id=1, source_target_pairs={{0,1},{1,2},{2,3},{5,4},{6,5},{7,6},{8,9},{9,10},{10,11},{13,12},{... | collective-permute-start | bytes 1572872 | tf_op jit(solution)/shard_map/ppermute | solution.py:976
  123.6 11.6 %collective-permute-start.33 = (bf16[256,1024]{1,0:T(8,128)(2,1)S(1)}, bf16[256,1024]{1,0:T(8,128)(2,1)S(1)}, u32[]{:S(2)}, u32[]{:S(2)}) collective-permute-start(bf16[256,1024]{1,0:T(8,128)(2,1)S(1)} %next_step.11), channel_id=1, source_target_pairs={{0,1},{1,2},{2,3},{5,4},{6,5},{7,6},{8,9},{9,10},{10,11},{13,12},{... | collective-permute-start | bytes 1572872 | tf_op jit(solution)/shard_map/ppermute | solution.py:976
  136.1 2.7 %collective-permute-start.34 = (bf16[2,256,1024]{2,1,0:T(8,128)(2,1)S(1)}, bf16[2,256,1024]{2,1,0:T(8,128)(2,1)S(1)}, u32[]{:S(2)}, u32[]{:S(2)}) collective-permute-start(bf16[2,256,1024]{2,1,0:T(8,128)(2,1)S(1)} %partner_sum.1), channel_id=1, source_target_pairs={{0,4},{4,0},{8,12},{12,8},{16,20},{20,16},{24,28},{28,24},{1,5},{5... | collective-permute-start | bytes 3145736 | tf_op jit(solution)/shard_map/ppermute | solution.py:977
  (2 other events, 5.9 us)

commit v6 on v5

--- a/solution.py
+++ b/solution.py
@@ -761,40 +761,35 @@
     )(corners, out_weight)
 
 
-def gather_weight(part):
+def swap_weight(part):
     devices = range(lax.axis_size("ctx"))
-    near = [(i, i ^ (4 if i & 1 else 2)) for i in devices]
+    return lax.ppermute(part, "ctx", [(i, i ^ (4 if i & 1 else 2)) for i in devices])
+
+
+def gather_weight(two, ready):
+    devices = range(lax.axis_size("ctx"))
     other = [(i, i ^ (2 if i & 1 else 4)) for i in devices]
-    two = [part, lax.ppermute(part, "ctx", near)]
-    return jnp.stack(two), jnp.stack([lax.ppermute(x, "ctx", other) for x in two])
-
-
-def pairs_of(refs):
-    return list(zip(refs[::2], refs[1::2]))
-
-
-def spots(first, pair):
-    return (first, pair[0]), (first + 2, pair[1])
-
-
-def add_parts(order, data, *weights):
-    total = None
-    for first, weight in weights:
-        count, lanes, columns = weight.shape
-        picked = []
-        for q in range(count):
-            index = order[first + q]
-            index = index // 2 if lanes == 2 * SUB else index
-            picked.append(data[:, pl.ds(pl.multiple_of(index * lanes, lanes), lanes)])
-        block = weight[...].reshape(count * lanes, columns)
-        picked = jnp.concatenate(picked, axis=1)
-        term = jnp.dot(picked, block, preferred_element_type=F32)
-        total = term if total is None else total + term
-    return total
+    near = [*two, *[lax.ppermute(x, "ctx", other) for x in two]]
+    apart = near[:2] + after(near[2:], ready)
+    return near + [lax.ppermute(x, "ctx", [(i, i ^ 1) for i in devices]) for x in apart]
+
+
+def add_parts(order, data, parts, hops):
+    chans = data.shape[1]
+    if hops == 2:
+        rows, row, chosen = chans // 8, chans // 4, range(8)
+    else:
+        rows, row, chosen = chans // 4, 0, range(4) if hops == 1 else range(4, 8)
+    picked = []
+    for q in chosen:
+        index = order[q] if hops == 2 else order[q] // 2
+        picked.append(data[:, pl.ds(pl.multiple_of(index * rows, rows), rows)])
+    block = jnp.concatenate([parts[q][row : row + rows, :] for q in chosen], axis=0)
+    return jnp.dot(jnp.concatenate(picked, axis=1), block, preferred_element_type=F32)
 
 
 def early_kernel(order, mine, got0, got1, partner0, partner1, weight, *refs):
-    (near, near2, far2), (out, own, first, own_weight, sem) = pairs_of(refs[:6]), refs[6:]
+    parts, (out, own, first, own_weight, sem) = refs[:8], refs[8:]
     turn_count = order[8]
     rows, chans = got0.shape
     columns = pl.ds(pl.multiple_of(order[9] * chans, chans), chans)
@@ -813,7 +808,7 @@
 
     @pl.when(turn_count >= 1)
     def _():
-        out[...] = add_parts(order, first, *spots(0, near))
+        out[...] = add_parts(order, first, parts, 1)
 
     @pl.when(turn_count < 1)
     def _():
@@ -823,7 +818,7 @@
     def _():
         first[:rows, :] = got1[...]
         first[rows:, :] = partner1[...]
-        out[...] += add_parts(order, first, *spots(0, near2), *spots(4, far2))
+        out[...] += add_parts(order, first, parts, 2)
 
     copy.wait()
     out[:rows, :] += jnp.dot(mine[0], own_weight[...], preferred_element_type=F32)
@@ -854,7 +849,7 @@
             jax.ShapeDtypeStruct((rows, chans), F32),
         ],
         compiler_params=grant(24),
-        cost_estimate=cost(5),
+        cost_estimate=cost(1),
         name="early_sum",
     )(order, mine, *arrivals, out_weight, *weights)
 
@@ -868,18 +863,18 @@
 
     @pl.when(behind == 2)
     def _():
-        total[...] = early[...] + add_parts(order, got2, *spots(0, weights[0]), *spots(4, weights[1]))
+        total[...] = early[...] + add_parts(order, got2, weights, 2)
 
     @pl.when(behind == 3)
     def _():
-        total[...] = early[...] + add_parts(order, got3, *spots(4, weights[2]))
+        total[...] = early[...] + add_parts(order, got3, weights, 3)
 
     summed = jnp.where(behind == 3, got2[...].astype(F32), got3[...].astype(F32))
     return jnp.where(behind == 0, 0.0, summed)
 
 
 def partner_kernel(order, early, got2, got3, *refs):
-    weights, (out, total) = pairs_of(refs[:6]), refs[6:]
+    weights, (out, total) = refs[:8], refs[8:]
     out[1] = late_sum(order, early, got2, got3, weights, total).astype(BF16)
     out[0] = total[...].astype(BF16)
 
@@ -906,7 +901,7 @@
 
 
 def mine_kernel(order, early, own, got2, got3, *refs):
-    weights, (out, total) = pairs_of(refs[:6]), refs[6:]
+    weights, (out, total) = refs[:8], refs[8:]
     rows = early.shape[0]
     out[rows:, :] = late_sum(order, early, got2, got3, weights, total) + own[...]
     out[:rows, :] = total[...]
@@ -979,6 +974,8 @@
     partner_first = partner_sent(spot, partners, far_weight)
     got = [[onward(sent), onward(partner_first)]]
     terms = sent_terms(plan, mine, partners, out_weight)
+    weight_part = after(jnp.concatenate(weight_parts), partner_first)
+    weight_two = [weight_part, swap_weight(weight_part)]
     steps = []
     for step in range(1, stages):
         row = []
@@ -987,13 +984,11 @@
         steps.append(row)
         got.append([onward(x) for x in row])
 
-    near, near2 = (gather_weight(part) for part in after(weight_parts, partner_first))
-    far2, far = ([core_swap(x) for x in pair] for pair in (near2, near))
+    weights = gather_weight(weight_two, steps[2][0])
     arrivals = [got[0][0], got[1][0], got[0][1], got[1][1]]
-    early, own = early_sum(order, mine, arrivals, out_weight, (*near, *near2, *far2))
-    late = (*near2, *far2, *far)
-    theirs = partner_sum(after(order, got[3][0]), early, [got[2][1], got[3][1]], late)
-    ours = mine_sum(order, early, own, [got[2][0], got[3][0]], late)
+    early, own = early_sum(order, mine, arrivals, out_weight, weights)
+    theirs = partner_sum(after(order, got[3][0]), early, [got[2][1], got[3][1]], weights)
+    ours = mine_sum(order, early, own, [got[2][0], got[3][0]], weights)
     return join_sums(ours, core_swap(theirs))
 
 

time: 141 us -> 135 us (0.957)
  waiting for transfers between devices: 29.5 us -> 26.5 us
  starting transfers between devices: 57.4 us -> 54.9 us
    ppermute x6 -> x7, waiting for transfers between devices: 6.03 us -> 0.02 us  [the longest x4 0.01 us: gather_weight(): lax.ppermute(x, 'ctx', [(i, i ^ 1) for i in devices])]
    ppermute x8, waiting for transfers between devices: 9.03 us -> 11.7 us  [project(): onward = lambda x: lax.ppermute(x, ('ctx', 'tp'), route)]
    ppermute x6 -> x7, starting transfers between devices: 7.28 us -> 4.7 us  [the longest x2 2.09 us: gather_weight(): near = [*two, *[lax.ppermute(x, 'ctx', other) for x in two]]]
  transfers between devices with their start and end apart: 35 -> 32, of which waited for: 14 -> 12; matrix products, arithmetic and copies ran while one was open for 4% -> 4% of each run, Pallas kernels for 28% -> 30%
where the time goes in v6:
time: 135 us; the launch traced here: 134 us
  starting transfers between devices  54.9 us (41%)
  Pallas kernels  45.3 us (34%)
  waiting for transfers between devices  26.5 us (20%)
  local copies, waits for them, and re-layouts  3.8 us (3%)
  other arithmetic  2.55 us (2%)
    ppermute x8, starting transfers between devices, project(): onward = lambda x: lax.ppermute(x, ('ctx', 'tp'), route)  28.9 us
    ppermute x9, starting transfers between devices, fast_per_device(): lax.ppermute(x, 'ctx', [(i, i ^ 2 * q + 2) for i in devices])  14.4 us
    pallas_call x1, Pallas kernels, long_conv(): pl.pallas_call(partial(conv_kernel, blocks), out_shape=jax.ShapeDtypeStru...  13.6 us
    ppermute x8, waiting for transfers between devices, project(): onward = lambda x: lax.ppermute(x, ('ctx', 'tp'), route)  11.7 us
    ppermute x9, waiting for transfers between devices, fast_per_device(): lax.ppermute(x, 'ctx', [(i, i ^ 2 * q + 2) for i in devices])  11 us
    pallas_call x1, Pallas kernels, taps_spectra_of(): pl.pallas_call(partial(taps_kernel, chips), out_shape=jax.ShapeDtypeStruc...  5.94 us
    pallas_call x1, Pallas kernels, gate_in(): pl.pallas_call(gate_in_kernel, in_specs=[SMEM, HBM, HBM, VMEM, VMEM], out...  4.26 us
    ppermute x2, starting transfers between devices, turn_weight(): found.append(lax.ppermute(part, ('ctx', 'tp'), route))  4.17 us
  transfers between devices with their start and end apart: 32, of which 12 were waited for; matrix products, arithmetic and copies ran while one was open for 4% of the time, Pallas kernels for 30%

profile of v6, /device:TPU:0, one launch (start us, length us, event | category | flops | bytes accessed | tf_op | source)
XLA Modules:
  0.0 134.2 jit_solution(6779170872187021246)
XLA Ops:
  0.0 1.5 %rims.1 = bf16[6,1024]{1,0:T(8,128)(2,1)} custom-call(bf16[512,1024]{1,0:T(8,128)(2,1)} %query.3, bf16[512,1024]{1,0:T(8,128)(2,1)} %key.3, bf16[512,1024]{1,0:T(8,128)(2,1)} %value.3), custom_call_target="tpu_custom_call" | custom-call | tf_op jit(solution)/shard_map/rims/pallas_call | solution.py:428
  1.5 2.4 %collective-permute-start = (bf16[6,1024]{1,0:T(8,128)(2,1)}, bf16[6,1024]{1,0:T(8,128)(2,1)S(1)}, u32[]{:S(2)}, u32[]{:S(2)}) collective-permute-start(bf16[6,1024]{1,0:T(8,128)(2,1)} %rims.1), channel_id=1, source_target_pairs={{0,4},{4,8},{8,12},{12,16},{16,20},{20,24},{24,28},{1,5},{5,9},{9,... | collective-permute-start | bytes 36872 | tf_op jit(solution)/shard_map/ppermute | solution.py:18
  5.1 4.9 %collective-permute-start.1 = (bf16[256,512]{1,0:T(8,128)(2,1)S(1)}, bf16[256,512]{1,0:T(8,128)(2,1)S(1)}, u32[]{:S(2)}, u32[]{:S(2)}) collective-permute-start(bf16[256,512]{1,0:T(8,128)(2,1)S(1)} %get-tuple-element.47), channel_id=1, source_target_pairs={{0,8},{4,12},{8,0},{12,4},{16,24},{20,28},{24,16},{28,20},{1,9},{5... | collective-permute-start | bytes 786440 | tf_op jit(solution)/shard_map/ppermute | solution.py:1018
  10.0 1.5 %collective-permute-start.2 = (bf16[256,512]{1,0:T(8,128)(2,1)S(1)}, bf16[256,512]{1,0:T(8,128)(2,1)S(1)}, u32[]{:S(2)}, u32[]{:S(2)}) collective-permute-start(bf16[256,512]{1,0:T(8,128)(2,1)S(1)} %get-tuple-element.48), channel_id=1, source_target_pairs={{0,16},{4,20},{8,24},{12,28},{16,0},{20,4},{24,8},{28,12},{1,17},{... | collective-permute-start | bytes 786440 | tf_op jit(solution)/shard_map/ppermute | solution.py:1018
  11.5 0.9 collective-permute-start.3
  13.0 2.7 %weight_corners.1 = (bf16[256,1024]{1,0:T(8,128)(2,1)}, bf16[128,1024]{1,0:T(8,128)(2,1)}) custom-call(s32[4]{0:T(128)} %pad_add_fusion.1.corners, bf16[1024,4096]{1,0:T(8,128)(2,1)} %weight.9), custom_call_target="tpu_custom_call" | custom-call | tf_op jit(solution)/shard_map/weight_corners/pallas_call | solution.py:753
  15.7 4.3 %gate_in.1 = (bf16[512,128]{1,0:T(8,128)(2,1)}, bf16[3,512,128]{2,1,0:T(8,128)(2,1)}, bf16[4,512,128]{2,1,0:T(8,128)(2,1)}) custom-call(s32[1]{0:T(128)} %bitcast.me_ref, bf16[512,1024]{1,0:T(8,128)(2,1)} %key.3, bf16[512,1024]{1,0:T(8,128)(2,1)} %value.3, bf16[6,1024]{1,0:T(8,128)(2,1)} %copy-done.5, f32[3,3,1024]{2,1,0:T(4,128)} %weight.7), custom_call_target="tpu_custom_call" | custom-call | tf_op jit(solution)/shard_map/gate_in/pallas_call | solution.py:479
  20.1 2.7 %collective-permute-done.2.refs_2_ = bf16[256,512]{1,0:T(8,128)(2,1)S(1)} collective-permute-done((bf16[256,512]{1,0:T(8,128)(2,1)S(1)}, bf16[256,512]{1,0:T(8,128)(2,1)S(1)}, u32[]{:S(2)}, u32[]{:S(2)}) %collective-permute-start.2) | collective-permute-done | bytes 262176 | tf_op jit(solution)/shard_map/ppermute | solution.py:1018
  23.0 1.0 copy-done.3
  24.7 1.5 %collective-permute-start.9 = (bf16[2,512,128]{2,1,0:T(8,128)(2,1)S(1)}, bf16[2,512,128]{2,1,0:T(8,128)(2,1)S(1)}, u32[]{:S(2)}, u32[]{:S(2)}) collective-permute-start(bf16[2,512,128]{2,1,0:T(8,128)(2,1)S(1)} %get-tuple-element.58), channel_id=1, source_target_pairs={{0,16},{4,20},{8,24},{12,28},{16,0},{20,4},{24,8},{28,12},{1,17},{... | collective-permute-start | bytes 786440 | tf_op jit(solution)/shard_map/ppermute | solution.py:1018
  26.2 1.4 %collective-permute-start.10 = (bf16[2,512,128]{2,1,0:T(8,128)(2,1)S(1)}, bf16[2,512,128]{2,1,0:T(8,128)(2,1)S(1)}, u32[]{:S(2)}, u32[]{:S(2)}) collective-permute-start(bf16[2,512,128]{2,1,0:T(8,128)(2,1)S(1)} %get-tuple-element.59), channel_id=1, source_target_pairs={{0,24},{4,28},{8,16},{12,20},{16,8},{20,12},{24,0},{28,4},{1,25},{... | collective-permute-start | bytes 786440 | tf_op jit(solution)/shard_map/ppermute | solution.py:1018
  27.6 2.6 %collective-permute-start.6 = (bf16[128,1024]{1,0:T(8,128)(2,1)}, bf16[128,1024]{1,0:T(8,128)(2,1)S(1)}, u32[]{:S(2)}, u32[]{:S(2)}) collective-permute-start(bf16[128,1024]{1,0:T(8,128)(2,1)} %get-tuple-element.51), channel_id=1, source_target_pairs={{0,2},{1,3},{2,0},{3,1},{4,6},{5,7},{6,4},{7,5},{8,10},{9,11},{10,... | collective-permute-start | bytes 786440 | tf_op jit(solution)/shard_map/ppermute | solution.py:732
  30.2 1.6 %collective-permute-start.5 = (bf16[256,1024]{1,0:T(8,128)(2,1)}, bf16[256,1024]{1,0:T(8,128)(2,1)}, u32[]{:S(2)}, u32[]{:S(2)}) collective-permute-start(bf16[256,1024]{1,0:T(8,128)(2,1)} %get-tuple-element.50), channel_id=1, source_target_pairs={{0,1},{1,2},{2,3},{3,0},{4,7},{5,4},{6,5},{7,6},{8,9},{9,10},{10,1... | collective-permute-start | bytes 1572872 | tf_op jit(solution)/shard_map/ppermute | solution.py:732
  31.8 5.9 %taps_spectra.1.refs_3_ = f32[17,256,256]{2,1,0:T(8,128)S(1)} custom-call(s32[1]{0:T(128)} %bitcast.me_ref, bf16[256,512]{1,0:T(8,128)(2,1)S(1)} %get-tuple-element.46.refs_0_, bf16[256,512]{1,0:T(8,128)(2,1)S(1)} %collective-permute-done.1.refs_1_, bf16[256,512]{1,0:T(8,128)(2,1)S(1)} %collective-permute-done.2.refs_2_, ...), custom_call_target="tpu_custom_call" | custom-call | flops 8000000000 | tf_op jit(solution)/shard_map/taps_spectra/pallas_call | solution.py:357
  37.8 0.9 collective-permute-done.10.refs_2_
  38.7 13.6 %long_conv.1.conv = f32[4096,128]{1,0:T(8,128)S(1)} custom-call(s32[1]{0:T(128)} %bitcast.me_ref, bf16[512,128]{1,0:T(8,128)(2,1)S(1)} %copy-done.7, bf16[4,512,128]{2,1,0:T(8,128)(2,1)S(1)} %collective-permute-done.7.swapped, bf16[2,512,128]{2,1,0:T(8,128)(2,1)S(1)} %collective-permute-done.8.refs_0_, ...), custom_call_target="tpu_custom_call" | custom-call | flops 20000000000 | tf_op jit(solution)/shard_map/long_conv/pallas_call | solution.py:376
  52.6 1.9 %collective-permute-done.11.swapped.refs_1_ = bf16[4,512,128]{2,1,0:T(8,128)(2,1)S(1)} collective-permute-done((bf16[4,512,128]{2,1,0:T(8,128)(2,1)S(1)}, bf16[4,512,128]{2,1,0:T(8,128)(2,1)S(1)}, u32[]{:S(2)}, u32[]{:S(2)}) %collective-permute-start.11) | collective-permute-done | bytes 524320 | tf_op jit(solution)/shard_map/ppermute | solution.py:1016
  54.5 1.6 %collective-permute-start.12 = (bf16[2,512,128]{2,1,0:T(8,128)(2,1)S(1)}, bf16[2,512,128]{2,1,0:T(8,128)(2,1)S(1)}, u32[]{:S(2)}, u32[]{:S(2)}) collective-permute-start(bf16[2,512,128]{2,1,0:T(8,128)(2,1)S(1)} %get-tuple-element.63), channel_id=1, source_target_pairs={{0,8},{4,12},{8,0},{12,4},{16,24},{20,28},{24,16},{28,20},{1,9},{5... | collective-permute-start | bytes 786440 | tf_op jit(solution)/shard_map/ppermute | solution.py:1018
  56.1 0.8 collective-permute-start.13
  56.9 1.2 collective-permute-start.14
  59.4 1.9 %constant_dynamic-slice_fusion.refs_6_.far_weight = bf16[1024,1024]{1,0:T(8,128)(2,1)S(1)} fusion(bf16[1024,4096]{1,0:T(8,128)(2,1)} %weight.9, s32[]{:T(128)S(6)} %select_n.62), kind=kLoop, calls=%fused_computation.5 | loop fusion | bytes 4194308 | tf_op jit(solution)/shard_map/dynamic_slice | solution.py:963
  61.3 1.1 mix_query.1.refs_5_
  62.4 1.3 collective-permute-done.12.refs_2_
  63.7 6.0 %collective-permute-done.13.refs_3_ = bf16[2,512,128]{2,1,0:T(8,128)(2,1)S(1)} collective-permute-done((bf16[2,512,128]{2,1,0:T(8,128)(2,1)S(1)}, bf16[2,512,128]{2,1,0:T(8,128)(2,1)S(1)}, u32[]{:S(2)}, u32[]{:S(2)}) %collective-permute-start.13) | collective-permute-done | bytes 262176 | tf_op jit(solution)/shard_map/ppermute | solution.py:1018
  69.8 1.6 %gate_out.1 = (bf16[2,256,1024]{2,1,0:T(8,128)(2,1)S(1)}, bf16[256,1024]{1,0:T(8,128)(2,1)S(1)}) custom-call(s32[3]{0:T(128)S(1)} %pad_add_fusion.spot, bf16[512,128]{1,0:T(8,128)(2,1)S(1)} %get-tuple-element.60.refs_0_, bf16[4,512,128]{2,1,0:T(8,128)(2,1)S(1)} %collective-permute-done.11.swapped.refs_1_, ...), custom_call_target="tpu_custom_call" | custom-call | tf_op jit(solution)/shard_map/gate_out/pallas_call | solution.py:621
  71.5 3.0 %collective-permute-start.15 = (bf16[256,1024]{1,0:T(8,128)(2,1)S(1)}, bf16[256,1024]{1,0:T(8,128)(2,1)S(1)}, u32[]{:S(2)}, u32[]{:S(2)}) collective-permute-start(bf16[256,1024]{1,0:T(8,128)(2,1)S(1)} %get-tuple-element.67), channel_id=1, source_target_pairs={{0,1},{1,2},{2,3},{5,4},{6,5},{7,6},{8,9},{9,10},{10,11},{13,12},{... | collective-permute-start | bytes 1572872 | tf_op jit(solution)/shard_map/ppermute | solution.py:971
  74.4 1.1 pad_maximum_fusion.refs_0_
  75.6 1.3 partner_sent.1
  76.8 3.1 %collective-permute-start.18 = (bf16[256,1024]{1,0:T(8,128)(2,1)S(1)}, bf16[256,1024]{1,0:T(8,128)(2,1)S(1)}, u32[]{:S(2)}, u32[]{:S(2)}) collective-permute-start(bf16[256,1024]{1,0:T(8,128)(2,1)S(1)} %partner_sent.1), channel_id=1, source_target_pairs={{0,1},{1,2},{2,3},{5,4},{6,5},{7,6},{8,9},{9,10},{10,11},{13,12},{... | collective-permute-start | bytes 1572872 | tf_op jit(solution)/shard_map/ppermute | solution.py:971
  80.0 1.5 %collective-permute-start.20 = (bf16[384,1024]{1,0:T(8,128)(2,1)S(1)}, bf16[384,1024]{1,0:T(8,128)(2,1)S(1)}, u32[]{:S(2)}, u32[]{:S(2)}) collective-permute-start(bf16[384,1024]{1,0:T(8,128)(2,1)S(1)} %pad_maximum_fusion.refs_0_), channel_id=1, source_target_pairs={{0,8},{4,20},{8,0},{12,28},{16,24},{20,4},{24,16},{28,12},{1,9},{5... | collective-permute-start | bytes 2359304 | tf_op jit(solution)/shard_map/ppermute | solution.py:766
  81.5 3.7 %sent_terms.1.term = bf16[2,2,256,1024]{3,2,1,0:T(8,128)(2,1)S(1)} custom-call(s32[5]{0:T(128)S(1)} %or_select_fusion.plan, bf16[2,256,1024]{2,1,0:T(8,128)(2,1)S(1)} %get-tuple-element.66.mine.head, bf16[2,256,1024]{2,1,0:T(8,128)(2,1)S(1)} %collective-permute-done.16.partners.gated.head, bf16[1024,4096]{1,0:T(8,128)(2,1)S(1)} %bitcast.20), custom_call_target="tpu_custom_call" | custom-call | flops 4000000000 | tf_op jit(solution)/shard_map/sent_terms/pallas_call | solution.py:702
  85.8 2.3 %collective-permute-start.17 = (bf16[256,1024]{1,0:T(8,128)(2,1)S(1)}, bf16[256,1024]{1,0:T(8,128)(2,1)S(1)}, u32[]{:S(2)}, u32[]{:S(2)}) collective-permute-start(bf16[256,1024]{1,0:T(8,128)(2,1)S(1)} %next_step.6), channel_id=1, source_target_pairs={{0,1},{1,2},{2,3},{5,4},{6,5},{7,6},{8,9},{9,10},{10,11},{13,12},{... | collective-permute-start | bytes 1572872 | tf_op jit(solution)/shard_map/ppermute | solution.py:971
  88.8 3.0 %collective-permute-start.19 = (bf16[256,1024]{1,0:T(8,128)(2,1)S(1)}, bf16[256,1024]{1,0:T(8,128)(2,1)S(1)}, u32[]{:S(2)}, u32[]{:S(2)}) collective-permute-start(bf16[256,1024]{1,0:T(8,128)(2,1)S(1)} %next_step.7), channel_id=1, source_target_pairs={{0,1},{1,2},{2,3},{5,4},{6,5},{7,6},{8,9},{9,10},{10,11},{13,12},{... | collective-permute-start | bytes 1572872 | tf_op jit(solution)/shard_map/ppermute | solution.py:971
  91.8 1.5 %collective-permute-start.21 = (bf16[384,1024]{1,0:T(8,128)(2,1)S(1)}, bf16[384,1024]{1,0:T(8,128)(2,1)S(1)}, u32[]{:S(2)}, u32[]{:S(2)}) collective-permute-start(bf16[384,1024]{1,0:T(8,128)(2,1)S(1)} %pad_maximum_fusion.refs_0_), channel_id=1, source_target_pairs={{0,16},{4,12},{8,24},{12,4},{16,0},{20,28},{24,8},{28,20},{1,17},{... | collective-permute-start | bytes 2359304 | tf_op jit(solution)/shard_map/ppermute | solution.py:772
  93.9 0.9 collective-permute-done.17.got.got1
  94.8 0.9 next_step.8
  95.7 4.3 %collective-permute-start.25 = (bf16[256,1024]{1,0:T(8,128)(2,1)S(1)}, bf16[256,1024]{1,0:T(8,128)(2,1)S(1)}, u32[]{:S(2)}, u32[]{:S(2)}) collective-permute-start(bf16[256,1024]{1,0:T(8,128)(2,1)S(1)} %next_step.8), channel_id=1, source_target_pairs={{0,1},{1,2},{2,3},{5,4},{6,5},{7,6},{8,9},{9,10},{10,11},{13,12},{... | collective-permute-start | bytes 1572872 | tf_op jit(solution)/shard_map/ppermute | solution.py:971
  101.1 4.3 %collective-permute-start.29 = (bf16[256,1024]{1,0:T(8,128)(2,1)S(1)}, bf16[256,1024]{1,0:T(8,128)(2,1)S(1)}, u32[]{:S(2)}, u32[]{:S(2)}) collective-permute-start(bf16[256,1024]{1,0:T(8,128)(2,1)S(1)} %next_step.10), channel_id=1, source_target_pairs={{0,1},{1,2},{2,3},{5,4},{6,5},{7,6},{8,9},{9,10},{10,11},{13,12},{... | collective-permute-start | bytes 1572872 | tf_op jit(solution)/shard_map/ppermute | solution.py:971
  105.4 1.2 collective-permute-done.25.got.got2
  107.4 4.4 %collective-permute-start.28 = (bf16[256,1024]{1,0:T(8,128)(2,1)S(1)}, bf16[256,1024]{1,0:T(8,128)(2,1)S(1)}, u32[]{:S(2)}, u32[]{:S(2)}) collective-permute-start(bf16[256,1024]{1,0:T(8,128)(2,1)S(1)} %next_step.9), channel_id=1, source_target_pairs={{0,1},{1,2},{2,3},{5,4},{6,5},{7,6},{8,9},{9,10},{10,11},{13,12},{... | collective-permute-start | bytes 1572872 | tf_op jit(solution)/shard_map/ppermute | solution.py:971
  113.6 4.9 %collective-permute-done.28.got3 = bf16[256,1024]{1,0:T(8,128)(2,1)S(1)} collective-permute-done((bf16[256,1024]{1,0:T(8,128)(2,1)S(1)}, bf16[256,1024]{1,0:T(8,128)(2,1)S(1)}, u32[]{:S(2)}, u32[]{:S(2)}) %collective-permute-start.28) | collective-permute-done | bytes 524320 | tf_op jit(solution)/shard_map/ppermute | solution.py:971
  118.4 4.4 %collective-permute-start.30 = (bf16[256,1024]{1,0:T(8,128)(2,1)S(1)}, bf16[256,1024]{1,0:T(8,128)(2,1)S(1)}, u32[]{:S(2)}, u32[]{:S(2)}) collective-permute-start(bf16[256,1024]{1,0:T(8,128)(2,1)S(1)} %next_step.11), channel_id=1, source_target_pairs={{0,1},{1,2},{2,3},{5,4},{6,5},{7,6},{8,9},{9,10},{10,11},{13,12},{... | collective-permute-start | bytes 1572872 | tf_op jit(solution)/shard_map/ppermute | solution.py:971
  122.9 2.4 %early_sum.1 = (f32[512,1024]{1,0:T(8,128)S(1)}, f32[256,1024]{1,0:T(8,128)S(1)}) custom-call(s32[10]{0:T(128)S(1)} %stack.63.order, bf16[2,256,1024]{2,1,0:T(8,128)(2,1)S(1)} %get-tuple-element.66.mine.head, bf16[256,1024]{1,0:T(8,128)(2,1)S(1)} %collective-permute-done.15.got.got0, bf16[256,1024]{1,0:T(8,128)(2,1)S(1)} %collective-permute-done.17.got.got1, ...), custom_call_target="tpu_custom_call" | custom-call | flops 1000000000 | tf_op jit(solution)/shard_map/early_sum/pallas_call | solution.py:831
  125.2 4.2 %collective-permute-done.30.got3 = bf16[256,1024]{1,0:T(8,128)(2,1)S(1)} collective-permute-done((bf16[256,1024]{1,0:T(8,128)(2,1)S(1)}, bf16[256,1024]{1,0:T(8,128)(2,1)S(1)}, u32[]{:S(2)}, u32[]{:S(2)}) %collective-permute-start.30) | collective-permute-done | bytes 524320 | tf_op jit(solution)/shard_map/ppermute | solution.py:971
  129.5 0.8 partner_sum.1
  130.4 0.9 mine_sum.1.mine
  131.3 1.7 %collective-permute-done.31.partners = bf16[2,256,1024]{2,1,0:T(8,128)(2,1)S(1)} collective-permute-done((bf16[2,256,1024]{2,1,0:T(8,128)(2,1)S(1)}, bf16[2,256,1024]{2,1,0:T(8,128)(2,1)S(1)}, u32[]{:S(2)}, u32[]{:S(2)}) %collective-permute-start.31) | collective-permute-done | bytes 1048608 | tf_op jit(solution)/shard_map/ppermute | solution.py:972
  133.1 1.1 join_sums.1
  (79 shorter events, 9.2 us)
Async XLA Ops:
  0.0 22.9 %copy-start = (f32[1024]{0:T(1024)S(1)}, f32[1024]{0:T(1024)}, u32[]{:S(2)}) copy-start(f32[1024]{0:T(1024)} %param.15) | copy-start | bytes 12292
  0.0 4.9 %copy-start.2 = (bf16[1024,512]{1,0:T(8,128)(2,1)S(1)}, bf16[1024,512]{1,0:T(8,128)(2,1)}, u32[]{:S(2)}) copy-start(bf16[1024,512]{1,0:T(8,128)(2,1)} %taps.1) | copy-start | bytes 3145732
  1.5 3.4 %collective-permute-start = (bf16[6,1024]{1,0:T(8,128)(2,1)}, bf16[6,1024]{1,0:T(8,128)(2,1)S(1)}, u32[]{:S(2)}, u32[]{:S(2)}) collective-permute-start(bf16[6,1024]{1,0:T(8,128)(2,1)} %rims.1), channel_id=1, source_target_pairs={{0,4},{4,8},{8,12},{12,16},{16,20},{20,24},{24,28},{1,5},{5,9},{9,... | collective-permute-start | bytes 36872 | tf_op jit(solution)/shard_map/ppermute | solution.py:18
  4.9 10.8 %copy-start.5 = (bf16[6,1024]{1,0:T(8,128)(2,1)}, bf16[6,1024]{1,0:T(8,128)(2,1)S(1)}, u32[]{:S(2)}) copy-start(bf16[6,1024]{1,0:T(8,128)(2,1)S(1)} %collective-permute-done.edges) | copy-start | bytes 36868
  5.1 15.0 %collective-permute-start.1 = (bf16[256,512]{1,0:T(8,128)(2,1)S(1)}, bf16[256,512]{1,0:T(8,128)(2,1)S(1)}, u32[]{:S(2)}, u32[]{:S(2)}) collective-permute-start(bf16[256,512]{1,0:T(8,128)(2,1)S(1)} %get-tuple-element.47), channel_id=1, source_target_pairs={{0,8},{4,12},{8,0},{12,4},{16,24},{20,28},{24,16},{28,20},{1,9},{5... | collective-permute-start | bytes 786440 | tf_op jit(solution)/shard_map/ppermute | solution.py:1018
  10.0 12.9 %collective-permute-start.2 = (bf16[256,512]{1,0:T(8,128)(2,1)S(1)}, bf16[256,512]{1,0:T(8,128)(2,1)S(1)}, u32[]{:S(2)}, u32[]{:S(2)}) collective-permute-start(bf16[256,512]{1,0:T(8,128)(2,1)S(1)} %get-tuple-element.48), channel_id=1, source_target_pairs={{0,16},{4,20},{8,24},{12,28},{16,0},{20,4},{24,8},{28,12},{1,17},{... | collective-permute-start | bytes 786440 | tf_op jit(solution)/shard_map/ppermute | solution.py:1018
  11.5 11.3 %collective-permute-start.3 = (bf16[256,512]{1,0:T(8,128)(2,1)S(1)}, bf16[256,512]{1,0:T(8,128)(2,1)S(1)}, u32[]{:S(2)}, u32[]{:S(2)}) collective-permute-start(bf16[256,512]{1,0:T(8,128)(2,1)S(1)} %get-tuple-element.49), channel_id=1, source_target_pairs={{0,24},{4,28},{8,16},{12,20},{16,8},{20,12},{24,0},{28,4},{1,25},{... | collective-permute-start | bytes 786440 | tf_op jit(solution)/shard_map/ppermute | solution.py:1018
  15.7 16.1 %copy-start.8 = (bf16[256,768]{1,0:T(8,128)(2,1)S(1)}, bf16[256,768]{1,0:T(8,128)(2,1)}, u32[]{:S(2)}) copy-start(bf16[256,768]{1,0:T(8,128)(2,1)} %constant.80.clone.refs_6_.refs_5_) | copy-start | bytes 1179652
  15.7 16.1 %copy-start.10 = (f32[128,66]{1,0:T(8,128)S(1)}, f32[128,66]{1,0:T(8,128)}, u32[]{:S(2)}) copy-start(f32[128,66]{1,0:T(8,128)} %constant.82.clone.refs_5_.refs_4_) | copy-start | bytes 101380
  20.0 3.0 %collective-permute-start.7 = (bf16[4,512,128]{2,1,0:T(8,128)(2,1)}, bf16[4,512,128]{2,1,0:T(8,128)(2,1)S(1)}, u32[]{:S(2)}, u32[]{:S(2)}) collective-permute-start(bf16[4,512,128]{2,1,0:T(8,128)(2,1)} %get-tuple-element.55), channel_id=1, source_target_pairs={{0,4},{4,0},{8,12},{12,8},{16,20},{20,16},{24,28},{28,24},{1,5},{5... | collective-permute-start | bytes 1572872 | tf_op jit(solution)/shard_map/ppermute | solution.py:1016
  22.9 4.8 %collective-permute-start.4 = (bf16[4,128,512]{2,1,0:T(8,128)(2,1)S(1)}, bf16[4,128,512]{2,1,0:T(8,128)(2,1)S(1)}, u32[]{:S(2)}, u32[]{:S(2)}) collective-permute-start(bf16[4,128,512]{2,1,0:T(8,128)(2,1)S(1)} %other_core.1), channel_id=1, source_target_pairs={{0,4},{4,0},{8,12},{12,8},{16,20},{20,16},{24,28},{28,24},{1,5},{5... | collective-permute-start | bytes 1572872 | tf_op jit(solution)/shard_map/ppermute | solution.py:1016
  23.0 1.0 copy-start.3
  24.1 13.7 %collective-permute-start.8 = (bf16[2,512,128]{2,1,0:T(8,128)(2,1)S(1)}, bf16[2,512,128]{2,1,0:T(8,128)(2,1)S(1)}, u32[]{:S(2)}, u32[]{:S(2)}) collective-permute-start(bf16[2,512,128]{2,1,0:T(8,128)(2,1)S(1)} %get-tuple-element.57), channel_id=1, source_target_pairs={{0,8},{4,12},{8,0},{12,4},{16,24},{20,28},{24,16},{28,20},{1,9},{5... | collective-permute-start | bytes 786440 | tf_op jit(solution)/shard_map/ppermute | solution.py:1018
  24.7 13.1 %collective-permute-start.9 = (bf16[2,512,128]{2,1,0:T(8,128)(2,1)S(1)}, bf16[2,512,128]{2,1,0:T(8,128)(2,1)S(1)}, u32[]{:S(2)}, u32[]{:S(2)}) collective-permute-start(bf16[2,512,128]{2,1,0:T(8,128)(2,1)S(1)} %get-tuple-element.58), channel_id=1, source_target_pairs={{0,16},{4,20},{8,24},{12,28},{16,0},{20,4},{24,8},{28,12},{1,17},{... | collective-permute-start | bytes 786440 | tf_op jit(solution)/shard_map/ppermute | solution.py:1018
  26.2 12.5 %copy-start.7 = (bf16[512,128]{1,0:T(8,128)(2,1)S(1)}, bf16[512,128]{1,0:T(8,128)(2,1)}, u32[]{:S(2)}) copy-start(bf16[512,128]{1,0:T(8,128)(2,1)} %get-tuple-element.54.stay) | copy-start | bytes 393220
  26.2 12.5 %copy-start.9 = (bf16[256,768]{1,0:T(8,128)(2,1)S(1)}, bf16[256,768]{1,0:T(8,128)(2,1)}, u32[]{:S(2)}) copy-start(bf16[256,768]{1,0:T(8,128)(2,1)} %constant.81.clone.refs_6_) | copy-start | bytes 1179652
  26.2 12.5 %collective-permute-start.10 = (bf16[2,512,128]{2,1,0:T(8,128)(2,1)S(1)}, bf16[2,512,128]{2,1,0:T(8,128)(2,1)S(1)}, u32[]{:S(2)}, u32[]{:S(2)}) collective-permute-start(bf16[2,512,128]{2,1,0:T(8,128)(2,1)S(1)} %get-tuple-element.59), channel_id=1, source_target_pairs={{0,24},{4,28},{8,16},{12,20},{16,8},{20,12},{24,0},{28,4},{1,25},{... | collective-permute-start | bytes 786440 | tf_op jit(solution)/shard_map/ppermute | solution.py:1018
  27.6 24.7 %collective-permute-start.6 = (bf16[128,1024]{1,0:T(8,128)(2,1)}, bf16[128,1024]{1,0:T(8,128)(2,1)S(1)}, u32[]{:S(2)}, u32[]{:S(2)}) collective-permute-start(bf16[128,1024]{1,0:T(8,128)(2,1)} %get-tuple-element.51), channel_id=1, source_target_pairs={{0,2},{1,3},{2,0},{3,1},{4,6},{5,7},{6,4},{7,5},{8,10},{9,11},{10,... | collective-permute-start | bytes 786440 | tf_op jit(solution)/shard_map/ppermute | solution.py:732
  30.2 22.1 %collective-permute-start.5 = (bf16[256,1024]{1,0:T(8,128)(2,1)}, bf16[256,1024]{1,0:T(8,128)(2,1)}, u32[]{:S(2)}, u32[]{:S(2)}) collective-permute-start(bf16[256,1024]{1,0:T(8,128)(2,1)} %get-tuple-element.50), channel_id=1, source_target_pairs={{0,1},{1,2},{2,3},{3,0},{4,7},{5,4},{6,5},{7,6},{8,9},{9,10},{10,1... | collective-permute-start | bytes 1572872 | tf_op jit(solution)/shard_map/ppermute | solution.py:732
  52.3 5.8 %copy-start.11 = (bf16[128,1024]{1,0:T(8,128)(2,1)}, bf16[128,1024]{1,0:T(8,128)(2,1)S(1)}, u32[]{:S(2)}) copy-start(bf16[128,1024]{1,0:T(8,128)(2,1)S(1)} %collective-permute-done.6) | copy-start | bytes 786436
  52.3 9.0 %copy-start.1 = (bf16[512,1024]{1,0:T(8,128)(2,1)S(1)}, bf16[512,1024]{1,0:T(8,128)(2,1)}, u32[]{:S(2)}) copy-start(bf16[512,1024]{1,0:T(8,128)(2,1)} %query.3) | copy-start | bytes 3145732
  52.3 9.0 %copy-start.4 = (f32[3,3,1024]{2,1,0:T(4,128)S(1)}, f32[3,3,1024]{2,1,0:T(4,128)}, u32[]{:S(2)}) copy-start(f32[3,3,1024]{2,1,0:T(4,128)} %weight.7) | copy-start | bytes 110596
  52.4 9.0 %copy-start.6 = (bf16[6,1024]{1,0:T(8,128)(2,1)S(1)}, bf16[6,1024]{1,0:T(8,128)(2,1)}, u32[]{:S(2)}) copy-start(bf16[6,1024]{1,0:T(8,128)(2,1)} %copy-done.5) | copy-start | bytes 36868
  52.5 2.0 %collective-permute-start.11 = (bf16[4,512,128]{2,1,0:T(8,128)(2,1)S(1)}, bf16[4,512,128]{2,1,0:T(8,128)(2,1)S(1)}, u32[]{:S(2)}, u32[]{:S(2)}) collective-permute-start(bf16[4,512,128]{2,1,0:T(8,128)(2,1)S(1)} %get-tuple-element.61), channel_id=1, source_target_pairs={{0,4},{4,0},{8,12},{12,8},{16,20},{20,16},{24,28},{28,24},{1,5},{5... | collective-permute-start | bytes 1572872 | tf_op jit(solution)/shard_map/ppermute | solution.py:1016
  54.5 9.2 %collective-permute-start.12 = (bf16[2,512,128]{2,1,0:T(8,128)(2,1)S(1)}, bf16[2,512,128]{2,1,0:T(8,128)(2,1)S(1)}, u32[]{:S(2)}, u32[]{:S(2)}) collective-permute-start(bf16[2,512,128]{2,1,0:T(8,128)(2,1)S(1)} %get-tuple-element.63), channel_id=1, source_target_pairs={{0,8},{4,12},{8,0},{12,4},{16,24},{20,28},{24,16},{28,20},{1,9},{5... | collective-permute-start | bytes 786440 | tf_op jit(solution)/shard_map/ppermute | solution.py:1018
  56.1 13.7 %collective-permute-start.13 = (bf16[2,512,128]{2,1,0:T(8,128)(2,1)S(1)}, bf16[2,512,128]{2,1,0:T(8,128)(2,1)S(1)}, u32[]{:S(2)}, u32[]{:S(2)}) collective-permute-start(bf16[2,512,128]{2,1,0:T(8,128)(2,1)S(1)} %get-tuple-element.64), channel_id=1, source_target_pairs={{0,16},{4,20},{8,24},{12,28},{16,0},{20,4},{24,8},{28,12},{1,17},{... | collective-permute-start | bytes 786440 | tf_op jit(solution)/shard_map/ppermute | solution.py:1018
  56.9 12.9 %collective-permute-start.14 = (bf16[2,512,128]{2,1,0:T(8,128)(2,1)S(1)}, bf16[2,512,128]{2,1,0:T(8,128)(2,1)S(1)}, u32[]{:S(2)}, u32[]{:S(2)}) collective-permute-start(bf16[2,512,128]{2,1,0:T(8,128)(2,1)S(1)} %get-tuple-element.65), channel_id=1, source_target_pairs={{0,24},{4,28},{8,16},{12,20},{16,8},{20,12},{24,0},{28,4},{1,25},{... | collective-permute-start | bytes 786440 | tf_op jit(solution)/shard_map/ppermute | solution.py:1018
  59.4 22.1 %slice-start = ((s8[8388608]{0:T(1024)(128)(4,1)}), s8[4194304]{0:T(1024)(128)(4,1)S(1)}, s32[]{:S(2)}) async-start(s8[8388608]{0:T(1024)(128)(4,1)} %bitcast.19), calls=%async_computation | async-start | bytes 8388608
  69.8 4.7 %copy-start.12 = (bf16[128,1024]{1,0:T(8,128)(2,1)S(1)}, bf16[128,1024]{1,0:T(8,128)(2,1)}, u32[]{:S(2)}) copy-start(bf16[128,1024]{1,0:T(8,128)(2,1)} %copy-done.11) | copy-start | bytes 786436
  69.8 11.8 %slice-start.1 = ((s8[8388608]{0:T(1024)(128)(4,1)}), s8[4194304]{0:T(1024)(128)(4,1)S(1)}, s32[]{:S(2)}) async-start(s8[8388608]{0:T(1024)(128)(4,1)} %bitcast.19), calls=%async_computation.1 | async-start | bytes 8388608
  71.4 4.2 %collective-permute-start.16 = (bf16[2,256,1024]{2,1,0:T(8,128)(2,1)S(1)}, bf16[2,256,1024]{2,1,0:T(8,128)(2,1)S(1)}, u32[]{:S(2)}, u32[]{:S(2)}) collective-permute-start(bf16[2,256,1024]{2,1,0:T(8,128)(2,1)S(1)} %get-tuple-element.66.mine.head), channel_id=1, source_target_pairs={{0,4},{4,0},{8,12},{12,8},{16,20},{20,16},{24,28},{28,24},{1,5},{5... | collective-permute-start | bytes 3145736 | tf_op jit(solution)/shard_map/ppermute | solution.py:972
  71.5 13.8 %collective-permute-start.15 = (bf16[256,1024]{1,0:T(8,128)(2,1)S(1)}, bf16[256,1024]{1,0:T(8,128)(2,1)S(1)}, u32[]{:S(2)}, u32[]{:S(2)}) collective-permute-start(bf16[256,1024]{1,0:T(8,128)(2,1)S(1)} %get-tuple-element.67), channel_id=1, source_target_pairs={{0,1},{1,2},{2,3},{5,4},{6,5},{7,6},{8,9},{9,10},{10,11},{13,12},{... | collective-permute-start | bytes 1572872 | tf_op jit(solution)/shard_map/ppermute | solution.py:971
  76.8 11.3 %collective-permute-start.18 = (bf16[256,1024]{1,0:T(8,128)(2,1)S(1)}, bf16[256,1024]{1,0:T(8,128)(2,1)S(1)}, u32[]{:S(2)}, u32[]{:S(2)}) collective-permute-start(bf16[256,1024]{1,0:T(8,128)(2,1)S(1)} %partner_sent.1), channel_id=1, source_target_pairs={{0,1},{1,2},{2,3},{5,4},{6,5},{7,6},{8,9},{9,10},{10,11},{13,12},{... | collective-permute-start | bytes 1572872 | tf_op jit(solution)/shard_map/ppermute | solution.py:971
  80.0 13.4 %collective-permute-start.20 = (bf16[384,1024]{1,0:T(8,128)(2,1)S(1)}, bf16[384,1024]{1,0:T(8,128)(2,1)S(1)}, u32[]{:S(2)}, u32[]{:S(2)}) collective-permute-start(bf16[384,1024]{1,0:T(8,128)(2,1)S(1)} %pad_maximum_fusion.refs_0_), channel_id=1, source_target_pairs={{0,8},{4,20},{8,0},{12,28},{16,24},{20,4},{24,16},{28,12},{1,9},{5... | collective-permute-start | bytes 2359304 | tf_op jit(solution)/shard_map/ppermute | solution.py:766
  85.8 9.0 %collective-permute-start.17 = (bf16[256,1024]{1,0:T(8,128)(2,1)S(1)}, bf16[256,1024]{1,0:T(8,128)(2,1)S(1)}, u32[]{:S(2)}, u32[]{:S(2)}) collective-permute-start(bf16[256,1024]{1,0:T(8,128)(2,1)S(1)} %next_step.6), channel_id=1, source_target_pairs={{0,1},{1,2},{2,3},{5,4},{6,5},{7,6},{8,9},{9,10},{10,11},{13,12},{... | collective-permute-start | bytes 1572872 | tf_op jit(solution)/shard_map/ppermute | solution.py:971
  88.8 11.7 %collective-permute-start.19 = (bf16[256,1024]{1,0:T(8,128)(2,1)S(1)}, bf16[256,1024]{1,0:T(8,128)(2,1)S(1)}, u32[]{:S(2)}, u32[]{:S(2)}) collective-permute-start(bf16[256,1024]{1,0:T(8,128)(2,1)S(1)} %next_step.7), channel_id=1, source_target_pairs={{0,1},{1,2},{2,3},{5,4},{6,5},{7,6},{8,9},{9,10},{10,11},{13,12},{... | collective-permute-start | bytes 1572872 | tf_op jit(solution)/shard_map/ppermute | solution.py:971
  91.8 20.1 %collective-permute-start.21 = (bf16[384,1024]{1,0:T(8,128)(2,1)S(1)}, bf16[384,1024]{1,0:T(8,128)(2,1)S(1)}, u32[]{:S(2)}, u32[]{:S(2)}) collective-permute-start(bf16[384,1024]{1,0:T(8,128)(2,1)S(1)} %pad_maximum_fusion.refs_0_), channel_id=1, source_target_pairs={{0,16},{4,12},{8,24},{12,4},{16,0},{20,28},{24,8},{28,20},{1,17},{... | collective-permute-start | bytes 2359304 | tf_op jit(solution)/shard_map/ppermute | solution.py:772
  93.3 19.0 %collective-permute-start.22 = (bf16[384,1024]{1,0:T(8,128)(2,1)S(1)}, bf16[384,1024]{1,0:T(8,128)(2,1)S(1)}, u32[]{:S(2)}, u32[]{:S(2)}) collective-permute-start(bf16[384,1024]{1,0:T(8,128)(2,1)S(1)} %collective-permute-done.20.refs_1_), channel_id=1, source_target_pairs={{0,16},{4,12},{8,24},{12,4},{16,0},{20,28},{24,8},{28,20},{1,17},{... | collective-permute-start | bytes 2359304 | tf_op jit(solution)/shard_map/ppermute | solution.py:772
  95.7 11.0 %collective-permute-start.25 = (bf16[256,1024]{1,0:T(8,128)(2,1)S(1)}, bf16[256,1024]{1,0:T(8,128)(2,1)S(1)}, u32[]{:S(2)}, u32[]{:S(2)}) collective-permute-start(bf16[256,1024]{1,0:T(8,128)(2,1)S(1)} %next_step.8), channel_id=1, source_target_pairs={{0,1},{1,2},{2,3},{5,4},{6,5},{7,6},{8,9},{9,10},{10,11},{13,12},{... | collective-permute-start | bytes 1572872 | tf_op jit(solution)/shard_map/ppermute | solution.py:971
  101.1 11.3 %collective-permute-start.29 = (bf16[256,1024]{1,0:T(8,128)(2,1)S(1)}, bf16[256,1024]{1,0:T(8,128)(2,1)S(1)}, u32[]{:S(2)}, u32[]{:S(2)}) collective-permute-start(bf16[256,1024]{1,0:T(8,128)(2,1)S(1)} %next_step.10), channel_id=1, source_target_pairs={{0,1},{1,2},{2,3},{5,4},{6,5},{7,6},{8,9},{9,10},{10,11},{13,12},{... | collective-permute-start | bytes 1572872 | tf_op jit(solution)/shard_map/ppermute | solution.py:971
  107.4 11.1 %collective-permute-start.28 = (bf16[256,1024]{1,0:T(8,128)(2,1)S(1)}, bf16[256,1024]{1,0:T(8,128)(2,1)S(1)}, u32[]{:S(2)}, u32[]{:S(2)}) collective-permute-start(bf16[256,1024]{1,0:T(8,128)(2,1)S(1)} %next_step.9), channel_id=1, source_target_pairs={{0,1},{1,2},{2,3},{5,4},{6,5},{7,6},{8,9},{9,10},{10,11},{13,12},{... | collective-permute-start | bytes 1572872 | tf_op jit(solution)/shard_map/ppermute | solution.py:971
  111.8 11.1 %collective-permute-start.23 = (bf16[384,1024]{1,0:T(8,128)(2,1)S(1)}, bf16[384,1024]{1,0:T(8,128)(2,1)S(1)}, u32[]{:S(2)}, u32[]{:S(2)}) collective-permute-start(bf16[384,1024]{1,0:T(8,128)(2,1)S(1)} %pad_maximum_fusion.refs_0_), channel_id=1, source_target_pairs={{0,4},{4,0},{8,12},{12,8},{16,20},{20,16},{24,28},{28,24},{1,5},{5... | collective-permute-start | bytes 2359304 | tf_op jit(solution)/shard_map/ppermute | solution.py:774
  111.9 11.0 %collective-permute-start.24 = (bf16[384,1024]{1,0:T(8,128)(2,1)S(1)}, bf16[384,1024]{1,0:T(8,128)(2,1)S(1)}, u32[]{:S(2)}, u32[]{:S(2)}) collective-permute-start(bf16[384,1024]{1,0:T(8,128)(2,1)S(1)} %collective-permute-done.20.refs_1_), channel_id=1, source_target_pairs={{0,4},{4,0},{8,12},{12,8},{16,20},{20,16},{24,28},{28,24},{1,5},{5... | collective-permute-start | bytes 2359304 | tf_op jit(solution)/shard_map/ppermute | solution.py:774
  112.4 10.5 %collective-permute-start.26 = (bf16[384,1024]{1,0:T(8,128)(2,1)S(1)}, bf16[384,1024]{1,0:T(8,128)(2,1)S(1)}, u32[]{:S(2)}, u32[]{:S(2)}) collective-permute-start(bf16[384,1024]{1,0:T(8,128)(2,1)S(1)} %collective-permute-done.21.refs_2_), channel_id=1, source_target_pairs={{0,4},{4,0},{8,12},{12,8},{16,20},{20,16},{24,28},{28,24},{1,5},{5... | collective-permute-start | bytes 2359304 | tf_op jit(solution)/shard_map/ppermute | solution.py:774
  112.5 10.4 %collective-permute-start.27 = (bf16[384,1024]{1,0:T(8,128)(2,1)S(1)}, bf16[384,1024]{1,0:T(8,128)(2,1)S(1)}, u32[]{:S(2)}, u32[]{:S(2)}) collective-permute-start(bf16[384,1024]{1,0:T(8,128)(2,1)S(1)} %collective-permute-done.22.refs_3_), channel_id=1, source_target_pairs={{0,4},{4,0},{8,12},{12,8},{16,20},{20,16},{24,28},{28,24},{1,5},{5... | collective-permute-start | bytes 2359304 | tf_op jit(solution)/shard_map/ppermute | solution.py:774
  118.4 11.1 %collective-permute-start.30 = (bf16[256,1024]{1,0:T(8,128)(2,1)S(1)}, bf16[256,1024]{1,0:T(8,128)(2,1)S(1)}, u32[]{:S(2)}, u32[]{:S(2)}) collective-permute-start(bf16[256,1024]{1,0:T(8,128)(2,1)S(1)} %next_step.11), channel_id=1, source_target_pairs={{0,1},{1,2},{2,3},{5,4},{6,5},{7,6},{8,9},{9,10},{10,11},{13,12},{... | collective-permute-start | bytes 1572872 | tf_op jit(solution)/shard_map/ppermute | solution.py:971
  130.3 2.7 %collective-permute-start.31 = (bf16[2,256,1024]{2,1,0:T(8,128)(2,1)S(1)}, bf16[2,256,1024]{2,1,0:T(8,128)(2,1)S(1)}, u32[]{:S(2)}, u32[]{:S(2)}) collective-permute-start(bf16[2,256,1024]{2,1,0:T(8,128)(2,1)S(1)} %partner_sum.1), channel_id=1, source_target_pairs={{0,4},{4,0},{8,12},{12,8},{16,20},{20,16},{24,28},{28,24},{1,5},{5... | collective-permute-start | bytes 3145736 | tf_op jit(solution)/shard_map/ppermute | solution.py:972

commit v7 on v6

--- a/solution.py
+++ b/solution.py
@@ -238,12 +238,12 @@
                 spectra[k, pl.ds(SUB + row, 8), :] = real * sin + imag * cos
         return carry
 
-    lax.fori_loop(0, SUB // 8, slab, 0)
+    lax.fori_loop(0, SUB // 8, slab, 0, unroll=2)
     for k in range(half + 1, spectra.shape[0]):
         spectra[k] = jnp.zeros(spectra.shape[1:], F32)
 
 
-def last_stage(spectra, series, twiddle):
+def last_stage(spectra, series, twiddle, signal, skip):
     half = series.shape[0] // SUB
     lanes = series.shape[1]
 
@@ -261,11 +261,13 @@
             sin = jnp.broadcast_to(factors[:, half + 1 + k : half + 2 + k], (8, lanes))
             turned = real * cos + imag * sin
             bins.append((turned, None if k == half else imag * cos - real * sin))
+        gain = jnp.broadcast_to(skip[...], (8, lanes))
         for n, value in enumerate(real_inverse(bins)):
-            series[pl.ds(SUB * n + row, 8), :] = value
+            rows = pl.ds(SUB * n + row, 8)
+            series[rows, :] = value + gain * signal[rows, :]
         return carry
 
-    lax.fori_loop(0, SUB // 8, slab, 0)
+    lax.fori_loop(0, SUB // 8, slab, 0, unroll=2)
 
 
 def taps_kernel(chips, me_ref, *refs):
@@ -315,10 +317,7 @@
         return carry
 
     over_pairs(taps_spectra.shape[0], pair)
-    last_stage(spectra, out, twiddle)
-    for m in range(blocks):
-        window = pl.ds(m * span, span)
-        out[window, :] += skip[...] * series[window, :]
+    last_stage(spectra, out, twiddle, series, skip)
 
 
 def spread_kernel(me_ref, conv, stay, same, swap):

time: 135 us -> 134 us (level)
  Pallas kernels: 45.3 us -> 43.3 us
  starting transfers between devices: 54.9 us -> 56.7 us
    ppermute x8, starting transfers between devices: 28.9 us -> 30.3 us  [project(): onward = lambda x: lax.ppermute(x, ('ctx', 'tp'), route)]
    ppermute x8, waiting for transfers between devices: 11.7 us -> 10.3 us  [project(): onward = lambda x: lax.ppermute(x, ('ctx', 'tp'), route)]
  transfers between devices with their start and end apart: 32 -> 32, of which waited for: 12 -> 14; matrix products, arithmetic and copies ran while one was open for 4% -> 4% of each run, Pallas kernels for 30% -> 28%
where the time goes in v7:
time: 134 us
  starting transfers between devices  56.7 us (42%)
  Pallas kernels  43.3 us (32%)
  waiting for transfers between devices  26.2 us (20%)
  local copies, waits for them, and re-layouts  3.8 us (3%)
  other arithmetic  2.55 us (2%)
    ppermute x8, starting transfers between devices, project(): onward = lambda x: lax.ppermute(x, ('ctx', 'tp'), route)  30.3 us
    ppermute x9, starting transfers between devices, fast_per_device(): lax.ppermute(x, 'ctx', [(i, i ^ 2 * q + 2) for i in devices])  14.4 us
    pallas_call x1, Pallas kernels, long_conv(): pl.pallas_call(partial(conv_kernel, blocks), out_shape=jax.ShapeDtypeStru...  12.2 us
    ppermute x9, waiting for transfers between devices, fast_per_device(): lax.ppermute(x, 'ctx', [(i, i ^ 2 * q + 2) for i in devices])  11.5 us
    ppermute x8, waiting for transfers between devices, project(): onward = lambda x: lax.ppermute(x, ('ctx', 'tp'), route)  10.3 us
    pallas_call x1, Pallas kernels, taps_spectra_of(): pl.pallas_call(partial(taps_kernel, chips), out_shape=jax.ShapeDtypeStruc...  5.45 us
    pallas_call x1, Pallas kernels, gate_in(): pl.pallas_call(gate_in_kernel, in_specs=[SMEM, HBM, HBM, VMEM, VMEM], out...  4.26 us
    ppermute x2, starting transfers between devices, turn_weight(): found.append(lax.ppermute(part, ('ctx', 'tp'), route))  4.17 us
  transfers between devices with their start and end apart: 32, of which 14 were waited for; matrix products, arithmetic and copies ran while one was open for 4% of the time, Pallas kernels for 28%

profile of v7, /device:TPU:0, one launch (start us, length us, event | category | flops | bytes accessed | tf_op | source)
XLA Modules:
  0.0 133.7 jit_solution(552900192446623907)
XLA Ops:
  0.0 1.5 %rims.1 = bf16[6,1024]{1,0:T(8,128)(2,1)} custom-call(bf16[512,1024]{1,0:T(8,128)(2,1)} %query.3, bf16[512,1024]{1,0:T(8,128)(2,1)} %key.3, bf16[512,1024]{1,0:T(8,128)(2,1)} %value.3), custom_call_target="tpu_custom_call" | custom-call | tf_op jit(solution)/shard_map/rims/pallas_call | solution.py:427
  1.5 2.4 %collective-permute-start = (bf16[6,1024]{1,0:T(8,128)(2,1)}, bf16[6,1024]{1,0:T(8,128)(2,1)S(1)}, u32[]{:S(2)}, u32[]{:S(2)}) collective-permute-start(bf16[6,1024]{1,0:T(8,128)(2,1)} %rims.1), channel_id=1, source_target_pairs={{0,4},{4,8},{8,12},{12,16},{16,20},{20,24},{24,28},{1,5},{5,9},{9,... | collective-permute-start | bytes 36872 | tf_op jit(solution)/shard_map/ppermute | solution.py:18
  3.9 0.7 or_select_fusion.plan
  5.1 4.9 %collective-permute-start.1 = (bf16[256,512]{1,0:T(8,128)(2,1)S(1)}, bf16[256,512]{1,0:T(8,128)(2,1)S(1)}, u32[]{:S(2)}, u32[]{:S(2)}) collective-permute-start(bf16[256,512]{1,0:T(8,128)(2,1)S(1)} %get-tuple-element.47), channel_id=1, source_target_pairs={{0,8},{4,12},{8,0},{12,4},{16,24},{20,28},{24,16},{28,20},{1,9},{5... | collective-permute-start | bytes 786440 | tf_op jit(solution)/shard_map/ppermute | solution.py:1017
  10.0 1.5 %collective-permute-start.2 = (bf16[256,512]{1,0:T(8,128)(2,1)S(1)}, bf16[256,512]{1,0:T(8,128)(2,1)S(1)}, u32[]{:S(2)}, u32[]{:S(2)}) collective-permute-start(bf16[256,512]{1,0:T(8,128)(2,1)S(1)} %get-tuple-element.48), channel_id=1, source_target_pairs={{0,16},{4,20},{8,24},{12,28},{16,0},{20,4},{24,8},{28,12},{1,17},{... | collective-permute-start | bytes 786440 | tf_op jit(solution)/shard_map/ppermute | solution.py:1017
  11.5 0.9 collective-permute-start.3
  13.0 2.7 %weight_corners.1 = (bf16[256,1024]{1,0:T(8,128)(2,1)}, bf16[128,1024]{1,0:T(8,128)(2,1)}) custom-call(s32[4]{0:T(128)} %pad_add_fusion.1.corners, bf16[1024,4096]{1,0:T(8,128)(2,1)} %weight.9), custom_call_target="tpu_custom_call" | custom-call | tf_op jit(solution)/shard_map/weight_corners/pallas_call | solution.py:752
  15.7 4.3 %gate_in.1 = (bf16[512,128]{1,0:T(8,128)(2,1)}, bf16[3,512,128]{2,1,0:T(8,128)(2,1)}, bf16[4,512,128]{2,1,0:T(8,128)(2,1)}) custom-call(s32[1]{0:T(128)} %bitcast.me_ref, bf16[512,1024]{1,0:T(8,128)(2,1)} %key.3, bf16[512,1024]{1,0:T(8,128)(2,1)} %value.3, bf16[6,1024]{1,0:T(8,128)(2,1)} %copy-done.5, f32[3,3,1024]{2,1,0:T(4,128)} %weight.7), custom_call_target="tpu_custom_call" | custom-call | tf_op jit(solution)/shard_map/gate_in/pallas_call | solution.py:478
  20.1 2.7 %collective-permute-done.2.refs_2_ = bf16[256,512]{1,0:T(8,128)(2,1)S(1)} collective-permute-done((bf16[256,512]{1,0:T(8,128)(2,1)S(1)}, bf16[256,512]{1,0:T(8,128)(2,1)S(1)}, u32[]{:S(2)}, u32[]{:S(2)}) %collective-permute-start.2) | collective-permute-done | bytes 262176 | tf_op jit(solution)/shard_map/ppermute | solution.py:1017
  23.0 1.0 copy-done.3
  24.7 1.5 %collective-permute-start.9 = (bf16[2,512,128]{2,1,0:T(8,128)(2,1)S(1)}, bf16[2,512,128]{2,1,0:T(8,128)(2,1)S(1)}, u32[]{:S(2)}, u32[]{:S(2)}) collective-permute-start(bf16[2,512,128]{2,1,0:T(8,128)(2,1)S(1)} %get-tuple-element.58), channel_id=1, source_target_pairs={{0,16},{4,20},{8,24},{12,28},{16,0},{20,4},{24,8},{28,12},{1,17},{... | collective-permute-start | bytes 786440 | tf_op jit(solution)/shard_map/ppermute | solution.py:1017
  26.2 1.4 %collective-permute-start.10 = (bf16[2,512,128]{2,1,0:T(8,128)(2,1)S(1)}, bf16[2,512,128]{2,1,0:T(8,128)(2,1)S(1)}, u32[]{:S(2)}, u32[]{:S(2)}) collective-permute-start(bf16[2,512,128]{2,1,0:T(8,128)(2,1)S(1)} %get-tuple-element.59), channel_id=1, source_target_pairs={{0,24},{4,28},{8,16},{12,20},{16,8},{20,12},{24,0},{28,4},{1,25},{... | collective-permute-start | bytes 786440 | tf_op jit(solution)/shard_map/ppermute | solution.py:1017
  27.6 2.6 %collective-permute-start.6 = (bf16[128,1024]{1,0:T(8,128)(2,1)}, bf16[128,1024]{1,0:T(8,128)(2,1)S(1)}, u32[]{:S(2)}, u32[]{:S(2)}) collective-permute-start(bf16[128,1024]{1,0:T(8,128)(2,1)} %get-tuple-element.51), channel_id=1, source_target_pairs={{0,2},{1,3},{2,0},{3,1},{4,6},{5,7},{6,4},{7,5},{8,10},{9,11},{10,... | collective-permute-start | bytes 786440 | tf_op jit(solution)/shard_map/ppermute | solution.py:731
  30.2 1.6 %collective-permute-start.5 = (bf16[256,1024]{1,0:T(8,128)(2,1)}, bf16[256,1024]{1,0:T(8,128)(2,1)}, u32[]{:S(2)}, u32[]{:S(2)}) collective-permute-start(bf16[256,1024]{1,0:T(8,128)(2,1)} %get-tuple-element.50), channel_id=1, source_target_pairs={{0,1},{1,2},{2,3},{3,0},{4,7},{5,4},{6,5},{7,6},{8,9},{9,10},{10,1... | collective-permute-start | bytes 1572872 | tf_op jit(solution)/shard_map/ppermute | solution.py:731
  31.8 5.5 %taps_spectra.1.refs_3_ = f32[17,256,256]{2,1,0:T(8,128)S(1)} custom-call(s32[1]{0:T(128)} %bitcast.me_ref, bf16[256,512]{1,0:T(8,128)(2,1)S(1)} %get-tuple-element.46.refs_0_, bf16[256,512]{1,0:T(8,128)(2,1)S(1)} %collective-permute-done.1.refs_1_, bf16[256,512]{1,0:T(8,128)(2,1)S(1)} %collective-permute-done.2.refs_2_, ...), custom_call_target="tpu_custom_call" | custom-call | flops 8000000000 | tf_op jit(solution)/shard_map/taps_spectra/pallas_call | solution.py:356
  37.8 0.9 collective-permute-done.10.refs_2_
  38.7 12.2 %long_conv.1.conv = f32[4096,128]{1,0:T(8,128)S(1)} custom-call(s32[1]{0:T(128)} %bitcast.me_ref, bf16[512,128]{1,0:T(8,128)(2,1)S(1)} %copy-done.7, bf16[4,512,128]{2,1,0:T(8,128)(2,1)S(1)} %collective-permute-done.7.swapped, bf16[2,512,128]{2,1,0:T(8,128)(2,1)S(1)} %collective-permute-done.8.refs_0_, ...), custom_call_target="tpu_custom_call" | custom-call | flops 20000000000 | tf_op jit(solution)/shard_map/long_conv/pallas_call | solution.py:375
  51.2 1.9 %collective-permute-done.11.swapped.refs_1_ = bf16[4,512,128]{2,1,0:T(8,128)(2,1)S(1)} collective-permute-done((bf16[4,512,128]{2,1,0:T(8,128)(2,1)S(1)}, bf16[4,512,128]{2,1,0:T(8,128)(2,1)S(1)}, u32[]{:S(2)}, u32[]{:S(2)}) %collective-permute-start.11) | collective-permute-done | bytes 524320 | tf_op jit(solution)/shard_map/ppermute | solution.py:1015
  53.2 1.6 %collective-permute-start.12 = (bf16[2,512,128]{2,1,0:T(8,128)(2,1)S(1)}, bf16[2,512,128]{2,1,0:T(8,128)(2,1)S(1)}, u32[]{:S(2)}, u32[]{:S(2)}) collective-permute-start(bf16[2,512,128]{2,1,0:T(8,128)(2,1)S(1)} %get-tuple-element.63), channel_id=1, source_target_pairs={{0,8},{4,12},{8,0},{12,4},{16,24},{20,28},{24,16},{28,20},{1,9},{5... | collective-permute-start | bytes 786440 | tf_op jit(solution)/shard_map/ppermute | solution.py:1017
  54.7 0.8 collective-permute-start.13
  55.6 1.2 collective-permute-start.14
  58.1 1.9 %constant_dynamic-slice_fusion.refs_6_.far_weight = bf16[1024,1024]{1,0:T(8,128)(2,1)S(1)} fusion(bf16[1024,4096]{1,0:T(8,128)(2,1)} %weight.9, s32[]{:T(128)S(6)} %select_n.62), kind=kLoop, calls=%fused_computation.5 | loop fusion | bytes 4194308 | tf_op jit(solution)/shard_map/dynamic_slice | solution.py:962
  60.0 1.1 mix_query.1.refs_5_
  61.1 1.3 collective-permute-done.12.refs_2_
  62.4 6.0 %collective-permute-done.13.refs_3_ = bf16[2,512,128]{2,1,0:T(8,128)(2,1)S(1)} collective-permute-done((bf16[2,512,128]{2,1,0:T(8,128)(2,1)S(1)}, bf16[2,512,128]{2,1,0:T(8,128)(2,1)S(1)}, u32[]{:S(2)}, u32[]{:S(2)}) %collective-permute-start.13) | collective-permute-done | bytes 262176 | tf_op jit(solution)/shard_map/ppermute | solution.py:1017
  68.4 1.6 %gate_out.1 = (bf16[2,256,1024]{2,1,0:T(8,128)(2,1)S(1)}, bf16[256,1024]{1,0:T(8,128)(2,1)S(1)}) custom-call(s32[3]{0:T(128)S(1)} %pad_add_fusion.spot, bf16[512,128]{1,0:T(8,128)(2,1)S(1)} %get-tuple-element.60.refs_0_, bf16[4,512,128]{2,1,0:T(8,128)(2,1)S(1)} %collective-permute-done.11.swapped.refs_1_, ...), custom_call_target="tpu_custom_call" | custom-call | tf_op jit(solution)/shard_map/gate_out/pallas_call | solution.py:620
  70.1 3.7 %collective-permute-start.15 = (bf16[256,1024]{1,0:T(8,128)(2,1)S(1)}, bf16[256,1024]{1,0:T(8,128)(2,1)S(1)}, u32[]{:S(2)}, u32[]{:S(2)}) collective-permute-start(bf16[256,1024]{1,0:T(8,128)(2,1)S(1)} %get-tuple-element.67), channel_id=1, source_target_pairs={{0,1},{1,2},{2,3},{5,4},{6,5},{7,6},{8,9},{9,10},{10,11},{13,12},{... | collective-permute-start | bytes 1572872 | tf_op jit(solution)/shard_map/ppermute | solution.py:970
  73.8 1.1 pad_maximum_fusion.refs_0_
  75.0 1.3 partner_sent.1
  76.2 3.7 %collective-permute-start.18 = (bf16[256,1024]{1,0:T(8,128)(2,1)S(1)}, bf16[256,1024]{1,0:T(8,128)(2,1)S(1)}, u32[]{:S(2)}, u32[]{:S(2)}) collective-permute-start(bf16[256,1024]{1,0:T(8,128)(2,1)S(1)} %partner_sent.1), channel_id=1, source_target_pairs={{0,1},{1,2},{2,3},{5,4},{6,5},{7,6},{8,9},{9,10},{10,11},{13,12},{... | collective-permute-start | bytes 1572872 | tf_op jit(solution)/shard_map/ppermute | solution.py:970
  80.0 1.5 %collective-permute-start.20 = (bf16[384,1024]{1,0:T(8,128)(2,1)S(1)}, bf16[384,1024]{1,0:T(8,128)(2,1)S(1)}, u32[]{:S(2)}, u32[]{:S(2)}) collective-permute-start(bf16[384,1024]{1,0:T(8,128)(2,1)S(1)} %pad_maximum_fusion.refs_0_), channel_id=1, source_target_pairs={{0,8},{4,20},{8,0},{12,28},{16,24},{20,4},{24,16},{28,12},{1,9},{5... | collective-permute-start | bytes 2359304 | tf_op jit(solution)/shard_map/ppermute | solution.py:765
  81.5 3.7 %sent_terms.1.term = bf16[2,2,256,1024]{3,2,1,0:T(8,128)(2,1)S(1)} custom-call(s32[5]{0:T(128)S(1)} %or_select_fusion.plan, bf16[2,256,1024]{2,1,0:T(8,128)(2,1)S(1)} %get-tuple-element.66.mine.head, bf16[2,256,1024]{2,1,0:T(8,128)(2,1)S(1)} %collective-permute-done.16.partners.gated.head, bf16[1024,4096]{1,0:T(8,128)(2,1)S(1)} %bitcast.20), custom_call_target="tpu_custom_call" | custom-call | flops 4000000000 | tf_op jit(solution)/shard_map/sent_terms/pallas_call | solution.py:701
  85.8 2.0 %collective-permute-start.17 = (bf16[256,1024]{1,0:T(8,128)(2,1)S(1)}, bf16[256,1024]{1,0:T(8,128)(2,1)S(1)}, u32[]{:S(2)}, u32[]{:S(2)}) collective-permute-start(bf16[256,1024]{1,0:T(8,128)(2,1)S(1)} %next_step.6), channel_id=1, source_target_pairs={{0,1},{1,2},{2,3},{5,4},{6,5},{7,6},{8,9},{9,10},{10,11},{13,12},{... | collective-permute-start | bytes 1572872 | tf_op jit(solution)/shard_map/ppermute | solution.py:970
  88.4 3.4 %collective-permute-start.19 = (bf16[256,1024]{1,0:T(8,128)(2,1)S(1)}, bf16[256,1024]{1,0:T(8,128)(2,1)S(1)}, u32[]{:S(2)}, u32[]{:S(2)}) collective-permute-start(bf16[256,1024]{1,0:T(8,128)(2,1)S(1)} %next_step.7), channel_id=1, source_target_pairs={{0,1},{1,2},{2,3},{5,4},{6,5},{7,6},{8,9},{9,10},{10,11},{13,12},{... | collective-permute-start | bytes 1572872 | tf_op jit(solution)/shard_map/ppermute | solution.py:970
  91.9 1.6 %collective-permute-start.21 = (bf16[384,1024]{1,0:T(8,128)(2,1)S(1)}, bf16[384,1024]{1,0:T(8,128)(2,1)S(1)}, u32[]{:S(2)}, u32[]{:S(2)}) collective-permute-start(bf16[384,1024]{1,0:T(8,128)(2,1)S(1)} %pad_maximum_fusion.refs_0_), channel_id=1, source_target_pairs={{0,16},{4,12},{8,24},{12,4},{16,0},{20,28},{24,8},{28,20},{1,17},{... | collective-permute-start | bytes 2359304 | tf_op jit(solution)/shard_map/ppermute | solution.py:771
  93.5 0.9 collective-permute-start.22
  95.2 4.3 %collective-permute-start.25 = (bf16[256,1024]{1,0:T(8,128)(2,1)S(1)}, bf16[256,1024]{1,0:T(8,128)(2,1)S(1)}, u32[]{:S(2)}, u32[]{:S(2)}) collective-permute-start(bf16[256,1024]{1,0:T(8,128)(2,1)S(1)} %next_step.8), channel_id=1, source_target_pairs={{0,1},{1,2},{2,3},{5,4},{6,5},{7,6},{8,9},{9,10},{10,11},{13,12},{... | collective-permute-start | bytes 1572872 | tf_op jit(solution)/shard_map/ppermute | solution.py:970
  100.8 4.3 %collective-permute-start.29 = (bf16[256,1024]{1,0:T(8,128)(2,1)S(1)}, bf16[256,1024]{1,0:T(8,128)(2,1)S(1)}, u32[]{:S(2)}, u32[]{:S(2)}) collective-permute-start(bf16[256,1024]{1,0:T(8,128)(2,1)S(1)} %next_step.10), channel_id=1, source_target_pairs={{0,1},{1,2},{2,3},{5,4},{6,5},{7,6},{8,9},{9,10},{10,11},{13,12},{... | collective-permute-start | bytes 1572872 | tf_op jit(solution)/shard_map/ppermute | solution.py:970
  105.1 1.0 collective-permute-done.25.got.got2
  106.8 4.4 %collective-permute-start.28 = (bf16[256,1024]{1,0:T(8,128)(2,1)S(1)}, bf16[256,1024]{1,0:T(8,128)(2,1)S(1)}, u32[]{:S(2)}, u32[]{:S(2)}) collective-permute-start(bf16[256,1024]{1,0:T(8,128)(2,1)S(1)} %next_step.9), channel_id=1, source_target_pairs={{0,1},{1,2},{2,3},{5,4},{6,5},{7,6},{8,9},{9,10},{10,11},{13,12},{... | collective-permute-start | bytes 1572872 | tf_op jit(solution)/shard_map/ppermute | solution.py:970
  113.6 4.3 %collective-permute-done.28.got3 = bf16[256,1024]{1,0:T(8,128)(2,1)S(1)} collective-permute-done((bf16[256,1024]{1,0:T(8,128)(2,1)S(1)}, bf16[256,1024]{1,0:T(8,128)(2,1)S(1)}, u32[]{:S(2)}, u32[]{:S(2)}) %collective-permute-start.28) | collective-permute-done | bytes 524320 | tf_op jit(solution)/shard_map/ppermute | solution.py:970
  117.9 4.4 %collective-permute-start.30 = (bf16[256,1024]{1,0:T(8,128)(2,1)S(1)}, bf16[256,1024]{1,0:T(8,128)(2,1)S(1)}, u32[]{:S(2)}, u32[]{:S(2)}) collective-permute-start(bf16[256,1024]{1,0:T(8,128)(2,1)S(1)} %next_step.11), channel_id=1, source_target_pairs={{0,1},{1,2},{2,3},{5,4},{6,5},{7,6},{8,9},{9,10},{10,11},{13,12},{... | collective-permute-start | bytes 1572872 | tf_op jit(solution)/shard_map/ppermute | solution.py:970
  122.4 2.4 %early_sum.1 = (f32[512,1024]{1,0:T(8,128)S(1)}, f32[256,1024]{1,0:T(8,128)S(1)}) custom-call(s32[10]{0:T(128)S(1)} %stack.63.order, bf16[2,256,1024]{2,1,0:T(8,128)(2,1)S(1)} %get-tuple-element.66.mine.head, bf16[256,1024]{1,0:T(8,128)(2,1)S(1)} %collective-permute-done.15.got.got0, bf16[256,1024]{1,0:T(8,128)(2,1)S(1)} %collective-permute-done.17.got.got1, ...), custom_call_target="tpu_custom_call" | custom-call | flops 1000000000 | tf_op jit(solution)/shard_map/early_sum/pallas_call | solution.py:830
  124.7 4.2 %collective-permute-done.30.got3 = bf16[256,1024]{1,0:T(8,128)(2,1)S(1)} collective-permute-done((bf16[256,1024]{1,0:T(8,128)(2,1)S(1)}, bf16[256,1024]{1,0:T(8,128)(2,1)S(1)}, u32[]{:S(2)}, u32[]{:S(2)}) %collective-permute-start.30) | collective-permute-done | bytes 524320 | tf_op jit(solution)/shard_map/ppermute | solution.py:970
  129.0 0.8 partner_sum.1
  129.9 0.9 mine_sum.1.mine
  130.8 1.7 %collective-permute-done.31.partners = bf16[2,256,1024]{2,1,0:T(8,128)(2,1)S(1)} collective-permute-done((bf16[2,256,1024]{2,1,0:T(8,128)(2,1)S(1)}, bf16[2,256,1024]{2,1,0:T(8,128)(2,1)S(1)}, u32[]{:S(2)}, u32[]{:S(2)}) %collective-permute-start.31) | collective-permute-done | bytes 1048608 | tf_op jit(solution)/shard_map/ppermute | solution.py:971
  132.6 1.1 join_sums.1
  (79 shorter events, 9.8 us)
Async XLA Ops:
  0.0 22.9 %copy-start = (f32[1024]{0:T(1024)S(1)}, f32[1024]{0:T(1024)}, u32[]{:S(2)}) copy-start(f32[1024]{0:T(1024)} %param.15) | copy-start | bytes 12292
  0.0 4.9 %copy-start.2 = (bf16[1024,512]{1,0:T(8,128)(2,1)S(1)}, bf16[1024,512]{1,0:T(8,128)(2,1)}, u32[]{:S(2)}) copy-start(bf16[1024,512]{1,0:T(8,128)(2,1)} %taps.1) | copy-start | bytes 3145732
  1.5 3.4 %collective-permute-start = (bf16[6,1024]{1,0:T(8,128)(2,1)}, bf16[6,1024]{1,0:T(8,128)(2,1)S(1)}, u32[]{:S(2)}, u32[]{:S(2)}) collective-permute-start(bf16[6,1024]{1,0:T(8,128)(2,1)} %rims.1), channel_id=1, source_target_pairs={{0,4},{4,8},{8,12},{12,16},{16,20},{20,24},{24,28},{1,5},{5,9},{9,... | collective-permute-start | bytes 36872 | tf_op jit(solution)/shard_map/ppermute | solution.py:18
  4.9 10.8 %copy-start.5 = (bf16[6,1024]{1,0:T(8,128)(2,1)}, bf16[6,1024]{1,0:T(8,128)(2,1)S(1)}, u32[]{:S(2)}) copy-start(bf16[6,1024]{1,0:T(8,128)(2,1)S(1)} %collective-permute-done.edges) | copy-start | bytes 36868
  5.1 15.0 %collective-permute-start.1 = (bf16[256,512]{1,0:T(8,128)(2,1)S(1)}, bf16[256,512]{1,0:T(8,128)(2,1)S(1)}, u32[]{:S(2)}, u32[]{:S(2)}) collective-permute-start(bf16[256,512]{1,0:T(8,128)(2,1)S(1)} %get-tuple-element.47), channel_id=1, source_target_pairs={{0,8},{4,12},{8,0},{12,4},{16,24},{20,28},{24,16},{28,20},{1,9},{5... | collective-permute-start | bytes 786440 | tf_op jit(solution)/shard_map/ppermute | solution.py:1017
  10.0 12.9 %collective-permute-start.2 = (bf16[256,512]{1,0:T(8,128)(2,1)S(1)}, bf16[256,512]{1,0:T(8,128)(2,1)S(1)}, u32[]{:S(2)}, u32[]{:S(2)}) collective-permute-start(bf16[256,512]{1,0:T(8,128)(2,1)S(1)} %get-tuple-element.48), channel_id=1, source_target_pairs={{0,16},{4,20},{8,24},{12,28},{16,0},{20,4},{24,8},{28,12},{1,17},{... | collective-permute-start | bytes 786440 | tf_op jit(solution)/shard_map/ppermute | solution.py:1017
  11.5 11.3 %collective-permute-start.3 = (bf16[256,512]{1,0:T(8,128)(2,1)S(1)}, bf16[256,512]{1,0:T(8,128)(2,1)S(1)}, u32[]{:S(2)}, u32[]{:S(2)}) collective-permute-start(bf16[256,512]{1,0:T(8,128)(2,1)S(1)} %get-tuple-element.49), channel_id=1, source_target_pairs={{0,24},{4,28},{8,16},{12,20},{16,8},{20,12},{24,0},{28,4},{1,25},{... | collective-permute-start | bytes 786440 | tf_op jit(solution)/shard_map/ppermute | solution.py:1017
  15.7 16.1 %copy-start.8 = (bf16[256,768]{1,0:T(8,128)(2,1)S(1)}, bf16[256,768]{1,0:T(8,128)(2,1)}, u32[]{:S(2)}) copy-start(bf16[256,768]{1,0:T(8,128)(2,1)} %constant.80.clone.refs_6_.refs_5_) | copy-start | bytes 1179652
  15.7 16.1 %copy-start.10 = (f32[128,66]{1,0:T(8,128)S(1)}, f32[128,66]{1,0:T(8,128)}, u32[]{:S(2)}) copy-start(f32[128,66]{1,0:T(8,128)} %constant.82.clone.refs_5_.refs_4_) | copy-start | bytes 101380
  20.0 3.0 %collective-permute-start.7 = (bf16[4,512,128]{2,1,0:T(8,128)(2,1)}, bf16[4,512,128]{2,1,0:T(8,128)(2,1)S(1)}, u32[]{:S(2)}, u32[]{:S(2)}) collective-permute-start(bf16[4,512,128]{2,1,0:T(8,128)(2,1)} %get-tuple-element.55), channel_id=1, source_target_pairs={{0,4},{4,0},{8,12},{12,8},{16,20},{20,16},{24,28},{28,24},{1,5},{5... | collective-permute-start | bytes 1572872 | tf_op jit(solution)/shard_map/ppermute | solution.py:1015
  22.9 4.8 %collective-permute-start.4 = (bf16[4,128,512]{2,1,0:T(8,128)(2,1)S(1)}, bf16[4,128,512]{2,1,0:T(8,128)(2,1)S(1)}, u32[]{:S(2)}, u32[]{:S(2)}) collective-permute-start(bf16[4,128,512]{2,1,0:T(8,128)(2,1)S(1)} %other_core.1), channel_id=1, source_target_pairs={{0,4},{4,0},{8,12},{12,8},{16,20},{20,16},{24,28},{28,24},{1,5},{5... | collective-permute-start | bytes 1572872 | tf_op jit(solution)/shard_map/ppermute | solution.py:1015
  23.0 1.0 copy-start.3
  24.1 13.2 %collective-permute-start.8 = (bf16[2,512,128]{2,1,0:T(8,128)(2,1)S(1)}, bf16[2,512,128]{2,1,0:T(8,128)(2,1)S(1)}, u32[]{:S(2)}, u32[]{:S(2)}) collective-permute-start(bf16[2,512,128]{2,1,0:T(8,128)(2,1)S(1)} %get-tuple-element.57), channel_id=1, source_target_pairs={{0,8},{4,12},{8,0},{12,4},{16,24},{20,28},{24,16},{28,20},{1,9},{5... | collective-permute-start | bytes 786440 | tf_op jit(solution)/shard_map/ppermute | solution.py:1017
  24.7 13.1 %collective-permute-start.9 = (bf16[2,512,128]{2,1,0:T(8,128)(2,1)S(1)}, bf16[2,512,128]{2,1,0:T(8,128)(2,1)S(1)}, u32[]{:S(2)}, u32[]{:S(2)}) collective-permute-start(bf16[2,512,128]{2,1,0:T(8,128)(2,1)S(1)} %get-tuple-element.58), channel_id=1, source_target_pairs={{0,16},{4,20},{8,24},{12,28},{16,0},{20,4},{24,8},{28,12},{1,17},{... | collective-permute-start | bytes 786440 | tf_op jit(solution)/shard_map/ppermute | solution.py:1017
  26.2 12.5 %copy-start.7 = (bf16[512,128]{1,0:T(8,128)(2,1)S(1)}, bf16[512,128]{1,0:T(8,128)(2,1)}, u32[]{:S(2)}) copy-start(bf16[512,128]{1,0:T(8,128)(2,1)} %get-tuple-element.54.stay) | copy-start | bytes 393220
  26.2 12.5 %copy-start.9 = (bf16[256,768]{1,0:T(8,128)(2,1)S(1)}, bf16[256,768]{1,0:T(8,128)(2,1)}, u32[]{:S(2)}) copy-start(bf16[256,768]{1,0:T(8,128)(2,1)} %constant.81.clone.refs_6_) | copy-start | bytes 1179652
  26.2 12.5 %collective-permute-start.10 = (bf16[2,512,128]{2,1,0:T(8,128)(2,1)S(1)}, bf16[2,512,128]{2,1,0:T(8,128)(2,1)S(1)}, u32[]{:S(2)}, u32[]{:S(2)}) collective-permute-start(bf16[2,512,128]{2,1,0:T(8,128)(2,1)S(1)} %get-tuple-element.59), channel_id=1, source_target_pairs={{0,24},{4,28},{8,16},{12,20},{16,8},{20,12},{24,0},{28,4},{1,25},{... | collective-permute-start | bytes 786440 | tf_op jit(solution)/shard_map/ppermute | solution.py:1017
  27.6 23.3 %collective-permute-start.6 = (bf16[128,1024]{1,0:T(8,128)(2,1)}, bf16[128,1024]{1,0:T(8,128)(2,1)S(1)}, u32[]{:S(2)}, u32[]{:S(2)}) collective-permute-start(bf16[128,1024]{1,0:T(8,128)(2,1)} %get-tuple-element.51), channel_id=1, source_target_pairs={{0,2},{1,3},{2,0},{3,1},{4,6},{5,7},{6,4},{7,5},{8,10},{9,11},{10,... | collective-permute-start | bytes 786440 | tf_op jit(solution)/shard_map/ppermute | solution.py:731
  30.2 20.8 %collective-permute-start.5 = (bf16[256,1024]{1,0:T(8,128)(2,1)}, bf16[256,1024]{1,0:T(8,128)(2,1)}, u32[]{:S(2)}, u32[]{:S(2)}) collective-permute-start(bf16[256,1024]{1,0:T(8,128)(2,1)} %get-tuple-element.50), channel_id=1, source_target_pairs={{0,1},{1,2},{2,3},{3,0},{4,7},{5,4},{6,5},{7,6},{8,9},{9,10},{10,1... | collective-permute-start | bytes 1572872 | tf_op jit(solution)/shard_map/ppermute | solution.py:731
  51.0 5.8 %copy-start.11 = (bf16[128,1024]{1,0:T(8,128)(2,1)}, bf16[128,1024]{1,0:T(8,128)(2,1)S(1)}, u32[]{:S(2)}) copy-start(bf16[128,1024]{1,0:T(8,128)(2,1)S(1)} %collective-permute-done.6) | copy-start | bytes 786436
  51.0 9.0 %copy-start.1 = (bf16[512,1024]{1,0:T(8,128)(2,1)S(1)}, bf16[512,1024]{1,0:T(8,128)(2,1)}, u32[]{:S(2)}) copy-start(bf16[512,1024]{1,0:T(8,128)(2,1)} %query.3) | copy-start | bytes 3145732
  51.0 9.0 %copy-start.4 = (f32[3,3,1024]{2,1,0:T(4,128)S(1)}, f32[3,3,1024]{2,1,0:T(4,128)}, u32[]{:S(2)}) copy-start(f32[3,3,1024]{2,1,0:T(4,128)} %weight.7) | copy-start | bytes 110596
  51.0 9.0 %copy-start.6 = (bf16[6,1024]{1,0:T(8,128)(2,1)S(1)}, bf16[6,1024]{1,0:T(8,128)(2,1)}, u32[]{:S(2)}) copy-start(bf16[6,1024]{1,0:T(8,128)(2,1)} %copy-done.5) | copy-start | bytes 36868
  51.2 2.0 %collective-permute-start.11 = (bf16[4,512,128]{2,1,0:T(8,128)(2,1)S(1)}, bf16[4,512,128]{2,1,0:T(8,128)(2,1)S(1)}, u32[]{:S(2)}, u32[]{:S(2)}) collective-permute-start(bf16[4,512,128]{2,1,0:T(8,128)(2,1)S(1)} %get-tuple-element.61), channel_id=1, source_target_pairs={{0,4},{4,0},{8,12},{12,8},{16,20},{20,16},{24,28},{28,24},{1,5},{5... | collective-permute-start | bytes 1572872 | tf_op jit(solution)/shard_map/ppermute | solution.py:1015
  53.2 9.2 %collective-permute-start.12 = (bf16[2,512,128]{2,1,0:T(8,128)(2,1)S(1)}, bf16[2,512,128]{2,1,0:T(8,128)(2,1)S(1)}, u32[]{:S(2)}, u32[]{:S(2)}) collective-permute-start(bf16[2,512,128]{2,1,0:T(8,128)(2,1)S(1)} %get-tuple-element.63), channel_id=1, source_target_pairs={{0,8},{4,12},{8,0},{12,4},{16,24},{20,28},{24,16},{28,20},{1,9},{5... | collective-permute-start | bytes 786440 | tf_op jit(solution)/shard_map/ppermute | solution.py:1017
  54.7 13.7 %collective-permute-start.13 = (bf16[2,512,128]{2,1,0:T(8,128)(2,1)S(1)}, bf16[2,512,128]{2,1,0:T(8,128)(2,1)S(1)}, u32[]{:S(2)}, u32[]{:S(2)}) collective-permute-start(bf16[2,512,128]{2,1,0:T(8,128)(2,1)S(1)} %get-tuple-element.64), channel_id=1, source_target_pairs={{0,16},{4,20},{8,24},{12,28},{16,0},{20,4},{24,8},{28,12},{1,17},{... | collective-permute-start | bytes 786440 | tf_op jit(solution)/shard_map/ppermute | solution.py:1017
  55.6 12.9 %collective-permute-start.14 = (bf16[2,512,128]{2,1,0:T(8,128)(2,1)S(1)}, bf16[2,512,128]{2,1,0:T(8,128)(2,1)S(1)}, u32[]{:S(2)}, u32[]{:S(2)}) collective-permute-start(bf16[2,512,128]{2,1,0:T(8,128)(2,1)S(1)} %get-tuple-element.65), channel_id=1, source_target_pairs={{0,24},{4,28},{8,16},{12,20},{16,8},{20,12},{24,0},{28,4},{1,25},{... | collective-permute-start | bytes 786440 | tf_op jit(solution)/shard_map/ppermute | solution.py:1017
  58.0 23.5 %slice-start = ((s8[8388608]{0:T(1024)(128)(4,1)}), s8[4194304]{0:T(1024)(128)(4,1)S(1)}, s32[]{:S(2)}) async-start(s8[8388608]{0:T(1024)(128)(4,1)} %bitcast.19), calls=%async_computation | async-start | bytes 8388608
  68.4 5.4 %copy-start.12 = (bf16[128,1024]{1,0:T(8,128)(2,1)S(1)}, bf16[128,1024]{1,0:T(8,128)(2,1)}, u32[]{:S(2)}) copy-start(bf16[128,1024]{1,0:T(8,128)(2,1)} %copy-done.11) | copy-start | bytes 786436
  68.4 13.1 %slice-start.1 = ((s8[8388608]{0:T(1024)(128)(4,1)}), s8[4194304]{0:T(1024)(128)(4,1)S(1)}, s32[]{:S(2)}) async-start(s8[8388608]{0:T(1024)(128)(4,1)} %bitcast.19), calls=%async_computation.1 | async-start | bytes 8388608
  70.1 4.9 %collective-permute-start.16 = (bf16[2,256,1024]{2,1,0:T(8,128)(2,1)S(1)}, bf16[2,256,1024]{2,1,0:T(8,128)(2,1)S(1)}, u32[]{:S(2)}, u32[]{:S(2)}) collective-permute-start(bf16[2,256,1024]{2,1,0:T(8,128)(2,1)S(1)} %get-tuple-element.66.mine.head), channel_id=1, source_target_pairs={{0,4},{4,0},{8,12},{12,8},{16,20},{20,16},{24,28},{28,24},{1,5},{5... | collective-permute-start | bytes 3145736 | tf_op jit(solution)/shard_map/ppermute | solution.py:971
  70.1 15.1 %collective-permute-start.15 = (bf16[256,1024]{1,0:T(8,128)(2,1)S(1)}, bf16[256,1024]{1,0:T(8,128)(2,1)S(1)}, u32[]{:S(2)}, u32[]{:S(2)}) collective-permute-start(bf16[256,1024]{1,0:T(8,128)(2,1)S(1)} %get-tuple-element.67), channel_id=1, source_target_pairs={{0,1},{1,2},{2,3},{5,4},{6,5},{7,6},{8,9},{9,10},{10,11},{13,12},{... | collective-permute-start | bytes 1572872 | tf_op jit(solution)/shard_map/ppermute | solution.py:970
  76.2 11.6 %collective-permute-start.18 = (bf16[256,1024]{1,0:T(8,128)(2,1)S(1)}, bf16[256,1024]{1,0:T(8,128)(2,1)S(1)}, u32[]{:S(2)}, u32[]{:S(2)}) collective-permute-start(bf16[256,1024]{1,0:T(8,128)(2,1)S(1)} %partner_sent.1), channel_id=1, source_target_pairs={{0,1},{1,2},{2,3},{5,4},{6,5},{7,6},{8,9},{9,10},{10,11},{13,12},{... | collective-permute-start | bytes 1572872 | tf_op jit(solution)/shard_map/ppermute | solution.py:970
  80.0 13.5 %collective-permute-start.20 = (bf16[384,1024]{1,0:T(8,128)(2,1)S(1)}, bf16[384,1024]{1,0:T(8,128)(2,1)S(1)}, u32[]{:S(2)}, u32[]{:S(2)}) collective-permute-start(bf16[384,1024]{1,0:T(8,128)(2,1)S(1)} %pad_maximum_fusion.refs_0_), channel_id=1, source_target_pairs={{0,8},{4,20},{8,0},{12,28},{16,24},{20,4},{24,16},{28,12},{1,9},{5... | collective-permute-start | bytes 2359304 | tf_op jit(solution)/shard_map/ppermute | solution.py:765
  85.8 8.7 %collective-permute-start.17 = (bf16[256,1024]{1,0:T(8,128)(2,1)S(1)}, bf16[256,1024]{1,0:T(8,128)(2,1)S(1)}, u32[]{:S(2)}, u32[]{:S(2)}) collective-permute-start(bf16[256,1024]{1,0:T(8,128)(2,1)S(1)} %next_step.6), channel_id=1, source_target_pairs={{0,1},{1,2},{2,3},{5,4},{6,5},{7,6},{8,9},{9,10},{10,11},{13,12},{... | collective-permute-start | bytes 1572872 | tf_op jit(solution)/shard_map/ppermute | solution.py:970
  88.4 11.7 %collective-permute-start.19 = (bf16[256,1024]{1,0:T(8,128)(2,1)S(1)}, bf16[256,1024]{1,0:T(8,128)(2,1)S(1)}, u32[]{:S(2)}, u32[]{:S(2)}) collective-permute-start(bf16[256,1024]{1,0:T(8,128)(2,1)S(1)} %next_step.7), channel_id=1, source_target_pairs={{0,1},{1,2},{2,3},{5,4},{6,5},{7,6},{8,9},{9,10},{10,11},{13,12},{... | collective-permute-start | bytes 1572872 | tf_op jit(solution)/shard_map/ppermute | solution.py:970
  91.9 19.5 %collective-permute-start.21 = (bf16[384,1024]{1,0:T(8,128)(2,1)S(1)}, bf16[384,1024]{1,0:T(8,128)(2,1)S(1)}, u32[]{:S(2)}, u32[]{:S(2)}) collective-permute-start(bf16[384,1024]{1,0:T(8,128)(2,1)S(1)} %pad_maximum_fusion.refs_0_), channel_id=1, source_target_pairs={{0,16},{4,12},{8,24},{12,4},{16,0},{20,28},{24,8},{28,20},{1,17},{... | collective-permute-start | bytes 2359304 | tf_op jit(solution)/shard_map/ppermute | solution.py:771
  93.5 18.9 %collective-permute-start.22 = (bf16[384,1024]{1,0:T(8,128)(2,1)S(1)}, bf16[384,1024]{1,0:T(8,128)(2,1)S(1)}, u32[]{:S(2)}, u32[]{:S(2)}) collective-permute-start(bf16[384,1024]{1,0:T(8,128)(2,1)S(1)} %collective-permute-done.20.refs_1_), channel_id=1, source_target_pairs={{0,16},{4,12},{8,24},{12,4},{16,0},{20,28},{24,8},{28,20},{1,17},{... | collective-permute-start | bytes 2359304 | tf_op jit(solution)/shard_map/ppermute | solution.py:771
  95.2 11.0 %collective-permute-start.25 = (bf16[256,1024]{1,0:T(8,128)(2,1)S(1)}, bf16[256,1024]{1,0:T(8,128)(2,1)S(1)}, u32[]{:S(2)}, u32[]{:S(2)}) collective-permute-start(bf16[256,1024]{1,0:T(8,128)(2,1)S(1)} %next_step.8), channel_id=1, source_target_pairs={{0,1},{1,2},{2,3},{5,4},{6,5},{7,6},{8,9},{9,10},{10,11},{13,12},{... | collective-permute-start | bytes 1572872 | tf_op jit(solution)/shard_map/ppermute | solution.py:970
  100.8 11.6 %collective-permute-start.29 = (bf16[256,1024]{1,0:T(8,128)(2,1)S(1)}, bf16[256,1024]{1,0:T(8,128)(2,1)S(1)}, u32[]{:S(2)}, u32[]{:S(2)}) collective-permute-start(bf16[256,1024]{1,0:T(8,128)(2,1)S(1)} %next_step.10), channel_id=1, source_target_pairs={{0,1},{1,2},{2,3},{5,4},{6,5},{7,6},{8,9},{9,10},{10,11},{13,12},{... | collective-permute-start | bytes 1572872 | tf_op jit(solution)/shard_map/ppermute | solution.py:970
  106.8 11.1 %collective-permute-start.28 = (bf16[256,1024]{1,0:T(8,128)(2,1)S(1)}, bf16[256,1024]{1,0:T(8,128)(2,1)S(1)}, u32[]{:S(2)}, u32[]{:S(2)}) collective-permute-start(bf16[256,1024]{1,0:T(8,128)(2,1)S(1)} %next_step.9), channel_id=1, source_target_pairs={{0,1},{1,2},{2,3},{5,4},{6,5},{7,6},{8,9},{9,10},{10,11},{13,12},{... | collective-permute-start | bytes 1572872 | tf_op jit(solution)/shard_map/ppermute | solution.py:970
  111.3 11.1 %collective-permute-start.23 = (bf16[384,1024]{1,0:T(8,128)(2,1)S(1)}, bf16[384,1024]{1,0:T(8,128)(2,1)S(1)}, u32[]{:S(2)}, u32[]{:S(2)}) collective-permute-start(bf16[384,1024]{1,0:T(8,128)(2,1)S(1)} %pad_maximum_fusion.refs_0_), channel_id=1, source_target_pairs={{0,4},{4,0},{8,12},{12,8},{16,20},{20,16},{24,28},{28,24},{1,5},{5... | collective-permute-start | bytes 2359304 | tf_op jit(solution)/shard_map/ppermute | solution.py:773
  111.4 11.0 %collective-permute-start.24 = (bf16[384,1024]{1,0:T(8,128)(2,1)S(1)}, bf16[384,1024]{1,0:T(8,128)(2,1)S(1)}, u32[]{:S(2)}, u32[]{:S(2)}) collective-permute-start(bf16[384,1024]{1,0:T(8,128)(2,1)S(1)} %collective-permute-done.20.refs_1_), channel_id=1, source_target_pairs={{0,4},{4,0},{8,12},{12,8},{16,20},{20,16},{24,28},{28,24},{1,5},{5... | collective-permute-start | bytes 2359304 | tf_op jit(solution)/shard_map/ppermute | solution.py:773
  112.4 10.0 %collective-permute-start.26 = (bf16[384,1024]{1,0:T(8,128)(2,1)S(1)}, bf16[384,1024]{1,0:T(8,128)(2,1)S(1)}, u32[]{:S(2)}, u32[]{:S(2)}) collective-permute-start(bf16[384,1024]{1,0:T(8,128)(2,1)S(1)} %collective-permute-done.21.refs_2_), channel_id=1, source_target_pairs={{0,4},{4,0},{8,12},{12,8},{16,20},{20,16},{24,28},{28,24},{1,5},{5... | collective-permute-start | bytes 2359304 | tf_op jit(solution)/shard_map/ppermute | solution.py:773
  112.4 10.0 %collective-permute-start.27 = (bf16[384,1024]{1,0:T(8,128)(2,1)S(1)}, bf16[384,1024]{1,0:T(8,128)(2,1)S(1)}, u32[]{:S(2)}, u32[]{:S(2)}) collective-permute-start(bf16[384,1024]{1,0:T(8,128)(2,1)S(1)} %collective-permute-done.22.refs_3_), channel_id=1, source_target_pairs={{0,4},{4,0},{8,12},{12,8},{16,20},{20,16},{24,28},{28,24},{1,5},{5... | collective-permute-start | bytes 2359304 | tf_op jit(solution)/shard_map/ppermute | solution.py:773
  117.9 11.1 %collective-permute-start.30 = (bf16[256,1024]{1,0:T(8,128)(2,1)S(1)}, bf16[256,1024]{1,0:T(8,128)(2,1)S(1)}, u32[]{:S(2)}, u32[]{:S(2)}) collective-permute-start(bf16[256,1024]{1,0:T(8,128)(2,1)S(1)} %next_step.11), channel_id=1, source_target_pairs={{0,1},{1,2},{2,3},{5,4},{6,5},{7,6},{8,9},{9,10},{10,11},{13,12},{... | collective-permute-start | bytes 1572872 | tf_op jit(solution)/shard_map/ppermute | solution.py:970
  129.8 2.7 %collective-permute-start.31 = (bf16[2,256,1024]{2,1,0:T(8,128)(2,1)S(1)}, bf16[2,256,1024]{2,1,0:T(8,128)(2,1)S(1)}, u32[]{:S(2)}, u32[]{:S(2)}) collective-permute-start(bf16[2,256,1024]{2,1,0:T(8,128)(2,1)S(1)} %partner_sum.1), channel_id=1, source_target_pairs={{0,4},{4,0},{8,12},{12,8},{16,20},{20,16},{24,28},{28,24},{1,5},{5... | collective-permute-start | bytes 3145736 | tf_op jit(solution)/shard_map/ppermute | solution.py:971

commit v8 on v7

--- a/solution.py
+++ b/solution.py
@@ -765,12 +765,10 @@
     return lax.ppermute(part, "ctx", [(i, i ^ (4 if i & 1 else 2)) for i in devices])
 
 
-def gather_weight(two, ready):
+def swap_other(two):
     devices = range(lax.axis_size("ctx"))
     other = [(i, i ^ (2 if i & 1 else 4)) for i in devices]
-    near = [*two, *[lax.ppermute(x, "ctx", other) for x in two]]
-    apart = near[:2] + after(near[2:], ready)
-    return near + [lax.ppermute(x, "ctx", [(i, i ^ 1) for i in devices]) for x in apart]
+    return [lax.ppermute(x, "ctx", other) for x in two]
 
 
 def add_parts(order, data, parts, hops):
@@ -975,15 +973,19 @@
     terms = sent_terms(plan, mine, partners, out_weight)
     weight_part = after(jnp.concatenate(weight_parts), partner_first)
     weight_two = [weight_part, swap_weight(weight_part)]
+    far_two = [core_swap(x) for x in weight_two]
+    later = after(plan, far_two)
     steps = []
     for step in range(1, stages):
         row = []
         for chain, gated in enumerate((mine, partners)):
-            row.append(next_step(plan, step, chain, gated, terms, got[-1][chain]))
+            row.append(next_step(later if chain and step == 3 else plan, step, chain, gated, terms, got[-1][chain]))
         steps.append(row)
         got.append([onward(x) for x in row])
 
-    weights = gather_weight(weight_two, steps[2][0])
+    near_two = swap_other(weight_two)
+    weights = weight_two + near_two + far_two
+    weights += [core_swap(x) for x in after(near_two, steps[2][0])]
     arrivals = [got[0][0], got[1][0], got[0][1], got[1][1]]
     early, own = early_sum(order, mine, arrivals, out_weight, weights)
     theirs = partner_sum(after(order, got[3][0]), early, [got[2][1], got[3][1]], weights)

time: 134 us -> 134 us (level)
    ppermute x6 -> x2, starting transfers between devices: 3.6 us -> 2.53 us  [swap_other(): return [lax.ppermute(x, 'ctx', other) for x in two]]
  transfers between devices with their start and end apart: 32 -> 32, of which waited for: 14 -> 15; matrix products, arithmetic and copies ran while one was open for 4% -> 4% of each run, Pallas kernels for 28% -> 28%
where the time goes in v8:
time: 134 us
  starting transfers between devices  55.9 us (42%)
  Pallas kernels  43.2 us (32%)
  waiting for transfers between devices  27 us (20%)
  local copies, waits for them, and re-layouts  3.8 us (3%)
  other arithmetic  2.55 us (2%)
    ppermute x8, starting transfers between devices, project(): onward = lambda x: lax.ppermute(x, ('ctx', 'tp'), route)  29.8 us
    ppermute x9, starting transfers between devices, fast_per_device(): lax.ppermute(x, 'ctx', [(i, i ^ 2 * q + 2) for i in devices])  14.4 us
    pallas_call x1, Pallas kernels, long_conv(): pl.pallas_call(partial(conv_kernel, blocks), out_shape=jax.ShapeDtypeStru...  12.2 us
    ppermute x9, waiting for transfers between devices, fast_per_device(): lax.ppermute(x, 'ctx', [(i, i ^ 2 * q + 2) for i in devices])  11.5 us
    ppermute x8, waiting for transfers between devices, project(): onward = lambda x: lax.ppermute(x, ('ctx', 'tp'), route)  10.8 us
    pallas_call x1, Pallas kernels, taps_spectra_of(): pl.pallas_call(partial(taps_kernel, chips), out_shape=jax.ShapeDtypeStruc...  5.45 us
    pallas_call x1, Pallas kernels, gate_in(): pl.pallas_call(gate_in_kernel, in_specs=[SMEM, HBM, HBM, VMEM, VMEM], out...  4.26 us
    ppermute x2, starting transfers between devices, turn_weight(): found.append(lax.ppermute(part, ('ctx', 'tp'), route))  4.17 us
  transfers between devices with their start and end apart: 32, of which 15 were waited for; matrix products, arithmetic and copies ran while one was open for 4% of the time, Pallas kernels for 28%

profile of v8, /device:TPU:0, one launch (start us, length us, event | category | flops | bytes accessed | tf_op | source)
XLA Modules:
  0.0 133.7 jit_solution(2460074122413154172)
XLA Ops:
  0.0 1.5 %rims.1 = bf16[6,1024]{1,0:T(8,128)(2,1)} custom-call(bf16[512,1024]{1,0:T(8,128)(2,1)} %query.3, bf16[512,1024]{1,0:T(8,128)(2,1)} %key.3, bf16[512,1024]{1,0:T(8,128)(2,1)} %value.3), custom_call_target="tpu_custom_call" | custom-call | tf_op jit(solution)/shard_map/rims/pallas_call | solution.py:427
  1.5 2.4 %collective-permute-start = (bf16[6,1024]{1,0:T(8,128)(2,1)}, bf16[6,1024]{1,0:T(8,128)(2,1)S(1)}, u32[]{:S(2)}, u32[]{:S(2)}) collective-permute-start(bf16[6,1024]{1,0:T(8,128)(2,1)} %rims.1), channel_id=1, source_target_pairs={{0,4},{4,8},{8,12},{12,16},{16,20},{20,24},{24,28},{1,5},{5,9},{9,... | collective-permute-start | bytes 36872 | tf_op jit(solution)/shard_map/ppermute | solution.py:18
  5.1 4.9 %collective-permute-start.1 = (bf16[256,512]{1,0:T(8,128)(2,1)S(1)}, bf16[256,512]{1,0:T(8,128)(2,1)S(1)}, u32[]{:S(2)}, u32[]{:S(2)}) collective-permute-start(bf16[256,512]{1,0:T(8,128)(2,1)S(1)} %get-tuple-element.48), channel_id=1, source_target_pairs={{0,8},{4,12},{8,0},{12,4},{16,24},{20,28},{24,16},{28,20},{1,9},{5... | collective-permute-start | bytes 786440 | tf_op jit(solution)/shard_map/ppermute | solution.py:1019
  10.0 1.5 %collective-permute-start.2 = (bf16[256,512]{1,0:T(8,128)(2,1)S(1)}, bf16[256,512]{1,0:T(8,128)(2,1)S(1)}, u32[]{:S(2)}, u32[]{:S(2)}) collective-permute-start(bf16[256,512]{1,0:T(8,128)(2,1)S(1)} %get-tuple-element.49), channel_id=1, source_target_pairs={{0,16},{4,20},{8,24},{12,28},{16,0},{20,4},{24,8},{28,12},{1,17},{... | collective-permute-start | bytes 786440 | tf_op jit(solution)/shard_map/ppermute | solution.py:1019
  11.5 0.9 collective-permute-start.3
  13.0 2.7 %weight_corners.1 = (bf16[256,1024]{1,0:T(8,128)(2,1)}, bf16[128,1024]{1,0:T(8,128)(2,1)}) custom-call(s32[4]{0:T(128)} %pad_add_fusion.1.corners, bf16[1024,4096]{1,0:T(8,128)(2,1)} %weight.9), custom_call_target="tpu_custom_call" | custom-call | tf_op jit(solution)/shard_map/weight_corners/pallas_call | solution.py:752
  15.7 4.3 %gate_in.1 = (bf16[512,128]{1,0:T(8,128)(2,1)}, bf16[3,512,128]{2,1,0:T(8,128)(2,1)}, bf16[4,512,128]{2,1,0:T(8,128)(2,1)}) custom-call(s32[1]{0:T(128)} %bitcast.me_ref, bf16[512,1024]{1,0:T(8,128)(2,1)} %key.3, bf16[512,1024]{1,0:T(8,128)(2,1)} %value.3, bf16[6,1024]{1,0:T(8,128)(2,1)} %copy-done.5, f32[3,3,1024]{2,1,0:T(4,128)} %weight.7), custom_call_target="tpu_custom_call" | custom-call | tf_op jit(solution)/shard_map/gate_in/pallas_call | solution.py:478
  20.1 2.7 %collective-permute-done.2.refs_2_ = bf16[256,512]{1,0:T(8,128)(2,1)S(1)} collective-permute-done((bf16[256,512]{1,0:T(8,128)(2,1)S(1)}, bf16[256,512]{1,0:T(8,128)(2,1)S(1)}, u32[]{:S(2)}, u32[]{:S(2)}) %collective-permute-start.2) | collective-permute-done | bytes 262176 | tf_op jit(solution)/shard_map/ppermute | solution.py:1019
  23.0 1.0 copy-done.3
  24.7 1.5 %collective-permute-start.9 = (bf16[2,512,128]{2,1,0:T(8,128)(2,1)S(1)}, bf16[2,512,128]{2,1,0:T(8,128)(2,1)S(1)}, u32[]{:S(2)}, u32[]{:S(2)}) collective-permute-start(bf16[2,512,128]{2,1,0:T(8,128)(2,1)S(1)} %get-tuple-element.59), channel_id=1, source_target_pairs={{0,16},{4,20},{8,24},{12,28},{16,0},{20,4},{24,8},{28,12},{1,17},{... | collective-permute-start | bytes 786440 | tf_op jit(solution)/shard_map/ppermute | solution.py:1019
  26.2 1.4 %collective-permute-start.10 = (bf16[2,512,128]{2,1,0:T(8,128)(2,1)S(1)}, bf16[2,512,128]{2,1,0:T(8,128)(2,1)S(1)}, u32[]{:S(2)}, u32[]{:S(2)}) collective-permute-start(bf16[2,512,128]{2,1,0:T(8,128)(2,1)S(1)} %get-tuple-element.60), channel_id=1, source_target_pairs={{0,24},{4,28},{8,16},{12,20},{16,8},{20,12},{24,0},{28,4},{1,25},{... | collective-permute-start | bytes 786440 | tf_op jit(solution)/shard_map/ppermute | solution.py:1019
  27.6 2.6 %collective-permute-start.6 = (bf16[128,1024]{1,0:T(8,128)(2,1)}, bf16[128,1024]{1,0:T(8,128)(2,1)S(1)}, u32[]{:S(2)}, u32[]{:S(2)}) collective-permute-start(bf16[128,1024]{1,0:T(8,128)(2,1)} %get-tuple-element.52), channel_id=1, source_target_pairs={{0,2},{1,3},{2,0},{3,1},{4,6},{5,7},{6,4},{7,5},{8,10},{9,11},{10,... | collective-permute-start | bytes 786440 | tf_op jit(solution)/shard_map/ppermute | solution.py:731
  30.2 1.6 %collective-permute-start.5 = (bf16[256,1024]{1,0:T(8,128)(2,1)}, bf16[256,1024]{1,0:T(8,128)(2,1)}, u32[]{:S(2)}, u32[]{:S(2)}) collective-permute-start(bf16[256,1024]{1,0:T(8,128)(2,1)} %get-tuple-element.51), channel_id=1, source_target_pairs={{0,1},{1,2},{2,3},{3,0},{4,7},{5,4},{6,5},{7,6},{8,9},{9,10},{10,1... | collective-permute-start | bytes 1572872 | tf_op jit(solution)/shard_map/ppermute | solution.py:731
  31.8 5.5 %taps_spectra.1.refs_3_ = f32[17,256,256]{2,1,0:T(8,128)S(1)} custom-call(s32[1]{0:T(128)} %bitcast.me_ref, bf16[256,512]{1,0:T(8,128)(2,1)S(1)} %get-tuple-element.47.refs_0_, bf16[256,512]{1,0:T(8,128)(2,1)S(1)} %collective-permute-done.1.refs_1_, bf16[256,512]{1,0:T(8,128)(2,1)S(1)} %collective-permute-done.2.refs_2_, ...), custom_call_target="tpu_custom_call" | custom-call | flops 8000000000 | tf_op jit(solution)/shard_map/taps_spectra/pallas_call | solution.py:356
  37.8 0.9 collective-permute-done.10.refs_2_
  38.7 12.2 %long_conv.1.conv = f32[4096,128]{1,0:T(8,128)S(1)} custom-call(s32[1]{0:T(128)} %bitcast.me_ref, bf16[512,128]{1,0:T(8,128)(2,1)S(1)} %copy-done.7, bf16[4,512,128]{2,1,0:T(8,128)(2,1)S(1)} %collective-permute-done.7.swapped, bf16[2,512,128]{2,1,0:T(8,128)(2,1)S(1)} %collective-permute-done.8.refs_0_, ...), custom_call_target="tpu_custom_call" | custom-call | flops 20000000000 | tf_op jit(solution)/shard_map/long_conv/pallas_call | solution.py:375
  51.2 1.9 %collective-permute-done.11.swapped.refs_1_ = bf16[4,512,128]{2,1,0:T(8,128)(2,1)S(1)} collective-permute-done((bf16[4,512,128]{2,1,0:T(8,128)(2,1)S(1)}, bf16[4,512,128]{2,1,0:T(8,128)(2,1)S(1)}, u32[]{:S(2)}, u32[]{:S(2)}) %collective-permute-start.11) | collective-permute-done | bytes 524320 | tf_op jit(solution)/shard_map/ppermute | solution.py:1017
  53.2 1.6 %collective-permute-start.12 = (bf16[2,512,128]{2,1,0:T(8,128)(2,1)S(1)}, bf16[2,512,128]{2,1,0:T(8,128)(2,1)S(1)}, u32[]{:S(2)}, u32[]{:S(2)}) collective-permute-start(bf16[2,512,128]{2,1,0:T(8,128)(2,1)S(1)} %get-tuple-element.64), channel_id=1, source_target_pairs={{0,8},{4,12},{8,0},{12,4},{16,24},{20,28},{24,16},{28,20},{1,9},{5... | collective-permute-start | bytes 786440 | tf_op jit(solution)/shard_map/ppermute | solution.py:1019
  54.7 0.8 collective-permute-start.13
  55.6 1.2 collective-permute-start.14
  58.1 1.9 %constant_dynamic-slice_fusion.refs_6_.far_weight = bf16[1024,1024]{1,0:T(8,128)(2,1)S(1)} fusion(bf16[1024,4096]{1,0:T(8,128)(2,1)} %weight.9, s32[]{:T(128)S(6)} %select_n.62), kind=kLoop, calls=%fused_computation.5 | loop fusion | bytes 4194308 | tf_op jit(solution)/shard_map/dynamic_slice | solution.py:960
  60.0 1.1 mix_query.1.refs_5_
  61.1 1.3 collective-permute-done.12.refs_2_
  62.4 6.0 %collective-permute-done.13.refs_3_ = bf16[2,512,128]{2,1,0:T(8,128)(2,1)S(1)} collective-permute-done((bf16[2,512,128]{2,1,0:T(8,128)(2,1)S(1)}, bf16[2,512,128]{2,1,0:T(8,128)(2,1)S(1)}, u32[]{:S(2)}, u32[]{:S(2)}) %collective-permute-start.13) | collective-permute-done | bytes 262176 | tf_op jit(solution)/shard_map/ppermute | solution.py:1019
  68.4 1.6 %gate_out.1 = (bf16[2,256,1024]{2,1,0:T(8,128)(2,1)S(1)}, bf16[256,1024]{1,0:T(8,128)(2,1)S(1)}) custom-call(s32[3]{0:T(128)S(1)} %pad_add_fusion.spot, bf16[512,128]{1,0:T(8,128)(2,1)S(1)} %get-tuple-element.61.refs_0_, bf16[4,512,128]{2,1,0:T(8,128)(2,1)S(1)} %collective-permute-done.11.swapped.refs_1_, ...), custom_call_target="tpu_custom_call" | custom-call | tf_op jit(solution)/shard_map/gate_out/pallas_call | solution.py:620
  70.1 3.7 %collective-permute-start.15 = (bf16[256,1024]{1,0:T(8,128)(2,1)S(1)}, bf16[256,1024]{1,0:T(8,128)(2,1)S(1)}, u32[]{:S(2)}, u32[]{:S(2)}) collective-permute-start(bf16[256,1024]{1,0:T(8,128)(2,1)S(1)} %get-tuple-element.68), channel_id=1, source_target_pairs={{0,1},{1,2},{2,3},{5,4},{6,5},{7,6},{8,9},{9,10},{10,11},{13,12},{... | collective-permute-start | bytes 1572872 | tf_op jit(solution)/shard_map/ppermute | solution.py:968
  73.8 1.1 pad_maximum_fusion.refs_0_
  75.0 1.3 partner_sent.1
  76.2 3.7 %collective-permute-start.18 = (bf16[256,1024]{1,0:T(8,128)(2,1)S(1)}, bf16[256,1024]{1,0:T(8,128)(2,1)S(1)}, u32[]{:S(2)}, u32[]{:S(2)}) collective-permute-start(bf16[256,1024]{1,0:T(8,128)(2,1)S(1)} %partner_sent.1), channel_id=1, source_target_pairs={{0,1},{1,2},{2,3},{5,4},{6,5},{7,6},{8,9},{9,10},{10,11},{13,12},{... | collective-permute-start | bytes 1572872 | tf_op jit(solution)/shard_map/ppermute | solution.py:968
  80.0 1.5 %collective-permute-start.20 = (bf16[384,1024]{1,0:T(8,128)(2,1)S(1)}, bf16[384,1024]{1,0:T(8,128)(2,1)S(1)}, u32[]{:S(2)}, u32[]{:S(2)}) collective-permute-start(bf16[384,1024]{1,0:T(8,128)(2,1)S(1)} %pad_maximum_fusion.refs_0_), channel_id=1, source_target_pairs={{0,8},{4,20},{8,0},{12,28},{16,24},{20,4},{24,16},{28,12},{1,9},{5... | collective-permute-start | bytes 2359304 | tf_op jit(solution)/shard_map/ppermute | solution.py:765
  81.5 3.7 %sent_terms.1.term = bf16[2,2,256,1024]{3,2,1,0:T(8,128)(2,1)S(1)} custom-call(s32[5]{0:T(128)S(1)} %or_select_fusion.plan, bf16[2,256,1024]{2,1,0:T(8,128)(2,1)S(1)} %get-tuple-element.67.mine.head, bf16[2,256,1024]{2,1,0:T(8,128)(2,1)S(1)} %collective-permute-done.16.partners.gated.head, bf16[1024,4096]{1,0:T(8,128)(2,1)S(1)} %bitcast.20), custom_call_target="tpu_custom_call" | custom-call | flops 4000000000 | tf_op jit(solution)/shard_map/sent_terms/pallas_call | solution.py:701
  85.8 2.0 %collective-permute-start.17 = (bf16[256,1024]{1,0:T(8,128)(2,1)S(1)}, bf16[256,1024]{1,0:T(8,128)(2,1)S(1)}, u32[]{:S(2)}, u32[]{:S(2)}) collective-permute-start(bf16[256,1024]{1,0:T(8,128)(2,1)S(1)} %next_step.6), channel_id=1, source_target_pairs={{0,1},{1,2},{2,3},{5,4},{6,5},{7,6},{8,9},{9,10},{10,11},{13,12},{... | collective-permute-start | bytes 1572872 | tf_op jit(solution)/shard_map/ppermute | solution.py:968
  88.4 3.4 %collective-permute-start.19 = (bf16[256,1024]{1,0:T(8,128)(2,1)S(1)}, bf16[256,1024]{1,0:T(8,128)(2,1)S(1)}, u32[]{:S(2)}, u32[]{:S(2)}) collective-permute-start(bf16[256,1024]{1,0:T(8,128)(2,1)S(1)} %next_step.7), channel_id=1, source_target_pairs={{0,1},{1,2},{2,3},{5,4},{6,5},{7,6},{8,9},{9,10},{10,11},{13,12},{... | collective-permute-start | bytes 1572872 | tf_op jit(solution)/shard_map/ppermute | solution.py:968
  91.9 1.6 %collective-permute-start.21 = (bf16[384,1024]{1,0:T(8,128)(2,1)S(1)}, bf16[384,1024]{1,0:T(8,128)(2,1)S(1)}, u32[]{:S(2)}, u32[]{:S(2)}) collective-permute-start(bf16[384,1024]{1,0:T(8,128)(2,1)S(1)} %pad_maximum_fusion.refs_0_), channel_id=1, source_target_pairs={{0,16},{4,12},{8,24},{12,4},{16,0},{20,28},{24,8},{28,20},{1,17},{... | collective-permute-start | bytes 2359304 | tf_op jit(solution)/shard_map/ppermute | solution.py:771
  93.5 0.9 collective-permute-start.22
  95.2 4.3 %collective-permute-start.25 = (bf16[256,1024]{1,0:T(8,128)(2,1)S(1)}, bf16[256,1024]{1,0:T(8,128)(2,1)S(1)}, u32[]{:S(2)}, u32[]{:S(2)}) collective-permute-start(bf16[256,1024]{1,0:T(8,128)(2,1)S(1)} %next_step.8), channel_id=1, source_target_pairs={{0,1},{1,2},{2,3},{5,4},{6,5},{7,6},{8,9},{9,10},{10,11},{13,12},{... | collective-permute-start | bytes 1572872 | tf_op jit(solution)/shard_map/ppermute | solution.py:968
  100.8 5.4 %collective-permute-done.25.got.got2 = bf16[256,1024]{1,0:T(8,128)(2,1)S(1)} collective-permute-done((bf16[256,1024]{1,0:T(8,128)(2,1)S(1)}, bf16[256,1024]{1,0:T(8,128)(2,1)S(1)}, u32[]{:S(2)}, u32[]{:S(2)}) %collective-permute-start.25) | collective-permute-done | bytes 524320 | tf_op jit(solution)/shard_map/ppermute | solution.py:968
  106.2 4.4 %collective-permute-start.29 = (bf16[256,1024]{1,0:T(8,128)(2,1)S(1)}, bf16[256,1024]{1,0:T(8,128)(2,1)S(1)}, u32[]{:S(2)}, u32[]{:S(2)}) collective-permute-start(bf16[256,1024]{1,0:T(8,128)(2,1)S(1)} %next_step.10), channel_id=1, source_target_pairs={{0,1},{1,2},{2,3},{5,4},{6,5},{7,6},{8,9},{9,10},{10,11},{13,12},{... | collective-permute-start | bytes 1572872 | tf_op jit(solution)/shard_map/ppermute | solution.py:968
  111.3 1.1 collective-permute-done.22.refs_3_
  112.9 3.8 %collective-permute-start.28 = (bf16[256,1024]{1,0:T(8,128)(2,1)S(1)}, bf16[256,1024]{1,0:T(8,128)(2,1)S(1)}, u32[]{:S(2)}, u32[]{:S(2)}) collective-permute-start(bf16[256,1024]{1,0:T(8,128)(2,1)S(1)} %next_step.9), channel_id=1, source_target_pairs={{0,1},{1,2},{2,3},{5,4},{6,5},{7,6},{8,9},{9,10},{10,11},{13,12},{... | collective-permute-start | bytes 1572872 | tf_op jit(solution)/shard_map/ppermute | solution.py:968
  117.9 4.4 %collective-permute-start.30 = (bf16[256,1024]{1,0:T(8,128)(2,1)S(1)}, bf16[256,1024]{1,0:T(8,128)(2,1)S(1)}, u32[]{:S(2)}, u32[]{:S(2)}) collective-permute-start(bf16[256,1024]{1,0:T(8,128)(2,1)S(1)} %next_step.11), channel_id=1, source_target_pairs={{0,1},{1,2},{2,3},{5,4},{6,5},{7,6},{8,9},{9,10},{10,11},{13,12},{... | collective-permute-start | bytes 1572872 | tf_op jit(solution)/shard_map/ppermute | solution.py:968
  122.3 1.0 collective-permute-done.28.got3
  123.3 2.3 %early_sum.1 = (f32[512,1024]{1,0:T(8,128)S(1)}, f32[256,1024]{1,0:T(8,128)S(1)}) custom-call(s32[10]{0:T(128)S(1)} %stack.63.order, bf16[2,256,1024]{2,1,0:T(8,128)(2,1)S(1)} %get-tuple-element.67.mine.head, bf16[256,1024]{1,0:T(8,128)(2,1)S(1)} %collective-permute-done.15.got.got0, bf16[256,1024]{1,0:T(8,128)(2,1)S(1)} %collective-permute-done.17.got.got1, ...), custom_call_target="tpu_custom_call" | custom-call | flops 1000000000 | tf_op jit(solution)/shard_map/early_sum/pallas_call | solution.py:828
  125.7 3.3 %collective-permute-done.30.got3 = bf16[256,1024]{1,0:T(8,128)(2,1)S(1)} collective-permute-done((bf16[256,1024]{1,0:T(8,128)(2,1)S(1)}, bf16[256,1024]{1,0:T(8,128)(2,1)S(1)}, u32[]{:S(2)}, u32[]{:S(2)}) %collective-permute-start.30) | collective-permute-done | bytes 524320 | tf_op jit(solution)/shard_map/ppermute | solution.py:968
  129.0 0.8 partner_sum.1
  130.1 0.9 mine_sum.1.mine
  131.0 1.5 %collective-permute-done.31.partners = bf16[2,256,1024]{2,1,0:T(8,128)(2,1)S(1)} collective-permute-done((bf16[2,256,1024]{2,1,0:T(8,128)(2,1)S(1)}, bf16[2,256,1024]{2,1,0:T(8,128)(2,1)S(1)}, u32[]{:S(2)}, u32[]{:S(2)}) %collective-permute-start.31) | collective-permute-done | bytes 1048608 | tf_op jit(solution)/shard_map/ppermute | solution.py:969
  132.5 1.1 join_sums.1
  (79 shorter events, 10.2 us)
Async XLA Ops:
  0.0 22.9 %copy-start = (f32[1024]{0:T(1024)S(1)}, f32[1024]{0:T(1024)}, u32[]{:S(2)}) copy-start(f32[1024]{0:T(1024)} %param.15) | copy-start | bytes 12292
  0.0 4.9 %copy-start.2 = (bf16[1024,512]{1,0:T(8,128)(2,1)S(1)}, bf16[1024,512]{1,0:T(8,128)(2,1)}, u32[]{:S(2)}) copy-start(bf16[1024,512]{1,0:T(8,128)(2,1)} %taps.1) | copy-start | bytes 3145732
  1.5 3.4 %collective-permute-start = (bf16[6,1024]{1,0:T(8,128)(2,1)}, bf16[6,1024]{1,0:T(8,128)(2,1)S(1)}, u32[]{:S(2)}, u32[]{:S(2)}) collective-permute-start(bf16[6,1024]{1,0:T(8,128)(2,1)} %rims.1), channel_id=1, source_target_pairs={{0,4},{4,8},{8,12},{12,16},{16,20},{20,24},{24,28},{1,5},{5,9},{9,... | collective-permute-start | bytes 36872 | tf_op jit(solution)/shard_map/ppermute | solution.py:18
  4.9 10.8 %copy-start.5 = (bf16[6,1024]{1,0:T(8,128)(2,1)}, bf16[6,1024]{1,0:T(8,128)(2,1)S(1)}, u32[]{:S(2)}) copy-start(bf16[6,1024]{1,0:T(8,128)(2,1)S(1)} %collective-permute-done.edges) | copy-start | bytes 36868
  5.1 15.0 %collective-permute-start.1 = (bf16[256,512]{1,0:T(8,128)(2,1)S(1)}, bf16[256,512]{1,0:T(8,128)(2,1)S(1)}, u32[]{:S(2)}, u32[]{:S(2)}) collective-permute-start(bf16[256,512]{1,0:T(8,128)(2,1)S(1)} %get-tuple-element.48), channel_id=1, source_target_pairs={{0,8},{4,12},{8,0},{12,4},{16,24},{20,28},{24,16},{28,20},{1,9},{5... | collective-permute-start | bytes 786440 | tf_op jit(solution)/shard_map/ppermute | solution.py:1019
  10.0 12.9 %collective-permute-start.2 = (bf16[256,512]{1,0:T(8,128)(2,1)S(1)}, bf16[256,512]{1,0:T(8,128)(2,1)S(1)}, u32[]{:S(2)}, u32[]{:S(2)}) collective-permute-start(bf16[256,512]{1,0:T(8,128)(2,1)S(1)} %get-tuple-element.49), channel_id=1, source_target_pairs={{0,16},{4,20},{8,24},{12,28},{16,0},{20,4},{24,8},{28,12},{1,17},{... | collective-permute-start | bytes 786440 | tf_op jit(solution)/shard_map/ppermute | solution.py:1019
  11.5 11.3 %collective-permute-start.3 = (bf16[256,512]{1,0:T(8,128)(2,1)S(1)}, bf16[256,512]{1,0:T(8,128)(2,1)S(1)}, u32[]{:S(2)}, u32[]{:S(2)}) collective-permute-start(bf16[256,512]{1,0:T(8,128)(2,1)S(1)} %get-tuple-element.50), channel_id=1, source_target_pairs={{0,24},{4,28},{8,16},{12,20},{16,8},{20,12},{24,0},{28,4},{1,25},{... | collective-permute-start | bytes 786440 | tf_op jit(solution)/shard_map/ppermute | solution.py:1019
  15.7 16.1 %copy-start.8 = (bf16[256,768]{1,0:T(8,128)(2,1)S(1)}, bf16[256,768]{1,0:T(8,128)(2,1)}, u32[]{:S(2)}) copy-start(bf16[256,768]{1,0:T(8,128)(2,1)} %constant.80.clone.refs_6_.refs_5_) | copy-start | bytes 1179652
  15.7 16.1 %copy-start.10 = (f32[128,66]{1,0:T(8,128)S(1)}, f32[128,66]{1,0:T(8,128)}, u32[]{:S(2)}) copy-start(f32[128,66]{1,0:T(8,128)} %constant.82.clone.refs_5_.refs_4_) | copy-start | bytes 101380
  20.0 3.0 %collective-permute-start.7 = (bf16[4,512,128]{2,1,0:T(8,128)(2,1)}, bf16[4,512,128]{2,1,0:T(8,128)(2,1)S(1)}, u32[]{:S(2)}, u32[]{:S(2)}) collective-permute-start(bf16[4,512,128]{2,1,0:T(8,128)(2,1)} %get-tuple-element.56), channel_id=1, source_target_pairs={{0,4},{4,0},{8,12},{12,8},{16,20},{20,16},{24,28},{28,24},{1,5},{5... | collective-permute-start | bytes 1572872 | tf_op jit(solution)/shard_map/ppermute | solution.py:1017
  22.9 4.8 %collective-permute-start.4 = (bf16[4,128,512]{2,1,0:T(8,128)(2,1)S(1)}, bf16[4,128,512]{2,1,0:T(8,128)(2,1)S(1)}, u32[]{:S(2)}, u32[]{:S(2)}) collective-permute-start(bf16[4,128,512]{2,1,0:T(8,128)(2,1)S(1)} %other_core.1), channel_id=1, source_target_pairs={{0,4},{4,0},{8,12},{12,8},{16,20},{20,16},{24,28},{28,24},{1,5},{5... | collective-permute-start | bytes 1572872 | tf_op jit(solution)/shard_map/ppermute | solution.py:1017
  23.0 1.0 copy-start.3
  24.1 13.2 %collective-permute-start.8 = (bf16[2,512,128]{2,1,0:T(8,128)(2,1)S(1)}, bf16[2,512,128]{2,1,0:T(8,128)(2,1)S(1)}, u32[]{:S(2)}, u32[]{:S(2)}) collective-permute-start(bf16[2,512,128]{2,1,0:T(8,128)(2,1)S(1)} %get-tuple-element.58), channel_id=1, source_target_pairs={{0,8},{4,12},{8,0},{12,4},{16,24},{20,28},{24,16},{28,20},{1,9},{5... | collective-permute-start | bytes 786440 | tf_op jit(solution)/shard_map/ppermute | solution.py:1019
  24.7 13.1 %collective-permute-start.9 = (bf16[2,512,128]{2,1,0:T(8,128)(2,1)S(1)}, bf16[2,512,128]{2,1,0:T(8,128)(2,1)S(1)}, u32[]{:S(2)}, u32[]{:S(2)}) collective-permute-start(bf16[2,512,128]{2,1,0:T(8,128)(2,1)S(1)} %get-tuple-element.59), channel_id=1, source_target_pairs={{0,16},{4,20},{8,24},{12,28},{16,0},{20,4},{24,8},{28,12},{1,17},{... | collective-permute-start | bytes 786440 | tf_op jit(solution)/shard_map/ppermute | solution.py:1019
  26.2 12.5 %copy-start.7 = (bf16[512,128]{1,0:T(8,128)(2,1)S(1)}, bf16[512,128]{1,0:T(8,128)(2,1)}, u32[]{:S(2)}) copy-start(bf16[512,128]{1,0:T(8,128)(2,1)} %get-tuple-element.55.stay) | copy-start | bytes 393220
  26.2 12.5 %copy-start.9 = (bf16[256,768]{1,0:T(8,128)(2,1)S(1)}, bf16[256,768]{1,0:T(8,128)(2,1)}, u32[]{:S(2)}) copy-start(bf16[256,768]{1,0:T(8,128)(2,1)} %constant.81.clone.refs_6_) | copy-start | bytes 1179652
  26.2 12.5 %collective-permute-start.10 = (bf16[2,512,128]{2,1,0:T(8,128)(2,1)S(1)}, bf16[2,512,128]{2,1,0:T(8,128)(2,1)S(1)}, u32[]{:S(2)}, u32[]{:S(2)}) collective-permute-start(bf16[2,512,128]{2,1,0:T(8,128)(2,1)S(1)} %get-tuple-element.60), channel_id=1, source_target_pairs={{0,24},{4,28},{8,16},{12,20},{16,8},{20,12},{24,0},{28,4},{1,25},{... | collective-permute-start | bytes 786440 | tf_op jit(solution)/shard_map/ppermute | solution.py:1019
  27.6 23.3 %collective-permute-start.6 = (bf16[128,1024]{1,0:T(8,128)(2,1)}, bf16[128,1024]{1,0:T(8,128)(2,1)S(1)}, u32[]{:S(2)}, u32[]{:S(2)}) collective-permute-start(bf16[128,1024]{1,0:T(8,128)(2,1)} %get-tuple-element.52), channel_id=1, source_target_pairs={{0,2},{1,3},{2,0},{3,1},{4,6},{5,7},{6,4},{7,5},{8,10},{9,11},{10,... | collective-permute-start | bytes 786440 | tf_op jit(solution)/shard_map/ppermute | solution.py:731
  30.2 20.8 %collective-permute-start.5 = (bf16[256,1024]{1,0:T(8,128)(2,1)}, bf16[256,1024]{1,0:T(8,128)(2,1)}, u32[]{:S(2)}, u32[]{:S(2)}) collective-permute-start(bf16[256,1024]{1,0:T(8,128)(2,1)} %get-tuple-element.51), channel_id=1, source_target_pairs={{0,1},{1,2},{2,3},{3,0},{4,7},{5,4},{6,5},{7,6},{8,9},{9,10},{10,1... | collective-permute-start | bytes 1572872 | tf_op jit(solution)/shard_map/ppermute | solution.py:731
  51.0 5.8 %copy-start.11 = (bf16[128,1024]{1,0:T(8,128)(2,1)}, bf16[128,1024]{1,0:T(8,128)(2,1)S(1)}, u32[]{:S(2)}) copy-start(bf16[128,1024]{1,0:T(8,128)(2,1)S(1)} %collective-permute-done.6) | copy-start | bytes 786436
  51.0 9.0 %copy-start.1 = (bf16[512,1024]{1,0:T(8,128)(2,1)S(1)}, bf16[512,1024]{1,0:T(8,128)(2,1)}, u32[]{:S(2)}) copy-start(bf16[512,1024]{1,0:T(8,128)(2,1)} %query.3) | copy-start | bytes 3145732
  51.0 9.0 %copy-start.4 = (f32[3,3,1024]{2,1,0:T(4,128)S(1)}, f32[3,3,1024]{2,1,0:T(4,128)}, u32[]{:S(2)}) copy-start(f32[3,3,1024]{2,1,0:T(4,128)} %weight.7) | copy-start | bytes 110596
  51.0 9.0 %copy-start.6 = (bf16[6,1024]{1,0:T(8,128)(2,1)S(1)}, bf16[6,1024]{1,0:T(8,128)(2,1)}, u32[]{:S(2)}) copy-start(bf16[6,1024]{1,0:T(8,128)(2,1)} %copy-done.5) | copy-start | bytes 36868
  51.2 2.0 %collective-permute-start.11 = (bf16[4,512,128]{2,1,0:T(8,128)(2,1)S(1)}, bf16[4,512,128]{2,1,0:T(8,128)(2,1)S(1)}, u32[]{:S(2)}, u32[]{:S(2)}) collective-permute-start(bf16[4,512,128]{2,1,0:T(8,128)(2,1)S(1)} %get-tuple-element.62), channel_id=1, source_target_pairs={{0,4},{4,0},{8,12},{12,8},{16,20},{20,16},{24,28},{28,24},{1,5},{5... | collective-permute-start | bytes 1572872 | tf_op jit(solution)/shard_map/ppermute | solution.py:1017
  53.2 9.2 %collective-permute-start.12 = (bf16[2,512,128]{2,1,0:T(8,128)(2,1)S(1)}, bf16[2,512,128]{2,1,0:T(8,128)(2,1)S(1)}, u32[]{:S(2)}, u32[]{:S(2)}) collective-permute-start(bf16[2,512,128]{2,1,0:T(8,128)(2,1)S(1)} %get-tuple-element.64), channel_id=1, source_target_pairs={{0,8},{4,12},{8,0},{12,4},{16,24},{20,28},{24,16},{28,20},{1,9},{5... | collective-permute-start | bytes 786440 | tf_op jit(solution)/shard_map/ppermute | solution.py:1019
  54.7 13.7 %collective-permute-start.13 = (bf16[2,512,128]{2,1,0:T(8,128)(2,1)S(1)}, bf16[2,512,128]{2,1,0:T(8,128)(2,1)S(1)}, u32[]{:S(2)}, u32[]{:S(2)}) collective-permute-start(bf16[2,512,128]{2,1,0:T(8,128)(2,1)S(1)} %get-tuple-element.65), channel_id=1, source_target_pairs={{0,16},{4,20},{8,24},{12,28},{16,0},{20,4},{24,8},{28,12},{1,17},{... | collective-permute-start | bytes 786440 | tf_op jit(solution)/shard_map/ppermute | solution.py:1019
  55.6 12.9 %collective-permute-start.14 = (bf16[2,512,128]{2,1,0:T(8,128)(2,1)S(1)}, bf16[2,512,128]{2,1,0:T(8,128)(2,1)S(1)}, u32[]{:S(2)}, u32[]{:S(2)}) collective-permute-start(bf16[2,512,128]{2,1,0:T(8,128)(2,1)S(1)} %get-tuple-element.66), channel_id=1, source_target_pairs={{0,24},{4,28},{8,16},{12,20},{16,8},{20,12},{24,0},{28,4},{1,25},{... | collective-permute-start | bytes 786440 | tf_op jit(solution)/shard_map/ppermute | solution.py:1019
  58.0 23.5 %slice-start = ((s8[8388608]{0:T(1024)(128)(4,1)}), s8[4194304]{0:T(1024)(128)(4,1)S(1)}, s32[]{:S(2)}) async-start(s8[8388608]{0:T(1024)(128)(4,1)} %bitcast.19), calls=%async_computation | async-start | bytes 8388608
  68.4 5.4 %copy-start.12 = (bf16[128,1024]{1,0:T(8,128)(2,1)S(1)}, bf16[128,1024]{1,0:T(8,128)(2,1)}, u32[]{:S(2)}) copy-start(bf16[128,1024]{1,0:T(8,128)(2,1)} %copy-done.11) | copy-start | bytes 786436
  68.4 13.1 %slice-start.1 = ((s8[8388608]{0:T(1024)(128)(4,1)}), s8[4194304]{0:T(1024)(128)(4,1)S(1)}, s32[]{:S(2)}) async-start(s8[8388608]{0:T(1024)(128)(4,1)} %bitcast.19), calls=%async_computation.1 | async-start | bytes 8388608
  70.1 4.9 %collective-permute-start.16 = (bf16[2,256,1024]{2,1,0:T(8,128)(2,1)S(1)}, bf16[2,256,1024]{2,1,0:T(8,128)(2,1)S(1)}, u32[]{:S(2)}, u32[]{:S(2)}) collective-permute-start(bf16[2,256,1024]{2,1,0:T(8,128)(2,1)S(1)} %get-tuple-element.67.mine.head), channel_id=1, source_target_pairs={{0,4},{4,0},{8,12},{12,8},{16,20},{20,16},{24,28},{28,24},{1,5},{5... | collective-permute-start | bytes 3145736 | tf_op jit(solution)/shard_map/ppermute | solution.py:969
  70.1 15.1 %collective-permute-start.15 = (bf16[256,1024]{1,0:T(8,128)(2,1)S(1)}, bf16[256,1024]{1,0:T(8,128)(2,1)S(1)}, u32[]{:S(2)}, u32[]{:S(2)}) collective-permute-start(bf16[256,1024]{1,0:T(8,128)(2,1)S(1)} %get-tuple-element.68), channel_id=1, source_target_pairs={{0,1},{1,2},{2,3},{5,4},{6,5},{7,6},{8,9},{9,10},{10,11},{13,12},{... | collective-permute-start | bytes 1572872 | tf_op jit(solution)/shard_map/ppermute | solution.py:968
  76.2 11.6 %collective-permute-start.18 = (bf16[256,1024]{1,0:T(8,128)(2,1)S(1)}, bf16[256,1024]{1,0:T(8,128)(2,1)S(1)}, u32[]{:S(2)}, u32[]{:S(2)}) collective-permute-start(bf16[256,1024]{1,0:T(8,128)(2,1)S(1)} %partner_sent.1), channel_id=1, source_target_pairs={{0,1},{1,2},{2,3},{5,4},{6,5},{7,6},{8,9},{9,10},{10,11},{13,12},{... | collective-permute-start | bytes 1572872 | tf_op jit(solution)/shard_map/ppermute | solution.py:968
  80.0 13.5 %collective-permute-start.20 = (bf16[384,1024]{1,0:T(8,128)(2,1)S(1)}, bf16[384,1024]{1,0:T(8,128)(2,1)S(1)}, u32[]{:S(2)}, u32[]{:S(2)}) collective-permute-start(bf16[384,1024]{1,0:T(8,128)(2,1)S(1)} %pad_maximum_fusion.refs_0_), channel_id=1, source_target_pairs={{0,8},{4,20},{8,0},{12,28},{16,24},{20,4},{24,16},{28,12},{1,9},{5... | collective-permute-start | bytes 2359304 | tf_op jit(solution)/shard_map/ppermute | solution.py:765
  85.8 8.7 %collective-permute-start.17 = (bf16[256,1024]{1,0:T(8,128)(2,1)S(1)}, bf16[256,1024]{1,0:T(8,128)(2,1)S(1)}, u32[]{:S(2)}, u32[]{:S(2)}) collective-permute-start(bf16[256,1024]{1,0:T(8,128)(2,1)S(1)} %next_step.6), channel_id=1, source_target_pairs={{0,1},{1,2},{2,3},{5,4},{6,5},{7,6},{8,9},{9,10},{10,11},{13,12},{... | collective-permute-start | bytes 1572872 | tf_op jit(solution)/shard_map/ppermute | solution.py:968
  88.4 11.7 %collective-permute-start.19 = (bf16[256,1024]{1,0:T(8,128)(2,1)S(1)}, bf16[256,1024]{1,0:T(8,128)(2,1)S(1)}, u32[]{:S(2)}, u32[]{:S(2)}) collective-permute-start(bf16[256,1024]{1,0:T(8,128)(2,1)S(1)} %next_step.7), channel_id=1, source_target_pairs={{0,1},{1,2},{2,3},{5,4},{6,5},{7,6},{8,9},{9,10},{10,11},{13,12},{... | collective-permute-start | bytes 1572872 | tf_op jit(solution)/shard_map/ppermute | solution.py:968
  91.9 19.4 %collective-permute-start.21 = (bf16[384,1024]{1,0:T(8,128)(2,1)S(1)}, bf16[384,1024]{1,0:T(8,128)(2,1)S(1)}, u32[]{:S(2)}, u32[]{:S(2)}) collective-permute-start(bf16[384,1024]{1,0:T(8,128)(2,1)S(1)} %pad_maximum_fusion.refs_0_), channel_id=1, source_target_pairs={{0,16},{4,12},{8,24},{12,4},{16,0},{20,28},{24,8},{28,20},{1,17},{... | collective-permute-start | bytes 2359304 | tf_op jit(solution)/shard_map/ppermute | solution.py:771
  93.5 18.9 %collective-permute-start.22 = (bf16[384,1024]{1,0:T(8,128)(2,1)S(1)}, bf16[384,1024]{1,0:T(8,128)(2,1)S(1)}, u32[]{:S(2)}, u32[]{:S(2)}) collective-permute-start(bf16[384,1024]{1,0:T(8,128)(2,1)S(1)} %collective-permute-done.20.refs_1_), channel_id=1, source_target_pairs={{0,16},{4,12},{8,24},{12,4},{16,0},{20,28},{24,8},{28,20},{1,17},{... | collective-permute-start | bytes 2359304 | tf_op jit(solution)/shard_map/ppermute | solution.py:771
  95.2 11.0 %collective-permute-start.25 = (bf16[256,1024]{1,0:T(8,128)(2,1)S(1)}, bf16[256,1024]{1,0:T(8,128)(2,1)S(1)}, u32[]{:S(2)}, u32[]{:S(2)}) collective-permute-start(bf16[256,1024]{1,0:T(8,128)(2,1)S(1)} %next_step.8), channel_id=1, source_target_pairs={{0,1},{1,2},{2,3},{5,4},{6,5},{7,6},{8,9},{9,10},{10,11},{13,12},{... | collective-permute-start | bytes 1572872 | tf_op jit(solution)/shard_map/ppermute | solution.py:968
  99.5 13.4 %collective-permute-start.23 = (bf16[384,1024]{1,0:T(8,128)(2,1)S(1)}, bf16[384,1024]{1,0:T(8,128)(2,1)S(1)}, u32[]{:S(2)}, u32[]{:S(2)}) collective-permute-start(bf16[384,1024]{1,0:T(8,128)(2,1)S(1)} %pad_maximum_fusion.refs_0_), channel_id=1, source_target_pairs={{0,4},{4,0},{8,12},{12,8},{16,20},{20,16},{24,28},{28,24},{1,5},{5... | collective-permute-start | bytes 2359304 | tf_op jit(solution)/shard_map/ppermute | solution.py:969
  100.1 16.6 %collective-permute-start.24 = (bf16[384,1024]{1,0:T(8,128)(2,1)S(1)}, bf16[384,1024]{1,0:T(8,128)(2,1)S(1)}, u32[]{:S(2)}, u32[]{:S(2)}) collective-permute-start(bf16[384,1024]{1,0:T(8,128)(2,1)S(1)} %collective-permute-done.20.refs_1_), channel_id=1, source_target_pairs={{0,4},{4,0},{8,12},{12,8},{16,20},{20,16},{24,28},{28,24},{1,5},{5... | collective-permute-start | bytes 2359304 | tf_op jit(solution)/shard_map/ppermute | solution.py:969
  106.2 11.1 %collective-permute-start.29 = (bf16[256,1024]{1,0:T(8,128)(2,1)S(1)}, bf16[256,1024]{1,0:T(8,128)(2,1)S(1)}, u32[]{:S(2)}, u32[]{:S(2)}) collective-permute-start(bf16[256,1024]{1,0:T(8,128)(2,1)S(1)} %next_step.10), channel_id=1, source_target_pairs={{0,1},{1,2},{2,3},{5,4},{6,5},{7,6},{8,9},{9,10},{10,11},{13,12},{... | collective-permute-start | bytes 1572872 | tf_op jit(solution)/shard_map/ppermute | solution.py:968
  112.4 10.9 %collective-permute-start.26 = (bf16[384,1024]{1,0:T(8,128)(2,1)S(1)}, bf16[384,1024]{1,0:T(8,128)(2,1)S(1)}, u32[]{:S(2)}, u32[]{:S(2)}) collective-permute-start(bf16[384,1024]{1,0:T(8,128)(2,1)S(1)} %collective-permute-done.21.refs_2_), channel_id=1, source_target_pairs={{0,4},{4,0},{8,12},{12,8},{16,20},{20,16},{24,28},{28,24},{1,5},{5... | collective-permute-start | bytes 2359304 | tf_op jit(solution)/shard_map/ppermute | solution.py:969
  112.4 10.9 %collective-permute-start.27 = (bf16[384,1024]{1,0:T(8,128)(2,1)S(1)}, bf16[384,1024]{1,0:T(8,128)(2,1)S(1)}, u32[]{:S(2)}, u32[]{:S(2)}) collective-permute-start(bf16[384,1024]{1,0:T(8,128)(2,1)S(1)} %collective-permute-done.22.refs_3_), channel_id=1, source_target_pairs={{0,4},{4,0},{8,12},{12,8},{16,20},{20,16},{24,28},{28,24},{1,5},{5... | collective-permute-start | bytes 2359304 | tf_op jit(solution)/shard_map/ppermute | solution.py:969
  112.9 10.4 %collective-permute-start.28 = (bf16[256,1024]{1,0:T(8,128)(2,1)S(1)}, bf16[256,1024]{1,0:T(8,128)(2,1)S(1)}, u32[]{:S(2)}, u32[]{:S(2)}) collective-permute-start(bf16[256,1024]{1,0:T(8,128)(2,1)S(1)} %next_step.9), channel_id=1, source_target_pairs={{0,1},{1,2},{2,3},{5,4},{6,5},{7,6},{8,9},{9,10},{10,11},{13,12},{... | collective-permute-start | bytes 1572872 | tf_op jit(solution)/shard_map/ppermute | solution.py:968
  117.9 11.1 %collective-permute-start.30 = (bf16[256,1024]{1,0:T(8,128)(2,1)S(1)}, bf16[256,1024]{1,0:T(8,128)(2,1)S(1)}, u32[]{:S(2)}, u32[]{:S(2)}) collective-permute-start(bf16[256,1024]{1,0:T(8,128)(2,1)S(1)} %next_step.11), channel_id=1, source_target_pairs={{0,1},{1,2},{2,3},{5,4},{6,5},{7,6},{8,9},{9,10},{10,11},{13,12},{... | collective-permute-start | bytes 1572872 | tf_op jit(solution)/shard_map/ppermute | solution.py:968
  129.8 2.7 %collective-permute-start.31 = (bf16[2,256,1024]{2,1,0:T(8,128)(2,1)S(1)}, bf16[2,256,1024]{2,1,0:T(8,128)(2,1)S(1)}, u32[]{:S(2)}, u32[]{:S(2)}) collective-permute-start(bf16[2,256,1024]{2,1,0:T(8,128)(2,1)S(1)} %partner_sum.1), channel_id=1, source_target_pairs={{0,4},{4,0},{8,12},{12,8},{16,20},{20,16},{24,28},{28,24},{1,5},{5... | collective-permute-start | bytes 3145736 | tf_op jit(solution)/shard_map/ppermute | solution.py:969
